TPU v7x, 32 devices: a whole 2x2x4 slice. The times are simulated.
32 devices in a mesh: lon: 8 (over y, x, core), lat: 2 (over z_hi), lev: 2 (over z_lo).
Axes of the slice: x: 2, y: 2, z: 4 (z_hi: 2, z_lo: 2; z = z_hi * 2 + z_lo), core: 2. Of those that a mesh axis runs over, the one named last changes fastest.
Arguments:
- tokens: bfloat16 [4, 12, 96, 768], P('lev', 'lat', 'lon'), may hold values from -6 to 6
- packed_weight: bfloat16 [768, 2304], replicated, may hold values from -0.21875 to 0.21875
- output_weight: bfloat16 [768, 768], replicated, may hold values from -0.21875 to 0.21875
- norm_gain: float32 [768], replicated, may hold values from 0.25 to 1.75
- merge_gain: float32 [3072], replicated, may hold values from 0.25 to 1.75
- bias_table: float32 [2, 2, 24, 3312], P('lev', 'lat'), may hold values from -4 to 304
- bias_index: int32 [144, 144], replicated, may hold values from 0 to 3311
- row_labels: int32 [12], P('lat'), may hold values from 0 to 9, as said below
- column_valid: int32 [96], replicated, may hold values 0 or 1
- merged_grad: bfloat16 [4, 6, 48, 3072], P(None, 'lat', ('lon', 'lev')), may hold values from -6 to 6
Outputs:
- merged: bfloat16 [4, 6, 48, 3072], P(None, 'lat', ('lon', 'lev'))
- grad_tokens: bfloat16 [4, 12, 96, 768], P('lev', 'lat', 'lon')
Inputs may be any that keep to these rules, and one draw needn't show every extreme that they name: `row_labels`: labels never fall from one row to the next; the last 3 rows share a label that no other row has.
All inputs are finite; a program needn't handle non-finite values.
Results may differ from a plain program's by a relative error of at most 0.012.
Values may be sent and summed in bfloat16 or wider, within the bound.
No kernel may reach another device: no remote copies, remote signals or barrier semaphores. Data moves between devices by JAX's collectives and lax.ppermute only.
A program may use at most 64 MiB of HBM per device.

v0:
```python
import jax
import jax.numpy as jnp
from jax import lax
from jax.sharding import PartitionSpec as P

HEADS = 24
HEAD = 32
WLAT = 6
WLON = 12


epsilon = 1e-05


def from_behind(block, axis, distance):
    devices = range(lax.axis_size(axis))
    route = [((i - distance) % len(devices), i) for i in devices]
    return lax.ppermute(block, axis, route)


def norm_rows(values, gain):
    data = values.astype(jnp.float32)
    center = data - jnp.mean(data, axis=-1, keepdims=True)
    scale = lax.rsqrt(jnp.mean(center * center, axis=-1, keepdims=True) + epsilon)
    unit = center * scale
    return ((unit * gain).astype(jnp.bfloat16), unit, scale)


def norm_back(grad, gain, unit, scale):
    scaled = grad.astype(jnp.float32) * gain
    return scale * (
        scaled
        - jnp.mean(scaled, axis=-1, keepdims=True)
        - unit * jnp.mean(scaled * unit, axis=-1, keepdims=True)
    )


def project(values, weight):
    flat = values.reshape(-1, values.shape[-1])
    product = jnp.dot(flat, weight, preferred_element_type=jnp.float32)
    return product.astype(jnp.bfloat16).reshape(values.shape[:-1] + (weight.shape[1],))


def project_back(values, weight):
    flat = values.reshape(-1, values.shape[-1])
    product = lax.dot_general(
        flat, weight, (((1,), (1,)), ((), ())), preferred_element_type=jnp.float32
    )
    return product.astype(jnp.bfloat16).reshape(values.shape[:-1] + (weight.shape[0],))


def to_windows(grid):
    levels, lines, columns, width = grid.shape
    parts = grid.reshape(levels, lines // WLAT, WLAT, columns // WLON, WLON, width)
    parts = parts.transpose(1, 3, 0, 2, 4, 5)
    return parts.reshape(-1, levels * WLAT * WLON, width)


def from_windows(blocks, levels, lines, columns):
    width = blocks.shape[-1]
    parts = blocks.reshape(lines // WLAT, columns // WLON, levels, WLAT, WLON, width)
    return parts.transpose(2, 0, 3, 1, 4, 5).reshape(levels, lines, columns, width)


def window_masks(labels, valid, levels):
    lines, columns = (labels.shape[0], valid.shape[0])
    window = levels * WLAT * WLON
    label_grid = jnp.broadcast_to(
        labels.reshape(lines // WLAT, 1, WLAT, 1), (lines // WLAT, levels, WLAT, WLON)
    ).reshape(lines // WLAT, 1, window)
    valid_grid = jnp.broadcast_to(
        valid.reshape(columns // WLON, 1, 1, WLON), (columns // WLON, levels, WLAT, WLON)
    ).reshape(1, columns // WLON, window)
    same = label_grid[:, :, :, None] == label_grid[:, :, None, :]
    keep = (valid_grid[:, :, None, :] > 0) | jnp.eye(window, dtype=bool)
    return (same & keep).reshape(-1, window, window)


def merge_cells(grid):
    levels, lines, columns, width = grid.shape
    parts = grid.reshape(levels, lines // 2, 2, columns // 2, 2, width).transpose(0, 1, 3, 4, 2, 5)
    return parts.reshape(levels, lines // 2, columns // 2, 4 * width)


def split_cells(cells):
    levels, lines, columns, width = cells.shape
    parts = cells.reshape(levels, lines, columns, 2, 2, width // 4).transpose(0, 1, 4, 2, 3, 5)
    return parts.reshape(levels, lines * 2, columns * 2, width // 4)


def roll_grid(grid, sign):
    half_lines = WLAT // 2
    if sign < 0:
        rim, rest = (grid[:, :half_lines], grid[:, half_lines:])
    else:
        rim, rest = (grid[:, -half_lines:], grid[:, :-half_lines])
    moved = from_behind(rim, "lat", sign)
    if sign < 0:
        grid = jnp.concatenate((rest, moved), axis=1)
    else:
        grid = jnp.concatenate((moved, rest), axis=1)
    half_columns = WLON // 2
    if sign < 0:
        rim, rest = (grid[:, :, :half_columns], grid[:, :, half_columns:])
    else:
        rim, rest = (grid[:, :, -half_columns:], grid[:, :, :-half_columns])
    moved = from_behind(rim, "lon", sign)
    if sign < 0:
        return jnp.concatenate((rest, moved), axis=2)
    return jnp.concatenate((moved, rest), axis=2)


def send_coarse(cells):
    return lax.all_to_all(cells, "lev", split_axis=2, concat_axis=0, tiled=True)


def return_coarse(cells):
    return lax.all_to_all(cells, "lev", split_axis=0, concat_axis=2, tiled=True)


def attend(triple, masked_bias):
    count, window = (triple.shape[0], triple.shape[1])
    parts = triple.reshape(count, window, 3, HEADS, HEAD)
    query, key, value = (parts[:, :, 0], parts[:, :, 1], parts[:, :, 2])
    scores = (
        jnp.einsum("wqhd,wkhd->whqk", query, key, preferred_element_type=jnp.float32)
        * HEAD ** (-0.5)
        + masked_bias
    )
    peak = jnp.max(scores, axis=-1, keepdims=True)
    raised = jnp.exp(scores - peak)
    weights = raised / jnp.sum(raised, axis=-1, keepdims=True)
    rounded = weights.astype(jnp.bfloat16)
    heads = jnp.einsum("whqk,wkhd->wqhd", rounded, value, preferred_element_type=jnp.float32)
    heads = heads.astype(jnp.bfloat16).reshape(count, window, HEADS * HEAD)
    return (heads, (query, key, value, weights, rounded))


def attend_back(grad_heads, saved):
    query, key, value, weights, rounded = saved
    count, window = (query.shape[0], query.shape[1])
    grad_split = grad_heads.reshape(count, window, HEADS, HEAD)
    grad_weights = jnp.einsum(
        "wqhd,wkhd->whqk", grad_split, value, preferred_element_type=jnp.float32
    )
    grad_values = jnp.einsum(
        "whqk,wqhd->wkhd", rounded, grad_split, preferred_element_type=jnp.float32
    ).astype(jnp.bfloat16)
    grad_scores = (
        weights
        * (grad_weights - jnp.sum(weights * grad_weights, axis=-1, keepdims=True))
        * HEAD ** (-0.5)
    ).astype(jnp.bfloat16)
    grad_queries = jnp.einsum(
        "whqk,wkhd->wqhd", grad_scores, key, preferred_element_type=jnp.float32
    ).astype(jnp.bfloat16)
    grad_keys = jnp.einsum(
        "whqk,wqhd->wkhd", grad_scores, query, preferred_element_type=jnp.float32
    ).astype(jnp.bfloat16)
    stacked = jnp.stack((grad_queries, grad_keys, grad_values), axis=2)
    return stacked.reshape(count, window, 3 * HEADS * HEAD)


def per_device(
    tokens,
    packed_weight,
    output_weight,
    norm_gain,
    merge_gain,
    bias_table,
    bias_index,
    row_labels,
    column_valid,
    merged_grad,
):
    levels, lines, columns, width = tokens.shape
    normed, unit_one, scale_one = norm_rows(tokens, norm_gain)
    positions = lax.axis_index("lon") * columns + jnp.arange(columns, dtype=jnp.int32) + WLON // 2
    valid_columns = jnp.take(column_valid, positions % column_valid.shape[0])
    allowed = window_masks(row_labels, valid_columns, levels)
    typed = jnp.take(bias_table[0], bias_index, axis=2)
    window = allowed.shape[-1]
    types = typed.shape[0]
    allowed_types = allowed.reshape(types, -1, 1, window, window)
    masked_bias = jnp.where(allowed_types, typed[:, None], -jnp.inf).reshape(
        -1, typed.shape[1], window, window
    )
    triple = project(to_windows(roll_grid(normed, -1)), packed_weight)
    heads, saved = attend(triple, masked_bias)
    attended = roll_grid(from_windows(project(heads, output_weight), levels, lines, columns), 1)
    residual = (tokens.astype(jnp.float32) + attended.astype(jnp.float32)).astype(jnp.bfloat16)
    cells = merge_cells(residual)
    cells_normed, unit_two, scale_two = norm_rows(cells, merge_gain)
    merged = send_coarse(cells_normed)
    grad_cells = norm_back(return_coarse(merged_grad), merge_gain, unit_two, scale_two).astype(
        jnp.bfloat16
    )
    grad_residual = split_cells(grad_cells)
    grad_heads = project_back(to_windows(roll_grid(grad_residual, -1)), output_weight)
    grad_triple = attend_back(grad_heads, saved)
    grad_normed = roll_grid(
        from_windows(project_back(grad_triple, packed_weight), levels, lines, columns), 1
    )
    grad_tokens = grad_residual.astype(jnp.float32) + norm_back(
        grad_normed, norm_gain, unit_one, scale_one
    )
    return (merged, grad_tokens.astype(jnp.bfloat16))


def solution(mesh):
    placed = (
        P("lev", "lat", "lon", None),
        P(),
        P(),
        P(),
        P(),
        P("lev", "lat", None, None),
        P(),
        P("lat"),
        P(),
        P(None, "lat", ("lon", "lev"), None),
    )
    return jax.shard_map(
        per_device,
        mesh=mesh,
        in_specs=placed,
        out_specs=(P(None, "lat", ("lon", "lev"), None), P("lev", "lat", "lon", None)),
        check_vma=False,
    )
```

profile of v0, /device:TPU:0, one launch (start us, length us, event | category | flops | bytes accessed | tf_op | source)
XLA Modules:
  0.0 232.3 jit_solution(17685317767743868108)
XLA Ops:
  5.0 4.0 %collective-permute-start = (bf16[2,3,12,768]{3,2,1,0:T(8,128)(2,1)}, bf16[2,3,12,768]{3,2,1,0:T(8,128)(2,1)}, u32[]{:S(2)}, u32[]{:S(2)}) collective-permute-start(bf16[2,3,12,768]{3,2,1,0:T(8,128)(2,1)} %get-tuple-element.21), channel_id=1, source_target_pairs={{2,0},{0,2},{3,1},{1,3},{6,4},{4,6},{7,5},{5,7},{10,8},{8,10},{11,... | collective-permute-start | bytes 331784 | tf_op jit(solution)/shard_map/ppermute | solution.py:18
  12.1 1.7 reshape.366
  17.7 1.8 fusion.54
  21.8 2.7 %copy.124 = f32[1,1,24,3312]{2,3,1,0:T(8,128)} copy(f32[1,1,24,3312]{3,2,1,0:T(8,128)} %param.15) | data formatting | bytes 635904 | tf_op args[5]
  24.5 43.9 %gather_fusion.1 = f32[20736,24]{1,0:T(8,128)} fusion(f32[24,3312]{0,1:T(8,128)} %bitcast.86, s32[21504]{0:T(1024)} %pad_clamp_fusion), kind=kCustom, calls=%fused_computation.1 | custom fusion | bytes 4064256 | tf_op jit(solution)/shard_map/jit(_take)/gather | solution.py:181
  68.3 12.5 %copy.126 = f32[144,144,24]{0,1,2:T(8,128)} copy(f32[144,144,24]{2,1,0:T(8,128)} %bitcast.87) | data formatting | bytes 3981312 | tf_op jit(solution)/shard_map/jit(_take)/gather | solution.py:181
  82.3 1.8 pad_maximum_fusion.3
  84.1 1.7 reshape_reshape_transpose_reshape.6
  85.8 2.5 %convolution_convert_fusion = bf16[144,2304]{1,0:T(8,128)(2,1)} fusion(bf16[144,768]{1,0:T(8,128)(2,1)} %reshape_reshape_transpose_reshape.6, bf16[768,2304]{1,0:T(8,128)(2,1)S(1)} %copy-done), kind=kOutput, calls=%fused_computation.4 | convolution fusion | flops 509939712 | bytes 4423680 | tf_op jit(solution)/shard_map/dot_general | solution.py:40
  88.4 2.3 copy.122
  90.6 3.1 %bitcast_add_fusion = f32[24,144,144]{1,2,0:T(8,128)S(1)} fusion(f32[144,144,24]{0,1,2:T(8,128)} %copy.126, pred[144,144]{0,1:T(8,128)(4,1)} %fusion.56, pred[144,144]{0,1:T(8,128)(4,1)} %copy.123, bf16[1,144,3,24,32]{1,4,3,2,0:T(8,128)(2,1)} %bitcast.92), kind=kOutput, calls=%fused_computation.5 | convolution fusion | flops 33841152 | bytes 6389760 | tf_op jit(solution)/shard_map/wqhd,wkhd->whqk/dot_general | solution.py:126
  93.8 3.4 %fusion.68 = (f32[24,144]{1,0:T(8,128)}, f32[24,144,144]{1,2,0:T(8,128)}) fusion(f32[24,144,144]{1,2,0:T(8,128)S(1)} %bitcast_add_fusion), kind=kOutput, calls=%fused_computation.114 | output fusion | flops 995471 | bytes 3995136 | tf_op jit(solution)/shard_map/sub | solution.py:131
  97.2 5.0 %convolution_convert_fusion.2 = bf16[24,32,144]{2,1,0:T(8,128)(2,1)} fusion(bf16[1,144,3,24,32]{1,4,3,2,0:T(8,128)(2,1)} %bitcast.93, f32[24,144]{1,0:T(8,128)} %get-tuple-element.26, f32[24,144,144]{1,2,0:T(8,128)} %copy-done.1), kind=kOutput, calls=%fused_computation.16 | convolution fusion | flops 33457680 | bytes 7716864 | tf_op jit(solution)/shard_map/whqk,wkhd->wqhd/dot_general | solution.py:134
  102.2 2.5 %convolution_convert_fusion.4 = bf16[144,768]{1,0:T(8,128)(2,1)} fusion(bf16[144,768]{0,1:T(8,128)(2,1)} %bitcast.103, bf16[768,768]{1,0:T(8,128)(2,1)} %param.12), kind=kOutput, calls=%fused_computation.23 | convolution fusion | flops 169979904 | bytes 1622016 | tf_op jit(solution)/shard_map/dot_general | solution.py:40
  104.6 1.7 reshape_transpose_reshape_reshape.6
  106.4 1.7 fusion.65
  108.4 1.9 copy.133
  110.3 4.1 %all-to-all-start.1 = ((bf16[4,3,3,3072]{3,2,1,0:T(4,128)(2,1)}), bf16[4,3,3,3072]{3,2,1,0:T(4,128)(2,1)}, u32[]{:S(2)}, u32[]{:S(2)}) async-start(bf16[4,3,3,3072]{3,2,1,0:T(4,128)(2,1)} %copy.133), calls=%async_computation.1 | async-start | bytes 589824 | tf_op jit(solution)/shard_map/all_to_all | solution.py:118
  117.2 1.7 fusion.53
  118.9 1.8 all-to-all-done.1
  120.7 1.9 copy_convert_fusion
  122.6 2.1 reshape.352
  124.8 1.8 copy.135
  126.6 2.4 %reshape.347 = f32[2,3,6,2,2,768]{5,4,3,0,2,1:T(2,128)} reshape(f32[2,3,2,3,3072]{4,0,3,2,1:T(2,128)} %copy.135) | data formatting | bytes 884736 | tf_op jit(solution)/shard_map/convert_element_type | solution.py:30
  132.4 1.8 reduce_sum.93
  134.9 2.0 multiply_reduce_fusion.1
  144.6 2.3 reshape.348
  146.8 2.4 %bitcast_reduce_fusion = (f32[2,3,2,3]{0,2,3,1:T(2,128)}, f32[2,3,2,3]{0,2,3,1:T(2,128)}) fusion(f32[2,2,3,3,3072]{4,1,0,3,2:T(2,128)} %reshape.352, f32[3072]{0:T(1024)} %param.14, f32[2,3,2,3]{0,2,3,1:T(2,128)} %copy.146, f32[2,3,2,3]{0,2,3,1:T(2,128)} %copy.143, f32[2,3,2,3,3072]{4,0,3,2,1:T(2,128)} %reshape.348), kind=kLoop, calls=%fused_computation.47 | loop fusion | flops 663480 | bytes 897600 | tf_op jit(solution)/shard_map/reduce_sum | solution.py:33
  157.5 1.7 fusion.47
  160.1 1.8 collective-permute-start.4
  161.9 5.9 %collective-permute-done.4 = bf16[2,3,12,768]{3,0,2,1:T(2,128)(2,1)S(1)} collective-permute-done((bf16[2,3,12,768]{3,0,2,1:T(2,128)(2,1)S(1)}, bf16[2,3,12,768]{3,0,2,1:T(2,128)(2,1)S(1)}, u32[]{:S(2)}, u32[]{:S(2)}) %collective-permute-start.4) | collective-permute-done | bytes 110624 | tf_op jit(solution)/shard_map/ppermute | solution.py:18
  168.7 2.2 collective-permute-start.5
  171.0 2.3 %reshape.346 = f32[2,3,6,3072]{3,0,2,1:T(2,128)} reshape(f32[2,3,6,2,2,768]{5,4,3,0,2,1:T(2,128)} %copy.129) | data formatting | bytes 884736 | tf_op jit(solution)/shard_map/convert_element_type | solution.py:22
  175.6 1.7 reshape_reshape_transpose_reshape.7
  177.3 2.6 %convolution_convert_fusion.3 = bf16[144,768]{1,0:T(8,128)(2,1)} fusion(bf16[144,768]{1,0:T(8,128)(2,1)} %reshape_reshape_transpose_reshape.7, bf16[768,768]{1,0:T(8,128)(2,1)} %param.12), kind=kOutput, calls=%fused_computation.22 | convolution fusion | flops 169979904 | bytes 1622016 | tf_op jit(solution)/shard_map/dot_general | solution.py:46
  180.0 1.9 copy.152
  181.9 5.0 %fusion.25 = bf16[1,144,1,24,32]{1,4,3,2,0:T(8,128)(2,1)} fusion(bf16[144,24,32]{0,2,1:T(8,128)(2,1)} %bitcast.101, f32[24,144]{1,0:T(8,128)} %get-tuple-element.26, f32[24,144,144]{1,2,0:T(8,128)} %copy-done.1), kind=kOutput, calls=%fused_computation.21 | convolution fusion | flops 33457680 | bytes 2446848 | tf_op jit(solution)/shard_map/whqk,wqhd->wkhd/dot_general | solution.py:146
  186.8 3.6 %fusion.48 = f32[24,144,144]{1,2,0:T(8,128)} fusion(bf16[144,24,32]{0,2,1:T(8,128)(2,1)} %bitcast.102, bf16[1,144,3,24,32]{1,4,3,2,0:T(8,128)(2,1)} %bitcast.94), kind=kOutput, calls=%fused_computation.62 | convolution fusion | flops 31850496 | bytes 2777088 | tf_op jit(solution)/shard_map/wqhd,wkhd->whqk/dot_general | solution.py:143
  190.4 7.1 %fusion.19 = bf16[1,144,1,24,32]{1,4,3,2,0:T(8,128)(2,1)} fusion(f32[24,144,144]{1,2,0:T(8,128)} %fusion.48, bf16[1,144,3,24,32]{1,4,3,2,0:T(8,128)(2,1)} %bitcast.95, f32[24,144,144]{1,2,0:T(8,128)} %get-tuple-element.27, f32[24,144]{1,0:T(8,128)} %get-tuple-element.26), kind=kOutput, calls=%fused_computation.19 | convolution fusion | flops 35448336 | bytes 14819328 | tf_op jit(solution)/shard_map/whqk,wqhd->wkhd/dot_general | solution.py:157
  197.5 7.2 %fusion.22 = bf16[1,144,1,24,32]{1,4,3,2,0:T(8,128)(2,1)} fusion(f32[24,144,144]{1,2,0:T(8,128)} %fusion.48, bf16[1,144,3,24,32]{1,4,3,2,0:T(8,128)(2,1)} %bitcast.96, f32[24,144,144]{1,2,0:T(8,128)} %get-tuple-element.27, f32[24,144]{1,0:T(8,128)} %get-tuple-element.26), kind=kOutput, calls=%fused_computation.20 | convolution fusion | flops 35448336 | bytes 14819328 | tf_op jit(solution)/shard_map/whqk,wkhd->wqhd/dot_general | solution.py:154
  206.2 2.1 convolution_convert_fusion.5
  208.3 1.7 reshape_transpose_reshape_reshape.7
  210.0 1.7 fusion.64
  213.9 4.1 %all-to-all-start = ((bf16[2,3,6,3072]{3,0,1,2:T(2,128)(2,1)}), bf16[2,3,6,3072]{3,0,1,2:T(2,128)(2,1)}, u32[]{:S(2)}, u32[]{:S(2)}) async-start(bf16[2,3,6,3072]{3,0,1,2:T(2,128)(2,1)} %copy.130), calls=%async_computation | async-start | bytes 442368 | tf_op jit(solution)/shard_map/all_to_all | solution.py:114
  218.0 2.7 %collective-permute-done.6 = bf16[2,3,12,768]{3,2,1,0:T(8,128)(2,1)} collective-permute-done((bf16[2,3,12,768]{3,2,1,0:T(8,128)(2,1)}, bf16[2,3,12,768]{3,2,1,0:T(8,128)(2,1)}, u32[]{:S(2)}, u32[]{:S(2)}) %collective-permute-start.6) | collective-permute-done | bytes 110624 | tf_op jit(solution)/shard_map/ppermute | solution.py:18
  220.7 1.7 fusion.52
  223.5 1.8 copy.132
  225.3 1.7 all_to_all.23
  (79 shorter events, 52.4 us)
Async XLA Ops:
  0.6 85.2 %copy-start = (bf16[768,2304]{1,0:T(8,128)(2,1)S(1)}, bf16[768,2304]{1,0:T(8,128)(2,1)}, u32[]{:S(2)}) copy-start(bf16[768,2304]{1,0:T(8,128)(2,1)} %param.11) | copy-start | bytes 10616836
  1.9 3.1 %copy-start.4 = (f32[2,6,12]{2,1,0:T(8,128)}, f32[2,6,12]{2,1,0:T(8,128)S(1)}, u32[]{:S(2)}) copy-start(f32[2,6,12]{2,1,0:T(8,128)S(1)} %broadcast_multiply_fusion.3) | copy-start | bytes 1732
  3.1 1.9 copy-start.5
  5.0 12.7 %collective-permute-start = (bf16[2,3,12,768]{3,2,1,0:T(8,128)(2,1)}, bf16[2,3,12,768]{3,2,1,0:T(8,128)(2,1)}, u32[]{:S(2)}, u32[]{:S(2)}) collective-permute-start(bf16[2,3,12,768]{3,2,1,0:T(8,128)(2,1)} %get-tuple-element.21), channel_id=1, source_target_pairs={{2,0},{0,2},{3,1},{1,3},{6,4},{4,6},{7,5},{5,7},{10,8},{8,10},{11,... | collective-permute-start | bytes 331784 | tf_op jit(solution)/shard_map/ppermute | solution.py:18
  19.5 62.9 %collective-permute-start.1 = (bf16[2,6,6,768]{3,2,1,0:T(8,128)(2,1)}, bf16[2,6,6,768]{3,2,1,0:T(8,128)(2,1)}, u32[]{:S(2)}, u32[]{:S(2)}) collective-permute-start(bf16[2,6,6,768]{3,2,1,0:T(8,128)(2,1)} %get-tuple-element.19), channel_id=1, source_target_pairs={{4,0},{8,4},{12,8},{16,12},{20,16},{24,20},{28,24},{0,28},{5,1},{9... | collective-permute-start | bytes 331784 | tf_op jit(solution)/shard_map/ppermute | solution.py:18
  93.8 3.4 %copy-start.1 = (f32[24,144,144]{1,2,0:T(8,128)}, f32[24,144,144]{1,2,0:T(8,128)S(1)}, u32[]{:S(2)}) copy-start(f32[24,144,144]{1,2,0:T(8,128)S(1)} %bitcast_add_fusion) | copy-start | bytes 5971972
  102.2 12.3 %copy-start.6 = (f32[3072]{0:T(1024)S(1)}, f32[3072]{0:T(1024)}, u32[]{:S(2)}) copy-start(f32[3072]{0:T(1024)} %param.14) | copy-start | bytes 36868
  108.1 9.1 %collective-permute-start.2 = (bf16[2,3,12,768]{3,2,1,0:T(8,128)(2,1)}, bf16[2,3,12,768]{3,2,1,0:T(8,128)(2,1)}, u32[]{:S(2)}, u32[]{:S(2)}) collective-permute-start(bf16[2,3,12,768]{3,2,1,0:T(8,128)(2,1)} %get-tuple-element.16), channel_id=1, source_target_pairs={{2,0},{0,2},{3,1},{1,3},{6,4},{4,6},{7,5},{5,7},{10,8},{8,10},{11,... | collective-permute-start | bytes 331784 | tf_op jit(solution)/shard_map/ppermute | solution.py:18
  110.3 10.4 %all-to-all-start.1 = ((bf16[4,3,3,3072]{3,2,1,0:T(4,128)(2,1)}), bf16[4,3,3,3072]{3,2,1,0:T(4,128)(2,1)}, u32[]{:S(2)}, u32[]{:S(2)}) async-start(bf16[4,3,3,3072]{3,2,1,0:T(4,128)(2,1)} %copy.133), calls=%async_computation.1 | async-start | bytes 589824 | tf_op jit(solution)/shard_map/all_to_all | solution.py:118
  118.9 10.1 %collective-permute-start.3 = (bf16[2,6,6,768]{3,2,1,0:T(8,128)(2,1)}, bf16[2,6,6,768]{3,2,1,0:T(8,128)(2,1)}, u32[]{:S(2)}, u32[]{:S(2)}) collective-permute-start(bf16[2,6,6,768]{3,2,1,0:T(8,128)(2,1)} %fusion.53), channel_id=1, source_target_pairs={{28,0},{0,4},{4,8},{8,12},{12,16},{16,20},{20,24},{24,28},{29,1},{... | collective-permute-start | bytes 331784 | tf_op jit(solution)/shard_map/ppermute | solution.py:18
  130.6 0.8 copy-start.2
  159.3 0.7 copy-start.3
  160.1 7.6 %collective-permute-start.4 = (bf16[2,3,12,768]{3,0,2,1:T(2,128)(2,1)S(1)}, bf16[2,3,12,768]{3,0,2,1:T(2,128)(2,1)S(1)}, u32[]{:S(2)}, u32[]{:S(2)}) collective-permute-start(bf16[2,3,12,768]{3,0,2,1:T(2,128)(2,1)S(1)} %get-tuple-element.25), channel_id=1, source_target_pairs={{2,0},{0,2},{3,1},{1,3},{6,4},{4,6},{7,5},{5,7},{10,8},{8,10},{11,... | collective-permute-start | bytes 331784 | tf_op jit(solution)/shard_map/ppermute | solution.py:18
  168.7 4.9 %collective-permute-start.5 = (bf16[2,6,6,768]{3,0,2,1:T(2,128)(2,1)}, bf16[2,6,6,768]{3,0,2,1:T(2,128)(2,1)}, u32[]{:S(2)}, u32[]{:S(2)}) collective-permute-start(bf16[2,6,6,768]{3,0,2,1:T(2,128)(2,1)} %get-tuple-element.23), channel_id=1, source_target_pairs={{4,0},{8,4},{12,8},{16,12},{20,16},{24,20},{28,24},{0,28},{5,1},{9... | collective-permute-start | bytes 331784 | tf_op jit(solution)/shard_map/ppermute | solution.py:18
  206.2 22.0 %copy-start.7 = (f32[768]{0:T(1024)S(1)}, f32[768]{0:T(1024)}, u32[]{:S(2)}) copy-start(f32[768]{0:T(1024)} %param.13) | copy-start | bytes 9220
  211.7 9.0 %collective-permute-start.6 = (bf16[2,3,12,768]{3,2,1,0:T(8,128)(2,1)}, bf16[2,3,12,768]{3,2,1,0:T(8,128)(2,1)}, u32[]{:S(2)}, u32[]{:S(2)}) collective-permute-start(bf16[2,3,12,768]{3,2,1,0:T(8,128)(2,1)} %get-tuple-element.14), channel_id=1, source_target_pairs={{2,0},{0,2},{3,1},{1,3},{6,4},{4,6},{7,5},{5,7},{10,8},{8,10},{11,... | collective-permute-start | bytes 331784 | tf_op jit(solution)/shard_map/ppermute | solution.py:18
  213.9 9.7 %all-to-all-start = ((bf16[2,3,6,3072]{3,0,1,2:T(2,128)(2,1)}), bf16[2,3,6,3072]{3,0,1,2:T(2,128)(2,1)}, u32[]{:S(2)}, u32[]{:S(2)}) async-start(bf16[2,3,6,3072]{3,0,1,2:T(2,128)(2,1)} %copy.130), calls=%async_computation | async-start | bytes 442368 | tf_op jit(solution)/shard_map/all_to_all | solution.py:114
  222.4 5.8 %collective-permute-start.7 = (bf16[2,6,6,768]{3,2,1,0:T(8,128)(2,1)}, bf16[2,6,6,768]{3,2,1,0:T(8,128)(2,1)}, u32[]{:S(2)}, u32[]{:S(2)}) collective-permute-start(bf16[2,6,6,768]{3,2,1,0:T(8,128)(2,1)} %fusion.52), channel_id=1, source_target_pairs={{28,0},{0,4},{4,8},{8,12},{12,16},{16,20},{20,24},{24,28},{29,1},{... | collective-permute-start | bytes 331784 | tf_op jit(solution)/shard_map/ppermute | solution.py:18
where the time goes:
time: 236 us; the launch traced here: 232 us
  local copies, waits for them, and re-layouts  115 us (49%)
  other arithmetic  43.3 us (18%)
  matrix products  40.6 us (17%)
  starting transfers between devices  18.3 us (8%)
  waiting for transfers between devices  13.8 us (6%)
    gather x2, local copies, waits for them, and re-layouts, per_device(): typed = jnp.take(bias_table[0], bias_index, axis=2)  56.4 us
    ppermute x8, waiting for transfers between devices, from_behind(): return lax.ppermute(block, axis, route)  10.8 us
    ppermute x8, starting transfers between devices, from_behind(): return lax.ppermute(block, axis, route)  10 us
    dot_general x1, matrix products, attend_back(): jnp.einsum('whqk,wkhd->wqhd', grad_scores, key, preferred_element_type=jn...  7.16 us
    dot_general x1, matrix products, attend_back(): jnp.einsum('whqk,wqhd->wkhd', grad_scores, query, preferred_element_type=...  7.13 us
    unnamed x19, local copies, waits for them, and re-layouts  6.89 us
    convert_element_type x3, local copies, waits for them, and re-layouts, norm_back(): scaled = grad.astype(jnp.float32) * gain  6.35 us
    convert_element_type x4, local copies, waits for them, and re-layouts, norm_rows(): data = values.astype(jnp.float32)  6 us
  transfers between devices with their start and end apart: 10, of which 7 were waited for; matrix products, arithmetic and copies ran while one was open for 39% of the time, Pallas kernels for 0%

commit v1 on v0

v1 whole, which is shorter than its diff:
```python
import functools

import jax
import jax.numpy as jnp
import numpy as np
from jax import lax
from jax.experimental import pallas as pl
from jax.experimental.pallas import tpu as pltpu
from jax.sharding import PartitionSpec as P

HEADS = 24
HEAD = 32
WLAT = 6
WLON = 12
HALF_LAT = WLAT // 2
HALF_LON = WLON // 2
LEVELS = 2
WIN = LEVELS * WLAT * WLON
QUAD = WIN // 4
CELLS = LEVELS * HALF_LON // 2
GROUP = 128 // HEAD
TAIL = WIN - 128
TAIL_GROUPS = WIN // 8
PAD = 16
BLOCKED = -1e30

epsilon = 1e-05
f32 = jnp.float32
bf16 = jnp.bfloat16

NN = (((1,), (0,)), ((), ()))
NT = (((1,), (1,)), ((), ()))


def token_table():
    rows = []
    for quad in range(4):
        for r in range(HALF_LAT):
            for s in range(2):
                for l in range(LEVELS):
                    for j in range(HALF_LON // 2):
                        rows.append((quad, r, s, l, j))
    return np.array(rows)


TOKENS = token_table()
QUADS, ROW3, SIDE, LEVEL, PAIR = TOKENS.T
ROW = (QUADS & 1) * HALF_LAT + ROW3
COL = (QUADS >> 1) * HALF_LON + 2 * PAIR + SIDE
NATURAL = LEVEL * WLAT * WLON + ROW * WLON + COL
LINE = ROW3 + np.where(QUADS & 1, 0, HALF_LAT)
COLUMN = 2 * PAIR + SIDE + np.where(QUADS >> 1, 0, HALF_LON)
PLACE = (LEVEL * WLAT + LINE) * PAD + COLUMN
HALVES = (ROW == 0) | (ROW == WLAT - 1)


def one_hot(index, width):
    return (index[:, None] == np.arange(width)[None, :]).astype(np.float32)


def constants():
    order = one_hot(NATURAL, WIN)
    pack = one_hot(PLACE, LEVELS * WLAT * PAD)
    cell_row = np.where(ROW == 0, 0, (ROW + 1) // 2)
    cell = ((cell_row * 2 + (QUADS >> 1)) * LEVELS + LEVEL) * (HALF_LON // 2) + PAIR
    same = (cell[:, None] == cell[None, :]).astype(np.float32)
    first = [t for t in range(WIN) if ROW[t] == 0 and SIDE[t] == 0]
    last = [t for t in range(WIN) if ROW[t] == WLAT - 1 and SIDE[t] == 0]
    pick = one_hot(np.array(first + last), WIN)
    spread = same @ pick.T
    rows = np.stack((ROW, COL)).astype(np.int32)
    return order, pack, same, pick, spread, rows


ORDER, PACK, SAME, PICK, SPREAD, COORDS = constants()


def mxu(a, b, dims=NN):
    return lax.dot_general(a, b, dims, preferred_element_type=f32)


def exact(a, b):
    return lax.dot_general(a, b, NN, precision=lax.Precision.HIGHEST, preferred_element_type=f32)


def params(megabytes=48):
    return pltpu.CompilerParams(vmem_limit_bytes=megabytes << 20)


def shape(dims, dtype):
    return jax.ShapeDtypeStruct(dims, dtype)


def cost(flops, nbytes):
    return pl.CostEstimate(flops=flops, bytes_accessed=nbytes, transcendentals=0)


def lev_index():
    return lax.axis_index("lev")


def pack_kernel(tokens, grad, pack, own, lat, lon, both, same_here, other_here, same_next, other_next, padded, rows):
    width = tokens.shape[-1]
    for l in range(LEVELS):
        for r in range(WLAT):
            at = (l * WLAT + r) * PAD
            line = tokens[l, r].astype(f32)
            padded[at : at + PAD, :] = jnp.concatenate(
                (line, jnp.zeros((PAD - WLON, width), f32)), axis=0
            ).astype(bf16)
    for quad, out in enumerate((own, lat, lon, both)):
        out[...] = mxu(pack[quad], padded[...]).astype(bf16)
    me = lev_index()
    pairs = HALF_LON // 2
    for out, level, full, half, odd in (
        (same_here, me, 2, 1, 1),
        (other_here, 1 - me, 2, 1, 1),
        (same_next, me, 0, 1, 0),
        (other_next, 1 - me, 0, 1, 0),
    ):
        for l in range(LEVELS):
            at = slice(l * pairs, (l + 1) * pairs)
            halved = grad[level * LEVELS + l, half].astype(f32)
            for s in range(2):
                block = s * 2 + odd
                rows[at, s * width : (s + 1) * width] = halved[:, block * width : (block + 1) * width]
            rows[at, 2 * width :] = grad[level * LEVELS + l, full].astype(f32)
        out[...] = rows[...].astype(bf16)


def pack_pieces(tokens, grad):
    width = tokens.shape[-1]
    token_piece = shape((QUAD, width), bf16)
    cell_piece = shape((CELLS, 6 * width), bf16)
    return pl.pallas_call(
        pack_kernel,
        out_shape=[token_piece] * 4 + [cell_piece] * 4,
        scratch_shapes=[
            pltpu.VMEM((LEVELS * WLAT * PAD, width), bf16),
            pltpu.VMEM((CELLS, 6 * width), f32),
        ],
        compiler_params=params(),
        name="pack",
    )(tokens, grad, jnp.asarray(PACK.reshape(4, QUAD, -1), bf16))


def bias_kernel(table, index, order, coords, coords_t, labels, valid, main, tail, padded, high, low, mask, mask_t):
    heads, entries = table.shape[-2:]
    chunks = (entries + 127) // 128
    whole = entries // 128 * 128
    padded[:, :whole] = table[0, 0, :, :whole]
    if whole < entries:
        padded[:, whole:] = jnp.concatenate(
            (table[0, 0, :, whole:], jnp.zeros((heads, chunks * 128 - entries), f32)), axis=1
        )

    row_q, row_k = coords[0:1, :], coords_t[:, 0:1]
    col_k = coords_t[:, 1:2]
    label_q, label_k = jnp.zeros_like(row_q), jnp.zeros_like(row_k)
    for r in range(WLAT):
        label_q = jnp.where(row_q == r, labels[r], label_q)
        label_k = jnp.where(row_k == r, labels[r], label_k)
    valid_k = jnp.zeros_like(col_k)
    start = lax.axis_index("lon") * WLON + HALF_LON
    total = valid.shape[0]
    for c in range(WLON):
        at = start + c
        at = jnp.where(at >= total, at - total, at)
        valid_k = jnp.where(col_k == c, valid[at], valid_k)
    rows = lax.broadcasted_iota(jnp.int32, (WIN, WIN), 0)
    columns = lax.broadcasted_iota(jnp.int32, (WIN, WIN), 1)
    seen = (label_k == label_q) & ((valid_k > 0) | (rows == columns))
    added = jnp.where(seen, 0.0, BLOCKED).astype(f32)
    mask[...] = added[:, :128]
    mask_t[...] = jnp.concatenate((added[:, 128:], jnp.zeros((WIN, 128 - TAIL), f32)), axis=1)

    entry = index[...]
    permute = order[...]

    def place(values, out):
        moved = mxu(mxu(permute, values.astype(f32).astype(bf16), NT).astype(bf16), permute, NT)
        moved = moved.astype(jnp.int32)
        out[0:WIN, :] = moved[:, :128]
        rest = jnp.concatenate((moved[:, 128:], jnp.zeros((WIN, 128 - TAIL), jnp.int32)), axis=1)
        for first in range(0, TAIL_GROUPS, 8):
            total = None
            for g in range(first, min(first + 8, TAIL_GROUPS)):
                piece = rest[g * 8 : g * 8 + 8]
                if g > first:
                    piece = pltpu.roll(piece, TAIL * (g - first), 1)
                total = piece if total is None else total + piece
            out[WIN + first : WIN + first + 8, :] = total

    place(lax.shift_right_logical(entry, 7), high)
    place(entry & 127, low)

    def lookup(row):
        chunk = jnp.broadcast_to(high[pl.ds(row, 1), :], (8, 128))
        lane = jnp.broadcast_to(low[pl.ds(row, 1), :], (8, 128))
        found = [None] * (heads // 8)
        for c in range(chunks):
            here = chunk == c
            for block in range(heads // 8):
                source = padded[block * 8 : block * 8 + 8, c * 128 : (c + 1) * 128]
                value = jnp.take_along_axis(source, lane, axis=1, mode="promise_in_bounds")
                found[block] = value if c == 0 else jnp.where(here, value, found[block])
        return found

    def main_row(key, _):
        extra = jnp.broadcast_to(mask[pl.ds(key, 1), :], (8, 128))
        for block, value in enumerate(lookup(key)):
            main[pl.ds(block * 8 * WIN + key, 8, stride=WIN), :] = value + extra
        return 0

    lax.fori_loop(0, WIN, main_row, 0, unroll=2)
    for first in range(0, TAIL_GROUPS, 8):
        for s in range(8):
            for block, value in enumerate(lookup(WIN + first + s)):
                for g in range(first, min(first + 8, TAIL_GROUPS)):
                    key = g * 8 + s
                    moved = pltpu.roll(value, 128 - TAIL * (g - first), 1) if g > first else value
                    extra = jnp.broadcast_to(mask_t[key : key + 1, :], (8, 128))
                    tail[pl.ds(block * 8 * WIN + key, 8, stride=WIN), :] = moved + extra


def window_bias(table, index, labels, valid):
    heads, entries = table.shape[-2:]
    chunks = (entries + 127) // 128
    scalar = pl.BlockSpec(memory_space=pltpu.SMEM)
    vector = pl.BlockSpec(memory_space=pltpu.VMEM)
    index_rows = WIN + (TAIL_GROUPS + 7) // 8 * 8
    return pl.pallas_call(
        bias_kernel,
        out_shape=[shape((heads * WIN, 128), f32)] * 2,
        in_specs=[vector] * 5 + [scalar] * 2,
        scratch_shapes=[
            pltpu.VMEM((heads, chunks * 128), f32),
            pltpu.VMEM((index_rows, 128), jnp.int32),
            pltpu.VMEM((index_rows, 128), jnp.int32),
            pltpu.VMEM((WIN, 128), f32),
            pltpu.VMEM((WIN, 128), f32),
        ],
        compiler_params=params(),
        cost_estimate=cost(10**9, 2 * 10**7),
        name="bias",
    )(table, index, jnp.asarray(ORDER, bf16), jnp.asarray(COORDS), jnp.asarray(COORDS.T), labels, valid)


def row_mean(values):
    return jnp.mean(values, axis=-1, keepdims=True)


def unit_rows(data):
    center = data - row_mean(data)
    scale = lax.rsqrt(row_mean(center * center) + epsilon)
    return center * scale, scale


def stacked(block):
    lane = lax.broadcasted_iota(jnp.int32, (1, 128), 1) // HEAD
    return jnp.concatenate(
        [jnp.where(lane == h, block, jnp.zeros((), block.dtype)) for h in range(GROUP)], axis=0
    )


def lanes_of(parts):
    lane = lax.broadcasted_iota(jnp.int32, (1, 128), 1) // HEAD
    out = parts[0]
    for h in range(1, GROUP):
        out = jnp.where(lane == h, parts[h], out)
    return out


def forward_kernel(
    own, lat, lon, both, packed, output, gain, main, tail,
    weights, triple, keys_t, residual, tokens,
    gathered, values_t, heads_t,
):
    width = own.shape[-1]
    for quad, piece in enumerate((own, lat, lon, both)):
        gathered[quad * QUAD : (quad + 1) * QUAD, :] = piece[...].astype(f32)
    data = gathered[...]
    tokens[...] = data.astype(bf16)
    unit, _ = unit_rows(data)
    normed = (unit * gain[...]).astype(bf16)
    triple[...] = mxu(normed, packed[...]).astype(bf16)
    keys_t[...] = triple[:, width : 2 * width].astype(f32).T.astype(bf16)
    values_t[...] = triple[:, 2 * width :].astype(f32).T.astype(bf16)
    for g in range(width // 128):
        query = triple[:, g * 128 : (g + 1) * 128]
        key = triple[:, width + g * 128 : width + (g + 1) * 128]
        product = mxu(stacked(key), query, NT) * HEAD ** (-0.5)
        for h in range(GROUP):
            head = g * GROUP + h
            at = slice(head * WIN, (head + 1) * WIN)
            bias = jnp.concatenate((main[at, :], tail[at, :TAIL]), axis=1)
            scores = product[h * WIN : (h + 1) * WIN] + bias
            raised = jnp.exp(scores - jnp.max(scores, axis=0, keepdims=True))
            share = (raised * (1.0 / jnp.sum(raised, axis=0, keepdims=True))).astype(bf16)
            weights[at, :] = share
            here = slice(head * HEAD, (head + 1) * HEAD)
            heads_t[here, :] = mxu(values_t[here, :], share)
    heads = heads_t[...].T.astype(bf16)
    attended = mxu(heads, output[...]).astype(bf16)
    residual[...] = (data + attended.astype(f32)).astype(bf16)


def forward(pieces, packed, output, gain, main, tail):
    width = output.shape[0]
    return pl.pallas_call(
        forward_kernel,
        out_shape=[
            shape((HEADS * WIN, WIN), bf16),
            shape((WIN, 3 * width), bf16),
            shape((width, WIN), bf16),
            shape((WIN, width), bf16),
            shape((WIN, width), bf16),
        ],
        scratch_shapes=[
            pltpu.VMEM((WIN, width), f32),
            pltpu.VMEM((width, WIN), bf16),
            pltpu.VMEM((width, WIN), f32),
        ],
        compiler_params=params(),
        cost_estimate=cost(10**9, 2 * 10**7),
        name="forward",
    )(*pieces, packed, output, gain, main, tail)


def cell_blocks():
    out = []
    for quad in range(4):
        for r in range(HALF_LAT):
            odd = 1 - (r + (quad & 1) * HALF_LAT) % 2
            half = r == (HALF_LAT - 1 if quad & 1 else 0)
            for s in range(2):
                block = s * 2 + odd
                at = quad * QUAD + (r * 2 + s) * CELLS
                out.append((quad, at, block, s if half else 2 + block))
    return out


def columns_of(parts):
    lane = lax.broadcasted_iota(jnp.int32, (1, 128), 1)
    out = jnp.zeros((WIN, 128), f32)
    for i, part in enumerate(parts):
        out = jnp.where(lane == i, part, out)
    return out


def moments_kernel(
    residual, same_here, other_here, same_next, other_next, gain, same, pick, count,
    scaled, moments, sent,
):
    width = residual.shape[-1]
    second = lev_index() == 1
    sides = {}
    for kind, (near, far) in enumerate(((same_here, other_here), (same_next, other_next))):
        a, b = near[...].astype(f32), far[...].astype(f32)
        sides[kind] = jnp.where(second, a, b)
        sides[kind + 2] = jnp.where(second, b, a)
    for quad, at, block, lane in cell_blocks():
        part = sides[quad][:, lane * width : (lane + 1) * width]
        scaled[at : at + CELLS, :] = part * gain[:, block * width : (block + 1) * width]
    data = residual[...].astype(f32)
    grouping = same[...]
    inverse = count[...]
    total = jnp.sum(data, axis=-1, keepdims=True)
    middle = exact(grouping, jnp.broadcast_to(total, (WIN, 128)))[:, 0:1] * inverse
    center = data - middle
    grad = scaled[...]
    sums = columns_of((
        jnp.sum(center * center, axis=-1, keepdims=True),
        jnp.sum(grad, axis=-1, keepdims=True),
        jnp.sum(grad * center, axis=-1, keepdims=True),
    ))
    sums = exact(grouping, sums)
    lane = lax.broadcasted_iota(jnp.int32, (1, 128), 1)
    sums = jnp.where(lane == 3, middle, sums)
    moments[...] = sums
    sent[...] = exact(pick[...], sums)


def cell_moments(residual, cells, gain):
    width = residual.shape[-1]
    count = np.where(HALVES, 1 / (2 * width), 1 / (4 * width)).astype(np.float32)[:, None]
    return pl.pallas_call(
        moments_kernel,
        out_shape=[shape((WIN, width), f32), shape((WIN, 128), f32), shape((4 * CELLS, 128), f32)],
        compiler_params=params(),
        cost_estimate=cost(10**8, 10**6),
        name="moments",
    )(residual, *cells, gain, jnp.asarray(SAME), jnp.asarray(PICK), jnp.asarray(count))


def merge_kernel(
    residual, scaled, moments, before, after, gain, spread, halves,
    same_here, other_here, same_next, other_next, grad, unit,
):
    width = residual.shape[-1]
    second = lev_index() == 1
    there = jnp.concatenate((before[2 * CELLS :], after[: 2 * CELLS]), axis=0)
    theirs = exact(spread[...], there)
    mine = moments[...]
    shared = halves[...] > 0
    full = 4.0 * width
    middle = jnp.where(shared, 0.5 * (mine[:, 3:4] + theirs[:, 3:4]), mine[:, 3:4])
    gap = theirs[:, 3:4] - mine[:, 3:4]
    spread_sum = jnp.where(shared, mine[:, 0:1] + theirs[:, 0:1] + gap * gap * width, mine[:, 0:1])
    scale = lax.rsqrt(spread_sum / full + epsilon)
    grad_sum = jnp.where(shared, mine[:, 1:2] + theirs[:, 1:2], mine[:, 1:2])
    cross = jnp.where(
        shared,
        mine[:, 2:3] + (mine[:, 3:4] - middle) * mine[:, 1:2]
        + theirs[:, 2:3] + (theirs[:, 3:4] - middle) * theirs[:, 1:2],
        mine[:, 2:3],
    )
    normed = (residual[...].astype(f32) - middle) * scale
    unit[...] = normed
    grad[...] = (scale * (scaled[...] - grad_sum / full - normed * (cross * scale / full))).astype(bf16)
    for kind, (near, far) in enumerate(((same_here, other_here), (same_next, other_next))):
        for quad, at, block, lane in cell_blocks():
            if quad != kind:
                continue
            factor = gain[:, block * width : (block + 1) * width]
            left = unit[at : at + CELLS, :] * factor
            right = unit[at + 2 * QUAD : at + 2 * QUAD + CELLS, :] * factor
            here = slice(lane * width, (lane + 1) * width)
            near[:, here] = jnp.where(second, left, right).astype(bf16)
            far[:, here] = jnp.where(second, right, left).astype(bf16)


def merge_back(residual, scaled, moments, before, after, gain):
    width = residual.shape[-1]
    piece = shape((CELLS, 6 * width), bf16)
    return pl.pallas_call(
        merge_kernel,
        out_shape=[piece] * 4 + [shape((WIN, width), bf16)],
        scratch_shapes=[pltpu.VMEM((WIN, width), f32)],
        compiler_params=params(),
        cost_estimate=cost(10**8, 10**6),
        name="merge",
    )(
        residual, scaled, moments, before, after, gain, jnp.asarray(SPREAD),
        jnp.asarray(HALVES.astype(np.float32)[:, None]),
    )


def backward_kernel(
    grad, weights, triple, keys_t, tokens, packed, output, gain,
    own, lat, lon, both,
    joined, queries_t,
):
    width = grad.shape[-1]
    upstream = grad[...]
    grad_heads = mxu(upstream, output[...], NT).astype(bf16)
    for g in range(width // 128):
        here = slice(g * 128, (g + 1) * 128)
        query = triple[:, g * 128 : (g + 1) * 128]
        value = triple[:, 2 * width + g * 128 : 2 * width + (g + 1) * 128]
        arriving = grad_heads[:, here]
        product = mxu(stacked(value), arriving, NT)
        shares = weights[g * GROUP * WIN : (g + 1) * GROUP * WIN, :]
        grad_value = mxu(shares, arriving)
        slopes = []
        for h in range(GROUP):
            head = g * GROUP + h
            share = shares[h * WIN : (h + 1) * WIN].astype(f32)
            change = product[h * WIN : (h + 1) * WIN]
            level = jnp.sum(share * change, axis=0, keepdims=True)
            slope = (share * (change - level) * HEAD ** (-0.5)).astype(bf16)
            at = slice(head * HEAD, (head + 1) * HEAD)
            queries_t[at, :] = mxu(keys_t[at, :], slope)
            slopes.append(slope)
        grad_key = mxu(jnp.concatenate(slopes, axis=0), query)
        split = [slice(h * WIN, (h + 1) * WIN) for h in range(GROUP)]
        joined[:, width + g * 128 : width + (g + 1) * 128] = lanes_of([grad_key[s] for s in split]).astype(bf16)
        joined[:, 2 * width + g * 128 : 2 * width + (g + 1) * 128] = lanes_of(
            [grad_value[s] for s in split]
        ).astype(bf16)
    joined[:, :width] = queries_t[...].T.astype(bf16)
    grad_inputs = mxu(joined[...], packed[...], NT).astype(bf16)
    unit, scale = unit_rows(tokens[...].astype(f32))
    scaled = grad_inputs.astype(f32) * gain[...]
    out = upstream.astype(f32) + scale * (scaled - row_mean(scaled) - unit * row_mean(scaled * unit))
    for quad, piece in enumerate((own, lat, lon, both)):
        piece[...] = out[quad * QUAD : (quad + 1) * QUAD].astype(bf16)


def backward(grad, weights, triple, keys_t, tokens, packed, output, gain):
    width = grad.shape[-1]
    return pl.pallas_call(
        backward_kernel,
        out_shape=[shape((QUAD, width), bf16)] * 4,
        scratch_shapes=[pltpu.VMEM((WIN, 3 * width), bf16), pltpu.VMEM((width, WIN), f32)],
        compiler_params=params(),
        cost_estimate=cost(2 * 10**9, 2 * 10**7),
        name="backward",
    )(grad, weights, triple, keys_t, tokens, packed, output, gain)


def unpack_kernel(own, lat, lon, both, place, same_here, other_here, same_next, other_next, merged, tokens):
    width = own.shape[-1]
    total = None
    for quad, piece in enumerate((own, lat, lon, both)):
        part = mxu(place[quad], piece[...])
        total = part if total is None else total + part
    for l in range(LEVELS):
        for r in range(WLAT):
            at = (l * WLAT + r) * PAD
            tokens[l, r] = total[at : at + WLON].astype(bf16)
    me = lev_index()
    pairs = HALF_LON // 2
    for level, full, odd, piece in (
        (me, 2, 1, same_here),
        (1 - me, 2, 1, other_here),
        (me, 0, 0, same_next),
        (1 - me, 0, 0, other_next),
    ):
        cells = piece[...].astype(f32)
        for l in range(LEVELS):
            part = cells[l * pairs : (l + 1) * pairs].astype(bf16)
            for s in range(2):
                block = s * 2 + odd
                merged[level * LEVELS + l, 1, :, block * width : (block + 1) * width] = part[
                    :, s * width : (s + 1) * width
                ]
            merged[level * LEVELS + l, full] = part[:, 2 * width :]


def unpack_pieces(token_pieces, cell_pieces):
    width = token_pieces[0].shape[-1]
    place = np.transpose(PACK.reshape(4, QUAD, -1), (0, 2, 1))
    return pl.pallas_call(
        unpack_kernel,
        out_shape=[
            shape((2 * LEVELS, HALF_LAT, HALF_LON // 2, 4 * width), bf16),
            shape((LEVELS, WLAT, WLON, width), bf16),
        ],
        compiler_params=params(),
        name="unpack",
    )(*token_pieces, jnp.asarray(place, bf16), *cell_pieces)


def routes(sizes, target):
    lons, lats, levs = sizes

    def number(i, a, k):
        return ((i % lons) * lats + a % lats) * levs + k % levs

    return [
        (number(i, a, k), number(*target(i, a, k)))
        for i in range(lons)
        for a in range(lats)
        for k in range(levs)
    ]


def send(block, sizes, target, back=False):
    pairs = routes(sizes, target)
    if back:
        pairs = [(b, a) for a, b in pairs]
    return lax.ppermute(block, ("lon", "lat", "lev"), pairs)


TOKEN_TARGETS = (
    lambda i, a, k: (i, a - 1, k),
    lambda i, a, k: (i - 1, a, k),
    lambda i, a, k: (i - 1, a - 1, k),
)
CELL_TARGETS = (
    lambda i, a, k: (i - (1 - k), a, k),
    lambda i, a, k: (i - (1 - k), a, 1 - k),
    lambda i, a, k: (i - (1 - k), a - 1, k),
    lambda i, a, k: (i - (1 - k), a - 1, 1 - k),
)


def per_device(
    sizes,
    tokens,
    packed_weight,
    output_weight,
    norm_gain,
    merge_gain,
    bias_table,
    bias_index,
    row_labels,
    column_valid,
    merged_grad,
):
    own, *rest = pack_pieces(tokens, merged_grad)
    pieces = [own] + [send(x, sizes, t) for x, t in zip(rest[:3], TOKEN_TARGETS)]
    cells = [send(x, sizes, t) for x, t in zip(rest[3:], CELL_TARGETS)]
    main, tail = window_bias(bias_table, bias_index, row_labels, column_valid)
    gain = norm_gain.reshape(1, -1)
    cell_gain = merge_gain.reshape(1, -1)
    weights, triple, keys_t, residual, data = forward(pieces, packed_weight, output_weight, gain, main, tail)
    scaled, moments, sent = cell_moments(residual, cells, cell_gain)
    before = send(sent, sizes, lambda i, a, k: (i, a + 1, k))
    after = before if sizes[1] == 2 else send(sent, sizes, lambda i, a, k: (i, a - 1, k))
    *merged, grad = merge_back(residual, scaled, moments, before, after, cell_gain)
    merged = [send(x, sizes, t, True) for x, t in zip(merged, CELL_TARGETS)]
    own, *rest = backward(grad, weights, triple, keys_t, data, packed_weight, output_weight, gain)
    grads = [own] + [send(x, sizes, t, True) for x, t in zip(rest, TOKEN_TARGETS)]
    return unpack_pieces(grads, merged)


def solution(mesh):
    sizes = tuple(mesh.shape[name] for name in ("lon", "lat", "lev"))
    placed = (
        P("lev", "lat", "lon", None),
        P(),
        P(),
        P(),
        P(),
        P("lev", "lat", None, None),
        P(),
        P("lat"),
        P(),
        P(None, "lat", ("lon", "lev"), None),
    )
    return jax.shard_map(
        functools.partial(per_device, sizes),
        mesh=mesh,
        in_specs=placed,
        out_specs=(P(None, "lat", ("lon", "lev"), None), P("lev", "lat", "lon", None)),
        check_vma=False,
    )
```

time: 236 us -> 87.3 us (0.37); the launches traced: 232 us -> 86.8 us
  local copies, waits for them, and re-layouts: 115 us -> 13.5 us
  other arithmetic: 43.3 us -> 0 us
  matrix products: 40.6 us -> 0 us
  Pallas kernels: 0 us -> 38.5 us
  starting transfers between devices: 18.3 us -> 25.5 us
  waiting for transfers between devices: 13.8 us -> 8.42 us
    gather x3 -> x0, local copies, waits for them, and re-layouts: 57.7 us -> none  [the longest x2 56.4 us: per_device(): typed = jnp.take(bias_table[0], bias_index, axis=2)]
    dot_general x10 -> x0, matrix products: 40.6 us -> none  [the longest x1 7.16 us: attend_back(): jnp.einsum('whqk,wkhd->wqhd', grad_scores, key, preferred_element_type=jn...]
    pallas_call x0 -> x7, Pallas kernels: none -> 38.5 us  [the longest x1 22.8 us: window_bias(): pl.pallas_call(bias_kernel, out_shape=[shape((heads * WIN, 128), f32)] *...]
    convert_element_type x10 -> x0, local copies, waits for them, and re-layouts: 17.4 us -> none  [the longest x3 6.35 us: norm_back(): scaled = grad.astype(jnp.float32) * gain]
    ppermute x8 -> x15, starting transfers between devices: 10 us -> 25.5 us  [send(): return lax.ppermute(block, ('lon', 'lat', 'lev'), pairs)]
    reduce_sum x6 -> x0, other arithmetic: 10.1 us -> none  [the longest x2 3.93 us: norm_back(): jnp.mean(scaled, axis=-1, keepdims=True)]
    concatenate x6 -> x0, other arithmetic: 9.23 us -> none  [the longest x2 3.41 us: roll_grid(): grid = jnp.concatenate((moved, rest), axis=1)]
    convert_element_type x6 -> x0, other arithmetic: 9.07 us -> none  [the longest x2 2.52 us: norm_rows(): return ((unit * gain).astype(jnp.bfloat16), unit, scale)]
  transfers between devices with their start and end apart: 10 -> 15, of which waited for: 7 -> 5; matrix products, arithmetic and copies ran while one was open for 39% -> 1% of each run, Pallas kernels for 0% -> 34%
where the time goes in v1:
time: 87.3 us; the launch traced here: 86.8 us
  Pallas kernels  38.5 us (44%)
  starting transfers between devices  25.5 us (29%)
  local copies, waits for them, and re-layouts  13.5 us (15%)
  waiting for transfers between devices  8.42 us (10%)
    ppermute x15, starting transfers between devices, send(): return lax.ppermute(block, ('lon', 'lat', 'lev'), pairs)  25.5 us
    pallas_call x1, Pallas kernels, window_bias(): pl.pallas_call(bias_kernel, out_shape=[shape((heads * WIN, 128), f32)] *...  22.8 us
    unnamed x38, local copies, waits for them, and re-layouts  11.1 us
    ppermute x15, waiting for transfers between devices, send(): return lax.ppermute(block, ('lon', 'lat', 'lev'), pairs)  8.42 us
    pallas_call x1, Pallas kernels, forward(): pl.pallas_call(forward_kernel, out_shape=[shape((HEADS * WIN, WIN), bf16)...  6.5 us
    pallas_call x1, Pallas kernels, backward(): pl.pallas_call(backward_kernel, out_shape=[shape((QUAD, width), bf16)] *...  6.47 us
  transfers between devices with their start and end apart: 15, of which 5 were waited for; matrix products, arithmetic and copies ran while one was open for 1% of the time, Pallas kernels for 34%

profile of v1, /device:TPU:0, one launch (start us, length us, event | category | flops | bytes accessed | tf_op | source)
XLA Modules:
  0.0 86.8 jit_solution(4136984030210995719)
XLA Ops:
  0.6 1.0 %copy.22.tokens = bf16[2,6,12,768]{3,2,1,0:T(8,128)(2,1)S(1)} copy(bf16[2,6,12,768]{3,0,2,1:T(2,128)(2,1)} %param.20) | data formatting | bytes 442368 | tf_op args[0]
  1.6 1.1 %copy.23.grad = bf16[4,3,3,3072]{3,2,1,0:T(4,128)(2,1)S(1)} copy(bf16[4,3,3,3072]{3,0,2,1:T(4,128)(2,1)} %param.29) | data formatting | bytes 442368 | tf_op args[9]
  2.7 0.0 copy-start.5
  2.7 0.9 %copy-done.5 = bf16[4,36,192]{2,1,0:T(8,128)(2,1)S(1)} copy-done((bf16[4,36,192]{2,1,0:T(8,128)(2,1)S(1)}, bf16[4,36,192]{2,1,0:T(8,128)(2,1)}, u32[]{:S(2)}) %copy-start.5) | copy-done | bytes 55320
  3.6 0.3 pack.2
  3.9 4.1 %collective-permute-start = (bf16[36,768]{1,0:T(8,128)(2,1)S(1)}, bf16[36,768]{1,0:T(8,128)(2,1)S(1)}, u32[]{:S(2)}, u32[]{:S(2)}) collective-permute-start(bf16[36,768]{1,0:T(8,128)(2,1)S(1)} %get-tuple-element.30), channel_id=1, source_target_pairs={{0,2},{1,3},{2,0},{3,1},{4,6},{5,7},{6,4},{7,5},{8,10},{9,11},{10,... | collective-permute-start | bytes 165896 | tf_op jit(solution)/shard_map/ppermute | solution.py:563
  8.0 1.6 %collective-permute-start.1 = (bf16[36,768]{1,0:T(8,128)(2,1)S(1)}, bf16[36,768]{1,0:T(8,128)(2,1)S(1)}, u32[]{:S(2)}, u32[]{:S(2)}) collective-permute-start(bf16[36,768]{1,0:T(8,128)(2,1)S(1)} %get-tuple-element.31), channel_id=1, source_target_pairs={{0,28},{1,29},{2,30},{3,31},{4,0},{5,1},{6,2},{7,3},{8,4},{9,5},{1... | collective-permute-start | bytes 165896 | tf_op jit(solution)/shard_map/ppermute | solution.py:563
  9.7 0.7 collective-permute-start.2
  10.4 2.1 %collective-permute-start.3 = (bf16[6,4608]{1,0:T(8,128)(2,1)S(1)}, bf16[6,4608]{1,0:T(8,128)(2,1)S(1)}, u32[]{:S(2)}, u32[]{:S(2)}) collective-permute-start(bf16[6,4608]{1,0:T(8,128)(2,1)S(1)} %get-tuple-element.36), channel_id=1, source_target_pairs={{0,28},{1,1},{2,30},{3,3},{4,0},{5,5},{6,2},{7,7},{8,4},{9,9},{10,... | collective-permute-start | bytes 165896 | tf_op jit(solution)/shard_map/ppermute | solution.py:563
  12.5 0.1 collective-permute-start.4
  12.6 0.7 reshape.10.gain
  13.3 1.0 %copy-done.11 = f32[1,1,24,3312]{3,2,1,0:T(8,128)S(1)} copy-done((f32[1,1,24,3312]{3,2,1,0:T(8,128)S(1)}, f32[1,1,24,3312]{3,2,1,0:T(8,128)}, u32[]{:S(2)}) %copy-start.11) | copy-done | bytes 317976
  14.3 0.9 %copy-done.12 = s32[144,144]{1,0:T(8,128)S(1)} copy-done((s32[144,144]{1,0:T(8,128)S(1)}, s32[144,144]{1,0:T(8,128)}, u32[]{:S(2)}) %copy-start.12) | copy-done | bytes 82968
  15.2 0.7 copy-done.13
  15.8 0.7 copy-done.14
  16.5 0.9 %copy-done.15 = s32[144,2]{1,0:T(8,128)S(1)} copy-done((s32[144,2]{1,0:T(8,128)S(1)}, s32[144,2]{1,0:T(8,128)}, u32[]{:S(2)}) %copy-start.15) | copy-done | bytes 1176
  17.4 0.9 %copy-done.16 = bf16[144,144]{1,0:T(8,128)(2,1)S(1)} copy-done((bf16[144,144]{1,0:T(8,128)(2,1)S(1)}, bf16[144,144]{1,0:T(8,128)(2,1)}, u32[]{:S(2)}) %copy-start.16) | copy-done | bytes 41496
  18.2 0.7 copy-done.17
  18.9 22.8 %bias.1 = (f32[3456,128]{1,0:T(8,128)S(1)}, f32[3456,128]{1,0:T(8,128)S(1)}) custom-call(f32[1,1,24,3312]{3,2,1,0:T(8,128)S(1)} %copy-done.11, s32[144,144]{1,0:T(8,128)S(1)} %copy-done.12, bf16[144,144]{1,0:T(8,128)(2,1)S(1)} %copy-done.16, s32[2,144]{1,0:T(2,128)S(1)} %copy-done.17, s32[144,2]{1,0:T(8,128)S(1)} %copy-done.15, s32[6]{0:T(128)S(1)} %copy-done.13, ...), custom_call_target="tpu_custom_call" | custom-call | flops 1000000000 | bytes 20000000 | tf_op jit(solution)/shard_map/bias/pallas_call | solution.py:232
  41.7 1.2 %copy-done.1 = f32[3456,128]{1,0:T(8,128)} copy-done((f32[3456,128]{1,0:T(8,128)}, f32[3456,128]{1,0:T(8,128)S(1)}, u32[]{:S(2)}) %copy-start.1) | copy-done | bytes 1769496
  43.0 1.2 %copy-done.2 = f32[3456,128]{1,0:T(8,128)} copy-done((f32[3456,128]{1,0:T(8,128)}, f32[3456,128]{1,0:T(8,128)S(1)}, u32[]{:S(2)}) %copy-start.2) | copy-done | bytes 1769496
  44.2 0.0 collective-permute-done.lat
  44.2 2.4 %collective-permute-start.5 = (bf16[6,4608]{1,0:T(8,128)(2,1)S(1)}, bf16[6,4608]{1,0:T(8,128)(2,1)S(1)}, u32[]{:S(2)}, u32[]{:S(2)}) collective-permute-start(bf16[6,4608]{1,0:T(8,128)(2,1)S(1)} %get-tuple-element.38), channel_id=1, source_target_pairs={{0,30},{1,3},{2,28},{3,1},{4,2},{5,7},{6,0},{7,5},{8,6},{9,11},{10... | collective-permute-start | bytes 165896 | tf_op jit(solution)/shard_map/ppermute | solution.py:563
  46.6 1.2 %collective-permute-start.6 = (bf16[6,4608]{1,0:T(8,128)(2,1)S(1)}, bf16[6,4608]{1,0:T(8,128)(2,1)S(1)}, u32[]{:S(2)}, u32[]{:S(2)}) collective-permute-start(bf16[6,4608]{1,0:T(8,128)(2,1)S(1)} %get-tuple-element.39), channel_id=1, source_target_pairs={{0,31},{1,2},{2,29},{3,0},{4,3},{5,6},{6,1},{7,4},{8,7},{9,10},{10... | collective-permute-start | bytes 165896 | tf_op jit(solution)/shard_map/ppermute | solution.py:563
  47.9 0.0 copy-start.9
  47.9 0.0 copy-start.10
  47.9 0.0 copy-start.6
  47.9 0.0 copy-start.7
  47.9 6.5 %forward.1 = (bf16[3456,144]{1,0:T(8,128)(2,1)S(1)}, bf16[144,2304]{1,0:T(8,128)(2,1)S(1)}, bf16[768,144]{1,0:T(8,128)(2,1)S(1)}, bf16[144,768]{1,0:T(8,128)(2,1)S(1)}, bf16[144,768]{1,0:T(8,128)(2,1)S(1)}) custom-call(bf16[36,768]{1,0:T(8,128)(2,1)S(1)} %get-tuple-element.29.own, bf16[36,768]{1,0:T(8,128)(2,1)S(1)} %collective-permute-done.lat, ...), custom_call_target="tpu_custom_call" | custom-call | flops 1000000000 | bytes 20000000 | tf_op jit(solution)/shard_map/forward/pallas_call | solution.py:310
  54.5 1.1 %moments.1 = (f32[144,768]{1,0:T(8,128)S(1)}, f32[144,128]{1,0:T(8,128)S(1)}, f32[24,128]{1,0:T(8,128)S(1)}) custom-call(bf16[144,768]{1,0:T(8,128)(2,1)S(1)} %get-tuple-element.35.residual, bf16[6,4608]{1,0:T(8,128)(2,1)S(1)} %collective-permute-done.3.same_here, bf16[6,4608]{1,0:T(8,128)(2,1)S(1)} %collective-permute-done.4.other_here, ...), custom_call_target="tpu_custom_call" | custom-call | flops 100000000 | bytes 1000000 | tf_op jit(solution)/shard_map/moments/pallas_call | solution.py:387
  55.7 2.5 %collective-permute-start.7 = (f32[24,128]{1,0:T(8,128)S(1)}, f32[24,128]{1,0:T(8,128)S(1)}, u32[]{:S(2)}, u32[]{:S(2)}) collective-permute-start(f32[24,128]{1,0:T(8,128)S(1)} %get-tuple-element.42), channel_id=1, source_target_pairs={{0,2},{1,3},{2,0},{3,1},{4,6},{5,7},{6,4},{7,5},{8,10},{9,11},{10,... | collective-permute-start | bytes 36872 | tf_op jit(solution)/shard_map/ppermute | solution.py:563
  58.1 2.2 %collective-permute-done.7.before.after = f32[24,128]{1,0:T(8,128)S(1)} collective-permute-done((f32[24,128]{1,0:T(8,128)S(1)}, f32[24,128]{1,0:T(8,128)S(1)}, u32[]{:S(2)}, u32[]{:S(2)}) %collective-permute-start.7) | collective-permute-done | bytes 12320 | tf_op jit(solution)/shard_map/ppermute | solution.py:563
  60.3 0.7 merge.1
  61.0 0.0 copy-start.3
  61.1 6.5 %backward.1 = (bf16[36,768]{1,0:T(8,128)(2,1)S(1)}, bf16[36,768]{1,0:T(8,128)(2,1)S(1)}, bf16[36,768]{1,0:T(8,128)(2,1)S(1)}, bf16[36,768]{1,0:T(8,128)(2,1)S(1)}) custom-call(bf16[144,768]{1,0:T(8,128)(2,1)S(1)} %get-tuple-element.43.grad, bf16[3456,144]{1,0:T(8,128)(2,1)S(1)} %get-tuple-element.44.weights, bf16[144,2304]{1,0:T(8,128)(2,1)S(1)} %get-tuple-element.45.triple, ...), custom_call_target="tpu_custom_call" | custom-call | flops 2000000000 | bytes 20000000 | tf_op jit(solution)/shard_map/backward/pallas_call | solution.py:492
  67.5 2.5 %collective-permute-start.8 = (bf16[36,768]{1,0:T(8,128)(2,1)S(1)}, bf16[36,768]{1,0:T(8,128)(2,1)S(1)}, u32[]{:S(2)}, u32[]{:S(2)}) collective-permute-start(bf16[36,768]{1,0:T(8,128)(2,1)S(1)} %get-tuple-element.49), channel_id=1, source_target_pairs={{2,0},{3,1},{0,2},{1,3},{6,4},{7,5},{4,6},{5,7},{10,8},{11,9},{8,1... | collective-permute-start | bytes 165896 | tf_op jit(solution)/shard_map/ppermute | solution.py:563
  70.0 1.7 %collective-permute-start.10 = (bf16[36,768]{1,0:T(8,128)(2,1)S(1)}, bf16[36,768]{1,0:T(8,128)(2,1)S(1)}, u32[]{:S(2)}, u32[]{:S(2)}) collective-permute-start(bf16[36,768]{1,0:T(8,128)(2,1)S(1)} %get-tuple-element.51), channel_id=1, source_target_pairs={{30,0},{31,1},{28,2},{29,3},{2,4},{3,5},{0,6},{1,7},{6,8},{7,9},{4... | collective-permute-start | bytes 165896 | tf_op jit(solution)/shard_map/ppermute | solution.py:563
  71.7 1.9 %collective-permute-start.11 = (bf16[6,4608]{1,0:T(8,128)(2,1)S(1)}, bf16[6,4608]{1,0:T(8,128)(2,1)S(1)}, u32[]{:S(2)}, u32[]{:S(2)}) collective-permute-start(bf16[6,4608]{1,0:T(8,128)(2,1)S(1)} %get-tuple-element.52), channel_id=1, source_target_pairs={{28,0},{1,1},{30,2},{3,3},{0,4},{5,5},{2,6},{7,7},{4,8},{9,9},{6,1... | collective-permute-start | bytes 165896 | tf_op jit(solution)/shard_map/ppermute | solution.py:563
  73.7 0.1 collective-permute-start.12
  73.7 2.7 %collective-permute-start.13 = (bf16[6,4608]{1,0:T(8,128)(2,1)S(1)}, bf16[6,4608]{1,0:T(8,128)(2,1)S(1)}, u32[]{:S(2)}, u32[]{:S(2)}) collective-permute-start(bf16[6,4608]{1,0:T(8,128)(2,1)S(1)} %get-tuple-element.54), channel_id=1, source_target_pairs={{30,0},{3,1},{28,2},{1,3},{2,4},{7,5},{0,6},{5,7},{6,8},{11,9},{4,... | collective-permute-start | bytes 165896 | tf_op jit(solution)/shard_map/ppermute | solution.py:563
  76.4 1.9 %collective-permute-start.14 = (bf16[6,4608]{1,0:T(8,128)(2,1)S(1)}, bf16[6,4608]{1,0:T(8,128)(2,1)S(1)}, u32[]{:S(2)}, u32[]{:S(2)}) collective-permute-start(bf16[6,4608]{1,0:T(8,128)(2,1)S(1)} %get-tuple-element.55), channel_id=1, source_target_pairs={{31,0},{2,1},{29,2},{0,3},{3,4},{6,5},{1,6},{4,7},{7,8},{10,9},{5,... | collective-permute-start | bytes 165896 | tf_op jit(solution)/shard_map/ppermute | solution.py:563
  78.3 0.3 collective-permute-done.11.same_here
  78.6 0.8 collective-permute-done.12.other_here
  79.4 1.0 %collective-permute-done.13.same_next = bf16[6,4608]{1,0:T(8,128)(2,1)S(1)} collective-permute-done((bf16[6,4608]{1,0:T(8,128)(2,1)S(1)}, bf16[6,4608]{1,0:T(8,128)(2,1)S(1)}, u32[]{:S(2)}, u32[]{:S(2)}) %collective-permute-start.13) | collective-permute-done | bytes 55328 | tf_op jit(solution)/shard_map/ppermute | solution.py:563
  80.4 4.2 %collective-permute-done.14.other_next = bf16[6,4608]{1,0:T(8,128)(2,1)S(1)} collective-permute-done((bf16[6,4608]{1,0:T(8,128)(2,1)S(1)}, bf16[6,4608]{1,0:T(8,128)(2,1)S(1)}, u32[]{:S(2)}, u32[]{:S(2)}) %collective-permute-start.14) | collective-permute-done | bytes 55328 | tf_op jit(solution)/shard_map/ppermute | solution.py:563
  84.5 0.5 unpack.1
  85.1 0.8 copy.24
  85.9 0.9 %copy.25 = bf16[2,6,12,768]{3,0,2,1:T(2,128)(2,1)} copy(bf16[2,6,12,768]{3,2,1,0:T(8,128)(2,1)S(1)} %get-tuple-element.57) | data formatting | bytes 442368 | tf_op jit(solution)/shard_map/unpack/pallas_call | solution.py:534
  (30 shorter events, 0.1 us)
Async XLA Ops:
  2.7 0.9 %copy-start.5 = (bf16[4,36,192]{2,1,0:T(8,128)(2,1)S(1)}, bf16[4,36,192]{2,1,0:T(8,128)(2,1)}, u32[]{:S(2)}) copy-start(bf16[4,36,192]{2,1,0:T(8,128)(2,1)} %constant.20.clone.pack) | copy-start | bytes 165892
  3.9 40.2 %collective-permute-start = (bf16[36,768]{1,0:T(8,128)(2,1)S(1)}, bf16[36,768]{1,0:T(8,128)(2,1)S(1)}, u32[]{:S(2)}, u32[]{:S(2)}) collective-permute-start(bf16[36,768]{1,0:T(8,128)(2,1)S(1)} %get-tuple-element.30), channel_id=1, source_target_pairs={{0,2},{1,3},{2,0},{3,1},{4,6},{5,7},{6,4},{7,5},{8,10},{9,11},{10,... | collective-permute-start | bytes 165896 | tf_op jit(solution)/shard_map/ppermute | solution.py:563
  8.0 38.6 %collective-permute-start.1 = (bf16[36,768]{1,0:T(8,128)(2,1)S(1)}, bf16[36,768]{1,0:T(8,128)(2,1)S(1)}, u32[]{:S(2)}, u32[]{:S(2)}) collective-permute-start(bf16[36,768]{1,0:T(8,128)(2,1)S(1)} %get-tuple-element.31), channel_id=1, source_target_pairs={{0,28},{1,29},{2,30},{3,31},{4,0},{5,1},{6,2},{7,3},{8,4},{9,5},{1... | collective-permute-start | bytes 165896 | tf_op jit(solution)/shard_map/ppermute | solution.py:563
  9.7 38.2 %collective-permute-start.2 = (bf16[36,768]{1,0:T(8,128)(2,1)S(1)}, bf16[36,768]{1,0:T(8,128)(2,1)S(1)}, u32[]{:S(2)}, u32[]{:S(2)}) collective-permute-start(bf16[36,768]{1,0:T(8,128)(2,1)S(1)} %get-tuple-element.32), channel_id=1, source_target_pairs={{0,30},{1,31},{2,28},{3,29},{4,2},{5,3},{6,0},{7,1},{8,6},{9,7},{1... | collective-permute-start | bytes 165896 | tf_op jit(solution)/shard_map/ppermute | solution.py:563
  10.4 44.1 %collective-permute-start.3 = (bf16[6,4608]{1,0:T(8,128)(2,1)S(1)}, bf16[6,4608]{1,0:T(8,128)(2,1)S(1)}, u32[]{:S(2)}, u32[]{:S(2)}) collective-permute-start(bf16[6,4608]{1,0:T(8,128)(2,1)S(1)} %get-tuple-element.36), channel_id=1, source_target_pairs={{0,28},{1,1},{2,30},{3,3},{4,0},{5,5},{6,2},{7,7},{8,4},{9,9},{10,... | collective-permute-start | bytes 165896 | tf_op jit(solution)/shard_map/ppermute | solution.py:563
  12.5 41.9 %collective-permute-start.4 = (bf16[6,4608]{1,0:T(8,128)(2,1)S(1)}, bf16[6,4608]{1,0:T(8,128)(2,1)S(1)}, u32[]{:S(2)}, u32[]{:S(2)}) collective-permute-start(bf16[6,4608]{1,0:T(8,128)(2,1)S(1)} %get-tuple-element.37), channel_id=1, source_target_pairs={{0,29},{1,0},{2,31},{3,2},{4,1},{5,4},{6,3},{7,6},{8,5},{9,8},{10,... | collective-permute-start | bytes 165896 | tf_op jit(solution)/shard_map/ppermute | solution.py:563
  13.3 1.0 %copy-start.11 = (f32[1,1,24,3312]{3,2,1,0:T(8,128)S(1)}, f32[1,1,24,3312]{3,2,1,0:T(8,128)}, u32[]{:S(2)}) copy-start(f32[1,1,24,3312]{3,2,1,0:T(8,128)} %table.1) | copy-start | bytes 953860
  14.3 0.9 %copy-start.12 = (s32[144,144]{1,0:T(8,128)S(1)}, s32[144,144]{1,0:T(8,128)}, u32[]{:S(2)}) copy-start(s32[144,144]{1,0:T(8,128)} %index.1) | copy-start | bytes 248836
  15.2 0.7 copy-start.13
  15.8 0.7 copy-start.14
  16.5 0.9 %copy-start.15 = (s32[144,2]{1,0:T(8,128)S(1)}, s32[144,2]{1,0:T(8,128)}, u32[]{:S(2)}) copy-start(s32[144,2]{1,0:T(8,128)} %constant.23.clone.coords_t) | copy-start | bytes 3460
  17.4 0.9 %copy-start.16 = (bf16[144,144]{1,0:T(8,128)(2,1)S(1)}, bf16[144,144]{1,0:T(8,128)(2,1)}, u32[]{:S(2)}) copy-start(bf16[144,144]{1,0:T(8,128)(2,1)} %constant.21.clone.order) | copy-start | bytes 124420
  18.2 0.7 copy-start.17
  18.9 28.9 %copy-start = (bf16[768,768]{1,0:T(8,128)(2,1)S(1)}, bf16[768,768]{1,0:T(8,128)(2,1)}, u32[]{:S(2)}) copy-start(bf16[768,768]{1,0:T(8,128)(2,1)} %output.3) | copy-start | bytes 3538948
  41.7 1.2 %copy-start.1 = (f32[3456,128]{1,0:T(8,128)}, f32[3456,128]{1,0:T(8,128)S(1)}, u32[]{:S(2)}) copy-start(f32[3456,128]{1,0:T(8,128)S(1)} %get-tuple-element.33.main) | copy-start | bytes 5308420
  43.0 1.2 %copy-start.2 = (f32[3456,128]{1,0:T(8,128)}, f32[3456,128]{1,0:T(8,128)S(1)}, u32[]{:S(2)}) copy-start(f32[3456,128]{1,0:T(8,128)S(1)} %get-tuple-element.34.tail) | copy-start | bytes 5308420
  44.2 10.3 %collective-permute-start.5 = (bf16[6,4608]{1,0:T(8,128)(2,1)S(1)}, bf16[6,4608]{1,0:T(8,128)(2,1)S(1)}, u32[]{:S(2)}, u32[]{:S(2)}) collective-permute-start(bf16[6,4608]{1,0:T(8,128)(2,1)S(1)} %get-tuple-element.38), channel_id=1, source_target_pairs={{0,30},{1,3},{2,28},{3,1},{4,2},{5,7},{6,0},{7,5},{8,6},{9,11},{10... | collective-permute-start | bytes 165896 | tf_op jit(solution)/shard_map/ppermute | solution.py:563
  46.6 7.8 %collective-permute-start.6 = (bf16[6,4608]{1,0:T(8,128)(2,1)S(1)}, bf16[6,4608]{1,0:T(8,128)(2,1)S(1)}, u32[]{:S(2)}, u32[]{:S(2)}) collective-permute-start(bf16[6,4608]{1,0:T(8,128)(2,1)S(1)} %get-tuple-element.39), channel_id=1, source_target_pairs={{0,31},{1,2},{2,29},{3,0},{4,3},{5,6},{6,1},{7,4},{8,7},{9,10},{10... | collective-permute-start | bytes 165896 | tf_op jit(solution)/shard_map/ppermute | solution.py:563
  47.9 6.6 %copy-start.4 = (f32[144,144]{1,0:T(8,128)S(1)}, f32[144,144]{1,0:T(8,128)}, u32[]{:S(2)}) copy-start(f32[144,144]{1,0:T(8,128)} %constant.24.clone.same) | copy-start | bytes 248836
  47.9 6.6 %copy-start.8 = (f32[144,1]{1,0:T(8,128)S(1)}, f32[144,1]{1,0:T(8,128)}, u32[]{:S(2)}) copy-start(f32[144,1]{1,0:T(8,128)} %constant.26.clone.count) | copy-start | bytes 1732
  47.9 6.6 %copy-start.9 = (f32[3072]{0:T(1024)S(1)}, f32[3072]{0:T(1024)}, u32[]{:S(2)}) copy-start(f32[3072]{0:T(1024)} %param.24) | copy-start | bytes 36868
  47.9 6.6 %copy-start.10 = (f32[24,144]{1,0:T(8,128)S(1)}, f32[24,144]{1,0:T(8,128)}, u32[]{:S(2)}) copy-start(f32[24,144]{1,0:T(8,128)} %constant.25.clone.pick) | copy-start | bytes 41476
  47.9 12.4 %copy-start.6 = (f32[144,1]{1,0:T(8,128)S(1)}, f32[144,1]{1,0:T(8,128)}, u32[]{:S(2)}) copy-start(f32[144,1]{1,0:T(8,128)} %constant.28.clone.halves) | copy-start | bytes 1732
  47.9 12.4 %copy-start.7 = (f32[144,24]{1,0:T(8,128)S(1)}, f32[144,24]{1,0:T(8,128)}, u32[]{:S(2)}) copy-start(f32[144,24]{1,0:T(8,128)} %constant.27.clone.spread) | copy-start | bytes 41476
  55.7 4.6 %collective-permute-start.7 = (f32[24,128]{1,0:T(8,128)S(1)}, f32[24,128]{1,0:T(8,128)S(1)}, u32[]{:S(2)}, u32[]{:S(2)}) collective-permute-start(f32[24,128]{1,0:T(8,128)S(1)} %get-tuple-element.42), channel_id=1, source_target_pairs={{0,2},{1,3},{2,0},{3,1},{4,6},{5,7},{6,4},{7,5},{8,10},{9,11},{10,... | collective-permute-start | bytes 36872 | tf_op jit(solution)/shard_map/ppermute | solution.py:563
  61.0 23.5 %copy-start.3 = (bf16[4,192,36]{2,1,0:T(8,128)(2,1)S(1)}, bf16[4,192,36]{2,1,0:T(8,128)(2,1)}, u32[]{:S(2)}) copy-start(bf16[4,192,36]{2,1,0:T(8,128)(2,1)} %constant.29.clone.place) | copy-start | bytes 165892
  67.5 6.2 %collective-permute-start.8 = (bf16[36,768]{1,0:T(8,128)(2,1)S(1)}, bf16[36,768]{1,0:T(8,128)(2,1)S(1)}, u32[]{:S(2)}, u32[]{:S(2)}) collective-permute-start(bf16[36,768]{1,0:T(8,128)(2,1)S(1)} %get-tuple-element.49), channel_id=1, source_target_pairs={{2,0},{3,1},{0,2},{1,3},{6,4},{7,5},{4,6},{5,7},{10,8},{11,9},{8,1... | collective-permute-start | bytes 165896 | tf_op jit(solution)/shard_map/ppermute | solution.py:563
  70.0 6.4 %collective-permute-start.9 = (bf16[36,768]{1,0:T(8,128)(2,1)S(1)}, bf16[36,768]{1,0:T(8,128)(2,1)S(1)}, u32[]{:S(2)}, u32[]{:S(2)}) collective-permute-start(bf16[36,768]{1,0:T(8,128)(2,1)S(1)} %get-tuple-element.50), channel_id=1, source_target_pairs={{28,0},{29,1},{30,2},{31,3},{0,4},{1,5},{2,6},{3,7},{4,8},{5,9},{6... | collective-permute-start | bytes 165896 | tf_op jit(solution)/shard_map/ppermute | solution.py:563
  70.0 8.3 %collective-permute-start.10 = (bf16[36,768]{1,0:T(8,128)(2,1)S(1)}, bf16[36,768]{1,0:T(8,128)(2,1)S(1)}, u32[]{:S(2)}, u32[]{:S(2)}) collective-permute-start(bf16[36,768]{1,0:T(8,128)(2,1)S(1)} %get-tuple-element.51), channel_id=1, source_target_pairs={{30,0},{31,1},{28,2},{29,3},{2,4},{3,5},{0,6},{1,7},{6,8},{7,9},{4... | collective-permute-start | bytes 165896 | tf_op jit(solution)/shard_map/ppermute | solution.py:563
  71.7 6.9 %collective-permute-start.11 = (bf16[6,4608]{1,0:T(8,128)(2,1)S(1)}, bf16[6,4608]{1,0:T(8,128)(2,1)S(1)}, u32[]{:S(2)}, u32[]{:S(2)}) collective-permute-start(bf16[6,4608]{1,0:T(8,128)(2,1)S(1)} %get-tuple-element.52), channel_id=1, source_target_pairs={{28,0},{1,1},{30,2},{3,3},{0,4},{5,5},{2,6},{7,7},{4,8},{9,9},{6,1... | collective-permute-start | bytes 165896 | tf_op jit(solution)/shard_map/ppermute | solution.py:563
  73.7 5.7 %collective-permute-start.12 = (bf16[6,4608]{1,0:T(8,128)(2,1)S(1)}, bf16[6,4608]{1,0:T(8,128)(2,1)S(1)}, u32[]{:S(2)}, u32[]{:S(2)}) collective-permute-start(bf16[6,4608]{1,0:T(8,128)(2,1)S(1)} %get-tuple-element.53), channel_id=1, source_target_pairs={{29,0},{0,1},{31,2},{2,3},{1,4},{4,5},{3,6},{6,7},{5,8},{8,9},{7,1... | collective-permute-start | bytes 165896 | tf_op jit(solution)/shard_map/ppermute | solution.py:563
  73.7 6.6 %collective-permute-start.13 = (bf16[6,4608]{1,0:T(8,128)(2,1)S(1)}, bf16[6,4608]{1,0:T(8,128)(2,1)S(1)}, u32[]{:S(2)}, u32[]{:S(2)}) collective-permute-start(bf16[6,4608]{1,0:T(8,128)(2,1)S(1)} %get-tuple-element.54), channel_id=1, source_target_pairs={{30,0},{3,1},{28,2},{1,3},{2,4},{7,5},{0,6},{5,7},{6,8},{11,9},{4,... | collective-permute-start | bytes 165896 | tf_op jit(solution)/shard_map/ppermute | solution.py:563
  76.4 8.1 %collective-permute-start.14 = (bf16[6,4608]{1,0:T(8,128)(2,1)S(1)}, bf16[6,4608]{1,0:T(8,128)(2,1)S(1)}, u32[]{:S(2)}, u32[]{:S(2)}) collective-permute-start(bf16[6,4608]{1,0:T(8,128)(2,1)S(1)} %get-tuple-element.55), channel_id=1, source_target_pairs={{31,0},{2,1},{29,2},{0,3},{3,4},{6,5},{1,6},{4,7},{7,8},{10,9},{5,... | collective-permute-start | bytes 165896 | tf_op jit(solution)/shard_map/ppermute | solution.py:563

commit v2 on v1

v2 whole, which is shorter than its diff:
```python
import functools

import jax
import jax.numpy as jnp
from jax import lax
from jax.experimental import pallas as pl
from jax.experimental.pallas import tpu as pltpu
from jax.sharding import PartitionSpec as P

HEADS = 24
HEAD = 32
WLAT = 6
WLON = 12
HALF_LAT = WLAT // 2
HALF_LON = WLON // 2
LEVELS = 2
WIN = LEVELS * WLAT * WLON
QUAD = WIN // 4
PAIRS = HALF_LON // 2
CELLS = LEVELS * PAIRS
GROUP = 128 // HEAD
TAIL = WIN - 128
TAIL_GROUPS = WIN // 8
BLOCKED = -1e30

epsilon = 1e-05
f32 = jnp.float32
bf16 = jnp.bfloat16

NN = (((1,), (0,)), ((), ()))
NT = (((1,), (1,)), ((), ()))


def token_row(quad, row, side, pair):
    return quad * QUAD + ((row * 2 + side) * PAIRS + pair) * LEVELS


def split_tokens(t):
    def digit(rest, size, count):
        found = jnp.zeros_like(rest)
        for i in range(1, count):
            found = found + (rest >= i * size).astype(jnp.int32)
        return found, rest - found * size

    quad, rest = digit(t, QUAD, 4)
    row, rest = digit(rest, 2 * CELLS, HALF_LAT)
    side, rest = digit(rest, CELLS, 2)
    pair, level = digit(rest, LEVELS, PAIRS)
    right, below = digit(quad, 2, 2)
    row = row + HALF_LAT * below
    column = right * HALF_LON + 2 * pair + side
    return row, column, level, right


def token_places(dims, axis):
    return split_tokens(lax.broadcasted_iota(jnp.int32, dims, axis))


def mxu(a, b, dims=NN):
    return lax.dot_general(a, b, dims, preferred_element_type=f32)


def exact(a, b):
    return lax.dot_general(a, b, NN, precision=lax.Precision.HIGHEST, preferred_element_type=f32)


def params(megabytes=12):
    return pltpu.CompilerParams(vmem_limit_bytes=megabytes << 20)


def shape(dims, dtype):
    return jax.ShapeDtypeStruct(dims, dtype)


def cost(flops, nbytes):
    return pl.CostEstimate(flops=flops, bytes_accessed=nbytes, transcendentals=0)


def lev_index():
    return lax.axis_index("lev")


def quadrant(values, quad):
    return values[quad * QUAD : (quad + 1) * QUAD]


def cell_places():
    return [(0, 0, True, 0), (0, 1, True, 1), (1, 0, True, 2), (1, 1, False, 0), (2, 0, False, 1), (2, 1, False, 2)]


def pack_kernel(tokens, grad, own, first, second, third, kept, fourth, fifth, rows, cells):
    width = tokens.shape[-1]
    for line in range(WLAT):
        for column in range(WLON):
            quad = (0 if line >= HALF_LAT else 1) + (0 if column >= HALF_LON else 2)
            inner = column % HALF_LON
            at = token_row(quad, line % HALF_LAT, inner % 2, inner // 2)
            rows[at : at + LEVELS, :] = tokens[line, column].astype(f32)
    upper = lax.axis_index("lev") == 1
    for row, odd, below, inner in cell_places():
        for pair in range(PAIRS):
            for side in range(2):
                block = side * 2 + odd
                part = grad[row, pair, :, block * width : (block + 1) * width].astype(f32)
                low, high = part[:LEVELS], part[LEVELS:]
                at = token_row(int(below), inner, side, pair)
                cells[at : at + LEVELS, :] = jnp.where(upper, high, low)
                at = at + 2 * QUAD
                cells[at : at + LEVELS, :] = jnp.where(upper, low, high)
    data, grads = rows[...], cells[...]
    lat, lon, both = quadrant(data, 1), quadrant(data, 2), quadrant(data, 3)
    here, below = quadrant(grads, 0), quadrant(grads, 1)
    own[...] = quadrant(data, 0).astype(bf16)
    first[...] = jnp.concatenate((jnp.where(upper, lat, both), below), axis=0).astype(bf16)
    second[...] = jnp.where(upper, both, lat).astype(bf16)
    third[...] = jnp.concatenate((lon, here), axis=0).astype(bf16)
    kept[...] = here.astype(bf16)
    fourth[...] = quadrant(grads, 2).astype(bf16)
    fifth[...] = quadrant(grads, 3).astype(bf16)


def pack_pieces(tokens, grad):
    width = tokens.shape[-1]
    piece, double = shape((QUAD, width), bf16), shape((2 * QUAD, width), bf16)
    return pl.pallas_call(
        pack_kernel,
        out_shape=[piece, double, piece, double, piece, piece, piece],
        scratch_shapes=[pltpu.VMEM((WIN, width), f32)] * 2,
        compiler_params=params(),
        name="pack",
    )(tokens, grad)


def bias_kernel(
    table_at, index_at, labels_at, valid_at, main, tail,
    table, index, labels, valid, split, fine, high, low, fine_high, fine_low, rest_rows, mask, mask_tail, done,
):
    copies = [
        pltpu.make_async_copy(source, target, done.at[i])
        for i, (source, target) in enumerate(
            ((table_at.at[0, 0], table), (index_at, index), (labels_at, labels), (valid_at, valid))
        )
    ]
    for copy in copies:
        copy.start()
    row_k, column_k, level_k, _ = token_places((WIN, 1), 0)
    row_q, _, _, _ = token_places((1, WIN), 1)
    natural = (level_k * WLAT + row_k) * WLON + column_k
    columns = lax.broadcasted_iota(jnp.int32, (WIN, WIN), 1)
    rows = lax.broadcasted_iota(jnp.int32, (WIN, WIN), 0)
    permute = jnp.where(natural == columns, 1.0, 0.0).astype(bf16)
    for copy in copies:
        copy.wait()

    label_q, label_k = jnp.zeros_like(row_q), jnp.zeros_like(row_k)
    for r in range(WLAT):
        label_q = jnp.where(row_q == r, labels[r], label_q)
        label_k = jnp.where(row_k == r, labels[r], label_k)
    valid_k = jnp.zeros_like(column_k)
    start = lax.axis_index("lon") * WLON + HALF_LON
    total = valid.shape[0]
    for c in range(WLON):
        at = start + c
        at = jnp.where(at >= total, at - total, at)
        valid_k = jnp.where(column_k == c, valid[at], valid_k)
    seen = (label_k == label_q) & ((valid_k > 0) | (rows == columns))
    added = jnp.where(seen, 0.0, BLOCKED).astype(f32)
    mask[...] = added[:, :128]
    mask_tail[...] = jnp.concatenate((added[:, 128:], jnp.zeros((WIN, 128 - TAIL), f32)), axis=1)

    heads, entries = table.shape
    gathered = 8
    wide = heads - gathered
    chunks = (entries + 255) // 256
    small_chunks = (entries + 127) // 128
    for c in range(small_chunks):
        size = min(128, entries - c * 128)
        part = table[wide:, c * 128 : c * 128 + size]
        if size < 128:
            part = jnp.concatenate((part, jnp.zeros((gathered, 128 - size), f32)), axis=1)
        fine[:, c * 128 : (c + 1) * 128] = part
    for c in range(chunks):
        size = min(256, entries - c * 256)
        part = table[:wide, c * 256 : c * 256 + size]
        if size < 256:
            part = jnp.concatenate((part, jnp.zeros((wide, 256 - size), f32)), axis=1)
        coarse = part.astype(bf16).astype(f32)
        split[c * wide : (c + 1) * wide, :] = coarse
        split[(chunks + c) * wide : (chunks + c + 1) * wide, :] = part - coarse
    source = split[...].astype(bf16)
    part_rows = chunks * wide

    def place(values, out):
        moved = mxu(mxu(permute, values.astype(f32).astype(bf16), NT).astype(bf16), permute, NT)
        out[0:WIN, :] = moved[:, :128]
        rest_rows[...] = jnp.concatenate((moved[:, 128:], jnp.zeros((WIN, 128 - TAIL), f32)), axis=1)
        total = None
        for g in range(8):
            piece = rest_rows[pl.ds(g, TAIL_GROUPS, stride=8), :]
            if g:
                piece = pltpu.roll(piece, TAIL * g, 1)
            total = piece if total is None else total + piece
        out[WIN : WIN + TAIL_GROUPS, :] = total

    entry = index[...]
    place(lax.shift_right_logical(entry, 8), high)
    place(entry & 255, low)
    upper, lower = high[...], low[...]
    far = lower >= 128.0
    fine_high[...] = (2.0 * upper + jnp.where(far, 1.0, 0.0)).astype(jnp.int32)
    fine_low[...] = jnp.where(far, lower - 128.0, lower).astype(jnp.int32)
    depth = lax.broadcasted_iota(jnp.int32, (256, 128), 0).astype(f32).astype(bf16)
    one, zero = jnp.ones((), bf16), jnp.zeros((), bf16)

    def lookup(row):
        hot = []
        for j in range(2):
            lane = jnp.broadcast_to(low[pl.ds(row + j, 1), :], (16, 128)).astype(bf16)
            hot.append(jnp.where(depth == jnp.concatenate([lane] * 16, axis=0), one, zero))
        product = mxu(source, jnp.concatenate(hot, axis=1))
        out = []
        for j in range(2):
            here = slice(j * 128, (j + 1) * 128)
            chunk = jnp.broadcast_to(high[pl.ds(row + j, 1), :], (8, 128))
            coarse, rest = [None] * (wide // 8), [None] * (wide // 8)
            for c in range(chunks):
                hit = chunk == c
                for block in range(wide // 8):
                    at = c * wide + block * 8
                    a = product[at : at + 8, here]
                    b = product[part_rows + at : part_rows + at + 8, here]
                    coarse[block] = a if c == 0 else jnp.where(hit, a, coarse[block])
                    rest[block] = b if c == 0 else jnp.where(hit, b, rest[block])
            found = [a + b for a, b in zip(coarse, rest)]
            chunk = jnp.broadcast_to(fine_high[pl.ds(row + j, 1), :], (8, 128))
            lane = jnp.broadcast_to(fine_low[pl.ds(row + j, 1), :], (8, 128))
            value = None
            for c in range(small_chunks):
                a = jnp.take_along_axis(fine[:, c * 128 : (c + 1) * 128], lane, axis=1, mode="promise_in_bounds")
                value = a if c == 0 else jnp.where(chunk == c, a, value)
            found.append(value)
            out.append(found)
        return out

    for key in range(0, WIN, 2):
        for j, found in enumerate(lookup(key)):
            extra = jnp.broadcast_to(mask[key + j : key + j + 1, :], (8, 128))
            for block, value in enumerate(found):
                main[pl.ds(block * 8 * WIN + key + j, 8, stride=WIN), :] = value + extra
    for row in range(0, TAIL_GROUPS, 2):
        for j, found in enumerate(lookup(WIN + row)):
            for block, value in enumerate(found):
                for g in range(8):
                    key = (row + j) * 8 + g
                    moved = pltpu.roll(value, 128 - TAIL * g, 1) if g else value
                    extra = jnp.broadcast_to(mask_tail[key : key + 1, :], (8, 128))
                    tail[pl.ds(block * 8 * WIN + key, 8, stride=WIN), :] = moved + extra


def window_bias(table, index, labels, valid):
    heads, entries = table.shape[-2:]
    whole = (entries + 255) // 256
    index_rows = WIN + TAIL_GROUPS
    return pl.pallas_call(
        bias_kernel,
        out_shape=[shape((heads * WIN, 128), f32)] * 2,
        in_specs=[pl.BlockSpec(memory_space=pltpu.MemorySpace.HBM)] * 4,
        scratch_shapes=[
            pltpu.VMEM((heads, entries), f32),
            pltpu.VMEM(index.shape, jnp.int32),
            pltpu.SMEM(labels.shape, jnp.int32),
            pltpu.SMEM(valid.shape, jnp.int32),
            pltpu.VMEM((2 * whole * (heads - 8), 256), f32),
            pltpu.VMEM((8, (entries + 127) // 128 * 128), f32),
            pltpu.VMEM((index_rows, 128), f32),
            pltpu.VMEM((index_rows, 128), f32),
            pltpu.VMEM((index_rows, 128), jnp.int32),
            pltpu.VMEM((index_rows, 128), jnp.int32),
            pltpu.VMEM((WIN, 128), f32),
            pltpu.VMEM((WIN, 128), f32),
            pltpu.VMEM((WIN, 128), f32),
            pltpu.SemaphoreType.DMA((4,)),
        ],
        compiler_params=params(),
        cost_estimate=cost(10**10, 2 * 10**7),
        name="bias",
    )(table, index, labels, valid)


def row_mean(values):
    return jnp.mean(values, axis=-1, keepdims=True)


def unit_rows(data):
    center = data - row_mean(data)
    scale = lax.rsqrt(row_mean(center * center) + epsilon)
    return center * scale, scale


def stacked(block):
    lane = lax.broadcasted_iota(jnp.int32, (1, 128), 1) // HEAD
    return jnp.concatenate(
        [jnp.where(lane == h, block, jnp.zeros((), block.dtype)) for h in range(GROUP)], axis=0
    )


def lanes_of(parts):
    lane = lax.broadcasted_iota(jnp.int32, (1, 128), 1) // HEAD
    out = parts[0]
    for h in range(1, GROUP):
        out = jnp.where(lane == h, parts[h], out)
    return out


def forward_kernel(
    own, first, second, third, packed, output, gain, main, tail,
    weights, triple, keys_t, residual, tokens,
    gathered, values_t, heads_t,
):
    width = own.shape[-1]
    upper = lax.axis_index("lev") == 1
    a, b = first[...].astype(f32)[:QUAD], second[...].astype(f32)
    lon = third[...].astype(f32)[:QUAD]
    for quad, piece in enumerate((own[...].astype(f32), jnp.where(upper, a, b), lon, jnp.where(upper, b, a))):
        gathered[quad * QUAD : (quad + 1) * QUAD, :] = piece
    data = gathered[...]
    tokens[...] = data.astype(bf16)
    unit, _ = unit_rows(data)
    normed = (unit * gain[...].reshape(1, -1)).astype(bf16)
    triple[...] = mxu(normed, packed[...]).astype(bf16)
    keys_t[...] = triple[:, width : 2 * width].astype(f32).T.astype(bf16)
    values_t[...] = triple[:, 2 * width :].astype(f32).T.astype(bf16)
    for g in range(width // 128):
        query = triple[:, g * 128 : (g + 1) * 128]
        key = triple[:, width + g * 128 : width + (g + 1) * 128]
        product = mxu(stacked(key), query, NT) * HEAD ** (-0.5)
        for h in range(GROUP):
            head = g * GROUP + h
            at = slice(head * WIN, (head + 1) * WIN)
            bias = jnp.concatenate((main[at, :], tail[at, :TAIL]), axis=1)
            scores = product[h * WIN : (h + 1) * WIN] + bias
            raised = jnp.exp(scores - jnp.max(scores, axis=0, keepdims=True))
            share = (raised * (1.0 / jnp.sum(raised, axis=0, keepdims=True))).astype(bf16)
            weights[at, :] = share
            here = slice(head * HEAD, (head + 1) * HEAD)
            heads_t[here, :] = mxu(values_t[here, :], share)
    heads = heads_t[...].T.astype(bf16)
    attended = mxu(heads, output[...]).astype(bf16)
    residual[...] = (data + attended.astype(f32)).astype(bf16)


def forward(pieces, packed, output, gain, main, tail):
    width = output.shape[0]
    return pl.pallas_call(
        forward_kernel,
        out_shape=[
            shape((HEADS * WIN, WIN), bf16),
            shape((WIN, 3 * width), bf16),
            shape((width, WIN), bf16),
            shape((WIN, width), bf16),
            shape((WIN, width), bf16),
        ],
        scratch_shapes=[
            pltpu.VMEM((WIN, width), f32),
            pltpu.VMEM((width, WIN), bf16),
            pltpu.VMEM((width, WIN), f32),
        ],
        compiler_params=params(),
        cost_estimate=cost(10**9, 2 * 10**7),
        name="forward",
    )(*pieces, packed, output, gain, main, tail)


def gain_rows(gain, out):
    width = out.shape[-1]
    for quad in range(4):
        for row in range(HALF_LAT):
            odd = 1 - (row + (quad & 1) * HALF_LAT) % 2
            for side in range(2):
                block = side * 2 + odd
                at = token_row(quad, row, side, 0)
                factor = gain[:, block * width : (block + 1) * width]
                out[at : at + CELLS, :] = jnp.broadcast_to(factor, (CELLS, width))


def cell_number(places):
    row, column, level, right = places
    band = lax.shift_right_logical(row + 1, 1)
    return (band * HALF_LON + lax.shift_right_logical(column, 1)) * LEVELS + level


def split_row(places):
    return (places[0] == 0) | (places[0] == WLAT - 1)


def sent_tokens(dims, axis):
    i = lax.broadcasted_iota(jnp.int32, dims, axis)
    last = (i >= 2 * CELLS).astype(jnp.int32)
    i = i - last * 2 * CELLS
    right = (i >= CELLS).astype(jnp.int32)
    cell = i - right * CELLS
    return (2 * right + last) * QUAD + last * (HALF_LAT - 1) * 2 * CELLS + cell


def columns_of(parts):
    lane = lax.broadcasted_iota(jnp.int32, (1, 128), 1)
    out = jnp.zeros((WIN, 128), f32)
    for i, part in enumerate(parts):
        out = jnp.where(lane == i, part, out)
    return out


def moments_kernel(residual, kept, first, third, fourth, fifth, gain, scaled, moments, sent, factors):
    width = residual.shape[-1]
    upper = lax.axis_index("lev") == 1
    own, a, b = kept[...].astype(f32), fourth[...].astype(f32), fifth[...].astype(f32)
    below, right = first[...].astype(f32)[QUAD:], third[...].astype(f32)[QUAD:]
    gain_rows(gain, factors)
    for quad, part in enumerate((
        jnp.where(upper, own, a),
        jnp.where(upper, below, b),
        jnp.where(upper, a, right),
        jnp.where(upper, b, below),
    )):
        scaled[quad * QUAD : (quad + 1) * QUAD, :] = part
    grad = scaled[...] * factors[...]
    scaled[...] = grad
    data = residual[...].astype(f32)
    down = token_places((WIN, 1), 0)
    grouping = jnp.where(cell_number(down) == cell_number(token_places((1, WIN), 1)), 1.0, 0.0).astype(f32)
    inverse = jnp.where(split_row(down), 1 / (2 * width), 1 / (4 * width)).astype(f32)
    total = jnp.sum(data, axis=-1, keepdims=True)
    middle = exact(grouping, jnp.broadcast_to(total, (WIN, 128)))[:, 0:1] * inverse
    center = data - middle
    sums = columns_of((
        jnp.sum(center * center, axis=-1, keepdims=True),
        jnp.sum(grad, axis=-1, keepdims=True),
        jnp.sum(grad * center, axis=-1, keepdims=True),
    ))
    sums = exact(grouping, sums)
    lane = lax.broadcasted_iota(jnp.int32, (1, 128), 1)
    sums = jnp.where(lane == 3, middle, sums)
    moments[...] = sums
    pick = sent_tokens((4 * CELLS, 1), 0) == lax.broadcasted_iota(jnp.int32, (4 * CELLS, WIN), 1)
    sent[...] = exact(jnp.where(pick, 1.0, 0.0).astype(f32), sums)


def cell_moments(residual, pieces, gain):
    width = residual.shape[-1]
    return pl.pallas_call(
        moments_kernel,
        out_shape=[shape((WIN, width), f32), shape((WIN, 128), f32), shape((4 * CELLS, 128), f32)],
        scratch_shapes=[pltpu.VMEM((WIN, width), f32)],
        compiler_params=params(),
        cost_estimate=cost(10**8, 10**6),
        name="moments",
    )(residual, *pieces, gain)


def merge_kernel(residual, scaled, moments, before, after, gain, kept, below, right, far, grad, factors):
    width = residual.shape[-1]
    upper = lax.axis_index("lev") == 1
    gain_rows(gain, factors)
    down = token_places((WIN, 1), 0)
    shared = split_row(down)
    row = down[0]
    sender = split_tokens(sent_tokens((1, 4 * CELLS), 1))
    match = (cell_number(down) == cell_number(sender)) & shared
    there = jnp.concatenate((before[2 * CELLS :], after[: 2 * CELLS]), axis=0)
    theirs = exact(jnp.where(match, 1.0, 0.0).astype(f32), there)
    mine = moments[...]
    full = 4.0 * width
    middle = jnp.where(shared, 0.5 * (mine[:, 3:4] + theirs[:, 3:4]), mine[:, 3:4])
    gap = theirs[:, 3:4] - mine[:, 3:4]
    square = jnp.where(shared, mine[:, 0:1] + theirs[:, 0:1] + gap * gap * width, mine[:, 0:1])
    scale = lax.rsqrt(square / full + epsilon)
    grad_sum = jnp.where(shared, mine[:, 1:2] + theirs[:, 1:2], mine[:, 1:2])
    cross = jnp.where(
        shared,
        mine[:, 2:3] + (mine[:, 3:4] - middle) * mine[:, 1:2]
        + theirs[:, 2:3] + (theirs[:, 3:4] - middle) * theirs[:, 1:2],
        mine[:, 2:3],
    )
    unit = (residual[...].astype(f32) - middle) * scale
    grad[...] = (scale * (scaled[...] - grad_sum / full - unit * (cross * scale / full))).astype(bf16)
    out = unit * factors[...]
    parts = [quadrant(out, quad) for quad in range(4)]
    kept[...] = jnp.where(upper, parts[0], parts[2]).astype(bf16)
    below[...] = jnp.where(upper, parts[1], parts[3]).astype(bf16)
    right[...] = jnp.where(upper, parts[2], parts[0]).astype(bf16)
    far[...] = jnp.where(upper, parts[3], parts[1]).astype(bf16)


def merge_back(residual, scaled, moments, before, after, gain):
    width = residual.shape[-1]
    piece = shape((QUAD, width), bf16)
    return pl.pallas_call(
        merge_kernel,
        out_shape=[piece] * 4 + [shape((WIN, width), bf16)],
        scratch_shapes=[pltpu.VMEM((WIN, width), f32)],
        compiler_params=params(),
        cost_estimate=cost(10**8, 10**6),
        name="merge",
    )(residual, scaled, moments, before, after, gain)


def backward_kernel(grad, weights, triple, keys_t, output, joined, queries_t):
    width = grad.shape[-1]
    upstream = grad[...]
    grad_heads = mxu(upstream, output[...], NT).astype(bf16)
    for g in range(width // 128):
        here = slice(g * 128, (g + 1) * 128)
        query = triple[:, g * 128 : (g + 1) * 128]
        value = triple[:, 2 * width + g * 128 : 2 * width + (g + 1) * 128]
        arriving = grad_heads[:, here]
        product = mxu(stacked(value), arriving, NT)
        shares = weights[g * GROUP * WIN : (g + 1) * GROUP * WIN, :]
        grad_value = mxu(shares, arriving)
        slopes = []
        for h in range(GROUP):
            head = g * GROUP + h
            share = shares[h * WIN : (h + 1) * WIN].astype(f32)
            change = product[h * WIN : (h + 1) * WIN]
            level = jnp.sum(share * change, axis=0, keepdims=True)
            slope = (share * (change - level) * HEAD ** (-0.5)).astype(bf16)
            at = slice(head * HEAD, (head + 1) * HEAD)
            queries_t[at, :] = mxu(keys_t[at, :], slope)
            slopes.append(slope)
        grad_key = mxu(jnp.concatenate(slopes, axis=0), query)
        split = [slice(h * WIN, (h + 1) * WIN) for h in range(GROUP)]
        joined[:, width + g * 128 : width + (g + 1) * 128] = lanes_of([grad_key[s] for s in split]).astype(bf16)
        joined[:, 2 * width + g * 128 : 2 * width + (g + 1) * 128] = lanes_of(
            [grad_value[s] for s in split]
        ).astype(bf16)
    joined[:, :width] = queries_t[...].T.astype(bf16)


def backward(grad, weights, triple, keys_t, output):
    width = grad.shape[-1]
    return pl.pallas_call(
        backward_kernel,
        out_shape=shape((WIN, 3 * width), bf16),
        scratch_shapes=[pltpu.VMEM((width, WIN), f32)],
        compiler_params=params(),
        cost_estimate=cost(10**10, 2 * 10**7),
        name="backward",
    )(grad, weights, triple, keys_t, output)


def finish_kernel(grad, joined, tokens, packed, gain, own, lat, lon, both):
    grad_inputs = mxu(joined[...], packed[...], NT).astype(bf16)
    unit, scale = unit_rows(tokens[...].astype(f32))
    scaled = grad_inputs.astype(f32) * gain[...].reshape(1, -1)
    out = grad[...].astype(f32) + scale * (scaled - row_mean(scaled) - unit * row_mean(scaled * unit))
    for quad, piece in enumerate((own, lat, lon, both)):
        piece[...] = quadrant(out, quad).astype(bf16)


def finish(grad, joined, tokens, packed, gain):
    width = grad.shape[-1]
    return pl.pallas_call(
        finish_kernel,
        out_shape=[shape((QUAD, width), bf16)] * 4,
        compiler_params=params(),
        cost_estimate=cost(10**9, 2 * 10**6),
        name="finish",
    )(grad, joined, tokens, packed, gain)


def unpack_kernel(own, lat, lon, both, same_here, other_here, same_next, other_next, merged, tokens):
    width = own.shape[-1]
    quads = [piece[...].astype(f32) for piece in (own, lat, lon, both)]
    for line in range(WLAT):
        for column in range(WLON):
            quad = (0 if line >= HALF_LAT else 1) + (0 if column >= HALF_LON else 2)
            inner = column % HALF_LON
            at = token_row(0, line % HALF_LAT, inner % 2, inner // 2)
            tokens[line, column] = quads[quad][at : at + LEVELS].astype(bf16)
    upper = lax.axis_index("lev") == 1
    same = (same_here[...].astype(f32), same_next[...].astype(f32))
    other = (other_here[...].astype(f32), other_next[...].astype(f32))
    low = [jnp.where(upper, b, a) for a, b in zip(same, other)]
    high = [jnp.where(upper, a, b) for a, b in zip(same, other)]
    for row, odd, below, inner in cell_places():
        for pair in range(PAIRS):
            for side in range(2):
                block = side * 2 + odd
                at = token_row(0, inner, side, pair)
                here = slice(at, at + LEVELS)
                merged[row, pair, :, block * width : (block + 1) * width] = jnp.concatenate(
                    (low[below][here], high[below][here]), axis=0
                ).astype(bf16)


def unpack_pieces(token_pieces, cell_pieces):
    width = token_pieces[0].shape[-1]
    return pl.pallas_call(
        unpack_kernel,
        out_shape=[
            shape((HALF_LAT, PAIRS, 2 * LEVELS, 4 * width), bf16),
            shape((WLAT, WLON, LEVELS, width), bf16),
        ],
        compiler_params=params(),
        name="unpack",
    )(*token_pieces, *cell_pieces)


def routes(sizes, target):
    lons, lats, levs = sizes

    def number(i, a, k):
        return ((i % lons) * lats + a % lats) * levs + k % levs

    return [
        (number(i, a, k), number(*target(i, a, k)))
        for i in range(lons)
        for a in range(lats)
        for k in range(levs)
    ]


def send(block, sizes, target, back=False):
    pairs = routes(sizes, target)
    if back:
        pairs = [(b, a) for a, b in pairs]
    return lax.ppermute(block, ("lon", "lat", "lev"), pairs)


FIRST = lambda i, a, k: (i - (1 - k), a - 1, k)
SECOND = lambda i, a, k: (i - k, a - 1, k)
THIRD = lambda i, a, k: (i - 1, a, k)
FOURTH = lambda i, a, k: (i - (1 - k), a, 1 - k)
FIFTH = lambda i, a, k: (i - (1 - k), a - 1, 1 - k)
LAT = lambda i, a, k: (i, a - 1, k)
LON = lambda i, a, k: (i - 1, a, k)
BOTH = lambda i, a, k: (i - 1, a - 1, k)
HERE = lambda i, a, k: (i - (1 - k), a, k)


def per_device(
    sizes,
    tokens,
    packed_weight,
    output_weight,
    norm_gain,
    merge_gain,
    bias_table,
    bias_index,
    row_labels,
    column_valid,
    merged_grad,
):
    own, first, second, third, kept, fourth, fifth = pack_pieces(
        tokens.transpose(1, 2, 0, 3), merged_grad.transpose(1, 2, 0, 3)
    )
    first = send(first, sizes, FIRST)
    second = send(second, sizes, SECOND)
    third = send(third, sizes, THIRD)
    fourth = send(fourth, sizes, FOURTH)
    fifth = send(fifth, sizes, FIFTH)
    main, tail = window_bias(bias_table, bias_index, row_labels, column_valid)
    cell_gain = merge_gain.reshape(1, -1)
    weights, triple, keys_t, residual, data = forward(
        (own, first, second, third), packed_weight, output_weight, norm_gain, main, tail
    )
    scaled, moments, sent = cell_moments(residual, (kept, first, third, fourth, fifth), cell_gain)
    before = send(sent, sizes, lambda i, a, k: (i, a + 1, k))
    after = before if sizes[1] == 2 else send(sent, sizes, lambda i, a, k: (i, a - 1, k))
    kept, below, right, far, grad = merge_back(residual, scaled, moments, before, after, cell_gain)
    below = send(below, sizes, FIRST, True)
    far = send(far, sizes, FIFTH, True)
    right = send(right, sizes, FOURTH, True)
    kept = send(kept, sizes, HERE, True)
    joined = backward(grad, weights, triple, keys_t, output_weight)
    joined, kept, below, right, far = lax.optimization_barrier((joined, kept, below, right, far))
    own, lat, lon, both = finish(grad, joined, data, packed_weight, norm_gain)
    lat = send(lat, sizes, LAT, True)
    both = send(both, sizes, BOTH, True)
    lon = send(lon, sizes, LON, True)
    merged, grads = unpack_pieces((own, lat, lon, both), (kept, right, below, far))
    return merged.transpose(2, 0, 1, 3), grads.transpose(2, 0, 1, 3)


def solution(mesh):
    sizes = tuple(mesh.shape[name] for name in ("lon", "lat", "lev"))
    placed = (
        P("lev", "lat", "lon", None),
        P(),
        P(),
        P(),
        P(),
        P("lev", "lat", None, None),
        P(),
        P("lat"),
        P(),
        P(None, "lat", ("lon", "lev"), None),
    )
    return jax.shard_map(
        functools.partial(per_device, sizes),
        mesh=mesh,
        in_specs=placed,
        out_specs=(P(None, "lat", ("lon", "lev"), None), P("lev", "lat", "lon", None)),
        check_vma=False,
    )
```

time: 87.3 us -> 56.7 us (0.65)
  Pallas kernels: 38.5 us -> 18.4 us
  local copies, waits for them, and re-layouts: 13.5 us -> 5.16 us
  starting transfers between devices: 25.5 us -> 20.4 us
  waiting for transfers between devices: 8.42 us -> 11.6 us
    pallas_call x1, Pallas kernels: 22.8 us -> 7.89 us  [window_bias(): pl.pallas_call(bias_kernel, out_shape=[shape((heads * WIN, 128), f32)] *...]
    unnamed x38 -> x20, local copies, waits for them, and re-layouts: 11.1 us -> 5.16 us
    ppermute x15 -> x13, starting transfers between devices: 25.5 us -> 20.4 us  [send(): return lax.ppermute(block, ('lon', 'lat', 'lev'), pairs)]
    ppermute x15 -> x13, waiting for transfers between devices: 8.42 us -> 11.6 us  [send(): return lax.ppermute(block, ('lon', 'lat', 'lev'), pairs)]
    pallas_call x1, Pallas kernels: 6.5 us -> 3.35 us  [forward(): pl.pallas_call(forward_kernel, out_shape=[shape((HEADS * WIN, WIN), bf16)...]
    pallas_call x3 -> x4, Pallas kernels: 7.35 us -> 5.51 us  [the longest x1 2.8 us: backward(): pl.pallas_call(backward_kernel, out_shape=shape((WIN, 3 * width), bf16),...]
    pallas_call x2 -> x0, local copies, waits for them, and re-layouts: 1.73 us -> none  [unpack_pieces(): pl.pallas_call(unpack_kernel, out_shape=[shape((2 * LEVELS, HALF_LAT, HAL...]
  transfers between devices with their start and end apart: 15 -> 13, of which waited for: 5 -> 5; matrix products, arithmetic and copies ran while one was open for 1% -> 0% of each run, Pallas kernels for 34% -> 25%
where the time goes in v2:
time: 56.7 us; the launch traced here: 56.4 us
  starting transfers between devices  20.4 us (36%)
  Pallas kernels  18.4 us (32%)
  waiting for transfers between devices  11.6 us (20%)
  local copies, waits for them, and re-layouts  5.16 us (9%)
  between operations  0.82 us (1%)
    ppermute x13, starting transfers between devices, send(): return lax.ppermute(block, ('lon', 'lat', 'lev'), pairs)  20.4 us
    ppermute x13, waiting for transfers between devices, send(): return lax.ppermute(block, ('lon', 'lat', 'lev'), pairs)  11.6 us
    pallas_call x1, Pallas kernels, window_bias(): pl.pallas_call(bias_kernel, out_shape=[shape((heads * WIN, 128), f32)] *...  7.89 us
    unnamed x20, local copies, waits for them, and re-layouts  5.16 us
    pallas_call x1, Pallas kernels, forward(): pl.pallas_call(forward_kernel, out_shape=[shape((HEADS * WIN, WIN), bf16)...  3.35 us
    pallas_call x1, Pallas kernels, backward(): pl.pallas_call(backward_kernel, out_shape=shape((WIN, 3 * width), bf16),...  2.8 us
    pallas_call x1, Pallas kernels, finish(): pl.pallas_call(finish_kernel, out_shape=[shape((QUAD, width), bf16)] * 4,...  1.51 us
    pallas_call x1, Pallas kernels, cell_moments(): pl.pallas_call(moments_kernel, out_shape=[shape((WIN, width), f32), shape...  1.15 us
  transfers between devices with their start and end apart: 13, of which 5 were waited for; matrix products, arithmetic and copies ran while one was open for 0% of the time, Pallas kernels for 25%

profile of v2, /device:TPU:0, one launch (start us, length us, event | category | flops | bytes accessed | tf_op | source)
XLA Modules:
  0.0 56.4 jit_solution(7176165988091351426)
XLA Ops:
  0.6 0.0 copy-start.2
  0.6 0.9 %copy-done.2 = bf16[2,6,12,768]{3,0,2,1:T(2,128)(2,1)S(1)} copy-done((bf16[2,6,12,768]{3,0,2,1:T(2,128)(2,1)S(1)}, bf16[2,6,12,768]{3,0,2,1:T(2,128)(2,1)}, u32[]{:S(2)}) %copy-start.2) | copy-done | bytes 221208
  1.6 0.0 copy-start.3
  1.6 0.9 %copy-done.3 = bf16[4,3,3,3072]{3,0,2,1:T(4,128)(2,1)S(1)} copy-done((bf16[4,3,3,3072]{3,0,2,1:T(4,128)(2,1)S(1)}, bf16[4,3,3,3072]{3,0,2,1:T(4,128)(2,1)}, u32[]{:S(2)}) %copy-start.3) | copy-done | bytes 221208
  2.5 0.3 pack.1
  2.8 4.1 %collective-permute-start.1 = (bf16[36,768]{1,0:T(8,128)(2,1)S(1)}, bf16[36,768]{1,0:T(8,128)(2,1)S(1)}, u32[]{:S(2)}, u32[]{:S(2)}) collective-permute-start(bf16[36,768]{1,0:T(8,128)(2,1)S(1)} %get-tuple-element.37), channel_id=1, source_target_pairs={{0,2},{1,31},{2,0},{3,29},{4,6},{5,3},{6,4},{7,1},{8,10},{9,7},{10... | collective-permute-start | bytes 165896 | tf_op jit(solution)/shard_map/ppermute | solution.py:626
  6.9 3.2 %collective-permute-start.3 = (bf16[36,768]{1,0:T(8,128)(2,1)S(1)}, bf16[36,768]{1,0:T(8,128)(2,1)S(1)}, u32[]{:S(2)}, u32[]{:S(2)}) collective-permute-start(bf16[36,768]{1,0:T(8,128)(2,1)S(1)} %get-tuple-element.43), channel_id=1, source_target_pairs={{0,29},{1,0},{2,31},{3,2},{4,1},{5,4},{6,3},{7,6},{8,5},{9,8},{10,... | collective-permute-start | bytes 165896 | tf_op jit(solution)/shard_map/ppermute | solution.py:626
  10.1 0.0 collective-permute-start.4
  10.1 1.9 %collective-permute-start = (bf16[72,768]{1,0:T(8,128)(2,1)S(1)}, bf16[72,768]{1,0:T(8,128)(2,1)S(1)}, u32[]{:S(2)}, u32[]{:S(2)}) collective-permute-start(bf16[72,768]{1,0:T(8,128)(2,1)S(1)} %get-tuple-element.36), channel_id=1, source_target_pairs={{0,30},{1,3},{2,28},{3,1},{4,2},{5,7},{6,0},{7,5},{8,6},{9,11},{10... | collective-permute-start | bytes 331784 | tf_op jit(solution)/shard_map/ppermute | solution.py:626
  12.0 0.0 copy-start.1
  12.0 0.0 collective-permute-start.2
  12.0 1.1 %copy-done.6 = f32[1,1,24,3312]{3,2,1,0:T(8,128)S(1)} copy-done((f32[1,1,24,3312]{3,2,1,0:T(8,128)S(1)}, f32[1,1,24,3312]{3,2,1,0:T(8,128)}, u32[]{:S(2)}) %copy-start.6) | copy-done | bytes 317976
  13.1 0.9 %copy-done.7 = s32[144,144]{1,0:T(8,128)S(1)} copy-done((s32[144,144]{1,0:T(8,128)S(1)}, s32[144,144]{1,0:T(8,128)}, u32[]{:S(2)}) %copy-start.7) | copy-done | bytes 82968
  14.0 0.7 %copy-done.8 = s32[6]{0:T(128)S(1)} copy-done((s32[6]{0:T(128)S(1)}, s32[6]{0:T(128)}, u32[]{:S(2)}) %copy-start.8) | copy-done | bytes 48
  14.7 0.7 %copy-done.9 = s32[96]{0:T(128)S(1)} copy-done((s32[96]{0:T(128)S(1)}, s32[96]{0:T(128)}, u32[]{:S(2)}) %copy-start.9) | copy-done | bytes 408
  15.3 7.9 %bias.1 = (f32[3456,128]{1,0:T(8,128)S(1)}, f32[3456,128]{1,0:T(8,128)S(1)}) custom-call(f32[1,1,24,3312]{3,2,1,0:T(8,128)S(1)} %copy-done.6, s32[144,144]{1,0:T(8,128)S(1)} %copy-done.7, s32[6]{0:T(128)S(1)} %copy-done.8, s32[96]{0:T(128)S(1)} %copy-done.9), custom_call_target="tpu_custom_call" | custom-call | flops 10000000000 | bytes 20000000 | tf_op jit(solution)/shard_map/bias/pallas_call | solution.py:264
  23.2 0.0 collective-permute-done.1.second
  23.2 0.0 collective-permute-done.first
  23.2 0.0 collective-permute-done.2.third
  23.2 0.0 copy-done.1
  23.3 0.0 copy-done.5
  23.3 0.0 copy-done
  23.3 0.0 copy-start.4
  23.3 3.4 %forward.1 = (bf16[3456,144]{1,0:T(8,128)(2,1)S(1)}, bf16[144,2304]{1,0:T(8,128)(2,1)S(1)}, bf16[768,144]{1,0:T(8,128)(2,1)S(1)}, bf16[144,768]{1,0:T(8,128)(2,1)S(1)}, bf16[144,768]{1,0:T(8,128)(2,1)S(1)}) custom-call(bf16[36,768]{1,0:T(8,128)(2,1)S(1)} %get-tuple-element.35.own, bf16[72,768]{1,0:T(8,128)(2,1)S(1)} %collective-permute-done.first, ...), custom_call_target="tpu_custom_call" | custom-call | flops 1000000000 | bytes 20000000 | tf_op jit(solution)/shard_map/forward/pallas_call | solution.py:354
  26.6 0.0 collective-permute-done.3.fourth
  26.7 0.0 collective-permute-done.4.fifth
  26.7 0.0 copy-done.4
  26.7 1.2 %moments.1 = (f32[144,768]{1,0:T(8,128)S(1)}, f32[144,128]{1,0:T(8,128)S(1)}, f32[24,128]{1,0:T(8,128)S(1)}) custom-call(bf16[144,768]{1,0:T(8,128)(2,1)S(1)} %get-tuple-element.41.residual, bf16[36,768]{1,0:T(8,128)(2,1)S(1)} %get-tuple-element.42.kept, bf16[72,768]{1,0:T(8,128)(2,1)S(1)} %collective-permute-done.first, ...), custom_call_target="tpu_custom_call" | custom-call | flops 100000000 | bytes 1000000 | tf_op jit(solution)/shard_map/moments/pallas_call | solution.py:450
  27.8 1.3 %collective-permute-start.5 = (f32[24,128]{1,0:T(8,128)S(1)}, f32[24,128]{1,0:T(8,128)S(1)}, u32[]{:S(2)}, u32[]{:S(2)}) collective-permute-start(f32[24,128]{1,0:T(8,128)S(1)} %get-tuple-element.47), channel_id=1, source_target_pairs={{0,2},{1,3},{2,0},{3,1},{4,6},{5,7},{6,4},{7,5},{8,10},{9,11},{10,... | collective-permute-start | bytes 36872 | tf_op jit(solution)/shard_map/ppermute | solution.py:626
  29.2 3.3 %collective-permute-done.5.before.after = f32[24,128]{1,0:T(8,128)S(1)} collective-permute-done((f32[24,128]{1,0:T(8,128)S(1)}, f32[24,128]{1,0:T(8,128)S(1)}, u32[]{:S(2)}, u32[]{:S(2)}) %collective-permute-start.5) | collective-permute-done | bytes 12320 | tf_op jit(solution)/shard_map/ppermute | solution.py:626
  32.5 0.5 merge.1
  33.0 2.1 %collective-permute-start.6 = (bf16[36,768]{1,0:T(8,128)(2,1)S(1)}, bf16[36,768]{1,0:T(8,128)(2,1)S(1)}, u32[]{:S(2)}, u32[]{:S(2)}) collective-permute-start(bf16[36,768]{1,0:T(8,128)(2,1)S(1)} %get-tuple-element.52), channel_id=1, source_target_pairs={{28,0},{1,1},{30,2},{3,3},{0,4},{5,5},{2,6},{7,7},{4,8},{9,9},{6,1... | collective-permute-start | bytes 165896 | tf_op jit(solution)/shard_map/ppermute | solution.py:626
  35.1 2.2 %collective-permute-start.7 = (bf16[36,768]{1,0:T(8,128)(2,1)S(1)}, bf16[36,768]{1,0:T(8,128)(2,1)S(1)}, u32[]{:S(2)}, u32[]{:S(2)}) collective-permute-start(bf16[36,768]{1,0:T(8,128)(2,1)S(1)} %get-tuple-element.53), channel_id=1, source_target_pairs={{30,0},{3,1},{28,2},{1,3},{2,4},{7,5},{0,6},{5,7},{6,8},{11,9},{4,... | collective-permute-start | bytes 165896 | tf_op jit(solution)/shard_map/ppermute | solution.py:626
  37.4 0.0 collective-permute-start.8
  37.4 2.6 %collective-permute-start.9 = (bf16[36,768]{1,0:T(8,128)(2,1)S(1)}, bf16[36,768]{1,0:T(8,128)(2,1)S(1)}, u32[]{:S(2)}, u32[]{:S(2)}) collective-permute-start(bf16[36,768]{1,0:T(8,128)(2,1)S(1)} %get-tuple-element.55), channel_id=1, source_target_pairs={{31,0},{2,1},{29,2},{0,3},{3,4},{6,5},{1,6},{4,7},{7,8},{10,9},{5,... | collective-permute-start | bytes 165896 | tf_op jit(solution)/shard_map/ppermute | solution.py:626
  39.9 2.8 %backward.1.joined = bf16[144,2304]{1,0:T(8,128)(2,1)S(1)} custom-call(bf16[144,768]{1,0:T(8,128)(2,1)S(1)} %get-tuple-element.48.grad, bf16[3456,144]{1,0:T(8,128)(2,1)S(1)} %get-tuple-element.49.weights, bf16[144,2304]{1,0:T(8,128)(2,1)S(1)} %get-tuple-element.50.triple, bf16[768,144]{1,0:T(8,128)(2,1)S(1)} %get-tuple-element.51.keys_t, ...), custom_call_target="tpu_custom_call" | custom-call | flops 10000000000 | bytes 20000000 | tf_op jit(solution)/shard_map/backward/pallas_call | solution.py:540
  42.7 0.0 collective-permute-done.6.same_here
  42.7 0.0 collective-permute-done.7.same_next
  42.8 1.3 %collective-permute-done.8.other_here = bf16[36,768]{1,0:T(8,128)(2,1)S(1)} collective-permute-done((bf16[36,768]{1,0:T(8,128)(2,1)S(1)}, bf16[36,768]{1,0:T(8,128)(2,1)S(1)}, u32[]{:S(2)}, u32[]{:S(2)}) %collective-permute-start.8) | collective-permute-done | bytes 55328 | tf_op jit(solution)/shard_map/ppermute | solution.py:626
  44.1 1.3 %collective-permute-done.9.other_next = bf16[36,768]{1,0:T(8,128)(2,1)S(1)} collective-permute-done((bf16[36,768]{1,0:T(8,128)(2,1)S(1)}, bf16[36,768]{1,0:T(8,128)(2,1)S(1)}, u32[]{:S(2)}, u32[]{:S(2)}) %collective-permute-start.9) | collective-permute-done | bytes 55328 | tf_op jit(solution)/shard_map/ppermute | solution.py:626
  45.4 1.5 %finish.1 = (bf16[36,768]{1,0:T(8,128)(2,1)S(1)}, bf16[36,768]{1,0:T(8,128)(2,1)S(1)}, bf16[36,768]{1,0:T(8,128)(2,1)S(1)}, bf16[36,768]{1,0:T(8,128)(2,1)S(1)}) custom-call(bf16[144,768]{1,0:T(8,128)(2,1)S(1)} %get-tuple-element.48.grad, bf16[144,2304]{1,0:T(8,128)(2,1)S(1)} %backward.1.joined, bf16[144,768]{1,0:T(8,128)(2,1)S(1)} %get-tuple-element.57.tokens, ...), custom_call_target="tpu_custom_call" | custom-call | flops 1000000000 | bytes 2000000 | tf_op jit(solution)/shard_map/finish/pallas_call | solution.py:561
  46.9 0.1 collective-permute-start.10
  47.0 0.1 collective-permute-start.11
  47.0 2.9 %collective-permute-start.12 = (bf16[36,768]{1,0:T(8,128)(2,1)S(1)}, bf16[36,768]{1,0:T(8,128)(2,1)S(1)}, u32[]{:S(2)}, u32[]{:S(2)}) collective-permute-start(bf16[36,768]{1,0:T(8,128)(2,1)S(1)} %get-tuple-element.61), channel_id=1, source_target_pairs={{30,0},{31,1},{28,2},{29,3},{2,4},{3,5},{0,6},{1,7},{6,8},{7,9},{4... | collective-permute-start | bytes 165896 | tf_op jit(solution)/shard_map/ppermute | solution.py:626
  49.9 3.9 %collective-permute-done.10.lat = bf16[36,768]{1,0:T(8,128)(2,1)S(1)} collective-permute-done((bf16[36,768]{1,0:T(8,128)(2,1)S(1)}, bf16[36,768]{1,0:T(8,128)(2,1)S(1)}, u32[]{:S(2)}, u32[]{:S(2)}) %collective-permute-start.10) | collective-permute-done | bytes 55328 | tf_op jit(solution)/shard_map/ppermute | solution.py:626
  53.8 0.0 collective-permute-done.11.lon
  53.8 1.8 %collective-permute-done.12.both = bf16[36,768]{1,0:T(8,128)(2,1)S(1)} collective-permute-done((bf16[36,768]{1,0:T(8,128)(2,1)S(1)}, bf16[36,768]{1,0:T(8,128)(2,1)S(1)}, u32[]{:S(2)}, u32[]{:S(2)}) %collective-permute-start.12) | collective-permute-done | bytes 55328 | tf_op jit(solution)/shard_map/ppermute | solution.py:626
  55.6 0.9 %unpack.1 = (bf16[3,3,4,3072]{3,2,1,0:T(4,128)(2,1)}, bf16[6,12,2,768]{3,2,1,0:T(2,128)(2,1)}) custom-call(bf16[36,768]{1,0:T(8,128)(2,1)S(1)} %get-tuple-element.58.own, bf16[36,768]{1,0:T(8,128)(2,1)S(1)} %collective-permute-done.10.lat, bf16[36,768]{1,0:T(8,128)(2,1)S(1)} %collective-permute-done.11.lon, ...), custom_call_target="tpu_custom_call" | custom-call | tf_op jit(solution)/shard_map/unpack/pallas_call | solution.py:597
  (6 shorter events, 0.0 us)
Async XLA Ops:
  0.6 0.9 %copy-start.2 = (bf16[2,6,12,768]{3,0,2,1:T(2,128)(2,1)S(1)}, bf16[2,6,12,768]{3,0,2,1:T(2,128)(2,1)}, u32[]{:S(2)}) copy-start(bf16[2,6,12,768]{3,0,2,1:T(2,128)(2,1)} %param.10) | copy-start | bytes 663556
  1.6 0.9 %copy-start.3 = (bf16[4,3,3,3072]{3,0,2,1:T(4,128)(2,1)S(1)}, bf16[4,3,3,3072]{3,0,2,1:T(4,128)(2,1)}, u32[]{:S(2)}) copy-start(bf16[4,3,3,3072]{3,0,2,1:T(4,128)(2,1)} %param.19) | copy-start | bytes 663556
  2.8 20.4 %collective-permute-start.1 = (bf16[36,768]{1,0:T(8,128)(2,1)S(1)}, bf16[36,768]{1,0:T(8,128)(2,1)S(1)}, u32[]{:S(2)}, u32[]{:S(2)}) collective-permute-start(bf16[36,768]{1,0:T(8,128)(2,1)S(1)} %get-tuple-element.37), channel_id=1, source_target_pairs={{0,2},{1,31},{2,0},{3,29},{4,6},{5,3},{6,4},{7,1},{8,10},{9,7},{10... | collective-permute-start | bytes 165896 | tf_op jit(solution)/shard_map/ppermute | solution.py:626
  6.9 19.7 %collective-permute-start.3 = (bf16[36,768]{1,0:T(8,128)(2,1)S(1)}, bf16[36,768]{1,0:T(8,128)(2,1)S(1)}, u32[]{:S(2)}, u32[]{:S(2)}) collective-permute-start(bf16[36,768]{1,0:T(8,128)(2,1)S(1)} %get-tuple-element.43), channel_id=1, source_target_pairs={{0,29},{1,0},{2,31},{3,2},{4,1},{5,4},{6,3},{7,6},{8,5},{9,8},{10,... | collective-permute-start | bytes 165896 | tf_op jit(solution)/shard_map/ppermute | solution.py:626
  10.1 16.6 %collective-permute-start.4 = (bf16[36,768]{1,0:T(8,128)(2,1)S(1)}, bf16[36,768]{1,0:T(8,128)(2,1)S(1)}, u32[]{:S(2)}, u32[]{:S(2)}) collective-permute-start(bf16[36,768]{1,0:T(8,128)(2,1)S(1)} %get-tuple-element.44), channel_id=1, source_target_pairs={{0,31},{1,2},{2,29},{3,0},{4,3},{5,6},{6,1},{7,4},{8,7},{9,10},{10... | collective-permute-start | bytes 165896 | tf_op jit(solution)/shard_map/ppermute | solution.py:626
  10.1 13.1 %collective-permute-start = (bf16[72,768]{1,0:T(8,128)(2,1)S(1)}, bf16[72,768]{1,0:T(8,128)(2,1)S(1)}, u32[]{:S(2)}, u32[]{:S(2)}) collective-permute-start(bf16[72,768]{1,0:T(8,128)(2,1)S(1)} %get-tuple-element.36), channel_id=1, source_target_pairs={{0,30},{1,3},{2,28},{3,1},{4,2},{5,7},{6,0},{7,5},{8,6},{9,11},{10... | collective-permute-start | bytes 331784 | tf_op jit(solution)/shard_map/ppermute | solution.py:626
  12.0 11.2 %copy-start.1 = (bf16[768,768]{1,0:T(8,128)(2,1)S(1)}, bf16[768,768]{1,0:T(8,128)(2,1)}, u32[]{:S(2)}) copy-start(bf16[768,768]{1,0:T(8,128)(2,1)} %output.3) | copy-start | bytes 3538948
  12.0 11.2 %copy-start.5 = (f32[768]{0:T(1024)S(1)}, f32[768]{0:T(1024)}, u32[]{:S(2)}) copy-start(f32[768]{0:T(1024)} %gain.3) | copy-start | bytes 9220
  12.0 11.2 %collective-permute-start.2 = (bf16[72,768]{1,0:T(8,128)(2,1)S(1)}, bf16[72,768]{1,0:T(8,128)(2,1)S(1)}, u32[]{:S(2)}, u32[]{:S(2)}) collective-permute-start(bf16[72,768]{1,0:T(8,128)(2,1)S(1)} %get-tuple-element.38), channel_id=1, source_target_pairs={{0,28},{1,29},{2,30},{3,31},{4,0},{5,1},{6,2},{7,3},{8,4},{9,5},{1... | collective-permute-start | bytes 331784 | tf_op jit(solution)/shard_map/ppermute | solution.py:626
  12.0 1.1 %copy-start.6 = (f32[1,1,24,3312]{3,2,1,0:T(8,128)S(1)}, f32[1,1,24,3312]{3,2,1,0:T(8,128)}, u32[]{:S(2)}) copy-start(f32[1,1,24,3312]{3,2,1,0:T(8,128)} %table_at.1) | copy-start | bytes 953860
  13.1 0.9 %copy-start.7 = (s32[144,144]{1,0:T(8,128)S(1)}, s32[144,144]{1,0:T(8,128)}, u32[]{:S(2)}) copy-start(s32[144,144]{1,0:T(8,128)} %index_at.1) | copy-start | bytes 248836
  14.0 0.7 %copy-start.8 = (s32[6]{0:T(128)S(1)}, s32[6]{0:T(128)}, u32[]{:S(2)}) copy-start(s32[6]{0:T(128)} %labels_at.1) | copy-start | bytes 76
  14.7 0.7 %copy-start.9 = (s32[96]{0:T(128)S(1)}, s32[96]{0:T(128)}, u32[]{:S(2)}) copy-start(s32[96]{0:T(128)} %valid_at.1) | copy-start | bytes 1156
  15.3 8.0 %copy-start = (bf16[768,2304]{1,0:T(8,128)(2,1)S(1)}, bf16[768,2304]{1,0:T(8,128)(2,1)}, u32[]{:S(2)}) copy-start(bf16[768,2304]{1,0:T(8,128)(2,1)} %packed.3) | copy-start | bytes 10616836
  23.3 3.4 %copy-start.4 = (f32[3072]{0:T(1024)S(1)}, f32[3072]{0:T(1024)}, u32[]{:S(2)}) copy-start(f32[3072]{0:T(1024)} %param.14) | copy-start | bytes 36868
  27.8 4.6 %collective-permute-start.5 = (f32[24,128]{1,0:T(8,128)S(1)}, f32[24,128]{1,0:T(8,128)S(1)}, u32[]{:S(2)}, u32[]{:S(2)}) collective-permute-start(f32[24,128]{1,0:T(8,128)S(1)} %get-tuple-element.47), channel_id=1, source_target_pairs={{0,2},{1,3},{2,0},{3,1},{4,6},{5,7},{6,4},{7,5},{8,10},{9,11},{10,... | collective-permute-start | bytes 36872 | tf_op jit(solution)/shard_map/ppermute | solution.py:626
  33.0 9.7 %collective-permute-start.6 = (bf16[36,768]{1,0:T(8,128)(2,1)S(1)}, bf16[36,768]{1,0:T(8,128)(2,1)S(1)}, u32[]{:S(2)}, u32[]{:S(2)}) collective-permute-start(bf16[36,768]{1,0:T(8,128)(2,1)S(1)} %get-tuple-element.52), channel_id=1, source_target_pairs={{28,0},{1,1},{30,2},{3,3},{0,4},{5,5},{2,6},{7,7},{4,8},{9,9},{6,1... | collective-permute-start | bytes 165896 | tf_op jit(solution)/shard_map/ppermute | solution.py:626
  35.1 7.6 %collective-permute-start.7 = (bf16[36,768]{1,0:T(8,128)(2,1)S(1)}, bf16[36,768]{1,0:T(8,128)(2,1)S(1)}, u32[]{:S(2)}, u32[]{:S(2)}) collective-permute-start(bf16[36,768]{1,0:T(8,128)(2,1)S(1)} %get-tuple-element.53), channel_id=1, source_target_pairs={{30,0},{3,1},{28,2},{1,3},{2,4},{7,5},{0,6},{5,7},{6,8},{11,9},{4,... | collective-permute-start | bytes 165896 | tf_op jit(solution)/shard_map/ppermute | solution.py:626
  37.4 6.7 %collective-permute-start.8 = (bf16[36,768]{1,0:T(8,128)(2,1)S(1)}, bf16[36,768]{1,0:T(8,128)(2,1)S(1)}, u32[]{:S(2)}, u32[]{:S(2)}) collective-permute-start(bf16[36,768]{1,0:T(8,128)(2,1)S(1)} %get-tuple-element.54), channel_id=1, source_target_pairs={{29,0},{0,1},{31,2},{2,3},{1,4},{4,5},{3,6},{6,7},{5,8},{8,9},{7,1... | collective-permute-start | bytes 165896 | tf_op jit(solution)/shard_map/ppermute | solution.py:626
  37.4 8.0 %collective-permute-start.9 = (bf16[36,768]{1,0:T(8,128)(2,1)S(1)}, bf16[36,768]{1,0:T(8,128)(2,1)S(1)}, u32[]{:S(2)}, u32[]{:S(2)}) collective-permute-start(bf16[36,768]{1,0:T(8,128)(2,1)S(1)} %get-tuple-element.55), channel_id=1, source_target_pairs={{31,0},{2,1},{29,2},{0,3},{3,4},{6,5},{1,6},{4,7},{7,8},{10,9},{5,... | collective-permute-start | bytes 165896 | tf_op jit(solution)/shard_map/ppermute | solution.py:626
  46.9 6.9 %collective-permute-start.10 = (bf16[36,768]{1,0:T(8,128)(2,1)S(1)}, bf16[36,768]{1,0:T(8,128)(2,1)S(1)}, u32[]{:S(2)}, u32[]{:S(2)}) collective-permute-start(bf16[36,768]{1,0:T(8,128)(2,1)S(1)} %get-tuple-element.59), channel_id=1, source_target_pairs={{2,0},{3,1},{0,2},{1,3},{6,4},{7,5},{4,6},{5,7},{10,8},{11,9},{8,1... | collective-permute-start | bytes 165896 | tf_op jit(solution)/shard_map/ppermute | solution.py:626
  47.0 6.8 %collective-permute-start.11 = (bf16[36,768]{1,0:T(8,128)(2,1)S(1)}, bf16[36,768]{1,0:T(8,128)(2,1)S(1)}, u32[]{:S(2)}, u32[]{:S(2)}) collective-permute-start(bf16[36,768]{1,0:T(8,128)(2,1)S(1)} %get-tuple-element.60), channel_id=1, source_target_pairs={{28,0},{29,1},{30,2},{31,3},{0,4},{1,5},{2,6},{3,7},{4,8},{5,9},{6... | collective-permute-start | bytes 165896 | tf_op jit(solution)/shard_map/ppermute | solution.py:626
  47.0 8.5 %collective-permute-start.12 = (bf16[36,768]{1,0:T(8,128)(2,1)S(1)}, bf16[36,768]{1,0:T(8,128)(2,1)S(1)}, u32[]{:S(2)}, u32[]{:S(2)}) collective-permute-start(bf16[36,768]{1,0:T(8,128)(2,1)S(1)} %get-tuple-element.61), channel_id=1, source_target_pairs={{30,0},{31,1},{28,2},{29,3},{2,4},{3,5},{0,6},{1,7},{6,8},{7,9},{4... | collective-permute-start | bytes 165896 | tf_op jit(solution)/shard_map/ppermute | solution.py:626

commit v3 on v2

--- a/solution.py
+++ b/solution.py
@@ -76,8 +76,15 @@
     return pl.CostEstimate(flops=flops, bytes_accessed=nbytes, transcendentals=0)
 
 
-def lev_index():
-    return lax.axis_index("lev")
+def in_hbm(*arrays):
+    return [pltpu.with_memory_space_constraint(x, pltpu.MemorySpace.HBM) for x in arrays]
+
+
+def start_copies(done, *pairs):
+    copies = [pltpu.make_async_copy(source, target, done.at[i]) for i, (source, target) in enumerate(pairs)]
+    for copy in copies:
+        copy.start()
+    return copies
 
 
 def quadrant(values, quad):
@@ -88,14 +95,19 @@
     return [(0, 0, True, 0), (0, 1, True, 1), (1, 0, True, 2), (1, 1, False, 0), (2, 0, False, 1), (2, 1, False, 2)]
 
 
-def pack_kernel(tokens, grad, own, first, second, third, kept, fourth, fifth, rows, cells):
+def pack_kernel(
+    tokens_at, grad_at, own, first, second, third, kept, fourth, fifth, tokens, grad, rows, cells, done
+):
     width = tokens.shape[-1]
+    copies = start_copies(done, (tokens_at, tokens), (grad_at, grad))
+    copies[0].wait()
     for line in range(WLAT):
         for column in range(WLON):
             quad = (0 if line >= HALF_LAT else 1) + (0 if column >= HALF_LON else 2)
             inner = column % HALF_LON
             at = token_row(quad, line % HALF_LAT, inner % 2, inner // 2)
             rows[at : at + LEVELS, :] = tokens[line, column].astype(f32)
+    copies[1].wait()
     upper = lax.axis_index("lev") == 1
     for row, odd, below, inner in cell_places():
         for pair in range(PAIRS):
@@ -125,24 +137,26 @@
     return pl.pallas_call(
         pack_kernel,
         out_shape=[piece, double, piece, double, piece, piece, piece],
-        scratch_shapes=[pltpu.VMEM((WIN, width), f32)] * 2,
+        in_specs=[pl.BlockSpec(memory_space=pltpu.MemorySpace.HBM)] * 2,
+        scratch_shapes=[
+            pltpu.VMEM(tokens.shape, bf16),
+            pltpu.VMEM(grad.shape, bf16),
+            pltpu.VMEM((WIN, width), f32),
+            pltpu.VMEM((WIN, width), f32),
+            pltpu.SemaphoreType.DMA((2,)),
+        ],
         compiler_params=params(),
         name="pack",
-    )(tokens, grad)
+    )(*in_hbm(tokens, grad))
 
 
 def bias_kernel(
     table_at, index_at, labels_at, valid_at, main, tail,
     table, index, labels, valid, split, fine, high, low, fine_high, fine_low, rest_rows, mask, mask_tail, done,
 ):
-    copies = [
-        pltpu.make_async_copy(source, target, done.at[i])
-        for i, (source, target) in enumerate(
-            ((table_at.at[0, 0], table), (index_at, index), (labels_at, labels), (valid_at, valid))
-        )
-    ]
-    for copy in copies:
-        copy.start()
+    copies = start_copies(
+        done, (table_at.at[0, 0], table), (index_at, index), (labels_at, labels), (valid_at, valid)
+    )
     row_k, column_k, level_k, _ = token_places((WIN, 1), 0)
     row_q, _, _, _ = token_places((1, WIN), 1)
     natural = (level_k * WLAT + row_k) * WLON + column_k
@@ -284,7 +298,7 @@
         compiler_params=params(),
         cost_estimate=cost(10**10, 2 * 10**7),
         name="bias",
-    )(table, index, labels, valid)
+    )(*in_hbm(table, index, labels, valid))
 
 
 def row_mean(values):
@@ -672,8 +686,8 @@
     right = send(right, sizes, FOURTH, True)
     kept = send(kept, sizes, HERE, True)
     joined = backward(grad, weights, triple, keys_t, output_weight)
-    joined, kept, below, right, far = lax.optimization_barrier((joined, kept, below, right, far))
     own, lat, lon, both = finish(grad, joined, data, packed_weight, norm_gain)
+    lat, lon, both, kept, below, right, far = lax.optimization_barrier((lat, lon, both, kept, below, right, far))
     lat = send(lat, sizes, LAT, True)
     both = send(both, sizes, BOTH, True)
     lon = send(lon, sizes, LON, True)

time: 56.7 us -> 51.2 us (0.903)
  local copies, waits for them, and re-layouts: 5.16 us -> 0.02 us
  waiting for transfers between devices: 11.6 us -> 9.97 us
  Pallas kernels: 18.4 us -> 19.8 us
    unnamed x20 -> x8, local copies, waits for them, and re-layouts: 5.16 us -> 0.02 us
    ppermute x13, waiting for transfers between devices: 11.6 us -> 9.97 us  [send(): return lax.ppermute(block, ('lon', 'lat', 'lev'), pairs)]
    pallas_call x1, Pallas kernels: 0.34 us -> 1.3 us  [pack_pieces(): pl.pallas_call(pack_kernel, out_shape=[piece, double, piece, double, piec...]
  transfers between devices with their start and end apart: 13 -> 13, of which waited for: 5 -> 4; matrix products, arithmetic and copies ran while one was open for 0% -> 0% of each run, Pallas kernels for 25% -> 31%
where the time goes in v3:
time: 51.2 us; the launch traced here: 51 us
  starting transfers between devices  20.5 us (40%)
  Pallas kernels  19.8 us (39%)
  waiting for transfers between devices  9.97 us (19%)
  between operations  0.79 us (2%)
    ppermute x13, starting transfers between devices, send(): return lax.ppermute(block, ('lon', 'lat', 'lev'), pairs)  20.5 us
    ppermute x13, waiting for transfers between devices, send(): return lax.ppermute(block, ('lon', 'lat', 'lev'), pairs)  9.97 us
    pallas_call x1, Pallas kernels, window_bias(): pl.pallas_call(bias_kernel, out_shape=[shape((heads * WIN, 128), f32)] *...  8.24 us
    pallas_call x1, Pallas kernels, forward(): pl.pallas_call(forward_kernel, out_shape=[shape((HEADS * WIN, WIN), bf16)...  3.35 us
    pallas_call x1, Pallas kernels, backward(): pl.pallas_call(backward_kernel, out_shape=shape((WIN, 3 * width), bf16),...  2.81 us
    pallas_call x1, Pallas kernels, finish(): pl.pallas_call(finish_kernel, out_shape=[shape((QUAD, width), bf16)] * 4,...  1.53 us
    pallas_call x1, Pallas kernels, pack_pieces(): pl.pallas_call(pack_kernel, out_shape=[piece, double, piece, double, piec...  1.3 us
    pallas_call x1, Pallas kernels, cell_moments(): pl.pallas_call(moments_kernel, out_shape=[shape((WIN, width), f32), shape...  1.15 us
  transfers between devices with their start and end apart: 13, of which 4 were waited for; matrix products, arithmetic and copies ran while one was open for 0% of the time, Pallas kernels for 31%

profile of v3, /device:TPU:0, one launch (start us, length us, event | category | flops | bytes accessed | tf_op | source)
XLA Modules:
  0.0 51.0 jit_solution(1832335422821669744)
XLA Ops:
  0.6 1.3 %pack.1 = (bf16[36,768]{1,0:T(8,128)(2,1)S(1)}, bf16[72,768]{1,0:T(8,128)(2,1)S(1)}, bf16[36,768]{1,0:T(8,128)(2,1)S(1)}, bf16[72,768]{1,0:T(8,128)(2,1)S(1)}, b...) custom-call(bf16[6,12,2,768]{3,2,1,0:T(2,128)(2,1)} %bitcast.7, ...), custom_call_target="tpu_custom_call" | custom-call | tf_op jit(solution)/shard_map/pack/pallas_call | solution.py:137
  1.9 4.1 %collective-permute-start.1 = (bf16[36,768]{1,0:T(8,128)(2,1)S(1)}, bf16[36,768]{1,0:T(8,128)(2,1)S(1)}, u32[]{:S(2)}, u32[]{:S(2)}) collective-permute-start(bf16[36,768]{1,0:T(8,128)(2,1)S(1)} %get-tuple-element.39), channel_id=1, source_target_pairs={{0,2},{1,31},{2,0},{3,29},{4,6},{5,3},{6,4},{7,1},{8,10},{9,7},{10... | collective-permute-start | bytes 165896 | tf_op jit(solution)/shard_map/ppermute | solution.py:640
  6.0 3.2 %collective-permute-start.3 = (bf16[36,768]{1,0:T(8,128)(2,1)S(1)}, bf16[36,768]{1,0:T(8,128)(2,1)S(1)}, u32[]{:S(2)}, u32[]{:S(2)}) collective-permute-start(bf16[36,768]{1,0:T(8,128)(2,1)S(1)} %get-tuple-element.45), channel_id=1, source_target_pairs={{0,29},{1,0},{2,31},{3,2},{4,1},{5,4},{6,3},{7,6},{8,5},{9,8},{10,... | collective-permute-start | bytes 165896 | tf_op jit(solution)/shard_map/ppermute | solution.py:640
  9.2 0.0 collective-permute-start.4
  9.2 1.9 %collective-permute-start = (bf16[72,768]{1,0:T(8,128)(2,1)S(1)}, bf16[72,768]{1,0:T(8,128)(2,1)S(1)}, u32[]{:S(2)}, u32[]{:S(2)}) collective-permute-start(bf16[72,768]{1,0:T(8,128)(2,1)S(1)} %get-tuple-element.38), channel_id=1, source_target_pairs={{0,30},{1,3},{2,28},{3,1},{4,2},{5,7},{6,0},{7,5},{8,6},{9,11},{10... | collective-permute-start | bytes 331784 | tf_op jit(solution)/shard_map/ppermute | solution.py:640
  11.1 0.0 copy-start.1
  11.1 0.0 copy-start.3
  11.1 0.0 collective-permute-start.2
  11.1 0.0 copy-start
  11.1 8.2 %bias.1 = (f32[3456,128]{1,0:T(8,128)S(1)}, f32[3456,128]{1,0:T(8,128)S(1)}) custom-call(f32[1,1,24,3312]{3,2,1,0:T(8,128)} %table_at.1, s32[144,144]{1,0:T(8,128)} %index_at.1, s32[6]{0:T(128)} %labels_at.1, s32[96]{0:T(128)} %valid_at.1), custom_call_target="tpu_custom_call" | custom-call | flops 10000000000 | bytes 20000000 | tf_op jit(solution)/shard_map/bias/pallas_call | solution.py:278
  19.4 0.0 collective-permute-done.1.second
  19.4 0.0 collective-permute-done.first
  19.4 0.0 collective-permute-done.2.third
  19.4 0.0 copy-done.1
  19.4 0.0 copy-done.3
  19.4 0.0 copy-done
  19.4 0.0 copy-start.2
  19.5 3.4 %forward.1 = (bf16[3456,144]{1,0:T(8,128)(2,1)S(1)}, bf16[144,2304]{1,0:T(8,128)(2,1)S(1)}, bf16[768,144]{1,0:T(8,128)(2,1)S(1)}, bf16[144,768]{1,0:T(8,128)(2,1)S(1)}, bf16[144,768]{1,0:T(8,128)(2,1)S(1)}) custom-call(bf16[36,768]{1,0:T(8,128)(2,1)S(1)} %get-tuple-element.37.own, bf16[72,768]{1,0:T(8,128)(2,1)S(1)} %collective-permute-done.first, ...), custom_call_target="tpu_custom_call" | custom-call | flops 1000000000 | bytes 20000000 | tf_op jit(solution)/shard_map/forward/pallas_call | solution.py:368
  22.8 0.0 collective-permute-done.3.fourth
  22.8 0.0 collective-permute-done.4.fifth
  22.8 0.0 copy-done.2
  22.8 1.2 %moments.1 = (f32[144,768]{1,0:T(8,128)S(1)}, f32[144,128]{1,0:T(8,128)S(1)}, f32[24,128]{1,0:T(8,128)S(1)}) custom-call(bf16[144,768]{1,0:T(8,128)(2,1)S(1)} %get-tuple-element.43.residual, bf16[36,768]{1,0:T(8,128)(2,1)S(1)} %get-tuple-element.44.kept, bf16[72,768]{1,0:T(8,128)(2,1)S(1)} %collective-permute-done.first, ...), custom_call_target="tpu_custom_call" | custom-call | flops 100000000 | bytes 1000000 | tf_op jit(solution)/shard_map/moments/pallas_call | solution.py:464
  24.0 1.3 %collective-permute-start.5 = (f32[24,128]{1,0:T(8,128)S(1)}, f32[24,128]{1,0:T(8,128)S(1)}, u32[]{:S(2)}, u32[]{:S(2)}) collective-permute-start(f32[24,128]{1,0:T(8,128)S(1)} %get-tuple-element.49), channel_id=1, source_target_pairs={{0,2},{1,3},{2,0},{3,1},{4,6},{5,7},{6,4},{7,5},{8,10},{9,11},{10,... | collective-permute-start | bytes 36872 | tf_op jit(solution)/shard_map/ppermute | solution.py:640
  25.3 3.3 %collective-permute-done.5.before.after = f32[24,128]{1,0:T(8,128)S(1)} collective-permute-done((f32[24,128]{1,0:T(8,128)S(1)}, f32[24,128]{1,0:T(8,128)S(1)}, u32[]{:S(2)}, u32[]{:S(2)}) %collective-permute-start.5) | collective-permute-done | bytes 12320 | tf_op jit(solution)/shard_map/ppermute | solution.py:640
  28.6 0.5 %merge.1 = (bf16[36,768]{1,0:T(8,128)(2,1)S(1)}, bf16[36,768]{1,0:T(8,128)(2,1)S(1)}, bf16[36,768]{1,0:T(8,128)(2,1)S(1)}, bf16[36,768]{1,0:T(8,128)(2,1)S(1)}, bf16[144,768]{1,0:T(8,128)(2,1)S(1)}) custom-call(bf16[144,768]{1,0:T(8,128)(2,1)S(1)} %get-tuple-element.43.residual, f32[144,768]{1,0:T(8,128)S(1)} %get-tuple-element.47.scaled, ...), custom_call_target="tpu_custom_call" | custom-call | flops 100000000 | bytes 1000000 | tf_op jit(solution)/shard_map/merge/pallas_call | solution.py:511
  29.2 1.9 %collective-permute-start.6 = (bf16[36,768]{1,0:T(8,128)(2,1)S(1)}, bf16[36,768]{1,0:T(8,128)(2,1)S(1)}, u32[]{:S(2)}, u32[]{:S(2)}) collective-permute-start(bf16[36,768]{1,0:T(8,128)(2,1)S(1)} %get-tuple-element.59), channel_id=1, source_target_pairs={{28,0},{1,1},{30,2},{3,3},{0,4},{5,5},{2,6},{7,7},{4,8},{9,9},{6,1... | collective-permute-start | bytes 165896 | tf_op jit(solution)/shard_map/ppermute | solution.py:640
  31.1 2.7 %collective-permute-start.7 = (bf16[36,768]{1,0:T(8,128)(2,1)S(1)}, bf16[36,768]{1,0:T(8,128)(2,1)S(1)}, u32[]{:S(2)}, u32[]{:S(2)}) collective-permute-start(bf16[36,768]{1,0:T(8,128)(2,1)S(1)} %get-tuple-element.60), channel_id=1, source_target_pairs={{30,0},{3,1},{28,2},{1,3},{2,4},{7,5},{0,6},{5,7},{6,8},{11,9},{4,... | collective-permute-start | bytes 165896 | tf_op jit(solution)/shard_map/ppermute | solution.py:640
  33.8 0.0 collective-permute-start.8
  33.8 2.4 %collective-permute-start.9 = (bf16[36,768]{1,0:T(8,128)(2,1)S(1)}, bf16[36,768]{1,0:T(8,128)(2,1)S(1)}, u32[]{:S(2)}, u32[]{:S(2)}) collective-permute-start(bf16[36,768]{1,0:T(8,128)(2,1)S(1)} %get-tuple-element.62), channel_id=1, source_target_pairs={{31,0},{2,1},{29,2},{0,3},{3,4},{6,5},{1,6},{4,7},{7,8},{10,9},{5,... | collective-permute-start | bytes 165896 | tf_op jit(solution)/shard_map/ppermute | solution.py:640
  36.2 2.8 %backward.1.joined = bf16[144,2304]{1,0:T(8,128)(2,1)S(1)} custom-call(bf16[144,768]{1,0:T(8,128)(2,1)S(1)} %get-tuple-element.50.grad, bf16[3456,144]{1,0:T(8,128)(2,1)S(1)} %get-tuple-element.51.weights, bf16[144,2304]{1,0:T(8,128)(2,1)S(1)} %get-tuple-element.52.triple, bf16[768,144]{1,0:T(8,128)(2,1)S(1)} %get-tuple-element.53.keys_t, ...), custom_call_target="tpu_custom_call" | custom-call | flops 10000000000 | bytes 20000000 | tf_op jit(solution)/shard_map/backward/pallas_call | solution.py:554
  39.0 1.5 %finish.1 = (bf16[36,768]{1,0:T(8,128)(2,1)S(1)}, bf16[36,768]{1,0:T(8,128)(2,1)S(1)}, bf16[36,768]{1,0:T(8,128)(2,1)S(1)}, bf16[36,768]{1,0:T(8,128)(2,1)S(1)}) custom-call(bf16[144,768]{1,0:T(8,128)(2,1)S(1)} %get-tuple-element.50.grad, bf16[144,2304]{1,0:T(8,128)(2,1)S(1)} %backward.1.joined, bf16[144,768]{1,0:T(8,128)(2,1)S(1)} %get-tuple-element.54.tokens, ...), custom_call_target="tpu_custom_call" | custom-call | flops 1000000000 | bytes 2000000 | tf_op jit(solution)/shard_map/finish/pallas_call | solution.py:575
  40.5 0.0 collective-permute-done.6.same_here
  40.5 0.0 collective-permute-done.7.same_next
  40.5 0.0 collective-permute-done.8.other_here
  40.6 1.0 %collective-permute-done.9.other_next = bf16[36,768]{1,0:T(8,128)(2,1)S(1)} collective-permute-done((bf16[36,768]{1,0:T(8,128)(2,1)S(1)}, bf16[36,768]{1,0:T(8,128)(2,1)S(1)}, u32[]{:S(2)}, u32[]{:S(2)}) %collective-permute-start.9) | collective-permute-done | bytes 55328 | tf_op jit(solution)/shard_map/ppermute | solution.py:640
  41.6 0.0 collective-permute-start.10
  41.6 0.0 collective-permute-start.11
  41.6 3.0 %collective-permute-start.12 = (bf16[36,768]{1,0:T(8,128)(2,1)S(1)}, bf16[36,768]{1,0:T(8,128)(2,1)S(1)}, u32[]{:S(2)}, u32[]{:S(2)}) collective-permute-start(bf16[36,768]{1,0:T(8,128)(2,1)S(1)} %get-tuple-element.65), channel_id=1, source_target_pairs={{30,0},{31,1},{28,2},{29,3},{2,4},{3,5},{0,6},{1,7},{6,8},{7,9},{4... | collective-permute-start | bytes 165896 | tf_op jit(solution)/shard_map/ppermute | solution.py:640
  44.6 4.1 %collective-permute-done.10.lat = bf16[36,768]{1,0:T(8,128)(2,1)S(1)} collective-permute-done((bf16[36,768]{1,0:T(8,128)(2,1)S(1)}, bf16[36,768]{1,0:T(8,128)(2,1)S(1)}, u32[]{:S(2)}, u32[]{:S(2)}) %collective-permute-start.10) | collective-permute-done | bytes 55328 | tf_op jit(solution)/shard_map/ppermute | solution.py:640
  48.6 0.0 collective-permute-done.11.lon
  48.7 1.5 %collective-permute-done.12.both = bf16[36,768]{1,0:T(8,128)(2,1)S(1)} collective-permute-done((bf16[36,768]{1,0:T(8,128)(2,1)S(1)}, bf16[36,768]{1,0:T(8,128)(2,1)S(1)}, u32[]{:S(2)}, u32[]{:S(2)}) %collective-permute-start.12) | collective-permute-done | bytes 55328 | tf_op jit(solution)/shard_map/ppermute | solution.py:640
  50.2 0.9 %unpack.1 = (bf16[3,3,4,3072]{3,2,1,0:T(4,128)(2,1)}, bf16[6,12,2,768]{3,2,1,0:T(2,128)(2,1)}) custom-call(bf16[36,768]{1,0:T(8,128)(2,1)S(1)} %get-tuple-element.55.own, bf16[36,768]{1,0:T(8,128)(2,1)S(1)} %collective-permute-done.10.lat, bf16[36,768]{1,0:T(8,128)(2,1)S(1)} %collective-permute-done.11.lon, ...), custom_call_target="tpu_custom_call" | custom-call | tf_op jit(solution)/shard_map/unpack/pallas_call | solution.py:611
Async XLA Ops:
  1.9 17.4 %collective-permute-start.1 = (bf16[36,768]{1,0:T(8,128)(2,1)S(1)}, bf16[36,768]{1,0:T(8,128)(2,1)S(1)}, u32[]{:S(2)}, u32[]{:S(2)}) collective-permute-start(bf16[36,768]{1,0:T(8,128)(2,1)S(1)} %get-tuple-element.39), channel_id=1, source_target_pairs={{0,2},{1,31},{2,0},{3,29},{4,6},{5,3},{6,4},{7,1},{8,10},{9,7},{10... | collective-permute-start | bytes 165896 | tf_op jit(solution)/shard_map/ppermute | solution.py:640
  6.0 16.8 %collective-permute-start.3 = (bf16[36,768]{1,0:T(8,128)(2,1)S(1)}, bf16[36,768]{1,0:T(8,128)(2,1)S(1)}, u32[]{:S(2)}, u32[]{:S(2)}) collective-permute-start(bf16[36,768]{1,0:T(8,128)(2,1)S(1)} %get-tuple-element.45), channel_id=1, source_target_pairs={{0,29},{1,0},{2,31},{3,2},{4,1},{5,4},{6,3},{7,6},{8,5},{9,8},{10,... | collective-permute-start | bytes 165896 | tf_op jit(solution)/shard_map/ppermute | solution.py:640
  9.2 13.6 %collective-permute-start.4 = (bf16[36,768]{1,0:T(8,128)(2,1)S(1)}, bf16[36,768]{1,0:T(8,128)(2,1)S(1)}, u32[]{:S(2)}, u32[]{:S(2)}) collective-permute-start(bf16[36,768]{1,0:T(8,128)(2,1)S(1)} %get-tuple-element.46), channel_id=1, source_target_pairs={{0,31},{1,2},{2,29},{3,0},{4,3},{5,6},{6,1},{7,4},{8,7},{9,10},{10... | collective-permute-start | bytes 165896 | tf_op jit(solution)/shard_map/ppermute | solution.py:640
  9.2 10.2 %collective-permute-start = (bf16[72,768]{1,0:T(8,128)(2,1)S(1)}, bf16[72,768]{1,0:T(8,128)(2,1)S(1)}, u32[]{:S(2)}, u32[]{:S(2)}) collective-permute-start(bf16[72,768]{1,0:T(8,128)(2,1)S(1)} %get-tuple-element.38), channel_id=1, source_target_pairs={{0,30},{1,3},{2,28},{3,1},{4,2},{5,7},{6,0},{7,5},{8,6},{9,11},{10... | collective-permute-start | bytes 331784 | tf_op jit(solution)/shard_map/ppermute | solution.py:640
  11.1 8.3 %copy-start.1 = (bf16[768,768]{1,0:T(8,128)(2,1)S(1)}, bf16[768,768]{1,0:T(8,128)(2,1)}, u32[]{:S(2)}) copy-start(bf16[768,768]{1,0:T(8,128)(2,1)} %output.3) | copy-start | bytes 3538948
  11.1 8.3 %copy-start.3 = (f32[768]{0:T(1024)S(1)}, f32[768]{0:T(1024)}, u32[]{:S(2)}) copy-start(f32[768]{0:T(1024)} %gain.3) | copy-start | bytes 9220
  11.1 8.3 %collective-permute-start.2 = (bf16[72,768]{1,0:T(8,128)(2,1)S(1)}, bf16[72,768]{1,0:T(8,128)(2,1)S(1)}, u32[]{:S(2)}, u32[]{:S(2)}) collective-permute-start(bf16[72,768]{1,0:T(8,128)(2,1)S(1)} %get-tuple-element.40), channel_id=1, source_target_pairs={{0,28},{1,29},{2,30},{3,31},{4,0},{5,1},{6,2},{7,3},{8,4},{9,5},{1... | collective-permute-start | bytes 331784 | tf_op jit(solution)/shard_map/ppermute | solution.py:640
  11.1 8.3 %copy-start = (bf16[768,2304]{1,0:T(8,128)(2,1)S(1)}, bf16[768,2304]{1,0:T(8,128)(2,1)}, u32[]{:S(2)}) copy-start(bf16[768,2304]{1,0:T(8,128)(2,1)} %packed.3) | copy-start | bytes 10616836
  19.4 3.4 %copy-start.2 = (f32[3072]{0:T(1024)S(1)}, f32[3072]{0:T(1024)}, u32[]{:S(2)}) copy-start(f32[3072]{0:T(1024)} %param.14) | copy-start | bytes 36868
  24.0 4.6 %collective-permute-start.5 = (f32[24,128]{1,0:T(8,128)S(1)}, f32[24,128]{1,0:T(8,128)S(1)}, u32[]{:S(2)}, u32[]{:S(2)}) collective-permute-start(f32[24,128]{1,0:T(8,128)S(1)} %get-tuple-element.49), channel_id=1, source_target_pairs={{0,2},{1,3},{2,0},{3,1},{4,6},{5,7},{6,4},{7,5},{8,10},{9,11},{10,... | collective-permute-start | bytes 36872 | tf_op jit(solution)/shard_map/ppermute | solution.py:640
  29.2 11.3 %collective-permute-start.6 = (bf16[36,768]{1,0:T(8,128)(2,1)S(1)}, bf16[36,768]{1,0:T(8,128)(2,1)S(1)}, u32[]{:S(2)}, u32[]{:S(2)}) collective-permute-start(bf16[36,768]{1,0:T(8,128)(2,1)S(1)} %get-tuple-element.59), channel_id=1, source_target_pairs={{28,0},{1,1},{30,2},{3,3},{0,4},{5,5},{2,6},{7,7},{4,8},{9,9},{6,1... | collective-permute-start | bytes 165896 | tf_op jit(solution)/shard_map/ppermute | solution.py:640
  31.1 9.4 %collective-permute-start.7 = (bf16[36,768]{1,0:T(8,128)(2,1)S(1)}, bf16[36,768]{1,0:T(8,128)(2,1)S(1)}, u32[]{:S(2)}, u32[]{:S(2)}) collective-permute-start(bf16[36,768]{1,0:T(8,128)(2,1)S(1)} %get-tuple-element.60), channel_id=1, source_target_pairs={{30,0},{3,1},{28,2},{1,3},{2,4},{7,5},{0,6},{5,7},{6,8},{11,9},{4,... | collective-permute-start | bytes 165896 | tf_op jit(solution)/shard_map/ppermute | solution.py:640
  33.8 6.8 %collective-permute-start.8 = (bf16[36,768]{1,0:T(8,128)(2,1)S(1)}, bf16[36,768]{1,0:T(8,128)(2,1)S(1)}, u32[]{:S(2)}, u32[]{:S(2)}) collective-permute-start(bf16[36,768]{1,0:T(8,128)(2,1)S(1)} %get-tuple-element.61), channel_id=1, source_target_pairs={{29,0},{0,1},{31,2},{2,3},{1,4},{4,5},{3,6},{6,7},{5,8},{8,9},{7,1... | collective-permute-start | bytes 165896 | tf_op jit(solution)/shard_map/ppermute | solution.py:640
  33.8 7.8 %collective-permute-start.9 = (bf16[36,768]{1,0:T(8,128)(2,1)S(1)}, bf16[36,768]{1,0:T(8,128)(2,1)S(1)}, u32[]{:S(2)}, u32[]{:S(2)}) collective-permute-start(bf16[36,768]{1,0:T(8,128)(2,1)S(1)} %get-tuple-element.62), channel_id=1, source_target_pairs={{31,0},{2,1},{29,2},{0,3},{3,4},{6,5},{1,6},{4,7},{7,8},{10,9},{5,... | collective-permute-start | bytes 165896 | tf_op jit(solution)/shard_map/ppermute | solution.py:640
  41.6 7.1 %collective-permute-start.10 = (bf16[36,768]{1,0:T(8,128)(2,1)S(1)}, bf16[36,768]{1,0:T(8,128)(2,1)S(1)}, u32[]{:S(2)}, u32[]{:S(2)}) collective-permute-start(bf16[36,768]{1,0:T(8,128)(2,1)S(1)} %get-tuple-element.63), channel_id=1, source_target_pairs={{2,0},{3,1},{0,2},{1,3},{6,4},{7,5},{4,6},{5,7},{10,8},{11,9},{8,1... | collective-permute-start | bytes 165896 | tf_op jit(solution)/shard_map/ppermute | solution.py:640
  41.6 7.1 %collective-permute-start.11 = (bf16[36,768]{1,0:T(8,128)(2,1)S(1)}, bf16[36,768]{1,0:T(8,128)(2,1)S(1)}, u32[]{:S(2)}, u32[]{:S(2)}) collective-permute-start(bf16[36,768]{1,0:T(8,128)(2,1)S(1)} %get-tuple-element.64), channel_id=1, source_target_pairs={{28,0},{29,1},{30,2},{31,3},{0,4},{1,5},{2,6},{3,7},{4,8},{5,9},{6... | collective-permute-start | bytes 165896 | tf_op jit(solution)/shard_map/ppermute | solution.py:640
  41.6 8.6 %collective-permute-start.12 = (bf16[36,768]{1,0:T(8,128)(2,1)S(1)}, bf16[36,768]{1,0:T(8,128)(2,1)S(1)}, u32[]{:S(2)}, u32[]{:S(2)}) collective-permute-start(bf16[36,768]{1,0:T(8,128)(2,1)S(1)} %get-tuple-element.65), channel_id=1, source_target_pairs={{30,0},{31,1},{28,2},{29,3},{2,4},{3,5},{0,6},{1,7},{6,8},{7,9},{4... | collective-permute-start | bytes 165896 | tf_op jit(solution)/shard_map/ppermute | solution.py:640

commit v4 on v3

--- a/solution.py
+++ b/solution.py
@@ -471,7 +471,7 @@
     )(residual, *pieces, gain)
 
 
-def merge_kernel(residual, scaled, moments, before, after, gain, kept, below, right, far, grad, factors):
+def merge_kernel(residual, scaled, moments, before, after, gain, near, over, grad, factors):
     width = residual.shape[-1]
     upper = lax.axis_index("lev") == 1
     gain_rows(gain, factors)
@@ -499,18 +499,17 @@
     grad[...] = (scale * (scaled[...] - grad_sum / full - unit * (cross * scale / full))).astype(bf16)
     out = unit * factors[...]
     parts = [quadrant(out, quad) for quad in range(4)]
-    kept[...] = jnp.where(upper, parts[0], parts[2]).astype(bf16)
-    below[...] = jnp.where(upper, parts[1], parts[3]).astype(bf16)
-    right[...] = jnp.where(upper, parts[2], parts[0]).astype(bf16)
-    far[...] = jnp.where(upper, parts[3], parts[1]).astype(bf16)
+    left, right = jnp.concatenate(parts[:2], axis=0), jnp.concatenate(parts[2:], axis=0)
+    near[...] = jnp.where(upper, left, right).astype(bf16)
+    over[...] = jnp.where(upper, right, left).astype(bf16)
 
 
 def merge_back(residual, scaled, moments, before, after, gain):
     width = residual.shape[-1]
-    piece = shape((QUAD, width), bf16)
+    piece = shape((2 * QUAD, width), bf16)
     return pl.pallas_call(
         merge_kernel,
-        out_shape=[piece] * 4 + [shape((WIN, width), bf16)],
+        out_shape=[piece] * 2 + [shape((WIN, width), bf16)],
         scratch_shapes=[pltpu.VMEM((WIN, width), f32)],
         compiler_params=params(),
         cost_estimate=cost(10**8, 10**6),
@@ -576,13 +575,25 @@
         finish_kernel,
         out_shape=[shape((QUAD, width), bf16)] * 4,
         compiler_params=params(),
-        cost_estimate=cost(10**9, 2 * 10**6),
+        cost_estimate=cost(10**10, 2 * 10**6),
         name="finish",
     )(grad, joined, tokens, packed, gain)
 
 
-def unpack_kernel(own, lat, lon, both, same_here, other_here, same_next, other_next, merged, tokens):
-    width = own.shape[-1]
+def relay_kernel(near, cross, out):
+    out[...] = jnp.concatenate((near[...].astype(f32)[QUAD:], cross[...].astype(f32)[QUAD:]), axis=0).astype(bf16)
+
+
+def relay(near, cross):
+    return pl.pallas_call(
+        relay_kernel,
+        out_shape=shape(near.shape, bf16),
+        compiler_params=params(),
+        name="relay",
+    )(near, cross)
+
+
+def token_kernel(own, lat, lon, both, tokens):
     quads = [piece[...].astype(f32) for piece in (own, lat, lon, both)]
     for line in range(WLAT):
         for column in range(WLON):
@@ -590,9 +601,24 @@
             inner = column % HALF_LON
             at = token_row(0, line % HALF_LAT, inner % 2, inner // 2)
             tokens[line, column] = quads[quad][at : at + LEVELS].astype(bf16)
+
+
+def unpack_tokens(*pieces):
+    width = pieces[0].shape[-1]
+    return pl.pallas_call(
+        token_kernel,
+        out_shape=shape((WLAT, WLON, LEVELS, width), bf16),
+        compiler_params=params(),
+        name="unpack_tokens",
+    )(*pieces)
+
+
+def cell_kernel(near, cross, onward, merged):
+    width = near.shape[-1]
     upper = lax.axis_index("lev") == 1
-    same = (same_here[...].astype(f32), same_next[...].astype(f32))
-    other = (other_here[...].astype(f32), other_next[...].astype(f32))
+    arrived = onward[...].astype(f32)
+    same = (near[...].astype(f32)[:QUAD], arrived[:QUAD])
+    other = (cross[...].astype(f32)[:QUAD], arrived[QUAD:])
     low = [jnp.where(upper, b, a) for a, b in zip(same, other)]
     high = [jnp.where(upper, a, b) for a, b in zip(same, other)]
     for row, odd, below, inner in cell_places():
@@ -606,17 +632,15 @@
                 ).astype(bf16)
 
 
-def unpack_pieces(token_pieces, cell_pieces):
-    width = token_pieces[0].shape[-1]
-    return pl.pallas_call(
-        unpack_kernel,
-        out_shape=[
-            shape((HALF_LAT, PAIRS, 2 * LEVELS, 4 * width), bf16),
-            shape((WLAT, WLON, LEVELS, width), bf16),
-        ],
-        compiler_params=params(),
-        name="unpack",
-    )(*token_pieces, *cell_pieces)
+def unpack_cells(near, cross, onward):
+    width = near.shape[-1]
+    return pl.pallas_call(
+        cell_kernel,
+        out_shape=shape((HALF_LAT, PAIRS, 2 * LEVELS, 4 * width), bf16),
+        compiler_params=params(),
+        cost_estimate=cost(10**9, 10**6),
+        name="unpack_cells",
+    )(near, cross, onward)
 
 
 def routes(sizes, target):
@@ -680,18 +704,19 @@
     scaled, moments, sent = cell_moments(residual, (kept, first, third, fourth, fifth), cell_gain)
     before = send(sent, sizes, lambda i, a, k: (i, a + 1, k))
     after = before if sizes[1] == 2 else send(sent, sizes, lambda i, a, k: (i, a - 1, k))
-    kept, below, right, far, grad = merge_back(residual, scaled, moments, before, after, cell_gain)
-    below = send(below, sizes, FIRST, True)
-    far = send(far, sizes, FIFTH, True)
-    right = send(right, sizes, FOURTH, True)
-    kept = send(kept, sizes, HERE, True)
+    near, cross, grad = merge_back(residual, scaled, moments, before, after, cell_gain)
+    near = send(near, sizes, HERE, True)
+    cross = send(cross, sizes, FOURTH, True)
     joined = backward(grad, weights, triple, keys_t, output_weight)
+    joined, near, cross = lax.optimization_barrier((joined, near, cross))
+    onward = send(relay(near, cross), sizes, LAT, True)
     own, lat, lon, both = finish(grad, joined, data, packed_weight, norm_gain)
-    lat, lon, both, kept, below, right, far = lax.optimization_barrier((lat, lon, both, kept, below, right, far))
     lat = send(lat, sizes, LAT, True)
     both = send(both, sizes, BOTH, True)
     lon = send(lon, sizes, LON, True)
-    merged, grads = unpack_pieces((own, lat, lon, both), (kept, right, below, far))
+    merged = unpack_cells(near, cross, onward)
+    merged, lat, both, lon = lax.optimization_barrier((merged, lat, both, lon))
+    grads = unpack_tokens(own, lat, lon, both)
     return merged.transpose(2, 0, 1, 3), grads.transpose(2, 0, 1, 3)
 
 

time: 51.2 us -> 52.5 us (1.025)
  waiting for transfers between devices: 9.97 us -> 12.7 us
  starting transfers between devices: 20.5 us -> 18.3 us
  Pallas kernels: 19.8 us -> 20.5 us
    ppermute x13 -> x12, waiting for transfers between devices: 9.97 us -> 12.7 us  [send(): return lax.ppermute(block, ('lon', 'lat', 'lev'), pairs)]
    ppermute x13 -> x12, starting transfers between devices: 20.5 us -> 18.3 us  [send(): return lax.ppermute(block, ('lon', 'lat', 'lev'), pairs)]
    pallas_call x2 -> x4, Pallas kernels: 1.4 us -> 2.12 us  [the longest x1 0.84 us: unpack_cells(): pl.pallas_call(cell_kernel, out_shape=shape((HALF_LAT, PAIRS, 2 * LEVELS,...]
  transfers between devices with their start and end apart: 13 -> 12, of which waited for: 4 -> 6; matrix products, arithmetic and copies ran while one was open for 0% -> 0% of each run, Pallas kernels for 31% -> 32%
where the time goes in v4:
time: 52.5 us; the launch traced here: 52.4 us
  Pallas kernels  20.5 us (39%)
  starting transfers between devices  18.3 us (35%)
  waiting for transfers between devices  12.7 us (24%)
  between operations  0.78 us (1%)
    ppermute x12, starting transfers between devices, send(): return lax.ppermute(block, ('lon', 'lat', 'lev'), pairs)  18.3 us
    ppermute x12, waiting for transfers between devices, send(): return lax.ppermute(block, ('lon', 'lat', 'lev'), pairs)  12.7 us
    pallas_call x1, Pallas kernels, window_bias(): pl.pallas_call(bias_kernel, out_shape=[shape((heads * WIN, 128), f32)] *...  8.24 us
    pallas_call x1, Pallas kernels, forward(): pl.pallas_call(forward_kernel, out_shape=[shape((HEADS * WIN, WIN), bf16)...  3.34 us
    pallas_call x1, Pallas kernels, backward(): pl.pallas_call(backward_kernel, out_shape=shape((WIN, 3 * width), bf16),...  2.8 us
    pallas_call x1, Pallas kernels, finish(): pl.pallas_call(finish_kernel, out_shape=[shape((QUAD, width), bf16)] * 4,...  1.51 us
    pallas_call x1, Pallas kernels, pack_pieces(): pl.pallas_call(pack_kernel, out_shape=[piece, double, piece, double, piec...  1.3 us
    pallas_call x1, Pallas kernels, cell_moments(): pl.pallas_call(moments_kernel, out_shape=[shape((WIN, width), f32), shape...  1.15 us
  transfers between devices with their start and end apart: 12, of which 6 were waited for; matrix products, arithmetic and copies ran while one was open for 0% of the time, Pallas kernels for 32%

profile of v4, /device:TPU:0, one launch (start us, length us, event | category | flops | bytes accessed | tf_op | source)
XLA Modules:
  0.0 52.4 jit_solution(17974141734844471994)
XLA Ops:
  0.6 1.3 %pack.1 = (bf16[36,768]{1,0:T(8,128)(2,1)S(1)}, bf16[72,768]{1,0:T(8,128)(2,1)S(1)}, bf16[36,768]{1,0:T(8,128)(2,1)S(1)}, bf16[72,768]{1,0:T(8,128)(2,1)S(1)}, b...) custom-call(bf16[6,12,2,768]{3,2,1,0:T(2,128)(2,1)} %bitcast.8, ...), custom_call_target="tpu_custom_call" | custom-call | tf_op jit(solution)/shard_map/pack/pallas_call | solution.py:137
  1.9 4.1 %collective-permute-start.1 = (bf16[36,768]{1,0:T(8,128)(2,1)S(1)}, bf16[36,768]{1,0:T(8,128)(2,1)S(1)}, u32[]{:S(2)}, u32[]{:S(2)}) collective-permute-start(bf16[36,768]{1,0:T(8,128)(2,1)S(1)} %get-tuple-element.35), channel_id=1, source_target_pairs={{0,2},{1,31},{2,0},{3,29},{4,6},{5,3},{6,4},{7,1},{8,10},{9,7},{10... | collective-permute-start | bytes 165896 | tf_op jit(solution)/shard_map/ppermute | solution.py:664
  6.0 3.2 %collective-permute-start.3 = (bf16[36,768]{1,0:T(8,128)(2,1)S(1)}, bf16[36,768]{1,0:T(8,128)(2,1)S(1)}, u32[]{:S(2)}, u32[]{:S(2)}) collective-permute-start(bf16[36,768]{1,0:T(8,128)(2,1)S(1)} %get-tuple-element.41), channel_id=1, source_target_pairs={{0,29},{1,0},{2,31},{3,2},{4,1},{5,4},{6,3},{7,6},{8,5},{9,8},{10,... | collective-permute-start | bytes 165896 | tf_op jit(solution)/shard_map/ppermute | solution.py:664
  9.2 0.0 collective-permute-start.4
  9.2 1.9 %collective-permute-start = (bf16[72,768]{1,0:T(8,128)(2,1)S(1)}, bf16[72,768]{1,0:T(8,128)(2,1)S(1)}, u32[]{:S(2)}, u32[]{:S(2)}) collective-permute-start(bf16[72,768]{1,0:T(8,128)(2,1)S(1)} %get-tuple-element.34), channel_id=1, source_target_pairs={{0,30},{1,3},{2,28},{3,1},{4,2},{5,7},{6,0},{7,5},{8,6},{9,11},{10... | collective-permute-start | bytes 331784 | tf_op jit(solution)/shard_map/ppermute | solution.py:664
  11.1 0.0 copy-start.1
  11.1 0.0 copy-start.3
  11.1 0.0 collective-permute-start.2
  11.1 0.0 copy-start
  11.1 8.2 %bias.1 = (f32[3456,128]{1,0:T(8,128)S(1)}, f32[3456,128]{1,0:T(8,128)S(1)}) custom-call(f32[1,1,24,3312]{3,2,1,0:T(8,128)} %table_at.1, s32[144,144]{1,0:T(8,128)} %index_at.1, s32[6]{0:T(128)} %labels_at.1, s32[96]{0:T(128)} %valid_at.1), custom_call_target="tpu_custom_call" | custom-call | flops 10000000000 | bytes 20000000 | tf_op jit(solution)/shard_map/bias/pallas_call | solution.py:278
  19.4 0.0 collective-permute-done.1.second
  19.4 0.0 collective-permute-done.first
  19.4 0.0 collective-permute-done.2.third
  19.4 0.0 copy-done.1
  19.4 0.0 copy-done.3
  19.4 0.0 copy-done
  19.4 0.0 copy-start.2
  19.5 3.3 %forward.1 = (bf16[3456,144]{1,0:T(8,128)(2,1)S(1)}, bf16[144,2304]{1,0:T(8,128)(2,1)S(1)}, bf16[768,144]{1,0:T(8,128)(2,1)S(1)}, bf16[144,768]{1,0:T(8,128)(2,1)S(1)}, bf16[144,768]{1,0:T(8,128)(2,1)S(1)}) custom-call(bf16[36,768]{1,0:T(8,128)(2,1)S(1)} %get-tuple-element.33.own, bf16[72,768]{1,0:T(8,128)(2,1)S(1)} %collective-permute-done.first, ...), custom_call_target="tpu_custom_call" | custom-call | flops 1000000000 | bytes 20000000 | tf_op jit(solution)/shard_map/forward/pallas_call | solution.py:368
  22.8 0.0 collective-permute-done.3.fourth
  22.8 0.0 collective-permute-done.4.fifth
  22.8 0.0 copy-done.2
  22.8 1.2 %moments.1 = (f32[144,768]{1,0:T(8,128)S(1)}, f32[144,128]{1,0:T(8,128)S(1)}, f32[24,128]{1,0:T(8,128)S(1)}) custom-call(bf16[144,768]{1,0:T(8,128)(2,1)S(1)} %get-tuple-element.39.residual, bf16[36,768]{1,0:T(8,128)(2,1)S(1)} %get-tuple-element.40.kept, bf16[72,768]{1,0:T(8,128)(2,1)S(1)} %collective-permute-done.first, ...), custom_call_target="tpu_custom_call" | custom-call | flops 100000000 | bytes 1000000 | tf_op jit(solution)/shard_map/moments/pallas_call | solution.py:464
  24.0 1.3 %collective-permute-start.5 = (f32[24,128]{1,0:T(8,128)S(1)}, f32[24,128]{1,0:T(8,128)S(1)}, u32[]{:S(2)}, u32[]{:S(2)}) collective-permute-start(f32[24,128]{1,0:T(8,128)S(1)} %get-tuple-element.45), channel_id=1, source_target_pairs={{0,2},{1,3},{2,0},{3,1},{4,6},{5,7},{6,4},{7,5},{8,10},{9,11},{10,... | collective-permute-start | bytes 36872 | tf_op jit(solution)/shard_map/ppermute | solution.py:664
  25.3 3.3 %collective-permute-done.5.before.after = f32[24,128]{1,0:T(8,128)S(1)} collective-permute-done((f32[24,128]{1,0:T(8,128)S(1)}, f32[24,128]{1,0:T(8,128)S(1)}, u32[]{:S(2)}, u32[]{:S(2)}) %collective-permute-start.5) | collective-permute-done | bytes 12320 | tf_op jit(solution)/shard_map/ppermute | solution.py:664
  28.6 0.5 %merge.1 = (bf16[72,768]{1,0:T(8,128)(2,1)S(1)}, bf16[72,768]{1,0:T(8,128)(2,1)S(1)}, bf16[144,768]{1,0:T(8,128)(2,1)S(1)}) custom-call(bf16[144,768]{1,0:T(8,128)(2,1)S(1)} %get-tuple-element.39.residual, f32[144,768]{1,0:T(8,128)S(1)} %get-tuple-element.43.scaled, f32[144,128]{1,0:T(8,128)S(1)} %get-tuple-element.44.moments, ...), custom_call_target="tpu_custom_call" | custom-call | flops 100000000 | bytes 1000000 | tf_op jit(solution)/shard_map/merge/pallas_call | solution.py:510
  29.2 1.9 %collective-permute-start.6 = (bf16[72,768]{1,0:T(8,128)(2,1)S(1)}, bf16[72,768]{1,0:T(8,128)(2,1)S(1)}, u32[]{:S(2)}, u32[]{:S(2)}) collective-permute-start(bf16[72,768]{1,0:T(8,128)(2,1)S(1)} %get-tuple-element.50), channel_id=1, source_target_pairs={{28,0},{1,1},{30,2},{3,3},{0,4},{5,5},{2,6},{7,7},{4,8},{9,9},{6,1... | collective-permute-start | bytes 331784 | tf_op jit(solution)/shard_map/ppermute | solution.py:664
  31.1 1.5 %collective-permute-start.7 = (bf16[72,768]{1,0:T(8,128)(2,1)S(1)}, bf16[72,768]{1,0:T(8,128)(2,1)S(1)}, u32[]{:S(2)}, u32[]{:S(2)}) collective-permute-start(bf16[72,768]{1,0:T(8,128)(2,1)S(1)} %get-tuple-element.51), channel_id=1, source_target_pairs={{29,0},{0,1},{31,2},{2,3},{1,4},{4,5},{3,6},{6,7},{5,8},{8,9},{7,1... | collective-permute-start | bytes 331784 | tf_op jit(solution)/shard_map/ppermute | solution.py:664
  32.6 2.8 %backward.1.joined = bf16[144,2304]{1,0:T(8,128)(2,1)S(1)} custom-call(bf16[144,768]{1,0:T(8,128)(2,1)S(1)} %get-tuple-element.46.grad, bf16[3456,144]{1,0:T(8,128)(2,1)S(1)} %get-tuple-element.47.weights, bf16[144,2304]{1,0:T(8,128)(2,1)S(1)} %get-tuple-element.48.triple, bf16[768,144]{1,0:T(8,128)(2,1)S(1)} %get-tuple-element.49.keys_t, ...), custom_call_target="tpu_custom_call" | custom-call | flops 10000000000 | bytes 20000000 | tf_op jit(solution)/shard_map/backward/pallas_call | solution.py:553
  35.4 0.8 %collective-permute-done.6.near = bf16[72,768]{1,0:T(8,128)(2,1)S(1)} collective-permute-done((bf16[72,768]{1,0:T(8,128)(2,1)S(1)}, bf16[72,768]{1,0:T(8,128)(2,1)S(1)}, u32[]{:S(2)}, u32[]{:S(2)}) %collective-permute-start.6) | collective-permute-done | bytes 110624 | tf_op jit(solution)/shard_map/ppermute | solution.py:664
  36.2 1.5 %collective-permute-done.7.cross = bf16[72,768]{1,0:T(8,128)(2,1)S(1)} collective-permute-done((bf16[72,768]{1,0:T(8,128)(2,1)S(1)}, bf16[72,768]{1,0:T(8,128)(2,1)S(1)}, u32[]{:S(2)}, u32[]{:S(2)}) %collective-permute-start.7) | collective-permute-done | bytes 110624 | tf_op jit(solution)/shard_map/ppermute | solution.py:664
  37.7 1.3 %collective-permute-start.8 = (bf16[72,768]{1,0:T(8,128)(2,1)S(1)}, bf16[72,768]{1,0:T(8,128)(2,1)S(1)}, u32[]{:S(2)}, u32[]{:S(2)}) collective-permute-start(bf16[72,768]{1,0:T(8,128)(2,1)S(1)} %relay.1), channel_id=1, source_target_pairs={{2,0},{3,1},{0,2},{1,3},{6,4},{7,5},{4,6},{5,7},{10,8},{11,9},{8,1... | collective-permute-start | bytes 331784 | tf_op jit(solution)/shard_map/ppermute | solution.py:664
  39.0 1.5 %finish.1 = (bf16[36,768]{1,0:T(8,128)(2,1)S(1)}, bf16[36,768]{1,0:T(8,128)(2,1)S(1)}, bf16[36,768]{1,0:T(8,128)(2,1)S(1)}, bf16[36,768]{1,0:T(8,128)(2,1)S(1)}) custom-call(bf16[144,768]{1,0:T(8,128)(2,1)S(1)} %get-tuple-element.46.grad, bf16[144,2304]{1,0:T(8,128)(2,1)S(1)} %backward.1.joined, bf16[144,768]{1,0:T(8,128)(2,1)S(1)} %get-tuple-element.55.tokens, ...), custom_call_target="tpu_custom_call" | custom-call | flops 10000000000 | bytes 2000000 | tf_op jit(solution)/shard_map/finish/pallas_call | solution.py:574
  40.6 1.7 %collective-permute-start.9 = (bf16[36,768]{1,0:T(8,128)(2,1)S(1)}, bf16[36,768]{1,0:T(8,128)(2,1)S(1)}, u32[]{:S(2)}, u32[]{:S(2)}) collective-permute-start(bf16[36,768]{1,0:T(8,128)(2,1)S(1)} %get-tuple-element.56), channel_id=1, source_target_pairs={{2,0},{3,1},{0,2},{1,3},{6,4},{7,5},{4,6},{5,7},{10,8},{11,9},{8,1... | collective-permute-start | bytes 165896 | tf_op jit(solution)/shard_map/ppermute | solution.py:664
  42.3 0.4 collective-permute-start.10
  42.7 1.0 %collective-permute-start.11 = (bf16[36,768]{1,0:T(8,128)(2,1)S(1)}, bf16[36,768]{1,0:T(8,128)(2,1)S(1)}, u32[]{:S(2)}, u32[]{:S(2)}) collective-permute-start(bf16[36,768]{1,0:T(8,128)(2,1)S(1)} %get-tuple-element.58), channel_id=1, source_target_pairs={{28,0},{29,1},{30,2},{31,3},{0,4},{1,5},{2,6},{3,7},{4,8},{5,9},{6... | collective-permute-start | bytes 165896 | tf_op jit(solution)/shard_map/ppermute | solution.py:664
  43.7 4.5 %collective-permute-done.8.onward = bf16[72,768]{1,0:T(8,128)(2,1)S(1)} collective-permute-done((bf16[72,768]{1,0:T(8,128)(2,1)S(1)}, bf16[72,768]{1,0:T(8,128)(2,1)S(1)}, u32[]{:S(2)}, u32[]{:S(2)}) %collective-permute-start.8) | collective-permute-done | bytes 110624 | tf_op jit(solution)/shard_map/ppermute | solution.py:664
  48.2 0.8 %unpack_cells.1 = bf16[3,3,4,3072]{3,2,1,0:T(4,128)(2,1)} custom-call(bf16[72,768]{1,0:T(8,128)(2,1)S(1)} %collective-permute-done.6.near, bf16[72,768]{1,0:T(8,128)(2,1)S(1)} %collective-permute-done.7.cross, bf16[72,768]{1,0:T(8,128)(2,1)S(1)} %collective-permute-done.8.onward), custom_call_target="tpu_custom_call" | custom-call | flops 1000000000 | bytes 1000000 | tf_op jit(solution)/shard_map/unpack_cells/pallas_call | solution.py:637
  49.0 0.5 collective-permute-done.9.lat
  49.5 2.2 %collective-permute-done.10.both = bf16[36,768]{1,0:T(8,128)(2,1)S(1)} collective-permute-done((bf16[36,768]{1,0:T(8,128)(2,1)S(1)}, bf16[36,768]{1,0:T(8,128)(2,1)S(1)}, u32[]{:S(2)}, u32[]{:S(2)}) %collective-permute-start.10) | collective-permute-done | bytes 55328 | tf_op jit(solution)/shard_map/ppermute | solution.py:664
  51.6 0.0 collective-permute-done.11.lon
  51.6 0.7 %unpack_tokens.1 = bf16[6,12,2,768]{3,2,1,0:T(2,128)(2,1)} custom-call(bf16[36,768]{1,0:T(8,128)(2,1)S(1)} %get-tuple-element.60.own, bf16[36,768]{1,0:T(8,128)(2,1)S(1)} %collective-permute-done.9.lat, bf16[36,768]{1,0:T(8,128)(2,1)S(1)} %collective-permute-done.11.lon, bf16[36,768]{1,0:T(8,128)(2,1)S(1)} %collective-permute-done.10.both), custom_call_target="tpu_custom_call" | custom-call | tf_op jit(solution)/shard_map/unpack_tokens/pallas_call | solution.py:608
  (1 shorter events, 0.0 us)
Async XLA Ops:
  1.9 17.4 %collective-permute-start.1 = (bf16[36,768]{1,0:T(8,128)(2,1)S(1)}, bf16[36,768]{1,0:T(8,128)(2,1)S(1)}, u32[]{:S(2)}, u32[]{:S(2)}) collective-permute-start(bf16[36,768]{1,0:T(8,128)(2,1)S(1)} %get-tuple-element.35), channel_id=1, source_target_pairs={{0,2},{1,31},{2,0},{3,29},{4,6},{5,3},{6,4},{7,1},{8,10},{9,7},{10... | collective-permute-start | bytes 165896 | tf_op jit(solution)/shard_map/ppermute | solution.py:664
  6.0 16.8 %collective-permute-start.3 = (bf16[36,768]{1,0:T(8,128)(2,1)S(1)}, bf16[36,768]{1,0:T(8,128)(2,1)S(1)}, u32[]{:S(2)}, u32[]{:S(2)}) collective-permute-start(bf16[36,768]{1,0:T(8,128)(2,1)S(1)} %get-tuple-element.41), channel_id=1, source_target_pairs={{0,29},{1,0},{2,31},{3,2},{4,1},{5,4},{6,3},{7,6},{8,5},{9,8},{10,... | collective-permute-start | bytes 165896 | tf_op jit(solution)/shard_map/ppermute | solution.py:664
  9.2 13.6 %collective-permute-start.4 = (bf16[36,768]{1,0:T(8,128)(2,1)S(1)}, bf16[36,768]{1,0:T(8,128)(2,1)S(1)}, u32[]{:S(2)}, u32[]{:S(2)}) collective-permute-start(bf16[36,768]{1,0:T(8,128)(2,1)S(1)} %get-tuple-element.42), channel_id=1, source_target_pairs={{0,31},{1,2},{2,29},{3,0},{4,3},{5,6},{6,1},{7,4},{8,7},{9,10},{10... | collective-permute-start | bytes 165896 | tf_op jit(solution)/shard_map/ppermute | solution.py:664
  9.2 10.2 %collective-permute-start = (bf16[72,768]{1,0:T(8,128)(2,1)S(1)}, bf16[72,768]{1,0:T(8,128)(2,1)S(1)}, u32[]{:S(2)}, u32[]{:S(2)}) collective-permute-start(bf16[72,768]{1,0:T(8,128)(2,1)S(1)} %get-tuple-element.34), channel_id=1, source_target_pairs={{0,30},{1,3},{2,28},{3,1},{4,2},{5,7},{6,0},{7,5},{8,6},{9,11},{10... | collective-permute-start | bytes 331784 | tf_op jit(solution)/shard_map/ppermute | solution.py:664
  11.1 8.3 %copy-start.1 = (bf16[768,768]{1,0:T(8,128)(2,1)S(1)}, bf16[768,768]{1,0:T(8,128)(2,1)}, u32[]{:S(2)}) copy-start(bf16[768,768]{1,0:T(8,128)(2,1)} %output.3) | copy-start | bytes 3538948
  11.1 8.3 %copy-start.3 = (f32[768]{0:T(1024)S(1)}, f32[768]{0:T(1024)}, u32[]{:S(2)}) copy-start(f32[768]{0:T(1024)} %gain.3) | copy-start | bytes 9220
  11.1 8.3 %collective-permute-start.2 = (bf16[72,768]{1,0:T(8,128)(2,1)S(1)}, bf16[72,768]{1,0:T(8,128)(2,1)S(1)}, u32[]{:S(2)}, u32[]{:S(2)}) collective-permute-start(bf16[72,768]{1,0:T(8,128)(2,1)S(1)} %get-tuple-element.36), channel_id=1, source_target_pairs={{0,28},{1,29},{2,30},{3,31},{4,0},{5,1},{6,2},{7,3},{8,4},{9,5},{1... | collective-permute-start | bytes 331784 | tf_op jit(solution)/shard_map/ppermute | solution.py:664
  11.1 8.3 %copy-start = (bf16[768,2304]{1,0:T(8,128)(2,1)S(1)}, bf16[768,2304]{1,0:T(8,128)(2,1)}, u32[]{:S(2)}) copy-start(bf16[768,2304]{1,0:T(8,128)(2,1)} %packed.3) | copy-start | bytes 10616836
  19.4 3.4 %copy-start.2 = (f32[3072]{0:T(1024)S(1)}, f32[3072]{0:T(1024)}, u32[]{:S(2)}) copy-start(f32[3072]{0:T(1024)} %param.14) | copy-start | bytes 36868
  24.0 4.6 %collective-permute-start.5 = (f32[24,128]{1,0:T(8,128)S(1)}, f32[24,128]{1,0:T(8,128)S(1)}, u32[]{:S(2)}, u32[]{:S(2)}) collective-permute-start(f32[24,128]{1,0:T(8,128)S(1)} %get-tuple-element.45), channel_id=1, source_target_pairs={{0,2},{1,3},{2,0},{3,1},{4,6},{5,7},{6,4},{7,5},{8,10},{9,11},{10,... | collective-permute-start | bytes 36872 | tf_op jit(solution)/shard_map/ppermute | solution.py:664
  29.2 7.0 %collective-permute-start.6 = (bf16[72,768]{1,0:T(8,128)(2,1)S(1)}, bf16[72,768]{1,0:T(8,128)(2,1)S(1)}, u32[]{:S(2)}, u32[]{:S(2)}) collective-permute-start(bf16[72,768]{1,0:T(8,128)(2,1)S(1)} %get-tuple-element.50), channel_id=1, source_target_pairs={{28,0},{1,1},{30,2},{3,3},{0,4},{5,5},{2,6},{7,7},{4,8},{9,9},{6,1... | collective-permute-start | bytes 331784 | tf_op jit(solution)/shard_map/ppermute | solution.py:664
  31.1 6.6 %collective-permute-start.7 = (bf16[72,768]{1,0:T(8,128)(2,1)S(1)}, bf16[72,768]{1,0:T(8,128)(2,1)S(1)}, u32[]{:S(2)}, u32[]{:S(2)}) collective-permute-start(bf16[72,768]{1,0:T(8,128)(2,1)S(1)} %get-tuple-element.51), channel_id=1, source_target_pairs={{29,0},{0,1},{31,2},{2,3},{1,4},{4,5},{3,6},{6,7},{5,8},{8,9},{7,1... | collective-permute-start | bytes 331784 | tf_op jit(solution)/shard_map/ppermute | solution.py:664
  37.7 10.5 %collective-permute-start.8 = (bf16[72,768]{1,0:T(8,128)(2,1)S(1)}, bf16[72,768]{1,0:T(8,128)(2,1)S(1)}, u32[]{:S(2)}, u32[]{:S(2)}) collective-permute-start(bf16[72,768]{1,0:T(8,128)(2,1)S(1)} %relay.1), channel_id=1, source_target_pairs={{2,0},{3,1},{0,2},{1,3},{6,4},{7,5},{4,6},{5,7},{10,8},{11,9},{8,1... | collective-permute-start | bytes 331784 | tf_op jit(solution)/shard_map/ppermute | solution.py:664
  40.6 8.9 %collective-permute-start.9 = (bf16[36,768]{1,0:T(8,128)(2,1)S(1)}, bf16[36,768]{1,0:T(8,128)(2,1)S(1)}, u32[]{:S(2)}, u32[]{:S(2)}) collective-permute-start(bf16[36,768]{1,0:T(8,128)(2,1)S(1)} %get-tuple-element.56), channel_id=1, source_target_pairs={{2,0},{3,1},{0,2},{1,3},{6,4},{7,5},{4,6},{5,7},{10,8},{11,9},{8,1... | collective-permute-start | bytes 165896 | tf_op jit(solution)/shard_map/ppermute | solution.py:664
  42.3 9.3 %collective-permute-start.10 = (bf16[36,768]{1,0:T(8,128)(2,1)S(1)}, bf16[36,768]{1,0:T(8,128)(2,1)S(1)}, u32[]{:S(2)}, u32[]{:S(2)}) collective-permute-start(bf16[36,768]{1,0:T(8,128)(2,1)S(1)} %get-tuple-element.57), channel_id=1, source_target_pairs={{30,0},{31,1},{28,2},{29,3},{2,4},{3,5},{0,6},{1,7},{6,8},{7,9},{4... | collective-permute-start | bytes 165896 | tf_op jit(solution)/shard_map/ppermute | solution.py:664
  42.7 9.0 %collective-permute-start.11 = (bf16[36,768]{1,0:T(8,128)(2,1)S(1)}, bf16[36,768]{1,0:T(8,128)(2,1)S(1)}, u32[]{:S(2)}, u32[]{:S(2)}) collective-permute-start(bf16[36,768]{1,0:T(8,128)(2,1)S(1)} %get-tuple-element.58), channel_id=1, source_target_pairs={{28,0},{29,1},{30,2},{31,3},{0,4},{1,5},{2,6},{3,7},{4,8},{5,9},{6... | collective-permute-start | bytes 165896 | tf_op jit(solution)/shard_map/ppermute | solution.py:664

commit v5 on v4

--- a/solution.py
+++ b/solution.py
@@ -424,7 +424,7 @@
     return out
 
 
-def moments_kernel(residual, kept, first, third, fourth, fifth, gain, scaled, moments, sent, factors):
+def moments_kernel(residual, kept, first, third, fourth, fifth, gain, scaled, moments, sent, near, over, factors):
     width = residual.shape[-1]
     upper = lax.axis_index("lev") == 1
     own, a, b = kept[...].astype(f32), fourth[...].astype(f32), fifth[...].astype(f32)
@@ -457,13 +457,19 @@
     moments[...] = sums
     pick = sent_tokens((4 * CELLS, 1), 0) == lax.broadcasted_iota(jnp.int32, (4 * CELLS, WIN), 1)
     sent[...] = exact(jnp.where(pick, 1.0, 0.0).astype(f32), sums)
+    scale = lax.rsqrt(sums[:, 0:1] * (1 / (4 * width)) + epsilon)
+    out = jnp.where(split_row(down), data, center * scale * factors[...])
+    left, right = out[: 2 * QUAD], out[2 * QUAD :]
+    near[...] = jnp.where(upper, left, right).astype(bf16)
+    over[...] = jnp.where(upper, right, left).astype(bf16)
 
 
 def cell_moments(residual, pieces, gain):
     width = residual.shape[-1]
     return pl.pallas_call(
         moments_kernel,
-        out_shape=[shape((WIN, width), f32), shape((WIN, 128), f32), shape((4 * CELLS, 128), f32)],
+        out_shape=[shape((WIN, width), f32), shape((WIN, 128), f32), shape((4 * CELLS, 128), f32)]
+        + [shape((2 * QUAD, width), bf16)] * 2,
         scratch_shapes=[pltpu.VMEM((WIN, width), f32)],
         compiler_params=params(),
         cost_estimate=cost(10**8, 10**6),
@@ -471,10 +477,8 @@
     )(residual, *pieces, gain)
 
 
-def merge_kernel(residual, scaled, moments, before, after, gain, near, over, grad, factors):
+def merge_kernel(residual, scaled, moments, before, after, grad):
     width = residual.shape[-1]
-    upper = lax.axis_index("lev") == 1
-    gain_rows(gain, factors)
     down = token_places((WIN, 1), 0)
     shared = split_row(down)
     row = down[0]
@@ -497,71 +501,67 @@
     )
     unit = (residual[...].astype(f32) - middle) * scale
     grad[...] = (scale * (scaled[...] - grad_sum / full - unit * (cross * scale / full))).astype(bf16)
-    out = unit * factors[...]
-    parts = [quadrant(out, quad) for quad in range(4)]
-    left, right = jnp.concatenate(parts[:2], axis=0), jnp.concatenate(parts[2:], axis=0)
-    near[...] = jnp.where(upper, left, right).astype(bf16)
-    over[...] = jnp.where(upper, right, left).astype(bf16)
-
-
-def merge_back(residual, scaled, moments, before, after, gain):
-    width = residual.shape[-1]
-    piece = shape((2 * QUAD, width), bf16)
+
+
+def merge_back(residual, scaled, moments, before, after):
     return pl.pallas_call(
         merge_kernel,
-        out_shape=[piece] * 2 + [shape((WIN, width), bf16)],
-        scratch_shapes=[pltpu.VMEM((WIN, width), f32)],
+        out_shape=shape(residual.shape, bf16),
         compiler_params=params(),
         cost_estimate=cost(10**8, 10**6),
         name="merge",
-    )(residual, scaled, moments, before, after, gain)
-
-
-def backward_kernel(grad, weights, triple, keys_t, output, joined, queries_t):
+    )(residual, scaled, moments, before, after)
+
+
+def backward_kernel(half, grad, weights, triple, keys_t, output, joined, queries_t):
     width = grad.shape[-1]
-    upstream = grad[...]
-    grad_heads = mxu(upstream, output[...], NT).astype(bf16)
-    for g in range(width // 128):
+    part = width // 2
+    begin = half * part
+    arriving_all = mxu(grad[...], output[begin : begin + part, :], NT).astype(bf16)
+    for g in range(part // 128):
         here = slice(g * 128, (g + 1) * 128)
-        query = triple[:, g * 128 : (g + 1) * 128]
-        value = triple[:, 2 * width + g * 128 : 2 * width + (g + 1) * 128]
-        arriving = grad_heads[:, here]
+        at = begin + g * 128
+        query = triple[:, at : at + 128]
+        value = triple[:, 2 * width + at : 2 * width + at + 128]
+        arriving = arriving_all[:, here]
         product = mxu(stacked(value), arriving, NT)
-        shares = weights[g * GROUP * WIN : (g + 1) * GROUP * WIN, :]
+        first = at // HEAD
+        shares = weights[first * WIN : (first + GROUP) * WIN, :]
         grad_value = mxu(shares, arriving)
         slopes = []
         for h in range(GROUP):
-            head = g * GROUP + h
             share = shares[h * WIN : (h + 1) * WIN].astype(f32)
             change = product[h * WIN : (h + 1) * WIN]
             level = jnp.sum(share * change, axis=0, keepdims=True)
             slope = (share * (change - level) * HEAD ** (-0.5)).astype(bf16)
-            at = slice(head * HEAD, (head + 1) * HEAD)
-            queries_t[at, :] = mxu(keys_t[at, :], slope)
+            head = at + h * HEAD
+            queries_t[head - begin : head - begin + HEAD, :] = mxu(keys_t[head : head + HEAD, :], slope)
             slopes.append(slope)
         grad_key = mxu(jnp.concatenate(slopes, axis=0), query)
-        split = [slice(h * WIN, (h + 1) * WIN) for h in range(GROUP)]
-        joined[:, width + g * 128 : width + (g + 1) * 128] = lanes_of([grad_key[s] for s in split]).astype(bf16)
-        joined[:, 2 * width + g * 128 : 2 * width + (g + 1) * 128] = lanes_of(
-            [grad_value[s] for s in split]
+        rows = [slice(h * WIN, (h + 1) * WIN) for h in range(GROUP)]
+        joined[:, part + g * 128 : part + (g + 1) * 128] = lanes_of([grad_key[r] for r in rows]).astype(bf16)
+        joined[:, 2 * part + g * 128 : 2 * part + (g + 1) * 128] = lanes_of(
+            [grad_value[r] for r in rows]
         ).astype(bf16)
-    joined[:, :width] = queries_t[...].T.astype(bf16)
-
-
-def backward(grad, weights, triple, keys_t, output):
+    joined[:, :part] = queries_t[...].T.astype(bf16)
+
+
+def backward(half, grad, weights, triple, keys_t, output):
     width = grad.shape[-1]
     return pl.pallas_call(
-        backward_kernel,
-        out_shape=shape((WIN, 3 * width), bf16),
-        scratch_shapes=[pltpu.VMEM((width, WIN), f32)],
+        functools.partial(backward_kernel, half),
+        out_shape=shape((WIN, 3 * width // 2), bf16),
+        scratch_shapes=[pltpu.VMEM((width // 2, WIN), f32)],
         compiler_params=params(),
         cost_estimate=cost(10**10, 2 * 10**7),
         name="backward",
     )(grad, weights, triple, keys_t, output)
 
 
-def finish_kernel(grad, joined, tokens, packed, gain, own, lat, lon, both):
-    grad_inputs = mxu(joined[...], packed[...], NT).astype(bf16)
+def finish_kernel(grad, first, second, tokens, packed, gain, own, lat, lon, both):
+    part = first.shape[-1] // 3
+    joined = [half[:, i * part : (i + 1) * part] for i in range(3) for half in (first, second)]
+    grad_inputs = mxu(jnp.concatenate(joined, axis=1), packed[...], NT).astype(bf16)
     unit, scale = unit_rows(tokens[...].astype(f32))
     scaled = grad_inputs.astype(f32) * gain[...].reshape(1, -1)
     out = grad[...].astype(f32) + scale * (scaled - row_mean(scaled) - unit * row_mean(scaled * unit))
@@ -569,15 +569,15 @@
         piece[...] = quadrant(out, quad).astype(bf16)
 
 
-def finish(grad, joined, tokens, packed, gain):
+def finish(grad, first, second, tokens, packed, gain):
     width = grad.shape[-1]
     return pl.pallas_call(
         finish_kernel,
         out_shape=[shape((QUAD, width), bf16)] * 4,
         compiler_params=params(),
-        cost_estimate=cost(10**10, 2 * 10**6),
+        cost_estimate=cost(10**7, 10**6),
         name="finish",
-    )(grad, joined, tokens, packed, gain)
+    )(grad, first, second, tokens, packed, gain)
 
 
 def relay_kernel(near, cross, out):
@@ -613,26 +613,40 @@
     )(*pieces)
 
 
-def cell_kernel(near, cross, onward, merged):
+def cell_kernel(near, cross, onward, gain, merged):
     width = near.shape[-1]
     upper = lax.axis_index("lev") == 1
     arrived = onward[...].astype(f32)
     same = (near[...].astype(f32)[:QUAD], arrived[:QUAD])
     other = (cross[...].astype(f32)[:QUAD], arrived[QUAD:])
-    low = [jnp.where(upper, b, a) for a, b in zip(same, other)]
-    high = [jnp.where(upper, a, b) for a, b in zip(same, other)]
+    levels = (
+        [jnp.where(upper, b, a) for a, b in zip(same, other)],
+        [jnp.where(upper, a, b) for a, b in zip(same, other)],
+    )
+    blocks = {}
     for row, odd, below, inner in cell_places():
+        for side in range(2):
+            at = token_row(0, inner, side, 0)
+            for part in range(2):
+                blocks[row, side * 2 + odd, part] = levels[part][below][at : at + CELLS]
+    for part in range(2):
+        parts = [blocks[1, block, part] for block in range(4)]
+        mean = sum(jnp.sum(x, axis=-1, keepdims=True) for x in parts) * (1 / (4 * width))
+        parts = [x - mean for x in parts]
+        spread = sum(jnp.sum(x * x, axis=-1, keepdims=True) for x in parts) * (1 / (4 * width))
+        scale = lax.rsqrt(spread + epsilon)
+        for block, x in enumerate(parts):
+            blocks[1, block, part] = x * scale * gain[:, block * width : (block + 1) * width]
+    for row in range(HALF_LAT):
         for pair in range(PAIRS):
-            for side in range(2):
-                block = side * 2 + odd
-                at = token_row(0, inner, side, pair)
-                here = slice(at, at + LEVELS)
+            here = slice(pair * LEVELS, (pair + 1) * LEVELS)
+            for block in range(4):
                 merged[row, pair, :, block * width : (block + 1) * width] = jnp.concatenate(
-                    (low[below][here], high[below][here]), axis=0
+                    (blocks[row, block, 0][here], blocks[row, block, 1][here]), axis=0
                 ).astype(bf16)
 
 
-def unpack_cells(near, cross, onward):
+def unpack_cells(near, cross, onward, gain):
     width = near.shape[-1]
     return pl.pallas_call(
         cell_kernel,
@@ -640,7 +654,7 @@
         compiler_params=params(),
         cost_estimate=cost(10**9, 10**6),
         name="unpack_cells",
-    )(near, cross, onward)
+    )(near, cross, onward, gain)
 
 
 def routes(sizes, target):
@@ -701,20 +715,22 @@
     weights, triple, keys_t, residual, data = forward(
         (own, first, second, third), packed_weight, output_weight, norm_gain, main, tail
     )
-    scaled, moments, sent = cell_moments(residual, (kept, first, third, fourth, fifth), cell_gain)
+    scaled, moments, sent, near, cross = cell_moments(residual, (kept, first, third, fourth, fifth), cell_gain)
     before = send(sent, sizes, lambda i, a, k: (i, a + 1, k))
     after = before if sizes[1] == 2 else send(sent, sizes, lambda i, a, k: (i, a - 1, k))
-    near, cross, grad = merge_back(residual, scaled, moments, before, after, cell_gain)
     near = send(near, sizes, HERE, True)
     cross = send(cross, sizes, FOURTH, True)
-    joined = backward(grad, weights, triple, keys_t, output_weight)
-    joined, near, cross = lax.optimization_barrier((joined, near, cross))
-    onward = send(relay(near, cross), sizes, LAT, True)
-    own, lat, lon, both = finish(grad, joined, data, packed_weight, norm_gain)
+    grad = merge_back(residual, scaled, moments, before, after)
+    first = backward(0, grad, weights, triple, keys_t, output_weight)
+    first, near, cross = lax.optimization_barrier((first, near, cross))
+    onward, grad = lax.optimization_barrier((relay(near, cross), grad))
+    onward = send(onward, sizes, LAT, True)
+    second = backward(1, grad, weights, triple, keys_t, output_weight)
+    own, lat, lon, both = finish(grad, first, second, data, packed_weight, norm_gain)
     lat = send(lat, sizes, LAT, True)
     both = send(both, sizes, BOTH, True)
     lon = send(lon, sizes, LON, True)
-    merged = unpack_cells(near, cross, onward)
+    merged = unpack_cells(near, cross, onward, cell_gain)
     merged, lat, both, lon = lax.optimization_barrier((merged, lat, both, lon))
     grads = unpack_tokens(own, lat, lon, both)
     return merged.transpose(2, 0, 1, 3), grads.transpose(2, 0, 1, 3)

time: 52.5 us -> 48.5 us (0.924)
  waiting for transfers between devices: 12.7 us -> 8.94 us
  starting transfers between devices: 18.3 us -> 17.1 us
  Pallas kernels: 20.5 us -> 21.5 us
    ppermute x12, waiting for transfers between devices: 12.7 us -> 8.94 us  [send(): return lax.ppermute(block, ('lon', 'lat', 'lev'), pairs)]
    ppermute x12, starting transfers between devices: 18.3 us -> 17.1 us  [send(): return lax.ppermute(block, ('lon', 'lat', 'lev'), pairs)]
    pallas_call x2 -> x3, Pallas kernels: 3.34 us -> 3.95 us  [the longest x2 3.43 us: backward(): pl.pallas_call(functools.partial(backward_kernel, half), out_shape=shape(...]
  transfers between devices with their start and end apart: 12 -> 12, of which waited for: 6 -> 5; matrix products, arithmetic and copies ran while one was open for 0% -> 0% of each run, Pallas kernels for 32% -> 38%
where the time goes in v5:
time: 48.5 us; the launch traced here: 48.3 us
  Pallas kernels  21.5 us (44%)
  starting transfers between devices  17.1 us (35%)
  waiting for transfers between devices  8.94 us (18%)
  between operations  0.79 us (2%)
    ppermute x12, starting transfers between devices, send(): return lax.ppermute(block, ('lon', 'lat', 'lev'), pairs)  17.1 us
    ppermute x12, waiting for transfers between devices, send(): return lax.ppermute(block, ('lon', 'lat', 'lev'), pairs)  8.94 us
    pallas_call x1, Pallas kernels, window_bias(): pl.pallas_call(bias_kernel, out_shape=[shape((heads * WIN, 128), f32)] *...  8.24 us
    pallas_call x2, Pallas kernels, backward(): pl.pallas_call(functools.partial(backward_kernel, half), out_shape=shape(...  3.43 us
    pallas_call x1, Pallas kernels, forward(): pl.pallas_call(forward_kernel, out_shape=[shape((HEADS * WIN, WIN), bf16)...  3.35 us
    pallas_call x1, Pallas kernels, finish(): pl.pallas_call(finish_kernel, out_shape=[shape((QUAD, width), bf16)] * 4,...  1.53 us
    pallas_call x1, Pallas kernels, pack_pieces(): pl.pallas_call(pack_kernel, out_shape=[piece, double, piece, double, piec...  1.3 us
    pallas_call x1, Pallas kernels, unpack_cells(): pl.pallas_call(cell_kernel, out_shape=shape((HALF_LAT, PAIRS, 2 * LEVELS,...  1.21 us
  transfers between devices with their start and end apart: 12, of which 5 were waited for; matrix products, arithmetic and copies ran while one was open for 0% of the time, Pallas kernels for 38%

profile of v5, /device:TPU:0, one launch (start us, length us, event | category | flops | bytes accessed | tf_op | source)
XLA Modules:
  0.0 48.3 jit_solution(17162879080413669379)
XLA Ops:
  0.6 1.3 %pack.1 = (bf16[36,768]{1,0:T(8,128)(2,1)S(1)}, bf16[72,768]{1,0:T(8,128)(2,1)S(1)}, bf16[36,768]{1,0:T(8,128)(2,1)S(1)}, bf16[72,768]{1,0:T(8,128)(2,1)S(1)}, b...) custom-call(bf16[6,12,2,768]{3,2,1,0:T(2,128)(2,1)} %bitcast.8, ...), custom_call_target="tpu_custom_call" | custom-call | tf_op jit(solution)/shard_map/pack/pallas_call | solution.py:137
  1.9 4.1 %collective-permute-start.1 = (bf16[36,768]{1,0:T(8,128)(2,1)S(1)}, bf16[36,768]{1,0:T(8,128)(2,1)S(1)}, u32[]{:S(2)}, u32[]{:S(2)}) collective-permute-start(bf16[36,768]{1,0:T(8,128)(2,1)S(1)} %get-tuple-element.36), channel_id=1, source_target_pairs={{0,2},{1,31},{2,0},{3,29},{4,6},{5,3},{6,4},{7,1},{8,10},{9,7},{10... | collective-permute-start | bytes 165896 | tf_op jit(solution)/shard_map/ppermute | solution.py:678
  6.0 3.2 %collective-permute-start.3 = (bf16[36,768]{1,0:T(8,128)(2,1)S(1)}, bf16[36,768]{1,0:T(8,128)(2,1)S(1)}, u32[]{:S(2)}, u32[]{:S(2)}) collective-permute-start(bf16[36,768]{1,0:T(8,128)(2,1)S(1)} %get-tuple-element.42), channel_id=1, source_target_pairs={{0,29},{1,0},{2,31},{3,2},{4,1},{5,4},{6,3},{7,6},{8,5},{9,8},{10,... | collective-permute-start | bytes 165896 | tf_op jit(solution)/shard_map/ppermute | solution.py:678
  9.2 0.0 collective-permute-start.4
  9.2 1.9 %collective-permute-start = (bf16[72,768]{1,0:T(8,128)(2,1)S(1)}, bf16[72,768]{1,0:T(8,128)(2,1)S(1)}, u32[]{:S(2)}, u32[]{:S(2)}) collective-permute-start(bf16[72,768]{1,0:T(8,128)(2,1)S(1)} %get-tuple-element.35), channel_id=1, source_target_pairs={{0,30},{1,3},{2,28},{3,1},{4,2},{5,7},{6,0},{7,5},{8,6},{9,11},{10... | collective-permute-start | bytes 331784 | tf_op jit(solution)/shard_map/ppermute | solution.py:678
  11.1 0.0 copy-start.1
  11.1 0.0 copy-start.2
  11.1 0.0 collective-permute-start.2
  11.1 0.0 copy-start
  11.1 8.2 %bias.1 = (f32[3456,128]{1,0:T(8,128)S(1)}, f32[3456,128]{1,0:T(8,128)S(1)}) custom-call(f32[1,1,24,3312]{3,2,1,0:T(8,128)} %table_at.1, s32[144,144]{1,0:T(8,128)} %index_at.1, s32[6]{0:T(128)} %labels_at.1, s32[96]{0:T(128)} %valid_at.1), custom_call_target="tpu_custom_call" | custom-call | flops 10000000000 | bytes 20000000 | tf_op jit(solution)/shard_map/bias/pallas_call | solution.py:278
  19.4 0.0 collective-permute-done.1.second
  19.4 0.0 collective-permute-done.first
  19.4 0.0 collective-permute-done.2.third
  19.4 0.0 copy-done.1
  19.4 0.0 copy-done.2
  19.4 0.0 copy-done
  19.4 0.0 copy-start.3
  19.5 3.3 %forward.1 = (bf16[3456,144]{1,0:T(8,128)(2,1)S(1)}, bf16[144,2304]{1,0:T(8,128)(2,1)S(1)}, bf16[768,144]{1,0:T(8,128)(2,1)S(1)}, bf16[144,768]{1,0:T(8,128)(2,1)S(1)}, bf16[144,768]{1,0:T(8,128)(2,1)S(1)}) custom-call(bf16[36,768]{1,0:T(8,128)(2,1)S(1)} %get-tuple-element.34.own, bf16[72,768]{1,0:T(8,128)(2,1)S(1)} %collective-permute-done.first, ...), custom_call_target="tpu_custom_call" | custom-call | flops 1000000000 | bytes 20000000 | tf_op jit(solution)/shard_map/forward/pallas_call | solution.py:368
  22.8 0.0 collective-permute-done.3.fourth
  22.8 0.0 collective-permute-done.4.fifth
  22.8 0.0 copy-done.3
  22.8 1.2 %moments.1 = (f32[144,768]{1,0:T(8,128)S(1)}, f32[144,128]{1,0:T(8,128)S(1)}, f32[24,128]{1,0:T(8,128)S(1)}, bf16[72,768]{1,0:T(8,128)(2,1)S(1)}, bf16[72,768]{1,0:T(8,128)(2,1)S(1)}) custom-call(bf16[144,768]{1,0:T(8,128)(2,1)S(1)} %get-tuple-element.40.residual, bf16[36,768]{1,0:T(8,128)(2,1)S(1)} %get-tuple-element.41.kept, ...), custom_call_target="tpu_custom_call" | custom-call | flops 100000000 | bytes 1000000 | tf_op jit(solution)/shard_map/moments/pallas_call | solution.py:469
  24.0 1.3 %collective-permute-start.5 = (f32[24,128]{1,0:T(8,128)S(1)}, f32[24,128]{1,0:T(8,128)S(1)}, u32[]{:S(2)}, u32[]{:S(2)}) collective-permute-start(f32[24,128]{1,0:T(8,128)S(1)} %get-tuple-element.46), channel_id=1, source_target_pairs={{0,2},{1,3},{2,0},{3,1},{4,6},{5,7},{6,4},{7,5},{8,10},{9,11},{10,... | collective-permute-start | bytes 36872 | tf_op jit(solution)/shard_map/ppermute | solution.py:678
  25.3 2.1 %collective-permute-start.6 = (bf16[72,768]{1,0:T(8,128)(2,1)S(1)}, bf16[72,768]{1,0:T(8,128)(2,1)S(1)}, u32[]{:S(2)}, u32[]{:S(2)}) collective-permute-start(bf16[72,768]{1,0:T(8,128)(2,1)S(1)} %get-tuple-element.50), channel_id=1, source_target_pairs={{28,0},{1,1},{30,2},{3,3},{0,4},{5,5},{2,6},{7,7},{4,8},{9,9},{6,1... | collective-permute-start | bytes 331784 | tf_op jit(solution)/shard_map/ppermute | solution.py:678
  27.4 0.2 collective-permute-start.7
  27.7 1.0 %collective-permute-done.5.before.after = f32[24,128]{1,0:T(8,128)S(1)} collective-permute-done((f32[24,128]{1,0:T(8,128)S(1)}, f32[24,128]{1,0:T(8,128)S(1)}, u32[]{:S(2)}, u32[]{:S(2)}) %collective-permute-start.5) | collective-permute-done | bytes 12320 | tf_op jit(solution)/shard_map/ppermute | solution.py:678
  28.7 0.5 %merge.1.grad = bf16[144,768]{1,0:T(8,128)(2,1)S(1)} custom-call(bf16[144,768]{1,0:T(8,128)(2,1)S(1)} %get-tuple-element.40.residual, f32[144,768]{1,0:T(8,128)S(1)} %get-tuple-element.44.scaled, f32[144,128]{1,0:T(8,128)S(1)} %get-tuple-element.45.moments, f32[24,128]{1,0:T(8,128)S(1)} %collective-permute-done.5.before.after, ...), custom_call_target="tpu_custom_call" | custom-call | flops 100000000 | bytes 1000000 | tf_op jit(solution)/shard_map/merge/pallas_call | solution.py:507
  29.2 1.7 %backward.2.first = bf16[144,1152]{1,0:T(8,128)(2,1)S(1)} custom-call(bf16[144,768]{1,0:T(8,128)(2,1)S(1)} %merge.1.grad, bf16[3456,144]{1,0:T(8,128)(2,1)S(1)} %get-tuple-element.47.weights, bf16[144,2304]{1,0:T(8,128)(2,1)S(1)} %get-tuple-element.48.triple, bf16[768,144]{1,0:T(8,128)(2,1)S(1)} %get-tuple-element.49.keys_t, bf16[768,768]{1,0:T(8,128)(2,1)S(1)} %copy-done.1), custom_call_target="tpu_custom_call" | custom-call | flops 10000000000 | bytes 20000000 | tf_op jit(solution)/shard_map/backward/pallas_call | solution.py:551
  30.9 1.4 %collective-permute-done.6.near = bf16[72,768]{1,0:T(8,128)(2,1)S(1)} collective-permute-done((bf16[72,768]{1,0:T(8,128)(2,1)S(1)}, bf16[72,768]{1,0:T(8,128)(2,1)S(1)}, u32[]{:S(2)}, u32[]{:S(2)}) %collective-permute-start.6) | collective-permute-done | bytes 110624 | tf_op jit(solution)/shard_map/ppermute | solution.py:678
  32.3 1.9 %collective-permute-done.7.cross = bf16[72,768]{1,0:T(8,128)(2,1)S(1)} collective-permute-done((bf16[72,768]{1,0:T(8,128)(2,1)S(1)}, bf16[72,768]{1,0:T(8,128)(2,1)S(1)}, u32[]{:S(2)}, u32[]{:S(2)}) %collective-permute-start.7) | collective-permute-done | bytes 110624 | tf_op jit(solution)/shard_map/ppermute | solution.py:678
  34.2 1.8 %collective-permute-start.8 = (bf16[72,768]{1,0:T(8,128)(2,1)S(1)}, bf16[72,768]{1,0:T(8,128)(2,1)S(1)}, u32[]{:S(2)}, u32[]{:S(2)}) collective-permute-start(bf16[72,768]{1,0:T(8,128)(2,1)S(1)} %relay.1), channel_id=1, source_target_pairs={{2,0},{3,1},{0,2},{1,3},{6,4},{7,5},{4,6},{5,7},{10,8},{11,9},{8,1... | collective-permute-start | bytes 331784 | tf_op jit(solution)/shard_map/ppermute | solution.py:678
  36.0 1.7 %backward.3.second = bf16[144,1152]{1,0:T(8,128)(2,1)S(1)} custom-call(bf16[144,768]{1,0:T(8,128)(2,1)S(1)} %merge.1.grad, bf16[3456,144]{1,0:T(8,128)(2,1)S(1)} %get-tuple-element.47.weights, bf16[144,2304]{1,0:T(8,128)(2,1)S(1)} %get-tuple-element.48.triple, bf16[768,144]{1,0:T(8,128)(2,1)S(1)} %get-tuple-element.49.keys_t, bf16[768,768]{1,0:T(8,128)(2,1)S(1)} %copy-done.1), custom_call_target="tpu_custom_call" | custom-call | flops 10000000000 | bytes 20000000 | tf_op jit(solution)/shard_map/backward/pallas_call | solution.py:551
  37.7 1.5 %finish.1 = (bf16[36,768]{1,0:T(8,128)(2,1)S(1)}, bf16[36,768]{1,0:T(8,128)(2,1)S(1)}, bf16[36,768]{1,0:T(8,128)(2,1)S(1)}, bf16[36,768]{1,0:T(8,128)(2,1)S(1)}) custom-call(bf16[144,768]{1,0:T(8,128)(2,1)S(1)} %merge.1.grad, bf16[144,1152]{1,0:T(8,128)(2,1)S(1)} %backward.2.first, bf16[144,1152]{1,0:T(8,128)(2,1)S(1)} %backward.3.second, ...), custom_call_target="tpu_custom_call" | custom-call | flops 10000000 | bytes 1000000 | tf_op jit(solution)/shard_map/finish/pallas_call | solution.py:574
  39.3 1.3 %collective-permute-start.9 = (bf16[36,768]{1,0:T(8,128)(2,1)S(1)}, bf16[36,768]{1,0:T(8,128)(2,1)S(1)}, u32[]{:S(2)}, u32[]{:S(2)}) collective-permute-start(bf16[36,768]{1,0:T(8,128)(2,1)S(1)} %get-tuple-element.58), channel_id=1, source_target_pairs={{2,0},{3,1},{0,2},{1,3},{6,4},{7,5},{4,6},{5,7},{10,8},{11,9},{8,1... | collective-permute-start | bytes 165896 | tf_op jit(solution)/shard_map/ppermute | solution.py:678
  40.5 0.2 collective-permute-start.10
  40.7 1.0 %collective-permute-start.11 = (bf16[36,768]{1,0:T(8,128)(2,1)S(1)}, bf16[36,768]{1,0:T(8,128)(2,1)S(1)}, u32[]{:S(2)}, u32[]{:S(2)}) collective-permute-start(bf16[36,768]{1,0:T(8,128)(2,1)S(1)} %get-tuple-element.60), channel_id=1, source_target_pairs={{28,0},{29,1},{30,2},{31,3},{0,4},{1,5},{2,6},{3,7},{4,8},{5,9},{6... | collective-permute-start | bytes 165896 | tf_op jit(solution)/shard_map/ppermute | solution.py:678
  41.7 0.0 collective-permute-done.8.onward
  41.8 1.2 %unpack_cells.1 = bf16[3,3,4,3072]{3,2,1,0:T(4,128)(2,1)} custom-call(bf16[72,768]{1,0:T(8,128)(2,1)S(1)} %collective-permute-done.6.near, bf16[72,768]{1,0:T(8,128)(2,1)S(1)} %collective-permute-done.7.cross, bf16[72,768]{1,0:T(8,128)(2,1)S(1)} %collective-permute-done.8.onward, f32[1,3072]{1,0:T(1,128)S(1)} %bitcast.6), custom_call_target="tpu_custom_call" | custom-call | flops 1000000000 | bytes 1000000 | tf_op jit(solution)/shard_map/unpack_cells/pallas_call | solution.py:651
  43.0 3.4 %collective-permute-done.9.lat = bf16[36,768]{1,0:T(8,128)(2,1)S(1)} collective-permute-done((bf16[36,768]{1,0:T(8,128)(2,1)S(1)}, bf16[36,768]{1,0:T(8,128)(2,1)S(1)}, u32[]{:S(2)}, u32[]{:S(2)}) %collective-permute-start.9) | collective-permute-done | bytes 55328 | tf_op jit(solution)/shard_map/ppermute | solution.py:678
  46.4 1.2 %collective-permute-done.10.both = bf16[36,768]{1,0:T(8,128)(2,1)S(1)} collective-permute-done((bf16[36,768]{1,0:T(8,128)(2,1)S(1)}, bf16[36,768]{1,0:T(8,128)(2,1)S(1)}, u32[]{:S(2)}, u32[]{:S(2)}) %collective-permute-start.10) | collective-permute-done | bytes 55328 | tf_op jit(solution)/shard_map/ppermute | solution.py:678
  47.6 0.0 collective-permute-done.11.lon
  47.6 0.7 %unpack_tokens.1 = bf16[6,12,2,768]{3,2,1,0:T(2,128)(2,1)} custom-call(bf16[36,768]{1,0:T(8,128)(2,1)S(1)} %get-tuple-element.62.own, bf16[36,768]{1,0:T(8,128)(2,1)S(1)} %collective-permute-done.9.lat, bf16[36,768]{1,0:T(8,128)(2,1)S(1)} %collective-permute-done.11.lon, bf16[36,768]{1,0:T(8,128)(2,1)S(1)} %collective-permute-done.10.both), custom_call_target="tpu_custom_call" | custom-call | tf_op jit(solution)/shard_map/unpack_tokens/pallas_call | solution.py:608
  (1 shorter events, 0.0 us)
Async XLA Ops:
  1.9 17.4 %collective-permute-start.1 = (bf16[36,768]{1,0:T(8,128)(2,1)S(1)}, bf16[36,768]{1,0:T(8,128)(2,1)S(1)}, u32[]{:S(2)}, u32[]{:S(2)}) collective-permute-start(bf16[36,768]{1,0:T(8,128)(2,1)S(1)} %get-tuple-element.36), channel_id=1, source_target_pairs={{0,2},{1,31},{2,0},{3,29},{4,6},{5,3},{6,4},{7,1},{8,10},{9,7},{10... | collective-permute-start | bytes 165896 | tf_op jit(solution)/shard_map/ppermute | solution.py:678
  6.0 16.8 %collective-permute-start.3 = (bf16[36,768]{1,0:T(8,128)(2,1)S(1)}, bf16[36,768]{1,0:T(8,128)(2,1)S(1)}, u32[]{:S(2)}, u32[]{:S(2)}) collective-permute-start(bf16[36,768]{1,0:T(8,128)(2,1)S(1)} %get-tuple-element.42), channel_id=1, source_target_pairs={{0,29},{1,0},{2,31},{3,2},{4,1},{5,4},{6,3},{7,6},{8,5},{9,8},{10,... | collective-permute-start | bytes 165896 | tf_op jit(solution)/shard_map/ppermute | solution.py:678
  9.2 13.6 %collective-permute-start.4 = (bf16[36,768]{1,0:T(8,128)(2,1)S(1)}, bf16[36,768]{1,0:T(8,128)(2,1)S(1)}, u32[]{:S(2)}, u32[]{:S(2)}) collective-permute-start(bf16[36,768]{1,0:T(8,128)(2,1)S(1)} %get-tuple-element.43), channel_id=1, source_target_pairs={{0,31},{1,2},{2,29},{3,0},{4,3},{5,6},{6,1},{7,4},{8,7},{9,10},{10... | collective-permute-start | bytes 165896 | tf_op jit(solution)/shard_map/ppermute | solution.py:678
  9.2 10.2 %collective-permute-start = (bf16[72,768]{1,0:T(8,128)(2,1)S(1)}, bf16[72,768]{1,0:T(8,128)(2,1)S(1)}, u32[]{:S(2)}, u32[]{:S(2)}) collective-permute-start(bf16[72,768]{1,0:T(8,128)(2,1)S(1)} %get-tuple-element.35), channel_id=1, source_target_pairs={{0,30},{1,3},{2,28},{3,1},{4,2},{5,7},{6,0},{7,5},{8,6},{9,11},{10... | collective-permute-start | bytes 331784 | tf_op jit(solution)/shard_map/ppermute | solution.py:678
  11.1 8.3 %copy-start.1 = (bf16[768,768]{1,0:T(8,128)(2,1)S(1)}, bf16[768,768]{1,0:T(8,128)(2,1)}, u32[]{:S(2)}) copy-start(bf16[768,768]{1,0:T(8,128)(2,1)} %output.5) | copy-start | bytes 3538948
  11.1 8.3 %copy-start.2 = (f32[768]{0:T(1024)S(1)}, f32[768]{0:T(1024)}, u32[]{:S(2)}) copy-start(f32[768]{0:T(1024)} %gain.3) | copy-start | bytes 9220
  11.1 8.3 %collective-permute-start.2 = (bf16[72,768]{1,0:T(8,128)(2,1)S(1)}, bf16[72,768]{1,0:T(8,128)(2,1)S(1)}, u32[]{:S(2)}, u32[]{:S(2)}) collective-permute-start(bf16[72,768]{1,0:T(8,128)(2,1)S(1)} %get-tuple-element.37), channel_id=1, source_target_pairs={{0,28},{1,29},{2,30},{3,31},{4,0},{5,1},{6,2},{7,3},{8,4},{9,5},{1... | collective-permute-start | bytes 331784 | tf_op jit(solution)/shard_map/ppermute | solution.py:678
  11.1 8.3 %copy-start = (bf16[768,2304]{1,0:T(8,128)(2,1)S(1)}, bf16[768,2304]{1,0:T(8,128)(2,1)}, u32[]{:S(2)}) copy-start(bf16[768,2304]{1,0:T(8,128)(2,1)} %packed.3) | copy-start | bytes 10616836
  19.4 3.4 %copy-start.3 = (f32[3072]{0:T(1024)S(1)}, f32[3072]{0:T(1024)}, u32[]{:S(2)}) copy-start(f32[3072]{0:T(1024)} %param.14) | copy-start | bytes 36868
  24.0 4.6 %collective-permute-start.5 = (f32[24,128]{1,0:T(8,128)S(1)}, f32[24,128]{1,0:T(8,128)S(1)}, u32[]{:S(2)}, u32[]{:S(2)}) collective-permute-start(f32[24,128]{1,0:T(8,128)S(1)} %get-tuple-element.46), channel_id=1, source_target_pairs={{0,2},{1,3},{2,0},{3,1},{4,6},{5,7},{6,4},{7,5},{8,10},{9,11},{10,... | collective-permute-start | bytes 36872 | tf_op jit(solution)/shard_map/ppermute | solution.py:678
  25.3 7.0 %collective-permute-start.6 = (bf16[72,768]{1,0:T(8,128)(2,1)S(1)}, bf16[72,768]{1,0:T(8,128)(2,1)S(1)}, u32[]{:S(2)}, u32[]{:S(2)}) collective-permute-start(bf16[72,768]{1,0:T(8,128)(2,1)S(1)} %get-tuple-element.50), channel_id=1, source_target_pairs={{28,0},{1,1},{30,2},{3,3},{0,4},{5,5},{2,6},{7,7},{4,8},{9,9},{6,1... | collective-permute-start | bytes 331784 | tf_op jit(solution)/shard_map/ppermute | solution.py:678
  27.4 6.8 %collective-permute-start.7 = (bf16[72,768]{1,0:T(8,128)(2,1)S(1)}, bf16[72,768]{1,0:T(8,128)(2,1)S(1)}, u32[]{:S(2)}, u32[]{:S(2)}) collective-permute-start(bf16[72,768]{1,0:T(8,128)(2,1)S(1)} %get-tuple-element.51), channel_id=1, source_target_pairs={{29,0},{0,1},{31,2},{2,3},{1,4},{4,5},{3,6},{6,7},{5,8},{8,9},{7,1... | collective-permute-start | bytes 331784 | tf_op jit(solution)/shard_map/ppermute | solution.py:678
  34.2 7.5 %collective-permute-start.8 = (bf16[72,768]{1,0:T(8,128)(2,1)S(1)}, bf16[72,768]{1,0:T(8,128)(2,1)S(1)}, u32[]{:S(2)}, u32[]{:S(2)}) collective-permute-start(bf16[72,768]{1,0:T(8,128)(2,1)S(1)} %relay.1), channel_id=1, source_target_pairs={{2,0},{3,1},{0,2},{1,3},{6,4},{7,5},{4,6},{5,7},{10,8},{11,9},{8,1... | collective-permute-start | bytes 331784 | tf_op jit(solution)/shard_map/ppermute | solution.py:678
  39.3 7.1 %collective-permute-start.9 = (bf16[36,768]{1,0:T(8,128)(2,1)S(1)}, bf16[36,768]{1,0:T(8,128)(2,1)S(1)}, u32[]{:S(2)}, u32[]{:S(2)}) collective-permute-start(bf16[36,768]{1,0:T(8,128)(2,1)S(1)} %get-tuple-element.58), channel_id=1, source_target_pairs={{2,0},{3,1},{0,2},{1,3},{6,4},{7,5},{4,6},{5,7},{10,8},{11,9},{8,1... | collective-permute-start | bytes 165896 | tf_op jit(solution)/shard_map/ppermute | solution.py:678
  40.5 7.1 %collective-permute-start.10 = (bf16[36,768]{1,0:T(8,128)(2,1)S(1)}, bf16[36,768]{1,0:T(8,128)(2,1)S(1)}, u32[]{:S(2)}, u32[]{:S(2)}) collective-permute-start(bf16[36,768]{1,0:T(8,128)(2,1)S(1)} %get-tuple-element.59), channel_id=1, source_target_pairs={{30,0},{31,1},{28,2},{29,3},{2,4},{3,5},{0,6},{1,7},{6,8},{7,9},{4... | collective-permute-start | bytes 165896 | tf_op jit(solution)/shard_map/ppermute | solution.py:678
  40.7 6.9 %collective-permute-start.11 = (bf16[36,768]{1,0:T(8,128)(2,1)S(1)}, bf16[36,768]{1,0:T(8,128)(2,1)S(1)}, u32[]{:S(2)}, u32[]{:S(2)}) collective-permute-start(bf16[36,768]{1,0:T(8,128)(2,1)S(1)} %get-tuple-element.60), channel_id=1, source_target_pairs={{28,0},{29,1},{30,2},{31,3},{0,4},{1,5},{2,6},{3,7},{4,8},{5,9},{6... | collective-permute-start | bytes 165896 | tf_op jit(solution)/shard_map/ppermute | solution.py:678

commit v6 on v5

--- a/solution.py
+++ b/solution.py
@@ -96,10 +96,11 @@
 
 
 def pack_kernel(
-    tokens_at, grad_at, own, first, second, third, kept, fourth, fifth, tokens, grad, rows, cells, done
+    tokens_at, grad_at, table_at, index_at, own, first, second, third, kept, table, index,
+    tokens, grad, rows, cells, done,
 ):
     width = tokens.shape[-1]
-    copies = start_copies(done, (tokens_at, tokens), (grad_at, grad))
+    copies = start_copies(done, (tokens_at, tokens), (grad_at, grad), (index_at, index), (table_at.at[0, 0], table))
     copies[0].wait()
     for line in range(WLAT):
         for column in range(WLON):
@@ -123,65 +124,46 @@
     lat, lon, both = quadrant(data, 1), quadrant(data, 2), quadrant(data, 3)
     here, below = quadrant(grads, 0), quadrant(grads, 1)
     own[...] = quadrant(data, 0).astype(bf16)
-    first[...] = jnp.concatenate((jnp.where(upper, lat, both), below), axis=0).astype(bf16)
+    more = quadrant(grads, 3)
+    sides = jnp.concatenate((here, quadrant(grads, 2)), axis=0)
+    first[...] = jnp.concatenate((jnp.where(upper, lat, both), below, more), axis=0).astype(bf16)
     second[...] = jnp.where(upper, both, lat).astype(bf16)
-    third[...] = jnp.concatenate((lon, here), axis=0).astype(bf16)
-    kept[...] = here.astype(bf16)
-    fourth[...] = quadrant(grads, 2).astype(bf16)
-    fifth[...] = quadrant(grads, 3).astype(bf16)
-
-
-def pack_pieces(tokens, grad):
+    third[...] = jnp.concatenate((lon, sides), axis=0).astype(bf16)
+    kept[...] = sides.astype(bf16)
+    copies[2].wait()
+    copies[3].wait()
+
+
+def pack_pieces(tokens, grad, table, index):
     width = tokens.shape[-1]
-    piece, double = shape((QUAD, width), bf16), shape((2 * QUAD, width), bf16)
+    piece, double, triple = (shape((n * QUAD, width), bf16) for n in (1, 2, 3))
     return pl.pallas_call(
         pack_kernel,
-        out_shape=[piece, double, piece, double, piece, piece, piece],
-        in_specs=[pl.BlockSpec(memory_space=pltpu.MemorySpace.HBM)] * 2,
+        out_shape=[piece, triple, piece, triple, double, shape(table.shape[2:], f32), shape(index.shape, jnp.int32)],
+        in_specs=[pl.BlockSpec(memory_space=pltpu.MemorySpace.HBM)] * 4,
         scratch_shapes=[
             pltpu.VMEM(tokens.shape, bf16),
             pltpu.VMEM(grad.shape, bf16),
             pltpu.VMEM((WIN, width), f32),
             pltpu.VMEM((WIN, width), f32),
-            pltpu.SemaphoreType.DMA((2,)),
+            pltpu.SemaphoreType.DMA((4,)),
         ],
         compiler_params=params(),
         name="pack",
-    )(*in_hbm(tokens, grad))
+    )(*in_hbm(tokens, grad, table, index))
 
 
 def bias_kernel(
-    table_at, index_at, labels_at, valid_at, main, tail,
-    table, index, labels, valid, split, fine, high, low, fine_high, fine_low, rest_rows, mask, mask_tail, done,
+    table, index, labels_at, valid_at, main, tail,
+    labels, valid, split, fine, high, low, fine_high, fine_low, rest_rows, mask, mask_tail, done,
 ):
-    copies = start_copies(
-        done, (table_at.at[0, 0], table), (index_at, index), (labels_at, labels), (valid_at, valid)
-    )
+    copies = start_copies(done, (labels_at, labels), (valid_at, valid))
     row_k, column_k, level_k, _ = token_places((WIN, 1), 0)
     row_q, _, _, _ = token_places((1, WIN), 1)
     natural = (level_k * WLAT + row_k) * WLON + column_k
     columns = lax.broadcasted_iota(jnp.int32, (WIN, WIN), 1)
     rows = lax.broadcasted_iota(jnp.int32, (WIN, WIN), 0)
     permute = jnp.where(natural == columns, 1.0, 0.0).astype(bf16)
-    for copy in copies:
-        copy.wait()
-
-    label_q, label_k = jnp.zeros_like(row_q), jnp.zeros_like(row_k)
-    for r in range(WLAT):
-        label_q = jnp.where(row_q == r, labels[r], label_q)
-        label_k = jnp.where(row_k == r, labels[r], label_k)
-    valid_k = jnp.zeros_like(column_k)
-    start = lax.axis_index("lon") * WLON + HALF_LON
-    total = valid.shape[0]
-    for c in range(WLON):
-        at = start + c
-        at = jnp.where(at >= total, at - total, at)
-        valid_k = jnp.where(column_k == c, valid[at], valid_k)
-    seen = (label_k == label_q) & ((valid_k > 0) | (rows == columns))
-    added = jnp.where(seen, 0.0, BLOCKED).astype(f32)
-    mask[...] = added[:, :128]
-    mask_tail[...] = jnp.concatenate((added[:, 128:], jnp.zeros((WIN, 128 - TAIL), f32)), axis=1)
-
     heads, entries = table.shape
     gathered = 8
     wide = heads - gathered
@@ -223,6 +205,25 @@
     far = lower >= 128.0
     fine_high[...] = (2.0 * upper + jnp.where(far, 1.0, 0.0)).astype(jnp.int32)
     fine_low[...] = jnp.where(far, lower - 128.0, lower).astype(jnp.int32)
+    for copy in copies:
+        copy.wait()
+
+    label_q, label_k = jnp.zeros_like(row_q), jnp.zeros_like(row_k)
+    for r in range(WLAT):
+        label_q = jnp.where(row_q == r, labels[r], label_q)
+        label_k = jnp.where(row_k == r, labels[r], label_k)
+    valid_k = jnp.zeros_like(column_k)
+    start = lax.axis_index("lon") * WLON + HALF_LON
+    total = valid.shape[0]
+    for c in range(WLON):
+        at = start + c
+        at = jnp.where(at >= total, at - total, at)
+        valid_k = jnp.where(column_k == c, valid[at], valid_k)
+    seen = (label_k == label_q) & ((valid_k > 0) | (rows == columns))
+    added = jnp.where(seen, 0.0, BLOCKED).astype(f32)
+    mask[...] = added[:, :128]
+    mask_tail[...] = jnp.concatenate((added[:, 128:], jnp.zeros((WIN, 128 - TAIL), f32)), axis=1)
+
     depth = lax.broadcasted_iota(jnp.int32, (256, 128), 0).astype(f32).astype(bf16)
     one, zero = jnp.ones((), bf16), jnp.zeros((), bf16)
 
@@ -272,16 +273,15 @@
 
 
 def window_bias(table, index, labels, valid):
-    heads, entries = table.shape[-2:]
+    heads, entries = table.shape
     whole = (entries + 255) // 256
     index_rows = WIN + TAIL_GROUPS
     return pl.pallas_call(
         bias_kernel,
         out_shape=[shape((heads * WIN, 128), f32)] * 2,
-        in_specs=[pl.BlockSpec(memory_space=pltpu.MemorySpace.HBM)] * 4,
+        in_specs=[pl.BlockSpec(memory_space=pltpu.MemorySpace.VMEM)] * 2
+        + [pl.BlockSpec(memory_space=pltpu.MemorySpace.HBM)] * 2,
         scratch_shapes=[
-            pltpu.VMEM((heads, entries), f32),
-            pltpu.VMEM(index.shape, jnp.int32),
             pltpu.SMEM(labels.shape, jnp.int32),
             pltpu.SMEM(valid.shape, jnp.int32),
             pltpu.VMEM((2 * whole * (heads - 8), 256), f32),
@@ -293,12 +293,12 @@
             pltpu.VMEM((WIN, 128), f32),
             pltpu.VMEM((WIN, 128), f32),
             pltpu.VMEM((WIN, 128), f32),
-            pltpu.SemaphoreType.DMA((4,)),
+            pltpu.SemaphoreType.DMA((2,)),
         ],
         compiler_params=params(),
         cost_estimate=cost(10**10, 2 * 10**7),
         name="bias",
-    )(*in_hbm(table, index, labels, valid))
+    )(table, index, *in_hbm(labels, valid))
 
 
 def row_mean(values):
@@ -380,7 +380,7 @@
             pltpu.VMEM((width, WIN), f32),
         ],
         compiler_params=params(),
-        cost_estimate=cost(10**9, 2 * 10**7),
+        cost_estimate=cost(10**10, 2 * 10**7),
         name="forward",
     )(*pieces, packed, output, gain, main, tail)
 
@@ -424,11 +424,12 @@
     return out
 
 
-def moments_kernel(residual, kept, first, third, fourth, fifth, gain, scaled, moments, sent, near, over, factors):
+def moments_kernel(residual, kept, first, third, hopped, gain, scaled, moments, sent, near, over, factors):
     width = residual.shape[-1]
     upper = lax.axis_index("lev") == 1
-    own, a, b = kept[...].astype(f32), fourth[...].astype(f32), fifth[...].astype(f32)
-    below, right = first[...].astype(f32)[QUAD:], third[...].astype(f32)[QUAD:]
+    own, hop = kept[...].astype(f32)[:QUAD], hopped[...].astype(f32)
+    a, b = hop[:QUAD], hop[QUAD:]
+    below, right = first[...].astype(f32)[QUAD : 2 * QUAD], third[...].astype(f32)[QUAD : 2 * QUAD]
     gain_rows(gain, factors)
     for quad, part in enumerate((
         jnp.where(upper, own, a),
@@ -580,6 +581,21 @@
     )(grad, first, second, tokens, packed, gain)
 
 
+def hop_kernel(kept, first, third, out):
+    upper = lax.axis_index("lev") == 1
+    here = jnp.where(upper, kept[...].astype(f32)[QUAD:], third[...].astype(f32)[2 * QUAD :])
+    out[...] = jnp.concatenate((here, first[...].astype(f32)[2 * QUAD :]), axis=0).astype(bf16)
+
+
+def hop(kept, first, third):
+    return pl.pallas_call(
+        hop_kernel,
+        out_shape=shape(kept.shape, bf16),
+        compiler_params=params(),
+        name="hop",
+    )(kept, first, third)
+
+
 def relay_kernel(near, cross, out):
     out[...] = jnp.concatenate((near[...].astype(f32)[QUAD:], cross[...].astype(f32)[QUAD:]), axis=0).astype(bf16)
 
@@ -682,7 +698,7 @@
 SECOND = lambda i, a, k: (i - k, a - 1, k)
 THIRD = lambda i, a, k: (i - 1, a, k)
 FOURTH = lambda i, a, k: (i - (1 - k), a, 1 - k)
-FIFTH = lambda i, a, k: (i - (1 - k), a - 1, 1 - k)
+LEV = lambda i, a, k: (i, a, 1 - k)
 LAT = lambda i, a, k: (i, a - 1, k)
 LON = lambda i, a, k: (i - 1, a, k)
 BOTH = lambda i, a, k: (i - 1, a - 1, k)
@@ -702,20 +718,20 @@
     column_valid,
     merged_grad,
 ):
-    own, first, second, third, kept, fourth, fifth = pack_pieces(
-        tokens.transpose(1, 2, 0, 3), merged_grad.transpose(1, 2, 0, 3)
+    own, first, second, third, kept, table, index = pack_pieces(
+        tokens.transpose(1, 2, 0, 3), merged_grad.transpose(1, 2, 0, 3), bias_table, bias_index
     )
     first = send(first, sizes, FIRST)
     second = send(second, sizes, SECOND)
     third = send(third, sizes, THIRD)
-    fourth = send(fourth, sizes, FOURTH)
-    fifth = send(fifth, sizes, FIFTH)
-    main, tail = window_bias(bias_table, bias_index, row_labels, column_valid)
+    main, tail = window_bias(table, index, row_labels, column_valid)
     cell_gain = merge_gain.reshape(1, -1)
+    hopped, own = lax.optimization_barrier((hop(kept, first, third), own))
+    hopped = send(hopped, sizes, LEV)
     weights, triple, keys_t, residual, data = forward(
         (own, first, second, third), packed_weight, output_weight, norm_gain, main, tail
     )
-    scaled, moments, sent, near, cross = cell_moments(residual, (kept, first, third, fourth, fifth), cell_gain)
+    scaled, moments, sent, near, cross = cell_moments(residual, (kept, first, third, hopped), cell_gain)
     before = send(sent, sizes, lambda i, a, k: (i, a + 1, k))
     after = before if sizes[1] == 2 else send(sent, sizes, lambda i, a, k: (i, a - 1, k))
     near = send(near, sizes, HERE, True)

time: 48.5 us -> 48.7 us (level)
  waiting for transfers between devices: 8.94 us -> 12 us
  starting transfers between devices: 17.1 us -> 15.4 us
  Pallas kernels: 21.5 us -> 20.4 us
    ppermute x12 -> x11, waiting for transfers between devices: 8.94 us -> 12 us  [send(): return lax.ppermute(block, ('lon', 'lat', 'lev'), pairs)]
    ppermute x12 -> x11, starting transfers between devices: 17.1 us -> 15.4 us  [send(): return lax.ppermute(block, ('lon', 'lat', 'lev'), pairs)]
    pallas_call x1, Pallas kernels: 8.24 us -> 7 us  [window_bias(): pl.pallas_call(bias_kernel, out_shape=[shape((heads * WIN, 128), f32)] *...]
    pallas_call x1 -> x2, Pallas kernels: 1.3 us -> 1.4 us  [the longest x1 1.35 us: pack_pieces(): pl.pallas_call(pack_kernel, out_shape=[piece, triple, piece, triple, doub...]
  transfers between devices with their start and end apart: 12 -> 11, of which waited for: 5 -> 7; matrix products, arithmetic and copies ran while one was open for 0% -> 0% of each run, Pallas kernels for 38% -> 35%
where the time goes in v6:
time: 48.7 us; the launch traced here: 48.5 us
  Pallas kernels  20.4 us (42%)
  starting transfers between devices  15.4 us (32%)
  waiting for transfers between devices  12 us (25%)
  between operations  0.76 us (2%)
    ppermute x11, starting transfers between devices, send(): return lax.ppermute(block, ('lon', 'lat', 'lev'), pairs)  15.4 us
    ppermute x11, waiting for transfers between devices, send(): return lax.ppermute(block, ('lon', 'lat', 'lev'), pairs)  12 us
    pallas_call x1, Pallas kernels, window_bias(): pl.pallas_call(bias_kernel, out_shape=[shape((heads * WIN, 128), f32)] *...  7 us
    pallas_call x2, Pallas kernels, backward(): pl.pallas_call(functools.partial(backward_kernel, half), out_shape=shape(...  3.43 us
    pallas_call x1, Pallas kernels, forward(): pl.pallas_call(forward_kernel, out_shape=[shape((HEADS * WIN, WIN), bf16)...  3.36 us
    pallas_call x1, Pallas kernels, finish(): pl.pallas_call(finish_kernel, out_shape=[shape((QUAD, width), bf16)] * 4,...  1.53 us
    pallas_call x1, Pallas kernels, pack_pieces(): pl.pallas_call(pack_kernel, out_shape=[piece, triple, piece, triple, doub...  1.35 us
    pallas_call x1, Pallas kernels, unpack_cells(): pl.pallas_call(cell_kernel, out_shape=shape((HALF_LAT, PAIRS, 2 * LEVELS,...  1.21 us
  transfers between devices with their start and end apart: 11, of which 7 were waited for; matrix products, arithmetic and copies ran while one was open for 0% of the time, Pallas kernels for 35%

profile of v6, /device:TPU:0, one launch (start us, length us, event | category | flops | bytes accessed | tf_op | source)
XLA Modules:
  0.0 48.5 jit_solution(1763182420042554420)
XLA Ops:
  0.6 1.3 %pack.1 = (bf16[36,768]{1,0:T(8,128)(2,1)S(1)}, bf16[108,768]{1,0:T(8,128)(2,1)S(1)}, bf16[36,768]{1,0:T(8,128)(2,1)S(1)}, bf16[108,768]{1,0:T(8,128)(2,1)S(1)},...) custom-call(bf16[6,12,2,768]{3,2,1,0:T(2,128)(2,1)} %bitcast.7, ...), custom_call_target="tpu_custom_call" | custom-call | tf_op jit(solution)/shard_map/pack/pallas_call | solution.py:140
  2.0 4.1 %collective-permute-start.2 = (bf16[36,768]{1,0:T(8,128)(2,1)S(1)}, bf16[36,768]{1,0:T(8,128)(2,1)S(1)}, u32[]{:S(2)}, u32[]{:S(2)}) collective-permute-start(bf16[36,768]{1,0:T(8,128)(2,1)S(1)} %get-tuple-element.41), channel_id=1, source_target_pairs={{0,2},{1,31},{2,0},{3,29},{4,6},{5,3},{6,4},{7,1},{8,10},{9,7},{10... | collective-permute-start | bytes 165896 | tf_op jit(solution)/shard_map/ppermute | solution.py:694
  6.1 1.4 %collective-permute-start = (bf16[108,768]{1,0:T(8,128)(2,1)S(1)}, bf16[108,768]{1,0:T(8,128)(2,1)S(1)}, u32[]{:S(2)}, u32[]{:S(2)}) collective-permute-start(bf16[108,768]{1,0:T(8,128)(2,1)S(1)} %get-tuple-element.37), channel_id=1, source_target_pairs={{0,30},{1,3},{2,28},{3,1},{4,2},{5,7},{6,0},{7,5},{8,6},{9,11},{10... | collective-permute-start | bytes 497672 | tf_op jit(solution)/shard_map/ppermute | solution.py:694
  7.5 1.1 %collective-permute-start.1 = (bf16[108,768]{1,0:T(8,128)(2,1)S(1)}, bf16[108,768]{1,0:T(8,128)(2,1)S(1)}, u32[]{:S(2)}, u32[]{:S(2)}) collective-permute-start(bf16[108,768]{1,0:T(8,128)(2,1)S(1)} %get-tuple-element.38), channel_id=1, source_target_pairs={{0,28},{1,29},{2,30},{3,31},{4,0},{5,1},{6,2},{7,3},{8,4},{9,5},{1... | collective-permute-start | bytes 497672 | tf_op jit(solution)/shard_map/ppermute | solution.py:694
  8.6 0.0 copy-start
  8.6 0.0 copy-start.2
  8.6 0.0 copy-start.3
  8.6 7.0 %bias.1 = (f32[3456,128]{1,0:T(8,128)S(1)}, f32[3456,128]{1,0:T(8,128)S(1)}) custom-call(f32[24,3312]{1,0:T(8,128)S(1)} %get-tuple-element.42.table, s32[144,144]{1,0:T(8,128)S(1)} %get-tuple-element.43.index, s32[6]{0:T(128)} %labels_at.1, s32[96]{0:T(128)} %valid_at.1), custom_call_target="tpu_custom_call" | custom-call | flops 10000000000 | bytes 20000000 | tf_op jit(solution)/shard_map/bias/pallas_call | solution.py:279
  15.6 1.9 %collective-permute-done.first = bf16[108,768]{1,0:T(8,128)(2,1)S(1)} collective-permute-done((bf16[108,768]{1,0:T(8,128)(2,1)S(1)}, bf16[108,768]{1,0:T(8,128)(2,1)S(1)}, u32[]{:S(2)}, u32[]{:S(2)}) %collective-permute-start) | collective-permute-done | bytes 165920 | tf_op jit(solution)/shard_map/ppermute | solution.py:694
  17.5 0.0 collective-permute-done.1.third
  17.6 0.1 collective-permute-start.3
  17.6 0.0 collective-permute-done.2.second
  17.6 0.0 copy-done
  17.7 0.0 copy-done.2
  17.7 0.0 copy-done.3
  17.7 0.0 copy-start.1
  17.7 3.4 %forward.1 = (bf16[3456,144]{1,0:T(8,128)(2,1)S(1)}, bf16[144,2304]{1,0:T(8,128)(2,1)S(1)}, bf16[768,144]{1,0:T(8,128)(2,1)S(1)}, bf16[144,768]{1,0:T(8,128)(2,1)S(1)}, bf16[144,768]{1,0:T(8,128)(2,1)S(1)}) custom-call(bf16[36,768]{1,0:T(8,128)(2,1)S(1)} %get-tuple-element.40.own, bf16[108,768]{1,0:T(8,128)(2,1)S(1)} %collective-permute-done.first, ...), custom_call_target="tpu_custom_call" | custom-call | flops 10000000000 | bytes 20000000 | tf_op jit(solution)/shard_map/forward/pallas_call | solution.py:368
  21.1 2.0 %collective-permute-done.3.hopped = bf16[72,768]{1,0:T(8,128)(2,1)S(1)} collective-permute-done((bf16[72,768]{1,0:T(8,128)(2,1)S(1)}, bf16[72,768]{1,0:T(8,128)(2,1)S(1)}, u32[]{:S(2)}, u32[]{:S(2)}) %collective-permute-start.3) | collective-permute-done | bytes 110624 | tf_op jit(solution)/shard_map/ppermute | solution.py:694
  23.0 0.0 copy-done.1
  23.0 1.2 %moments.1 = (f32[144,768]{1,0:T(8,128)S(1)}, f32[144,128]{1,0:T(8,128)S(1)}, f32[24,128]{1,0:T(8,128)S(1)}, bf16[72,768]{1,0:T(8,128)(2,1)S(1)}, bf16[72,768]{1,0:T(8,128)(2,1)S(1)}) custom-call(bf16[144,768]{1,0:T(8,128)(2,1)S(1)} %get-tuple-element.46.residual, bf16[72,768]{1,0:T(8,128)(2,1)S(1)} %get-tuple-element.36.kept, ...), custom_call_target="tpu_custom_call" | custom-call | flops 100000000 | bytes 1000000 | tf_op jit(solution)/shard_map/moments/pallas_call | solution.py:470
  24.2 1.4 %collective-permute-start.4 = (f32[24,128]{1,0:T(8,128)S(1)}, f32[24,128]{1,0:T(8,128)S(1)}, u32[]{:S(2)}, u32[]{:S(2)}) collective-permute-start(f32[24,128]{1,0:T(8,128)S(1)} %get-tuple-element.50), channel_id=1, source_target_pairs={{0,2},{1,3},{2,0},{3,1},{4,6},{5,7},{6,4},{7,5},{8,10},{9,11},{10,... | collective-permute-start | bytes 36872 | tf_op jit(solution)/shard_map/ppermute | solution.py:694
  25.6 1.9 %collective-permute-start.5 = (bf16[72,768]{1,0:T(8,128)(2,1)S(1)}, bf16[72,768]{1,0:T(8,128)(2,1)S(1)}, u32[]{:S(2)}, u32[]{:S(2)}) collective-permute-start(bf16[72,768]{1,0:T(8,128)(2,1)S(1)} %get-tuple-element.54), channel_id=1, source_target_pairs={{28,0},{1,1},{30,2},{3,3},{0,4},{5,5},{2,6},{7,7},{4,8},{9,9},{6,1... | collective-permute-start | bytes 331784 | tf_op jit(solution)/shard_map/ppermute | solution.py:694
  27.6 0.5 %collective-permute-start.6 = (bf16[72,768]{1,0:T(8,128)(2,1)S(1)}, bf16[72,768]{1,0:T(8,128)(2,1)S(1)}, u32[]{:S(2)}, u32[]{:S(2)}) collective-permute-start(bf16[72,768]{1,0:T(8,128)(2,1)S(1)} %get-tuple-element.55), channel_id=1, source_target_pairs={{29,0},{0,1},{31,2},{2,3},{1,4},{4,5},{3,6},{6,7},{5,8},{8,9},{7,1... | collective-permute-start | bytes 331784 | tf_op jit(solution)/shard_map/ppermute | solution.py:694
  28.1 0.8 %collective-permute-done.4.before.after = f32[24,128]{1,0:T(8,128)S(1)} collective-permute-done((f32[24,128]{1,0:T(8,128)S(1)}, f32[24,128]{1,0:T(8,128)S(1)}, u32[]{:S(2)}, u32[]{:S(2)}) %collective-permute-start.4) | collective-permute-done | bytes 12320 | tf_op jit(solution)/shard_map/ppermute | solution.py:694
  28.9 0.5 %merge.1.grad = bf16[144,768]{1,0:T(8,128)(2,1)S(1)} custom-call(bf16[144,768]{1,0:T(8,128)(2,1)S(1)} %get-tuple-element.46.residual, f32[144,768]{1,0:T(8,128)S(1)} %get-tuple-element.48.scaled, f32[144,128]{1,0:T(8,128)S(1)} %get-tuple-element.49.moments, f32[24,128]{1,0:T(8,128)S(1)} %collective-permute-done.4.before.after, ...), custom_call_target="tpu_custom_call" | custom-call | flops 100000000 | bytes 1000000 | tf_op jit(solution)/shard_map/merge/pallas_call | solution.py:508
  29.4 1.7 %backward.2.first = bf16[144,1152]{1,0:T(8,128)(2,1)S(1)} custom-call(bf16[144,768]{1,0:T(8,128)(2,1)S(1)} %merge.1.grad, bf16[3456,144]{1,0:T(8,128)(2,1)S(1)} %get-tuple-element.51.weights, bf16[144,2304]{1,0:T(8,128)(2,1)S(1)} %get-tuple-element.52.triple, bf16[768,144]{1,0:T(8,128)(2,1)S(1)} %get-tuple-element.53.keys_t, bf16[768,768]{1,0:T(8,128)(2,1)S(1)} %copy-done.3), custom_call_target="tpu_custom_call" | custom-call | flops 10000000000 | bytes 20000000 | tf_op jit(solution)/shard_map/backward/pallas_call | solution.py:552
  31.1 1.5 %collective-permute-done.5.near = bf16[72,768]{1,0:T(8,128)(2,1)S(1)} collective-permute-done((bf16[72,768]{1,0:T(8,128)(2,1)S(1)}, bf16[72,768]{1,0:T(8,128)(2,1)S(1)}, u32[]{:S(2)}, u32[]{:S(2)}) %collective-permute-start.5) | collective-permute-done | bytes 110624 | tf_op jit(solution)/shard_map/ppermute | solution.py:694
  32.6 1.5 %collective-permute-done.6.cross = bf16[72,768]{1,0:T(8,128)(2,1)S(1)} collective-permute-done((bf16[72,768]{1,0:T(8,128)(2,1)S(1)}, bf16[72,768]{1,0:T(8,128)(2,1)S(1)}, u32[]{:S(2)}, u32[]{:S(2)}) %collective-permute-start.6) | collective-permute-done | bytes 110624 | tf_op jit(solution)/shard_map/ppermute | solution.py:694
  34.2 1.6 %collective-permute-start.7 = (bf16[72,768]{1,0:T(8,128)(2,1)S(1)}, bf16[72,768]{1,0:T(8,128)(2,1)S(1)}, u32[]{:S(2)}, u32[]{:S(2)}) collective-permute-start(bf16[72,768]{1,0:T(8,128)(2,1)S(1)} %relay.1), channel_id=1, source_target_pairs={{2,0},{3,1},{0,2},{1,3},{6,4},{7,5},{4,6},{5,7},{10,8},{11,9},{8,1... | collective-permute-start | bytes 331784 | tf_op jit(solution)/shard_map/ppermute | solution.py:694
  35.8 1.7 %backward.3.second = bf16[144,1152]{1,0:T(8,128)(2,1)S(1)} custom-call(bf16[144,768]{1,0:T(8,128)(2,1)S(1)} %merge.1.grad, bf16[3456,144]{1,0:T(8,128)(2,1)S(1)} %get-tuple-element.51.weights, bf16[144,2304]{1,0:T(8,128)(2,1)S(1)} %get-tuple-element.52.triple, bf16[768,144]{1,0:T(8,128)(2,1)S(1)} %get-tuple-element.53.keys_t, bf16[768,768]{1,0:T(8,128)(2,1)S(1)} %copy-done.3), custom_call_target="tpu_custom_call" | custom-call | flops 10000000000 | bytes 20000000 | tf_op jit(solution)/shard_map/backward/pallas_call | solution.py:552
  37.5 1.5 %finish.1 = (bf16[36,768]{1,0:T(8,128)(2,1)S(1)}, bf16[36,768]{1,0:T(8,128)(2,1)S(1)}, bf16[36,768]{1,0:T(8,128)(2,1)S(1)}, bf16[36,768]{1,0:T(8,128)(2,1)S(1)}) custom-call(bf16[144,768]{1,0:T(8,128)(2,1)S(1)} %merge.1.grad, bf16[144,1152]{1,0:T(8,128)(2,1)S(1)} %backward.2.first, bf16[144,1152]{1,0:T(8,128)(2,1)S(1)} %backward.3.second, ...), custom_call_target="tpu_custom_call" | custom-call | flops 10000000 | bytes 1000000 | tf_op jit(solution)/shard_map/finish/pallas_call | solution.py:575
  39.0 1.5 %collective-permute-start.8 = (bf16[36,768]{1,0:T(8,128)(2,1)S(1)}, bf16[36,768]{1,0:T(8,128)(2,1)S(1)}, u32[]{:S(2)}, u32[]{:S(2)}) collective-permute-start(bf16[36,768]{1,0:T(8,128)(2,1)S(1)} %get-tuple-element.62), channel_id=1, source_target_pairs={{2,0},{3,1},{0,2},{1,3},{6,4},{7,5},{4,6},{5,7},{10,8},{11,9},{8,1... | collective-permute-start | bytes 165896 | tf_op jit(solution)/shard_map/ppermute | solution.py:694
  40.5 0.7 %collective-permute-start.9 = (bf16[36,768]{1,0:T(8,128)(2,1)S(1)}, bf16[36,768]{1,0:T(8,128)(2,1)S(1)}, u32[]{:S(2)}, u32[]{:S(2)}) collective-permute-start(bf16[36,768]{1,0:T(8,128)(2,1)S(1)} %get-tuple-element.63), channel_id=1, source_target_pairs={{30,0},{31,1},{28,2},{29,3},{2,4},{3,5},{0,6},{1,7},{6,8},{7,9},{4... | collective-permute-start | bytes 165896 | tf_op jit(solution)/shard_map/ppermute | solution.py:694
  41.2 1.1 %collective-permute-start.10 = (bf16[36,768]{1,0:T(8,128)(2,1)S(1)}, bf16[36,768]{1,0:T(8,128)(2,1)S(1)}, u32[]{:S(2)}, u32[]{:S(2)}) collective-permute-start(bf16[36,768]{1,0:T(8,128)(2,1)S(1)} %get-tuple-element.64), channel_id=1, source_target_pairs={{28,0},{29,1},{30,2},{31,3},{0,4},{1,5},{2,6},{3,7},{4,8},{5,9},{6... | collective-permute-start | bytes 165896 | tf_op jit(solution)/shard_map/ppermute | solution.py:694
  42.3 0.0 collective-permute-done.7.onward
  42.3 1.2 %unpack_cells.1 = bf16[3,3,4,3072]{3,2,1,0:T(4,128)(2,1)} custom-call(bf16[72,768]{1,0:T(8,128)(2,1)S(1)} %collective-permute-done.5.near, bf16[72,768]{1,0:T(8,128)(2,1)S(1)} %collective-permute-done.6.cross, bf16[72,768]{1,0:T(8,128)(2,1)S(1)} %collective-permute-done.7.onward, f32[1,3072]{1,0:T(1,128)S(1)} %bitcast.6), custom_call_target="tpu_custom_call" | custom-call | flops 1000000000 | bytes 1000000 | tf_op jit(solution)/shard_map/unpack_cells/pallas_call | solution.py:667
  43.5 2.5 %collective-permute-done.8.lat = bf16[36,768]{1,0:T(8,128)(2,1)S(1)} collective-permute-done((bf16[36,768]{1,0:T(8,128)(2,1)S(1)}, bf16[36,768]{1,0:T(8,128)(2,1)S(1)}, u32[]{:S(2)}, u32[]{:S(2)}) %collective-permute-start.8) | collective-permute-done | bytes 55328 | tf_op jit(solution)/shard_map/ppermute | solution.py:694
  46.0 1.8 %collective-permute-done.9.both = bf16[36,768]{1,0:T(8,128)(2,1)S(1)} collective-permute-done((bf16[36,768]{1,0:T(8,128)(2,1)S(1)}, bf16[36,768]{1,0:T(8,128)(2,1)S(1)}, u32[]{:S(2)}, u32[]{:S(2)}) %collective-permute-start.9) | collective-permute-done | bytes 55328 | tf_op jit(solution)/shard_map/ppermute | solution.py:694
  47.8 0.0 collective-permute-done.10.lon
  47.8 0.7 %unpack_tokens.1 = bf16[6,12,2,768]{3,2,1,0:T(2,128)(2,1)} custom-call(bf16[36,768]{1,0:T(8,128)(2,1)S(1)} %get-tuple-element.66.own, bf16[36,768]{1,0:T(8,128)(2,1)S(1)} %collective-permute-done.8.lat, bf16[36,768]{1,0:T(8,128)(2,1)S(1)} %collective-permute-done.10.lon, bf16[36,768]{1,0:T(8,128)(2,1)S(1)} %collective-permute-done.9.both), custom_call_target="tpu_custom_call" | custom-call | tf_op jit(solution)/shard_map/unpack_tokens/pallas_call | solution.py:624
  (2 shorter events, 0.1 us)
Async XLA Ops:
  2.0 15.7 %collective-permute-start.2 = (bf16[36,768]{1,0:T(8,128)(2,1)S(1)}, bf16[36,768]{1,0:T(8,128)(2,1)S(1)}, u32[]{:S(2)}, u32[]{:S(2)}) collective-permute-start(bf16[36,768]{1,0:T(8,128)(2,1)S(1)} %get-tuple-element.41), channel_id=1, source_target_pairs={{0,2},{1,31},{2,0},{3,29},{4,6},{5,3},{6,4},{7,1},{8,10},{9,7},{10... | collective-permute-start | bytes 165896 | tf_op jit(solution)/shard_map/ppermute | solution.py:694
  6.1 11.4 %collective-permute-start = (bf16[108,768]{1,0:T(8,128)(2,1)S(1)}, bf16[108,768]{1,0:T(8,128)(2,1)S(1)}, u32[]{:S(2)}, u32[]{:S(2)}) collective-permute-start(bf16[108,768]{1,0:T(8,128)(2,1)S(1)} %get-tuple-element.37), channel_id=1, source_target_pairs={{0,30},{1,3},{2,28},{3,1},{4,2},{5,7},{6,0},{7,5},{8,6},{9,11},{10... | collective-permute-start | bytes 497672 | tf_op jit(solution)/shard_map/ppermute | solution.py:694
  7.5 10.0 %collective-permute-start.1 = (bf16[108,768]{1,0:T(8,128)(2,1)S(1)}, bf16[108,768]{1,0:T(8,128)(2,1)S(1)}, u32[]{:S(2)}, u32[]{:S(2)}) collective-permute-start(bf16[108,768]{1,0:T(8,128)(2,1)S(1)} %get-tuple-element.38), channel_id=1, source_target_pairs={{0,28},{1,29},{2,30},{3,31},{4,0},{5,1},{6,2},{7,3},{8,4},{9,5},{1... | collective-permute-start | bytes 497672 | tf_op jit(solution)/shard_map/ppermute | solution.py:694
  8.6 9.1 %copy-start = (bf16[768,2304]{1,0:T(8,128)(2,1)S(1)}, bf16[768,2304]{1,0:T(8,128)(2,1)}, u32[]{:S(2)}) copy-start(bf16[768,2304]{1,0:T(8,128)(2,1)} %packed.3) | copy-start | bytes 10616836
  8.6 9.1 %copy-start.2 = (f32[768]{0:T(1024)S(1)}, f32[768]{0:T(1024)}, u32[]{:S(2)}) copy-start(f32[768]{0:T(1024)} %gain.3) | copy-start | bytes 9220
  8.6 9.1 %copy-start.3 = (bf16[768,768]{1,0:T(8,128)(2,1)S(1)}, bf16[768,768]{1,0:T(8,128)(2,1)}, u32[]{:S(2)}) copy-start(bf16[768,768]{1,0:T(8,128)(2,1)} %output.5) | copy-start | bytes 3538948
  17.6 5.5 %collective-permute-start.3 = (bf16[72,768]{1,0:T(8,128)(2,1)S(1)}, bf16[72,768]{1,0:T(8,128)(2,1)S(1)}, u32[]{:S(2)}, u32[]{:S(2)}) collective-permute-start(bf16[72,768]{1,0:T(8,128)(2,1)S(1)} %hop.1), channel_id=1, source_target_pairs={{0,1},{1,0},{2,3},{3,2},{4,5},{5,4},{6,7},{7,6},{8,9},{9,8},{10,11... | collective-permute-start | bytes 331784 | tf_op jit(solution)/shard_map/ppermute | solution.py:694
  17.7 5.4 %copy-start.1 = (f32[3072]{0:T(1024)S(1)}, f32[3072]{0:T(1024)}, u32[]{:S(2)}) copy-start(f32[3072]{0:T(1024)} %param.14) | copy-start | bytes 36868
  24.2 4.6 %collective-permute-start.4 = (f32[24,128]{1,0:T(8,128)S(1)}, f32[24,128]{1,0:T(8,128)S(1)}, u32[]{:S(2)}, u32[]{:S(2)}) collective-permute-start(f32[24,128]{1,0:T(8,128)S(1)} %get-tuple-element.50), channel_id=1, source_target_pairs={{0,2},{1,3},{2,0},{3,1},{4,6},{5,7},{6,4},{7,5},{8,10},{9,11},{10,... | collective-permute-start | bytes 36872 | tf_op jit(solution)/shard_map/ppermute | solution.py:694
  25.6 7.0 %collective-permute-start.5 = (bf16[72,768]{1,0:T(8,128)(2,1)S(1)}, bf16[72,768]{1,0:T(8,128)(2,1)S(1)}, u32[]{:S(2)}, u32[]{:S(2)}) collective-permute-start(bf16[72,768]{1,0:T(8,128)(2,1)S(1)} %get-tuple-element.54), channel_id=1, source_target_pairs={{28,0},{1,1},{30,2},{3,3},{0,4},{5,5},{2,6},{7,7},{4,8},{9,9},{6,1... | collective-permute-start | bytes 331784 | tf_op jit(solution)/shard_map/ppermute | solution.py:694
  27.6 6.6 %collective-permute-start.6 = (bf16[72,768]{1,0:T(8,128)(2,1)S(1)}, bf16[72,768]{1,0:T(8,128)(2,1)S(1)}, u32[]{:S(2)}, u32[]{:S(2)}) collective-permute-start(bf16[72,768]{1,0:T(8,128)(2,1)S(1)} %get-tuple-element.55), channel_id=1, source_target_pairs={{29,0},{0,1},{31,2},{2,3},{1,4},{4,5},{3,6},{6,7},{5,8},{8,9},{7,1... | collective-permute-start | bytes 331784 | tf_op jit(solution)/shard_map/ppermute | solution.py:694
  34.2 8.1 %collective-permute-start.7 = (bf16[72,768]{1,0:T(8,128)(2,1)S(1)}, bf16[72,768]{1,0:T(8,128)(2,1)S(1)}, u32[]{:S(2)}, u32[]{:S(2)}) collective-permute-start(bf16[72,768]{1,0:T(8,128)(2,1)S(1)} %relay.1), channel_id=1, source_target_pairs={{2,0},{3,1},{0,2},{1,3},{6,4},{7,5},{4,6},{5,7},{10,8},{11,9},{8,1... | collective-permute-start | bytes 331784 | tf_op jit(solution)/shard_map/ppermute | solution.py:694
  39.0 7.0 %collective-permute-start.8 = (bf16[36,768]{1,0:T(8,128)(2,1)S(1)}, bf16[36,768]{1,0:T(8,128)(2,1)S(1)}, u32[]{:S(2)}, u32[]{:S(2)}) collective-permute-start(bf16[36,768]{1,0:T(8,128)(2,1)S(1)} %get-tuple-element.62), channel_id=1, source_target_pairs={{2,0},{3,1},{0,2},{1,3},{6,4},{7,5},{4,6},{5,7},{10,8},{11,9},{8,1... | collective-permute-start | bytes 165896 | tf_op jit(solution)/shard_map/ppermute | solution.py:694
  40.5 7.3 %collective-permute-start.9 = (bf16[36,768]{1,0:T(8,128)(2,1)S(1)}, bf16[36,768]{1,0:T(8,128)(2,1)S(1)}, u32[]{:S(2)}, u32[]{:S(2)}) collective-permute-start(bf16[36,768]{1,0:T(8,128)(2,1)S(1)} %get-tuple-element.63), channel_id=1, source_target_pairs={{30,0},{31,1},{28,2},{29,3},{2,4},{3,5},{0,6},{1,7},{6,8},{7,9},{4... | collective-permute-start | bytes 165896 | tf_op jit(solution)/shard_map/ppermute | solution.py:694
  41.2 6.6 %collective-permute-start.10 = (bf16[36,768]{1,0:T(8,128)(2,1)S(1)}, bf16[36,768]{1,0:T(8,128)(2,1)S(1)}, u32[]{:S(2)}, u32[]{:S(2)}) collective-permute-start(bf16[36,768]{1,0:T(8,128)(2,1)S(1)} %get-tuple-element.64), channel_id=1, source_target_pairs={{28,0},{29,1},{30,2},{31,3},{0,4},{1,5},{2,6},{3,7},{4,8},{5,9},{6... | collective-permute-start | bytes 165896 | tf_op jit(solution)/shard_map/ppermute | solution.py:694

commit v7 on v6

--- a/solution.py
+++ b/solution.py
@@ -96,7 +96,7 @@
 
 
 def pack_kernel(
-    tokens_at, grad_at, table_at, index_at, own, first, second, third, kept, table, index,
+    tokens_at, grad_at, table_at, index_at, own, first, second, third, kept, fourth, fifth, table, index,
     tokens, grad, rows, cells, done,
 ):
     width = tokens.shape[-1]
@@ -124,22 +124,23 @@
     lat, lon, both = quadrant(data, 1), quadrant(data, 2), quadrant(data, 3)
     here, below = quadrant(grads, 0), quadrant(grads, 1)
     own[...] = quadrant(data, 0).astype(bf16)
-    more = quadrant(grads, 3)
-    sides = jnp.concatenate((here, quadrant(grads, 2)), axis=0)
-    first[...] = jnp.concatenate((jnp.where(upper, lat, both), below, more), axis=0).astype(bf16)
+    first[...] = jnp.concatenate((jnp.where(upper, lat, both), below), axis=0).astype(bf16)
     second[...] = jnp.where(upper, both, lat).astype(bf16)
-    third[...] = jnp.concatenate((lon, sides), axis=0).astype(bf16)
-    kept[...] = sides.astype(bf16)
+    third[...] = jnp.concatenate((lon, here), axis=0).astype(bf16)
+    kept[...] = here.astype(bf16)
+    fourth[...] = quadrant(grads, 2).astype(bf16)
+    fifth[...] = quadrant(grads, 3).astype(bf16)
     copies[2].wait()
     copies[3].wait()
 
 
 def pack_pieces(tokens, grad, table, index):
     width = tokens.shape[-1]
-    piece, double, triple = (shape((n * QUAD, width), bf16) for n in (1, 2, 3))
+    piece, double = shape((QUAD, width), bf16), shape((2 * QUAD, width), bf16)
     return pl.pallas_call(
         pack_kernel,
-        out_shape=[piece, triple, piece, triple, double, shape(table.shape[2:], f32), shape(index.shape, jnp.int32)],
+        out_shape=[piece, double, piece, double, piece, piece, piece]
+        + [shape(table.shape[2:], f32), shape(index.shape, jnp.int32)],
         in_specs=[pl.BlockSpec(memory_space=pltpu.MemorySpace.HBM)] * 4,
         scratch_shapes=[
             pltpu.VMEM(tokens.shape, bf16),
@@ -165,26 +166,24 @@
     rows = lax.broadcasted_iota(jnp.int32, (WIN, WIN), 0)
     permute = jnp.where(natural == columns, 1.0, 0.0).astype(bf16)
     heads, entries = table.shape
-    gathered = 8
-    wide = heads - gathered
     chunks = (entries + 255) // 256
     small_chunks = (entries + 127) // 128
     for c in range(small_chunks):
         size = min(128, entries - c * 128)
-        part = table[wide:, c * 128 : c * 128 + size]
+        part = table[:, c * 128 : c * 128 + size]
         if size < 128:
-            part = jnp.concatenate((part, jnp.zeros((gathered, 128 - size), f32)), axis=1)
+            part = jnp.concatenate((part, jnp.zeros((heads, 128 - size), f32)), axis=1)
         fine[:, c * 128 : (c + 1) * 128] = part
     for c in range(chunks):
         size = min(256, entries - c * 256)
-        part = table[:wide, c * 256 : c * 256 + size]
+        part = table[:, c * 256 : c * 256 + size]
         if size < 256:
-            part = jnp.concatenate((part, jnp.zeros((wide, 256 - size), f32)), axis=1)
+            part = jnp.concatenate((part, jnp.zeros((heads, 256 - size), f32)), axis=1)
         coarse = part.astype(bf16).astype(f32)
-        split[c * wide : (c + 1) * wide, :] = coarse
-        split[(chunks + c) * wide : (chunks + c + 1) * wide, :] = part - coarse
+        split[c * heads : (c + 1) * heads, :] = coarse
+        split[(chunks + c) * heads : (chunks + c + 1) * heads, :] = part - coarse
     source = split[...].astype(bf16)
-    part_rows = chunks * wide
+    part_rows = chunks * heads
 
     def place(values, out):
         moved = mxu(mxu(permute, values.astype(f32).astype(bf16), NT).astype(bf16), permute, NT)
@@ -227,7 +226,28 @@
     depth = lax.broadcasted_iota(jnp.int32, (256, 128), 0).astype(f32).astype(bf16)
     one, zero = jnp.ones((), bf16), jnp.zeros((), bf16)
 
+    def pick(chunk, parts, count):
+        found = [None] * (heads // 8)
+        for c in range(count):
+            hit = chunk == c
+            for block in range(heads // 8):
+                a = parts(c, block)
+                found[block] = a if c == 0 else jnp.where(hit, a, found[block])
+        return found
+
+    def gathered(row):
+        chunk = jnp.broadcast_to(fine_high[pl.ds(row, 1), :], (8, 128))
+        lane = jnp.broadcast_to(fine_low[pl.ds(row, 1), :], (8, 128))
+
+        def part(c, block):
+            values = fine[block * 8 : block * 8 + 8, c * 128 : (c + 1) * 128]
+            return jnp.take_along_axis(values, lane, axis=1, mode="promise_in_bounds")
+
+        return pick(chunk, part, small_chunks)
+
     def lookup(row):
+        if row // 2 % 4 == 3:
+            return [gathered(row), gathered(row + 1)]
         hot = []
         for j in range(2):
             lane = jnp.broadcast_to(low[pl.ds(row + j, 1), :], (16, 128)).astype(bf16)
@@ -235,26 +255,16 @@
         product = mxu(source, jnp.concatenate(hot, axis=1))
         out = []
         for j in range(2):
-            here = slice(j * 128, (j + 1) * 128)
             chunk = jnp.broadcast_to(high[pl.ds(row + j, 1), :], (8, 128))
-            coarse, rest = [None] * (wide // 8), [None] * (wide // 8)
-            for c in range(chunks):
-                hit = chunk == c
-                for block in range(wide // 8):
-                    at = c * wide + block * 8
-                    a = product[at : at + 8, here]
-                    b = product[part_rows + at : part_rows + at + 8, here]
-                    coarse[block] = a if c == 0 else jnp.where(hit, a, coarse[block])
-                    rest[block] = b if c == 0 else jnp.where(hit, b, rest[block])
-            found = [a + b for a, b in zip(coarse, rest)]
-            chunk = jnp.broadcast_to(fine_high[pl.ds(row + j, 1), :], (8, 128))
-            lane = jnp.broadcast_to(fine_low[pl.ds(row + j, 1), :], (8, 128))
-            value = None
-            for c in range(small_chunks):
-                a = jnp.take_along_axis(fine[:, c * 128 : (c + 1) * 128], lane, axis=1, mode="promise_in_bounds")
-                value = a if c == 0 else jnp.where(chunk == c, a, value)
-            found.append(value)
-            out.append(found)
+            halves = []
+            for begin in (0, part_rows):
+
+                def part(c, block):
+                    at = begin + c * heads + block * 8
+                    return product[at : at + 8, j * 128 : (j + 1) * 128]
+
+                halves.append(pick(chunk, part, chunks))
+            out.append([a + b for a, b in zip(*halves)])
         return out
 
     for key in range(0, WIN, 2):
@@ -284,8 +294,8 @@
         scratch_shapes=[
             pltpu.SMEM(labels.shape, jnp.int32),
             pltpu.SMEM(valid.shape, jnp.int32),
-            pltpu.VMEM((2 * whole * (heads - 8), 256), f32),
-            pltpu.VMEM((8, (entries + 127) // 128 * 128), f32),
+            pltpu.VMEM((2 * whole * heads, 256), f32),
+            pltpu.VMEM((heads, (entries + 127) // 128 * 128), f32),
             pltpu.VMEM((index_rows, 128), f32),
             pltpu.VMEM((index_rows, 128), f32),
             pltpu.VMEM((index_rows, 128), jnp.int32),
@@ -424,12 +434,11 @@
     return out
 
 
-def moments_kernel(residual, kept, first, third, hopped, gain, scaled, moments, sent, near, over, factors):
+def moments_kernel(residual, kept, first, third, fourth, fifth, gain, scaled, moments, sent, near, over, factors):
     width = residual.shape[-1]
     upper = lax.axis_index("lev") == 1
-    own, hop = kept[...].astype(f32)[:QUAD], hopped[...].astype(f32)
-    a, b = hop[:QUAD], hop[QUAD:]
-    below, right = first[...].astype(f32)[QUAD : 2 * QUAD], third[...].astype(f32)[QUAD : 2 * QUAD]
+    own, a, b = kept[...].astype(f32), fourth[...].astype(f32), fifth[...].astype(f32)
+    below, right = first[...].astype(f32)[QUAD:], third[...].astype(f32)[QUAD:]
     gain_rows(gain, factors)
     for quad, part in enumerate((
         jnp.where(upper, own, a),
@@ -559,41 +568,32 @@
     )(grad, weights, triple, keys_t, output)
 
 
-def finish_kernel(grad, first, second, tokens, packed, gain, own, lat, lon, both):
+def finish_kernel(quads, grad, first, second, tokens, packed, gain, *outs):
     part = first.shape[-1] // 3
+
+    def rows(values):
+        values = values.astype(f32)
+        return jnp.concatenate([quadrant(values, quad) for quad in quads], axis=0)
+
     joined = [half[:, i * part : (i + 1) * part] for i in range(3) for half in (first, second)]
-    grad_inputs = mxu(jnp.concatenate(joined, axis=1), packed[...], NT).astype(bf16)
-    unit, scale = unit_rows(tokens[...].astype(f32))
+    joined = rows(jnp.concatenate(joined, axis=1)).astype(bf16)
+    grad_inputs = mxu(joined, packed[...], NT).astype(bf16)
+    unit, scale = unit_rows(rows(tokens[...]))
     scaled = grad_inputs.astype(f32) * gain[...].reshape(1, -1)
-    out = grad[...].astype(f32) + scale * (scaled - row_mean(scaled) - unit * row_mean(scaled * unit))
-    for quad, piece in enumerate((own, lat, lon, both)):
-        piece[...] = quadrant(out, quad).astype(bf16)
-
-
-def finish(grad, first, second, tokens, packed, gain):
+    out = rows(grad[...]) + scale * (scaled - row_mean(scaled) - unit * row_mean(scaled * unit))
+    for i, piece in enumerate(outs):
+        piece[...] = quadrant(out, i).astype(bf16)
+
+
+def finish(quads, grad, first, second, tokens, packed, gain, flops):
     width = grad.shape[-1]
     return pl.pallas_call(
-        finish_kernel,
-        out_shape=[shape((QUAD, width), bf16)] * 4,
-        compiler_params=params(),
-        cost_estimate=cost(10**7, 10**6),
+        functools.partial(finish_kernel, quads),
+        out_shape=[shape((QUAD, width), bf16)] * 2,
+        compiler_params=params(),
+        cost_estimate=cost(flops, 10**6),
         name="finish",
     )(grad, first, second, tokens, packed, gain)
-
-
-def hop_kernel(kept, first, third, out):
-    upper = lax.axis_index("lev") == 1
-    here = jnp.where(upper, kept[...].astype(f32)[QUAD:], third[...].astype(f32)[2 * QUAD :])
-    out[...] = jnp.concatenate((here, first[...].astype(f32)[2 * QUAD :]), axis=0).astype(bf16)
-
-
-def hop(kept, first, third):
-    return pl.pallas_call(
-        hop_kernel,
-        out_shape=shape(kept.shape, bf16),
-        compiler_params=params(),
-        name="hop",
-    )(kept, first, third)
 
 
 def relay_kernel(near, cross, out):
@@ -668,7 +668,7 @@
         cell_kernel,
         out_shape=shape((HALF_LAT, PAIRS, 2 * LEVELS, 4 * width), bf16),
         compiler_params=params(),
-        cost_estimate=cost(10**9, 10**6),
+        cost_estimate=cost(10**6, 10**5),
         name="unpack_cells",
     )(near, cross, onward, gain)
 
@@ -698,7 +698,7 @@
 SECOND = lambda i, a, k: (i - k, a - 1, k)
 THIRD = lambda i, a, k: (i - 1, a, k)
 FOURTH = lambda i, a, k: (i - (1 - k), a, 1 - k)
-LEV = lambda i, a, k: (i, a, 1 - k)
+FIFTH = lambda i, a, k: (i - (1 - k), a - 1, 1 - k)
 LAT = lambda i, a, k: (i, a - 1, k)
 LON = lambda i, a, k: (i - 1, a, k)
 BOTH = lambda i, a, k: (i - 1, a - 1, k)
@@ -718,20 +718,22 @@
     column_valid,
     merged_grad,
 ):
-    own, first, second, third, kept, table, index = pack_pieces(
+    own, first, second, third, kept, fourth, fifth, table, index = pack_pieces(
         tokens.transpose(1, 2, 0, 3), merged_grad.transpose(1, 2, 0, 3), bias_table, bias_index
     )
     first = send(first, sizes, FIRST)
     second = send(second, sizes, SECOND)
     third = send(third, sizes, THIRD)
+    fourth = send(fourth, sizes, FOURTH)
+    fifth = send(fifth, sizes, FIFTH)
     main, tail = window_bias(table, index, row_labels, column_valid)
     cell_gain = merge_gain.reshape(1, -1)
-    hopped, own = lax.optimization_barrier((hop(kept, first, third), own))
-    hopped = send(hopped, sizes, LEV)
     weights, triple, keys_t, residual, data = forward(
         (own, first, second, third), packed_weight, output_weight, norm_gain, main, tail
     )
-    scaled, moments, sent, near, cross = cell_moments(residual, (kept, first, third, hopped), cell_gain)
+    scaled, moments, sent, near, cross = cell_moments(
+        residual, (kept, first, third, fourth, fifth), cell_gain
+    )
     before = send(sent, sizes, lambda i, a, k: (i, a + 1, k))
     after = before if sizes[1] == 2 else send(sent, sizes, lambda i, a, k: (i, a - 1, k))
     near = send(near, sizes, HERE, True)
@@ -742,7 +744,9 @@
     onward, grad = lax.optimization_barrier((relay(near, cross), grad))
     onward = send(onward, sizes, LAT, True)
     second = backward(1, grad, weights, triple, keys_t, output_weight)
-    own, lat, lon, both = finish(grad, first, second, data, packed_weight, norm_gain)
+    lat, both = finish((1, 3), grad, first, second, data, packed_weight, norm_gain, 10**7)
+    lat, both, second = lax.optimization_barrier((lat, both, second))
+    own, lon = finish((0, 2), grad, first, second, data, packed_weight, norm_gain, 10**7)
     lat = send(lat, sizes, LAT, True)
     both = send(both, sizes, BOTH, True)
     lon = send(lon, sizes, LON, True)

time: 48.7 us -> 48.3 us (level)
  waiting for transfers between devices: 12 us -> 7.2 us
  starting transfers between devices: 15.4 us -> 19.1 us
  Pallas kernels: 20.4 us -> 21.1 us
    ppermute x11 -> x12, waiting for transfers between devices: 12 us -> 7.2 us  [send(): return lax.ppermute(block, ('lon', 'lat', 'lev'), pairs)]
    ppermute x11 -> x12, starting transfers between devices: 15.4 us -> 19.1 us  [send(): return lax.ppermute(block, ('lon', 'lat', 'lev'), pairs)]
    pallas_call x3, Pallas kernels: 2.92 us -> 4.01 us  [the longest x2 2.68 us: finish(): pl.pallas_call(functools.partial(finish_kernel, quads), out_shape=[shape(...]
  transfers between devices with their start and end apart: 11 -> 12, of which waited for: 7 -> 6; matrix products, arithmetic and copies ran while one was open for 0% -> 0% of each run, Pallas kernels for 35% -> 37%
where the time goes in v7:
time: 48.3 us; the launch traced here: 48.1 us
  Pallas kernels  21.1 us (44%)
  starting transfers between devices  19.1 us (40%)
  waiting for transfers between devices  7.2 us (15%)
  between operations  0.77 us (2%)
    ppermute x12, starting transfers between devices, send(): return lax.ppermute(block, ('lon', 'lat', 'lev'), pairs)  19.1 us
    ppermute x12, waiting for transfers between devices, send(): return lax.ppermute(block, ('lon', 'lat', 'lev'), pairs)  7.2 us
    pallas_call x1, Pallas kernels, window_bias(): pl.pallas_call(bias_kernel, out_shape=[shape((heads * WIN, 128), f32)] *...  6.57 us
    pallas_call x2, Pallas kernels, backward(): pl.pallas_call(functools.partial(backward_kernel, half), out_shape=shape(...  3.42 us
    pallas_call x1, Pallas kernels, forward(): pl.pallas_call(forward_kernel, out_shape=[shape((HEADS * WIN, WIN), bf16)...  3.42 us
    pallas_call x2, Pallas kernels, finish(): pl.pallas_call(functools.partial(finish_kernel, quads), out_shape=[shape(...  2.68 us
    pallas_call x1, Pallas kernels, pack_pieces(): pl.pallas_call(pack_kernel, out_shape=[piece, double, piece, double, piec...  1.32 us
    pallas_call x1, Pallas kernels, unpack_cells(): pl.pallas_call(cell_kernel, out_shape=shape((HALF_LAT, PAIRS, 2 * LEVELS,...  1.21 us
  transfers between devices with their start and end apart: 12, of which 6 were waited for; matrix products, arithmetic and copies ran while one was open for 0% of the time, Pallas kernels for 37%

profile of v7, /device:TPU:0, one launch (start us, length us, event | category | flops | bytes accessed | tf_op | source)
XLA Modules:
  0.0 48.1 jit_solution(2246768163489220756)
XLA Ops:
  0.6 1.3 %pack.1 = (bf16[36,768]{1,0:T(8,128)(2,1)S(1)}, bf16[72,768]{1,0:T(8,128)(2,1)S(1)}, bf16[36,768]{1,0:T(8,128)(2,1)S(1)}, bf16[72,768]{1,0:T(8,128)(2,1)S(1)}, b...) custom-call(bf16[6,12,2,768]{3,2,1,0:T(2,128)(2,1)} %bitcast.7, ...), custom_call_target="tpu_custom_call" | custom-call | tf_op jit(solution)/shard_map/pack/pallas_call | solution.py:140
  2.0 4.1 %collective-permute-start.1 = (bf16[36,768]{1,0:T(8,128)(2,1)S(1)}, bf16[36,768]{1,0:T(8,128)(2,1)S(1)}, u32[]{:S(2)}, u32[]{:S(2)}) collective-permute-start(bf16[36,768]{1,0:T(8,128)(2,1)S(1)} %get-tuple-element.41), channel_id=1, source_target_pairs={{0,2},{1,31},{2,0},{3,29},{4,6},{5,3},{6,4},{7,1},{8,10},{9,7},{10... | collective-permute-start | bytes 165896 | tf_op jit(solution)/shard_map/ppermute | solution.py:694
  6.0 3.2 %collective-permute-start.3 = (bf16[36,768]{1,0:T(8,128)(2,1)S(1)}, bf16[36,768]{1,0:T(8,128)(2,1)S(1)}, u32[]{:S(2)}, u32[]{:S(2)}) collective-permute-start(bf16[36,768]{1,0:T(8,128)(2,1)S(1)} %get-tuple-element.49), channel_id=1, source_target_pairs={{0,29},{1,0},{2,31},{3,2},{4,1},{5,4},{6,3},{7,6},{8,5},{9,8},{10,... | collective-permute-start | bytes 165896 | tf_op jit(solution)/shard_map/ppermute | solution.py:694
  9.2 0.0 collective-permute-start.4
  9.2 1.9 %collective-permute-start = (bf16[72,768]{1,0:T(8,128)(2,1)S(1)}, bf16[72,768]{1,0:T(8,128)(2,1)S(1)}, u32[]{:S(2)}, u32[]{:S(2)}) collective-permute-start(bf16[72,768]{1,0:T(8,128)(2,1)S(1)} %get-tuple-element.40), channel_id=1, source_target_pairs={{0,30},{1,3},{2,28},{3,1},{4,2},{5,7},{6,0},{7,5},{8,6},{9,11},{10... | collective-permute-start | bytes 331784 | tf_op jit(solution)/shard_map/ppermute | solution.py:694
  11.1 0.0 collective-permute-start.2
  11.1 0.0 copy-start
  11.1 0.0 copy-start.2
  11.1 0.0 copy-start.3
  11.2 6.6 %bias.1 = (f32[3456,128]{1,0:T(8,128)S(1)}, f32[3456,128]{1,0:T(8,128)S(1)}) custom-call(f32[24,3312]{1,0:T(8,128)S(1)} %get-tuple-element.43.table, s32[144,144]{1,0:T(8,128)S(1)} %get-tuple-element.44.index, s32[6]{0:T(128)} %labels_at.1, s32[96]{0:T(128)} %valid_at.1), custom_call_target="tpu_custom_call" | custom-call | flops 10000000000 | bytes 20000000 | tf_op jit(solution)/shard_map/bias/pallas_call | solution.py:289
  17.7 0.0 collective-permute-done.1.second
  17.7 1.0 %collective-permute-done.first = bf16[72,768]{1,0:T(8,128)(2,1)S(1)} collective-permute-done((bf16[72,768]{1,0:T(8,128)(2,1)S(1)}, bf16[72,768]{1,0:T(8,128)(2,1)S(1)}, u32[]{:S(2)}, u32[]{:S(2)}) %collective-permute-start) | collective-permute-done | bytes 110624 | tf_op jit(solution)/shard_map/ppermute | solution.py:694
  18.8 0.0 collective-permute-done.2.third
  18.8 0.0 copy-done
  18.8 0.0 copy-done.2
  18.8 0.0 copy-done.3
  18.8 0.0 copy-start.1
  18.8 3.4 %forward.1 = (bf16[3456,144]{1,0:T(8,128)(2,1)S(1)}, bf16[144,2304]{1,0:T(8,128)(2,1)S(1)}, bf16[768,144]{1,0:T(8,128)(2,1)S(1)}, bf16[144,768]{1,0:T(8,128)(2,1)S(1)}, bf16[144,768]{1,0:T(8,128)(2,1)S(1)}) custom-call(bf16[36,768]{1,0:T(8,128)(2,1)S(1)} %get-tuple-element.39.own, bf16[72,768]{1,0:T(8,128)(2,1)S(1)} %collective-permute-done.first, ...), custom_call_target="tpu_custom_call" | custom-call | flops 10000000000 | bytes 20000000 | tf_op jit(solution)/shard_map/forward/pallas_call | solution.py:378
  22.2 0.0 collective-permute-done.3.fourth
  22.2 0.0 collective-permute-done.4.fifth
  22.2 0.0 copy-done.1
  22.3 1.2 %moments.1 = (f32[144,768]{1,0:T(8,128)S(1)}, f32[144,128]{1,0:T(8,128)S(1)}, f32[24,128]{1,0:T(8,128)S(1)}, bf16[72,768]{1,0:T(8,128)(2,1)S(1)}, bf16[72,768]{1,0:T(8,128)(2,1)S(1)}) custom-call(bf16[144,768]{1,0:T(8,128)(2,1)S(1)} %get-tuple-element.47.residual, bf16[36,768]{1,0:T(8,128)(2,1)S(1)} %get-tuple-element.48.kept, ...), custom_call_target="tpu_custom_call" | custom-call | flops 100000000 | bytes 1000000 | tf_op jit(solution)/shard_map/moments/pallas_call | solution.py:479
  23.4 0.3 collective-permute-start.5
  23.7 2.1 %collective-permute-start.6 = (bf16[72,768]{1,0:T(8,128)(2,1)S(1)}, bf16[72,768]{1,0:T(8,128)(2,1)S(1)}, u32[]{:S(2)}, u32[]{:S(2)}) collective-permute-start(bf16[72,768]{1,0:T(8,128)(2,1)S(1)} %get-tuple-element.57), channel_id=1, source_target_pairs={{28,0},{1,1},{30,2},{3,3},{0,4},{5,5},{2,6},{7,7},{4,8},{9,9},{6,1... | collective-permute-start | bytes 331784 | tf_op jit(solution)/shard_map/ppermute | solution.py:694
  25.8 1.4 %collective-permute-start.7 = (bf16[72,768]{1,0:T(8,128)(2,1)S(1)}, bf16[72,768]{1,0:T(8,128)(2,1)S(1)}, u32[]{:S(2)}, u32[]{:S(2)}) collective-permute-start(bf16[72,768]{1,0:T(8,128)(2,1)S(1)} %get-tuple-element.58), channel_id=1, source_target_pairs={{29,0},{0,1},{31,2},{2,3},{1,4},{4,5},{3,6},{6,7},{5,8},{8,9},{7,1... | collective-permute-start | bytes 331784 | tf_op jit(solution)/shard_map/ppermute | solution.py:694
  27.3 0.8 %collective-permute-done.5.before.after = f32[24,128]{1,0:T(8,128)S(1)} collective-permute-done((f32[24,128]{1,0:T(8,128)S(1)}, f32[24,128]{1,0:T(8,128)S(1)}, u32[]{:S(2)}, u32[]{:S(2)}) %collective-permute-start.5) | collective-permute-done | bytes 12320 | tf_op jit(solution)/shard_map/ppermute | solution.py:694
  28.1 0.5 %merge.1.grad = bf16[144,768]{1,0:T(8,128)(2,1)S(1)} custom-call(bf16[144,768]{1,0:T(8,128)(2,1)S(1)} %get-tuple-element.47.residual, f32[144,768]{1,0:T(8,128)S(1)} %get-tuple-element.51.scaled, f32[144,128]{1,0:T(8,128)S(1)} %get-tuple-element.52.moments, f32[24,128]{1,0:T(8,128)S(1)} %collective-permute-done.5.before.after, ...), custom_call_target="tpu_custom_call" | custom-call | flops 100000000 | bytes 1000000 | tf_op jit(solution)/shard_map/merge/pallas_call | solution.py:517
  28.6 1.7 %backward.2.first = bf16[144,1152]{1,0:T(8,128)(2,1)S(1)} custom-call(bf16[144,768]{1,0:T(8,128)(2,1)S(1)} %merge.1.grad, bf16[3456,144]{1,0:T(8,128)(2,1)S(1)} %get-tuple-element.54.weights, bf16[144,2304]{1,0:T(8,128)(2,1)S(1)} %get-tuple-element.55.triple, bf16[768,144]{1,0:T(8,128)(2,1)S(1)} %get-tuple-element.56.keys_t, bf16[768,768]{1,0:T(8,128)(2,1)S(1)} %copy-done.3), custom_call_target="tpu_custom_call" | custom-call | flops 10000000000 | bytes 20000000 | tf_op jit(solution)/shard_map/backward/pallas_call | solution.py:561
  30.3 0.4 collective-permute-done.6.near
  30.7 1.9 %collective-permute-done.7.cross = bf16[72,768]{1,0:T(8,128)(2,1)S(1)} collective-permute-done((bf16[72,768]{1,0:T(8,128)(2,1)S(1)}, bf16[72,768]{1,0:T(8,128)(2,1)S(1)}, u32[]{:S(2)}, u32[]{:S(2)}) %collective-permute-start.7) | collective-permute-done | bytes 110624 | tf_op jit(solution)/shard_map/ppermute | solution.py:694
  32.6 2.4 %collective-permute-start.8 = (bf16[72,768]{1,0:T(8,128)(2,1)S(1)}, bf16[72,768]{1,0:T(8,128)(2,1)S(1)}, u32[]{:S(2)}, u32[]{:S(2)}) collective-permute-start(bf16[72,768]{1,0:T(8,128)(2,1)S(1)} %relay.1), channel_id=1, source_target_pairs={{2,0},{3,1},{0,2},{1,3},{6,4},{7,5},{4,6},{5,7},{10,8},{11,9},{8,1... | collective-permute-start | bytes 331784 | tf_op jit(solution)/shard_map/ppermute | solution.py:694
  35.0 1.7 %backward.3.second = bf16[144,1152]{1,0:T(8,128)(2,1)S(1)} custom-call(bf16[144,768]{1,0:T(8,128)(2,1)S(1)} %merge.1.grad, bf16[3456,144]{1,0:T(8,128)(2,1)S(1)} %get-tuple-element.54.weights, bf16[144,2304]{1,0:T(8,128)(2,1)S(1)} %get-tuple-element.55.triple, bf16[768,144]{1,0:T(8,128)(2,1)S(1)} %get-tuple-element.56.keys_t, bf16[768,768]{1,0:T(8,128)(2,1)S(1)} %copy-done.3), custom_call_target="tpu_custom_call" | custom-call | flops 10000000000 | bytes 20000000 | tf_op jit(solution)/shard_map/backward/pallas_call | solution.py:561
  36.7 1.3 %finish.2 = (bf16[36,768]{1,0:T(8,128)(2,1)S(1)}, bf16[36,768]{1,0:T(8,128)(2,1)S(1)}) custom-call(bf16[144,768]{1,0:T(8,128)(2,1)S(1)} %merge.1.grad, bf16[144,1152]{1,0:T(8,128)(2,1)S(1)} %backward.2.first, bf16[144,1152]{1,0:T(8,128)(2,1)S(1)} %backward.3.second, bf16[144,768]{1,0:T(8,128)(2,1)S(1)} %get-tuple-element.64.tokens, ...), custom_call_target="tpu_custom_call" | custom-call | flops 10000000 | bytes 1000000 | tf_op jit(solution)/shard_map/finish/pallas_call | solution.py:590
  38.0 0.7 %collective-permute-start.9 = (bf16[36,768]{1,0:T(8,128)(2,1)S(1)}, bf16[36,768]{1,0:T(8,128)(2,1)S(1)}, u32[]{:S(2)}, u32[]{:S(2)}) collective-permute-start(bf16[36,768]{1,0:T(8,128)(2,1)S(1)} %get-tuple-element.67), channel_id=1, source_target_pairs={{2,0},{3,1},{0,2},{1,3},{6,4},{7,5},{4,6},{5,7},{10,8},{11,9},{8,1... | collective-permute-start | bytes 165896 | tf_op jit(solution)/shard_map/ppermute | solution.py:694
  38.8 1.3 %finish.3 = (bf16[36,768]{1,0:T(8,128)(2,1)S(1)}, bf16[36,768]{1,0:T(8,128)(2,1)S(1)}) custom-call(bf16[144,768]{1,0:T(8,128)(2,1)S(1)} %merge.1.grad, bf16[144,1152]{1,0:T(8,128)(2,1)S(1)} %backward.2.first, bf16[144,1152]{1,0:T(8,128)(2,1)S(1)} %backward.3.second, bf16[144,768]{1,0:T(8,128)(2,1)S(1)} %get-tuple-element.64.tokens, ...), custom_call_target="tpu_custom_call" | custom-call | flops 10000000 | bytes 1000000 | tf_op jit(solution)/shard_map/finish/pallas_call | solution.py:590
  40.1 1.0 %collective-permute-start.10 = (bf16[36,768]{1,0:T(8,128)(2,1)S(1)}, bf16[36,768]{1,0:T(8,128)(2,1)S(1)}, u32[]{:S(2)}, u32[]{:S(2)}) collective-permute-start(bf16[36,768]{1,0:T(8,128)(2,1)S(1)} %get-tuple-element.68), channel_id=1, source_target_pairs={{30,0},{31,1},{28,2},{29,3},{2,4},{3,5},{0,6},{1,7},{6,8},{7,9},{4... | collective-permute-start | bytes 165896 | tf_op jit(solution)/shard_map/ppermute | solution.py:694
  41.1 2.0 %collective-permute-start.11 = (bf16[36,768]{1,0:T(8,128)(2,1)S(1)}, bf16[36,768]{1,0:T(8,128)(2,1)S(1)}, u32[]{:S(2)}, u32[]{:S(2)}) collective-permute-start(bf16[36,768]{1,0:T(8,128)(2,1)S(1)} %get-tuple-element.70), channel_id=1, source_target_pairs={{28,0},{29,1},{30,2},{31,3},{0,4},{1,5},{2,6},{3,7},{4,8},{5,9},{6... | collective-permute-start | bytes 165896 | tf_op jit(solution)/shard_map/ppermute | solution.py:694
  43.1 0.0 collective-permute-done.8.onward
  43.1 1.2 %unpack_cells.1 = bf16[3,3,4,3072]{3,2,1,0:T(4,128)(2,1)} custom-call(bf16[72,768]{1,0:T(8,128)(2,1)S(1)} %collective-permute-done.6.near, bf16[72,768]{1,0:T(8,128)(2,1)S(1)} %collective-permute-done.7.cross, bf16[72,768]{1,0:T(8,128)(2,1)S(1)} %collective-permute-done.8.onward, f32[1,3072]{1,0:T(1,128)S(1)} %bitcast.6), custom_call_target="tpu_custom_call" | custom-call | flops 1000000 | bytes 100000 | tf_op jit(solution)/shard_map/unpack_cells/pallas_call | solution.py:667
  44.3 0.4 collective-permute-done.9.lat
  44.7 2.7 %collective-permute-done.10.both = bf16[36,768]{1,0:T(8,128)(2,1)S(1)} collective-permute-done((bf16[36,768]{1,0:T(8,128)(2,1)S(1)}, bf16[36,768]{1,0:T(8,128)(2,1)S(1)}, u32[]{:S(2)}, u32[]{:S(2)}) %collective-permute-start.10) | collective-permute-done | bytes 55328 | tf_op jit(solution)/shard_map/ppermute | solution.py:694
  47.4 0.0 collective-permute-done.11.lon
  47.4 0.7 %unpack_tokens.1 = bf16[6,12,2,768]{3,2,1,0:T(2,128)(2,1)} custom-call(bf16[36,768]{1,0:T(8,128)(2,1)S(1)} %get-tuple-element.72.own, bf16[36,768]{1,0:T(8,128)(2,1)S(1)} %collective-permute-done.9.lat, bf16[36,768]{1,0:T(8,128)(2,1)S(1)} %collective-permute-done.11.lon, bf16[36,768]{1,0:T(8,128)(2,1)S(1)} %collective-permute-done.10.both), custom_call_target="tpu_custom_call" | custom-call | tf_op jit(solution)/shard_map/unpack_tokens/pallas_call | solution.py:624
  (1 shorter events, 0.0 us)
Async XLA Ops:
  2.0 15.8 %collective-permute-start.1 = (bf16[36,768]{1,0:T(8,128)(2,1)S(1)}, bf16[36,768]{1,0:T(8,128)(2,1)S(1)}, u32[]{:S(2)}, u32[]{:S(2)}) collective-permute-start(bf16[36,768]{1,0:T(8,128)(2,1)S(1)} %get-tuple-element.41), channel_id=1, source_target_pairs={{0,2},{1,31},{2,0},{3,29},{4,6},{5,3},{6,4},{7,1},{8,10},{9,7},{10... | collective-permute-start | bytes 165896 | tf_op jit(solution)/shard_map/ppermute | solution.py:694
  6.0 16.2 %collective-permute-start.3 = (bf16[36,768]{1,0:T(8,128)(2,1)S(1)}, bf16[36,768]{1,0:T(8,128)(2,1)S(1)}, u32[]{:S(2)}, u32[]{:S(2)}) collective-permute-start(bf16[36,768]{1,0:T(8,128)(2,1)S(1)} %get-tuple-element.49), channel_id=1, source_target_pairs={{0,29},{1,0},{2,31},{3,2},{4,1},{5,4},{6,3},{7,6},{8,5},{9,8},{10,... | collective-permute-start | bytes 165896 | tf_op jit(solution)/shard_map/ppermute | solution.py:694
  9.2 13.0 %collective-permute-start.4 = (bf16[36,768]{1,0:T(8,128)(2,1)S(1)}, bf16[36,768]{1,0:T(8,128)(2,1)S(1)}, u32[]{:S(2)}, u32[]{:S(2)}) collective-permute-start(bf16[36,768]{1,0:T(8,128)(2,1)S(1)} %get-tuple-element.50), channel_id=1, source_target_pairs={{0,31},{1,2},{2,29},{3,0},{4,3},{5,6},{6,1},{7,4},{8,7},{9,10},{10... | collective-permute-start | bytes 165896 | tf_op jit(solution)/shard_map/ppermute | solution.py:694
  9.2 9.5 %collective-permute-start = (bf16[72,768]{1,0:T(8,128)(2,1)S(1)}, bf16[72,768]{1,0:T(8,128)(2,1)S(1)}, u32[]{:S(2)}, u32[]{:S(2)}) collective-permute-start(bf16[72,768]{1,0:T(8,128)(2,1)S(1)} %get-tuple-element.40), channel_id=1, source_target_pairs={{0,30},{1,3},{2,28},{3,1},{4,2},{5,7},{6,0},{7,5},{8,6},{9,11},{10... | collective-permute-start | bytes 331784 | tf_op jit(solution)/shard_map/ppermute | solution.py:694
  11.1 7.6 %collective-permute-start.2 = (bf16[72,768]{1,0:T(8,128)(2,1)S(1)}, bf16[72,768]{1,0:T(8,128)(2,1)S(1)}, u32[]{:S(2)}, u32[]{:S(2)}) collective-permute-start(bf16[72,768]{1,0:T(8,128)(2,1)S(1)} %get-tuple-element.42), channel_id=1, source_target_pairs={{0,28},{1,29},{2,30},{3,31},{4,0},{5,1},{6,2},{7,3},{8,4},{9,5},{1... | collective-permute-start | bytes 331784 | tf_op jit(solution)/shard_map/ppermute | solution.py:694
  11.1 7.6 %copy-start = (bf16[768,2304]{1,0:T(8,128)(2,1)S(1)}, bf16[768,2304]{1,0:T(8,128)(2,1)}, u32[]{:S(2)}) copy-start(bf16[768,2304]{1,0:T(8,128)(2,1)} %packed.5) | copy-start | bytes 10616836
  11.1 7.6 %copy-start.2 = (f32[768]{0:T(1024)S(1)}, f32[768]{0:T(1024)}, u32[]{:S(2)}) copy-start(f32[768]{0:T(1024)} %gain.5) | copy-start | bytes 9220
  11.1 7.6 %copy-start.3 = (bf16[768,768]{1,0:T(8,128)(2,1)S(1)}, bf16[768,768]{1,0:T(8,128)(2,1)}, u32[]{:S(2)}) copy-start(bf16[768,768]{1,0:T(8,128)(2,1)} %output.5) | copy-start | bytes 3538948
  18.8 3.5 %copy-start.1 = (f32[3072]{0:T(1024)S(1)}, f32[3072]{0:T(1024)}, u32[]{:S(2)}) copy-start(f32[3072]{0:T(1024)} %param.14) | copy-start | bytes 36868
  23.4 4.6 %collective-permute-start.5 = (f32[24,128]{1,0:T(8,128)S(1)}, f32[24,128]{1,0:T(8,128)S(1)}, u32[]{:S(2)}, u32[]{:S(2)}) collective-permute-start(f32[24,128]{1,0:T(8,128)S(1)} %get-tuple-element.53), channel_id=1, source_target_pairs={{0,2},{1,3},{2,0},{3,1},{4,6},{5,7},{6,4},{7,5},{8,10},{9,11},{10,... | collective-permute-start | bytes 36872 | tf_op jit(solution)/shard_map/ppermute | solution.py:694
  23.7 7.0 %collective-permute-start.6 = (bf16[72,768]{1,0:T(8,128)(2,1)S(1)}, bf16[72,768]{1,0:T(8,128)(2,1)S(1)}, u32[]{:S(2)}, u32[]{:S(2)}) collective-permute-start(bf16[72,768]{1,0:T(8,128)(2,1)S(1)} %get-tuple-element.57), channel_id=1, source_target_pairs={{28,0},{1,1},{30,2},{3,3},{0,4},{5,5},{2,6},{7,7},{4,8},{9,9},{6,1... | collective-permute-start | bytes 331784 | tf_op jit(solution)/shard_map/ppermute | solution.py:694
  25.8 6.8 %collective-permute-start.7 = (bf16[72,768]{1,0:T(8,128)(2,1)S(1)}, bf16[72,768]{1,0:T(8,128)(2,1)S(1)}, u32[]{:S(2)}, u32[]{:S(2)}) collective-permute-start(bf16[72,768]{1,0:T(8,128)(2,1)S(1)} %get-tuple-element.58), channel_id=1, source_target_pairs={{29,0},{0,1},{31,2},{2,3},{1,4},{4,5},{3,6},{6,7},{5,8},{8,9},{7,1... | collective-permute-start | bytes 331784 | tf_op jit(solution)/shard_map/ppermute | solution.py:694
  32.6 10.5 %collective-permute-start.8 = (bf16[72,768]{1,0:T(8,128)(2,1)S(1)}, bf16[72,768]{1,0:T(8,128)(2,1)S(1)}, u32[]{:S(2)}, u32[]{:S(2)}) collective-permute-start(bf16[72,768]{1,0:T(8,128)(2,1)S(1)} %relay.1), channel_id=1, source_target_pairs={{2,0},{3,1},{0,2},{1,3},{6,4},{7,5},{4,6},{5,7},{10,8},{11,9},{8,1... | collective-permute-start | bytes 331784 | tf_op jit(solution)/shard_map/ppermute | solution.py:694
  38.0 6.6 %collective-permute-start.9 = (bf16[36,768]{1,0:T(8,128)(2,1)S(1)}, bf16[36,768]{1,0:T(8,128)(2,1)S(1)}, u32[]{:S(2)}, u32[]{:S(2)}) collective-permute-start(bf16[36,768]{1,0:T(8,128)(2,1)S(1)} %get-tuple-element.67), channel_id=1, source_target_pairs={{2,0},{3,1},{0,2},{1,3},{6,4},{7,5},{4,6},{5,7},{10,8},{11,9},{8,1... | collective-permute-start | bytes 165896 | tf_op jit(solution)/shard_map/ppermute | solution.py:694
  40.1 7.3 %collective-permute-start.10 = (bf16[36,768]{1,0:T(8,128)(2,1)S(1)}, bf16[36,768]{1,0:T(8,128)(2,1)S(1)}, u32[]{:S(2)}, u32[]{:S(2)}) collective-permute-start(bf16[36,768]{1,0:T(8,128)(2,1)S(1)} %get-tuple-element.68), channel_id=1, source_target_pairs={{30,0},{31,1},{28,2},{29,3},{2,4},{3,5},{0,6},{1,7},{6,8},{7,9},{4... | collective-permute-start | bytes 165896 | tf_op jit(solution)/shard_map/ppermute | solution.py:694
  41.1 6.3 %collective-permute-start.11 = (bf16[36,768]{1,0:T(8,128)(2,1)S(1)}, bf16[36,768]{1,0:T(8,128)(2,1)S(1)}, u32[]{:S(2)}, u32[]{:S(2)}) collective-permute-start(bf16[36,768]{1,0:T(8,128)(2,1)S(1)} %get-tuple-element.70), channel_id=1, source_target_pairs={{28,0},{29,1},{30,2},{31,3},{0,4},{1,5},{2,6},{3,7},{4,8},{5,9},{6... | collective-permute-start | bytes 165896 | tf_op jit(solution)/shard_map/ppermute | solution.py:694

commit v8 on v7

--- a/solution.py
+++ b/solution.py
@@ -523,77 +523,67 @@
     )(residual, scaled, moments, before, after)
 
 
-def backward_kernel(half, grad, weights, triple, keys_t, output, joined, queries_t):
+def backward_kernel(grad, weights, triple, keys_t, output, joined, queries_t):
     width = grad.shape[-1]
-    part = width // 2
-    begin = half * part
-    arriving_all = mxu(grad[...], output[begin : begin + part, :], NT).astype(bf16)
-    for g in range(part // 128):
+    upstream = grad[...]
+    grad_heads = mxu(upstream, output[...], NT).astype(bf16)
+    for g in range(width // 128):
         here = slice(g * 128, (g + 1) * 128)
-        at = begin + g * 128
-        query = triple[:, at : at + 128]
-        value = triple[:, 2 * width + at : 2 * width + at + 128]
-        arriving = arriving_all[:, here]
+        query = triple[:, g * 128 : (g + 1) * 128]
+        value = triple[:, 2 * width + g * 128 : 2 * width + (g + 1) * 128]
+        arriving = grad_heads[:, here]
         product = mxu(stacked(value), arriving, NT)
-        first = at // HEAD
-        shares = weights[first * WIN : (first + GROUP) * WIN, :]
+        shares = weights[g * GROUP * WIN : (g + 1) * GROUP * WIN, :]
         grad_value = mxu(shares, arriving)
         slopes = []
         for h in range(GROUP):
+            head = g * GROUP + h
             share = shares[h * WIN : (h + 1) * WIN].astype(f32)
             change = product[h * WIN : (h + 1) * WIN]
             level = jnp.sum(share * change, axis=0, keepdims=True)
             slope = (share * (change - level) * HEAD ** (-0.5)).astype(bf16)
-            head = at + h * HEAD
-            queries_t[head - begin : head - begin + HEAD, :] = mxu(keys_t[head : head + HEAD, :], slope)
+            at = slice(head * HEAD, (head + 1) * HEAD)
+            queries_t[at, :] = mxu(keys_t[at, :], slope)
             slopes.append(slope)
         grad_key = mxu(jnp.concatenate(slopes, axis=0), query)
-        rows = [slice(h * WIN, (h + 1) * WIN) for h in range(GROUP)]
-        joined[:, part + g * 128 : part + (g + 1) * 128] = lanes_of([grad_key[r] for r in rows]).astype(bf16)
-        joined[:, 2 * part + g * 128 : 2 * part + (g + 1) * 128] = lanes_of(
-            [grad_value[r] for r in rows]
+        split = [slice(h * WIN, (h + 1) * WIN) for h in range(GROUP)]
+        joined[:, width + g * 128 : width + (g + 1) * 128] = lanes_of([grad_key[s] for s in split]).astype(bf16)
+        joined[:, 2 * width + g * 128 : 2 * width + (g + 1) * 128] = lanes_of(
+            [grad_value[s] for s in split]
         ).astype(bf16)
-    joined[:, :part] = queries_t[...].T.astype(bf16)
-
-
-def backward(half, grad, weights, triple, keys_t, output):
+    joined[:, :width] = queries_t[...].T.astype(bf16)
+
+
+def backward(grad, weights, triple, keys_t, output):
     width = grad.shape[-1]
     return pl.pallas_call(
-        functools.partial(backward_kernel, half),
-        out_shape=shape((WIN, 3 * width // 2), bf16),
-        scratch_shapes=[pltpu.VMEM((width // 2, WIN), f32)],
+        backward_kernel,
+        out_shape=shape((WIN, 3 * width), bf16),
+        scratch_shapes=[pltpu.VMEM((width, WIN), f32)],
         compiler_params=params(),
         cost_estimate=cost(10**10, 2 * 10**7),
         name="backward",
     )(grad, weights, triple, keys_t, output)
 
 
-def finish_kernel(quads, grad, first, second, tokens, packed, gain, *outs):
-    part = first.shape[-1] // 3
-
-    def rows(values):
-        values = values.astype(f32)
-        return jnp.concatenate([quadrant(values, quad) for quad in quads], axis=0)
-
-    joined = [half[:, i * part : (i + 1) * part] for i in range(3) for half in (first, second)]
-    joined = rows(jnp.concatenate(joined, axis=1)).astype(bf16)
-    grad_inputs = mxu(joined, packed[...], NT).astype(bf16)
-    unit, scale = unit_rows(rows(tokens[...]))
+def finish_kernel(grad, joined, tokens, packed, gain, own, lat, lon, both):
+    grad_inputs = mxu(joined[...], packed[...], NT).astype(bf16)
+    unit, scale = unit_rows(tokens[...].astype(f32))
     scaled = grad_inputs.astype(f32) * gain[...].reshape(1, -1)
-    out = rows(grad[...]) + scale * (scaled - row_mean(scaled) - unit * row_mean(scaled * unit))
-    for i, piece in enumerate(outs):
-        piece[...] = quadrant(out, i).astype(bf16)
-
-
-def finish(quads, grad, first, second, tokens, packed, gain, flops):
+    out = grad[...].astype(f32) + scale * (scaled - row_mean(scaled) - unit * row_mean(scaled * unit))
+    for quad, piece in enumerate((own, lat, lon, both)):
+        piece[...] = quadrant(out, quad).astype(bf16)
+
+
+def finish(grad, joined, tokens, packed, gain):
     width = grad.shape[-1]
     return pl.pallas_call(
-        functools.partial(finish_kernel, quads),
-        out_shape=[shape((QUAD, width), bf16)] * 2,
-        compiler_params=params(),
-        cost_estimate=cost(flops, 10**6),
+        finish_kernel,
+        out_shape=[shape((QUAD, width), bf16)] * 4,
+        compiler_params=params(),
+        cost_estimate=cost(10**10, 2 * 10**6),
         name="finish",
-    )(grad, first, second, tokens, packed, gain)
+    )(grad, joined, tokens, packed, gain)
 
 
 def relay_kernel(near, cross, out):
@@ -724,9 +714,10 @@
     first = send(first, sizes, FIRST)
     second = send(second, sizes, SECOND)
     third = send(third, sizes, THIRD)
+    main, tail = window_bias(table, index, row_labels, column_valid)
+    main, fourth, fifth = lax.optimization_barrier((main, fourth, fifth))
+    fifth = send(fifth, sizes, FIFTH)
     fourth = send(fourth, sizes, FOURTH)
-    fifth = send(fifth, sizes, FIFTH)
-    main, tail = window_bias(table, index, row_labels, column_valid)
     cell_gain = merge_gain.reshape(1, -1)
     weights, triple, keys_t, residual, data = forward(
         (own, first, second, third), packed_weight, output_weight, norm_gain, main, tail
@@ -739,14 +730,11 @@
     near = send(near, sizes, HERE, True)
     cross = send(cross, sizes, FOURTH, True)
     grad = merge_back(residual, scaled, moments, before, after)
-    first = backward(0, grad, weights, triple, keys_t, output_weight)
-    first, near, cross = lax.optimization_barrier((first, near, cross))
-    onward, grad = lax.optimization_barrier((relay(near, cross), grad))
+    joined = backward(grad, weights, triple, keys_t, output_weight)
+    joined, near, cross = lax.optimization_barrier((joined, near, cross))
+    onward, joined = lax.optimization_barrier((relay(near, cross), joined))
     onward = send(onward, sizes, LAT, True)
-    second = backward(1, grad, weights, triple, keys_t, output_weight)
-    lat, both = finish((1, 3), grad, first, second, data, packed_weight, norm_gain, 10**7)
-    lat, both, second = lax.optimization_barrier((lat, both, second))
-    own, lon = finish((0, 2), grad, first, second, data, packed_weight, norm_gain, 10**7)
+    own, lat, lon, both = finish(grad, joined, data, packed_weight, norm_gain)
     lat = send(lat, sizes, LAT, True)
     both = send(both, sizes, BOTH, True)
     lon = send(lon, sizes, LON, True)

time: 48.3 us -> 49 us (1.014)
  waiting for transfers between devices: 7.2 us -> 11.3 us
  Pallas kernels: 21.1 us -> 19.2 us
  starting transfers between devices: 19.1 us -> 17.6 us
    ppermute x12, waiting for transfers between devices: 7.2 us -> 11.3 us  [send(): return lax.ppermute(block, ('lon', 'lat', 'lev'), pairs)]
    pallas_call x4 -> x2, Pallas kernels: 6.11 us -> 4.28 us  [the longest x1 2.76 us: backward(): pl.pallas_call(backward_kernel, out_shape=shape((WIN, 3 * width), bf16),...]
    ppermute x12, starting transfers between devices: 19.1 us -> 17.6 us  [send(): return lax.ppermute(block, ('lon', 'lat', 'lev'), pairs)]
  transfers between devices with their start and end apart: 12 -> 12, of which waited for: 6 -> 7; matrix products, arithmetic and copies ran while one was open for 0% -> 0% of each run, Pallas kernels for 37% -> 33%
where the time goes in v8:
time: 49 us; the launch traced here: 48.8 us
  Pallas kernels  19.2 us (39%)
  starting transfers between devices  17.6 us (36%)
  waiting for transfers between devices  11.3 us (23%)
  between operations  0.74 us (2%)
    ppermute x12, starting transfers between devices, send(): return lax.ppermute(block, ('lon', 'lat', 'lev'), pairs)  17.6 us
    ppermute x12, waiting for transfers between devices, send(): return lax.ppermute(block, ('lon', 'lat', 'lev'), pairs)  11.3 us
    pallas_call x1, Pallas kernels, window_bias(): pl.pallas_call(bias_kernel, out_shape=[shape((heads * WIN, 128), f32)] *...  6.57 us
    pallas_call x1, Pallas kernels, forward(): pl.pallas_call(forward_kernel, out_shape=[shape((HEADS * WIN, WIN), bf16)...  3.34 us
    pallas_call x1, Pallas kernels, backward(): pl.pallas_call(backward_kernel, out_shape=shape((WIN, 3 * width), bf16),...  2.76 us
    pallas_call x1, Pallas kernels, finish(): pl.pallas_call(finish_kernel, out_shape=[shape((QUAD, width), bf16)] * 4,...  1.52 us
    pallas_call x1, Pallas kernels, pack_pieces(): pl.pallas_call(pack_kernel, out_shape=[piece, double, piece, double, piec...  1.32 us
    pallas_call x1, Pallas kernels, unpack_cells(): pl.pallas_call(cell_kernel, out_shape=shape((HALF_LAT, PAIRS, 2 * LEVELS,...  1.21 us
  transfers between devices with their start and end apart: 12, of which 7 were waited for; matrix products, arithmetic and copies ran while one was open for 0% of the time, Pallas kernels for 33%

profile of v8, /device:TPU:0, one launch (start us, length us, event | category | flops | bytes accessed | tf_op | source)
XLA Modules:
  0.0 48.8 jit_solution(3387081218136938513)
XLA Ops:
  0.6 1.3 %pack.1 = (bf16[36,768]{1,0:T(8,128)(2,1)S(1)}, bf16[72,768]{1,0:T(8,128)(2,1)S(1)}, bf16[36,768]{1,0:T(8,128)(2,1)S(1)}, bf16[72,768]{1,0:T(8,128)(2,1)S(1)}, b...) custom-call(bf16[6,12,2,768]{3,2,1,0:T(2,128)(2,1)} %bitcast.7, ...), custom_call_target="tpu_custom_call" | custom-call | tf_op jit(solution)/shard_map/pack/pallas_call | solution.py:140
  2.0 4.1 %collective-permute-start.1 = (bf16[36,768]{1,0:T(8,128)(2,1)S(1)}, bf16[36,768]{1,0:T(8,128)(2,1)S(1)}, u32[]{:S(2)}, u32[]{:S(2)}) collective-permute-start(bf16[36,768]{1,0:T(8,128)(2,1)S(1)} %get-tuple-element.41), channel_id=1, source_target_pairs={{0,2},{1,31},{2,0},{3,29},{4,6},{5,3},{6,4},{7,1},{8,10},{9,7},{10... | collective-permute-start | bytes 165896 | tf_op jit(solution)/shard_map/ppermute | solution.py:684
  6.0 1.4 %collective-permute-start = (bf16[72,768]{1,0:T(8,128)(2,1)S(1)}, bf16[72,768]{1,0:T(8,128)(2,1)S(1)}, u32[]{:S(2)}, u32[]{:S(2)}) collective-permute-start(bf16[72,768]{1,0:T(8,128)(2,1)S(1)} %get-tuple-element.40), channel_id=1, source_target_pairs={{0,30},{1,3},{2,28},{3,1},{4,2},{5,7},{6,0},{7,5},{8,6},{9,11},{10... | collective-permute-start | bytes 331784 | tf_op jit(solution)/shard_map/ppermute | solution.py:684
  7.4 1.1 %collective-permute-start.2 = (bf16[72,768]{1,0:T(8,128)(2,1)S(1)}, bf16[72,768]{1,0:T(8,128)(2,1)S(1)}, u32[]{:S(2)}, u32[]{:S(2)}) collective-permute-start(bf16[72,768]{1,0:T(8,128)(2,1)S(1)} %get-tuple-element.42), channel_id=1, source_target_pairs={{0,28},{1,29},{2,30},{3,31},{4,0},{5,1},{6,2},{7,3},{8,4},{9,5},{1... | collective-permute-start | bytes 331784 | tf_op jit(solution)/shard_map/ppermute | solution.py:684
  8.5 0.0 copy-start.1
  8.6 0.0 copy-start.2
  8.6 0.0 copy-start.3
  8.6 6.6 %bias.1 = (f32[3456,128]{1,0:T(8,128)S(1)}, f32[3456,128]{1,0:T(8,128)S(1)}) custom-call(f32[24,3312]{1,0:T(8,128)S(1)} %get-tuple-element.43.table, s32[144,144]{1,0:T(8,128)S(1)} %get-tuple-element.44.index, s32[6]{0:T(128)} %labels_at.1, s32[96]{0:T(128)} %valid_at.1), custom_call_target="tpu_custom_call" | custom-call | flops 10000000000 | bytes 20000000 | tf_op jit(solution)/shard_map/bias/pallas_call | solution.py:289
  15.1 1.2 %collective-permute-start.3 = (bf16[36,768]{1,0:T(8,128)(2,1)S(1)}, bf16[36,768]{1,0:T(8,128)(2,1)S(1)}, u32[]{:S(2)}, u32[]{:S(2)}) collective-permute-start(bf16[36,768]{1,0:T(8,128)(2,1)S(1)} %get-tuple-element.52), channel_id=1, source_target_pairs={{0,29},{1,0},{2,31},{3,2},{4,1},{5,4},{6,3},{7,6},{8,5},{9,8},{10,... | collective-permute-start | bytes 165896 | tf_op jit(solution)/shard_map/ppermute | solution.py:684
  16.4 2.1 %collective-permute-start.4 = (bf16[36,768]{1,0:T(8,128)(2,1)S(1)}, bf16[36,768]{1,0:T(8,128)(2,1)S(1)}, u32[]{:S(2)}, u32[]{:S(2)}) collective-permute-start(bf16[36,768]{1,0:T(8,128)(2,1)S(1)} %get-tuple-element.53), channel_id=1, source_target_pairs={{0,31},{1,2},{2,29},{3,0},{4,3},{5,6},{6,1},{7,4},{8,7},{9,10},{10... | collective-permute-start | bytes 165896 | tf_op jit(solution)/shard_map/ppermute | solution.py:684
  18.4 0.0 collective-permute-done.1.second
  18.4 0.0 collective-permute-done.first
  18.4 0.0 collective-permute-done.2.third
  18.4 0.0 copy-done.1
  18.4 0.0 copy-done.2
  18.4 0.0 copy-done.3
  18.5 0.0 copy-start
  18.5 3.3 %forward.1 = (bf16[3456,144]{1,0:T(8,128)(2,1)S(1)}, bf16[144,2304]{1,0:T(8,128)(2,1)S(1)}, bf16[768,144]{1,0:T(8,128)(2,1)S(1)}, bf16[144,768]{1,0:T(8,128)(2,1)S(1)}, bf16[144,768]{1,0:T(8,128)(2,1)S(1)}) custom-call(bf16[36,768]{1,0:T(8,128)(2,1)S(1)} %get-tuple-element.39.own, bf16[72,768]{1,0:T(8,128)(2,1)S(1)} %collective-permute-done.first, ...), custom_call_target="tpu_custom_call" | custom-call | flops 10000000000 | bytes 20000000 | tf_op jit(solution)/shard_map/forward/pallas_call | solution.py:378
  21.8 0.0 collective-permute-done.3.fourth
  21.8 0.9 %collective-permute-done.4.fifth = bf16[36,768]{1,0:T(8,128)(2,1)S(1)} collective-permute-done((bf16[36,768]{1,0:T(8,128)(2,1)S(1)}, bf16[36,768]{1,0:T(8,128)(2,1)S(1)}, u32[]{:S(2)}, u32[]{:S(2)}) %collective-permute-start.4) | collective-permute-done | bytes 55328 | tf_op jit(solution)/shard_map/ppermute | solution.py:684
  22.8 0.0 copy-done
  22.8 1.2 %moments.1 = (f32[144,768]{1,0:T(8,128)S(1)}, f32[144,128]{1,0:T(8,128)S(1)}, f32[24,128]{1,0:T(8,128)S(1)}, bf16[72,768]{1,0:T(8,128)(2,1)S(1)}, bf16[72,768]{1,0:T(8,128)(2,1)S(1)}) custom-call(bf16[144,768]{1,0:T(8,128)(2,1)S(1)} %get-tuple-element.50.residual, bf16[36,768]{1,0:T(8,128)(2,1)S(1)} %get-tuple-element.51.kept, ...), custom_call_target="tpu_custom_call" | custom-call | flops 100000000 | bytes 1000000 | tf_op jit(solution)/shard_map/moments/pallas_call | solution.py:479
  23.9 1.7 %collective-permute-start.5 = (f32[24,128]{1,0:T(8,128)S(1)}, f32[24,128]{1,0:T(8,128)S(1)}, u32[]{:S(2)}, u32[]{:S(2)}) collective-permute-start(f32[24,128]{1,0:T(8,128)S(1)} %get-tuple-element.56), channel_id=1, source_target_pairs={{0,2},{1,3},{2,0},{3,1},{4,6},{5,7},{6,4},{7,5},{8,10},{9,11},{10,... | collective-permute-start | bytes 36872 | tf_op jit(solution)/shard_map/ppermute | solution.py:684
  25.6 1.9 %collective-permute-start.6 = (bf16[72,768]{1,0:T(8,128)(2,1)S(1)}, bf16[72,768]{1,0:T(8,128)(2,1)S(1)}, u32[]{:S(2)}, u32[]{:S(2)}) collective-permute-start(bf16[72,768]{1,0:T(8,128)(2,1)S(1)} %get-tuple-element.60), channel_id=1, source_target_pairs={{28,0},{1,1},{30,2},{3,3},{0,4},{5,5},{2,6},{7,7},{4,8},{9,9},{6,1... | collective-permute-start | bytes 331784 | tf_op jit(solution)/shard_map/ppermute | solution.py:684
  27.6 0.3 collective-permute-start.7
  27.9 0.7 %collective-permute-done.5.before.after = f32[24,128]{1,0:T(8,128)S(1)} collective-permute-done((f32[24,128]{1,0:T(8,128)S(1)}, f32[24,128]{1,0:T(8,128)S(1)}, u32[]{:S(2)}, u32[]{:S(2)}) %collective-permute-start.5) | collective-permute-done | bytes 12320 | tf_op jit(solution)/shard_map/ppermute | solution.py:684
  28.6 0.5 %merge.1.grad = bf16[144,768]{1,0:T(8,128)(2,1)S(1)} custom-call(bf16[144,768]{1,0:T(8,128)(2,1)S(1)} %get-tuple-element.50.residual, f32[144,768]{1,0:T(8,128)S(1)} %get-tuple-element.54.scaled, f32[144,128]{1,0:T(8,128)S(1)} %get-tuple-element.55.moments, f32[24,128]{1,0:T(8,128)S(1)} %collective-permute-done.5.before.after, ...), custom_call_target="tpu_custom_call" | custom-call | flops 100000000 | bytes 1000000 | tf_op jit(solution)/shard_map/merge/pallas_call | solution.py:517
  29.1 2.8 %backward.1.joined = bf16[144,2304]{1,0:T(8,128)(2,1)S(1)} custom-call(bf16[144,768]{1,0:T(8,128)(2,1)S(1)} %merge.1.grad, bf16[3456,144]{1,0:T(8,128)(2,1)S(1)} %get-tuple-element.57.weights, bf16[144,2304]{1,0:T(8,128)(2,1)S(1)} %get-tuple-element.58.triple, bf16[768,144]{1,0:T(8,128)(2,1)S(1)} %get-tuple-element.59.keys_t, bf16[768,768]{1,0:T(8,128)(2,1)S(1)} %copy-done.2), custom_call_target="tpu_custom_call" | custom-call | flops 10000000000 | bytes 20000000 | tf_op jit(solution)/shard_map/backward/pallas_call | solution.py:559
  31.9 0.7 %collective-permute-done.6.near = bf16[72,768]{1,0:T(8,128)(2,1)S(1)} collective-permute-done((bf16[72,768]{1,0:T(8,128)(2,1)S(1)}, bf16[72,768]{1,0:T(8,128)(2,1)S(1)}, u32[]{:S(2)}, u32[]{:S(2)}) %collective-permute-start.6) | collective-permute-done | bytes 110624 | tf_op jit(solution)/shard_map/ppermute | solution.py:684
  32.6 1.5 %collective-permute-done.7.cross = bf16[72,768]{1,0:T(8,128)(2,1)S(1)} collective-permute-done((bf16[72,768]{1,0:T(8,128)(2,1)S(1)}, bf16[72,768]{1,0:T(8,128)(2,1)S(1)}, u32[]{:S(2)}, u32[]{:S(2)}) %collective-permute-start.7) | collective-permute-done | bytes 110624 | tf_op jit(solution)/shard_map/ppermute | solution.py:684
  34.2 1.3 %collective-permute-start.8 = (bf16[72,768]{1,0:T(8,128)(2,1)S(1)}, bf16[72,768]{1,0:T(8,128)(2,1)S(1)}, u32[]{:S(2)}, u32[]{:S(2)}) collective-permute-start(bf16[72,768]{1,0:T(8,128)(2,1)S(1)} %relay.1), channel_id=1, source_target_pairs={{2,0},{3,1},{0,2},{1,3},{6,4},{7,5},{4,6},{5,7},{10,8},{11,9},{8,1... | collective-permute-start | bytes 331784 | tf_op jit(solution)/shard_map/ppermute | solution.py:684
  35.5 1.5 %finish.1 = (bf16[36,768]{1,0:T(8,128)(2,1)S(1)}, bf16[36,768]{1,0:T(8,128)(2,1)S(1)}, bf16[36,768]{1,0:T(8,128)(2,1)S(1)}, bf16[36,768]{1,0:T(8,128)(2,1)S(1)}) custom-call(bf16[144,768]{1,0:T(8,128)(2,1)S(1)} %merge.1.grad, bf16[144,2304]{1,0:T(8,128)(2,1)S(1)} %backward.1.joined, bf16[144,768]{1,0:T(8,128)(2,1)S(1)} %get-tuple-element.67.tokens, ...), custom_call_target="tpu_custom_call" | custom-call | flops 10000000000 | bytes 2000000 | tf_op jit(solution)/shard_map/finish/pallas_call | solution.py:580
  37.0 1.7 %collective-permute-start.9 = (bf16[36,768]{1,0:T(8,128)(2,1)S(1)}, bf16[36,768]{1,0:T(8,128)(2,1)S(1)}, u32[]{:S(2)}, u32[]{:S(2)}) collective-permute-start(bf16[36,768]{1,0:T(8,128)(2,1)S(1)} %get-tuple-element.68), channel_id=1, source_target_pairs={{2,0},{3,1},{0,2},{1,3},{6,4},{7,5},{4,6},{5,7},{10,8},{11,9},{8,1... | collective-permute-start | bytes 165896 | tf_op jit(solution)/shard_map/ppermute | solution.py:684
  38.7 0.0 collective-permute-start.10
  38.7 0.7 %collective-permute-start.11 = (bf16[36,768]{1,0:T(8,128)(2,1)S(1)}, bf16[36,768]{1,0:T(8,128)(2,1)S(1)}, u32[]{:S(2)}, u32[]{:S(2)}) collective-permute-start(bf16[36,768]{1,0:T(8,128)(2,1)S(1)} %get-tuple-element.70), channel_id=1, source_target_pairs={{28,0},{29,1},{30,2},{31,3},{0,4},{1,5},{2,6},{3,7},{4,8},{5,9},{6... | collective-permute-start | bytes 165896 | tf_op jit(solution)/shard_map/ppermute | solution.py:684
  39.5 4.7 %collective-permute-done.8.onward = bf16[72,768]{1,0:T(8,128)(2,1)S(1)} collective-permute-done((bf16[72,768]{1,0:T(8,128)(2,1)S(1)}, bf16[72,768]{1,0:T(8,128)(2,1)S(1)}, u32[]{:S(2)}, u32[]{:S(2)}) %collective-permute-start.8) | collective-permute-done | bytes 110624 | tf_op jit(solution)/shard_map/ppermute | solution.py:684
  44.2 1.2 %unpack_cells.1 = bf16[3,3,4,3072]{3,2,1,0:T(4,128)(2,1)} custom-call(bf16[72,768]{1,0:T(8,128)(2,1)S(1)} %collective-permute-done.6.near, bf16[72,768]{1,0:T(8,128)(2,1)S(1)} %collective-permute-done.7.cross, bf16[72,768]{1,0:T(8,128)(2,1)S(1)} %collective-permute-done.8.onward, f32[1,3072]{1,0:T(1,128)S(1)} %bitcast.6), custom_call_target="tpu_custom_call" | custom-call | flops 1000000 | bytes 100000 | tf_op jit(solution)/shard_map/unpack_cells/pallas_call | solution.py:657
  45.4 0.1 collective-permute-done.9.lat
  45.5 2.6 %collective-permute-done.10.both = bf16[36,768]{1,0:T(8,128)(2,1)S(1)} collective-permute-done((bf16[36,768]{1,0:T(8,128)(2,1)S(1)}, bf16[36,768]{1,0:T(8,128)(2,1)S(1)}, u32[]{:S(2)}, u32[]{:S(2)}) %collective-permute-start.10) | collective-permute-done | bytes 55328 | tf_op jit(solution)/shard_map/ppermute | solution.py:684
  48.1 0.0 collective-permute-done.11.lon
  48.1 0.7 %unpack_tokens.1 = bf16[6,12,2,768]{3,2,1,0:T(2,128)(2,1)} custom-call(bf16[36,768]{1,0:T(8,128)(2,1)S(1)} %get-tuple-element.72.own, bf16[36,768]{1,0:T(8,128)(2,1)S(1)} %collective-permute-done.9.lat, bf16[36,768]{1,0:T(8,128)(2,1)S(1)} %collective-permute-done.11.lon, bf16[36,768]{1,0:T(8,128)(2,1)S(1)} %collective-permute-done.10.both), custom_call_target="tpu_custom_call" | custom-call | tf_op jit(solution)/shard_map/unpack_tokens/pallas_call | solution.py:614
  (1 shorter events, 0.0 us)
Async XLA Ops:
  2.0 16.5 %collective-permute-start.1 = (bf16[36,768]{1,0:T(8,128)(2,1)S(1)}, bf16[36,768]{1,0:T(8,128)(2,1)S(1)}, u32[]{:S(2)}, u32[]{:S(2)}) collective-permute-start(bf16[36,768]{1,0:T(8,128)(2,1)S(1)} %get-tuple-element.41), channel_id=1, source_target_pairs={{0,2},{1,31},{2,0},{3,29},{4,6},{5,3},{6,4},{7,1},{8,10},{9,7},{10... | collective-permute-start | bytes 165896 | tf_op jit(solution)/shard_map/ppermute | solution.py:684
  6.0 12.4 %collective-permute-start = (bf16[72,768]{1,0:T(8,128)(2,1)S(1)}, bf16[72,768]{1,0:T(8,128)(2,1)S(1)}, u32[]{:S(2)}, u32[]{:S(2)}) collective-permute-start(bf16[72,768]{1,0:T(8,128)(2,1)S(1)} %get-tuple-element.40), channel_id=1, source_target_pairs={{0,30},{1,3},{2,28},{3,1},{4,2},{5,7},{6,0},{7,5},{8,6},{9,11},{10... | collective-permute-start | bytes 331784 | tf_op jit(solution)/shard_map/ppermute | solution.py:684
  7.4 11.0 %collective-permute-start.2 = (bf16[72,768]{1,0:T(8,128)(2,1)S(1)}, bf16[72,768]{1,0:T(8,128)(2,1)S(1)}, u32[]{:S(2)}, u32[]{:S(2)}) collective-permute-start(bf16[72,768]{1,0:T(8,128)(2,1)S(1)} %get-tuple-element.42), channel_id=1, source_target_pairs={{0,28},{1,29},{2,30},{3,31},{4,0},{5,1},{6,2},{7,3},{8,4},{9,5},{1... | collective-permute-start | bytes 331784 | tf_op jit(solution)/shard_map/ppermute | solution.py:684
  8.5 9.9 %copy-start.1 = (bf16[768,2304]{1,0:T(8,128)(2,1)S(1)}, bf16[768,2304]{1,0:T(8,128)(2,1)}, u32[]{:S(2)}) copy-start(bf16[768,2304]{1,0:T(8,128)(2,1)} %packed.3) | copy-start | bytes 10616836
  8.6 9.9 %copy-start.2 = (bf16[768,768]{1,0:T(8,128)(2,1)S(1)}, bf16[768,768]{1,0:T(8,128)(2,1)}, u32[]{:S(2)}) copy-start(bf16[768,768]{1,0:T(8,128)(2,1)} %output.3) | copy-start | bytes 3538948
  8.6 9.9 %copy-start.3 = (f32[768]{0:T(1024)S(1)}, f32[768]{0:T(1024)}, u32[]{:S(2)}) copy-start(f32[768]{0:T(1024)} %gain.3) | copy-start | bytes 9220
  15.1 6.7 %collective-permute-start.3 = (bf16[36,768]{1,0:T(8,128)(2,1)S(1)}, bf16[36,768]{1,0:T(8,128)(2,1)S(1)}, u32[]{:S(2)}, u32[]{:S(2)}) collective-permute-start(bf16[36,768]{1,0:T(8,128)(2,1)S(1)} %get-tuple-element.52), channel_id=1, source_target_pairs={{0,29},{1,0},{2,31},{3,2},{4,1},{5,4},{6,3},{7,6},{8,5},{9,8},{10,... | collective-permute-start | bytes 165896 | tf_op jit(solution)/shard_map/ppermute | solution.py:684
  16.4 6.4 %collective-permute-start.4 = (bf16[36,768]{1,0:T(8,128)(2,1)S(1)}, bf16[36,768]{1,0:T(8,128)(2,1)S(1)}, u32[]{:S(2)}, u32[]{:S(2)}) collective-permute-start(bf16[36,768]{1,0:T(8,128)(2,1)S(1)} %get-tuple-element.53), channel_id=1, source_target_pairs={{0,31},{1,2},{2,29},{3,0},{4,3},{5,6},{6,1},{7,4},{8,7},{9,10},{10... | collective-permute-start | bytes 165896 | tf_op jit(solution)/shard_map/ppermute | solution.py:684
  18.5 4.3 %copy-start = (f32[3072]{0:T(1024)S(1)}, f32[3072]{0:T(1024)}, u32[]{:S(2)}) copy-start(f32[3072]{0:T(1024)} %param.14) | copy-start | bytes 36868
  23.9 4.6 %collective-permute-start.5 = (f32[24,128]{1,0:T(8,128)S(1)}, f32[24,128]{1,0:T(8,128)S(1)}, u32[]{:S(2)}, u32[]{:S(2)}) collective-permute-start(f32[24,128]{1,0:T(8,128)S(1)} %get-tuple-element.56), channel_id=1, source_target_pairs={{0,2},{1,3},{2,0},{3,1},{4,6},{5,7},{6,4},{7,5},{8,10},{9,11},{10,... | collective-permute-start | bytes 36872 | tf_op jit(solution)/shard_map/ppermute | solution.py:684
  25.6 7.0 %collective-permute-start.6 = (bf16[72,768]{1,0:T(8,128)(2,1)S(1)}, bf16[72,768]{1,0:T(8,128)(2,1)S(1)}, u32[]{:S(2)}, u32[]{:S(2)}) collective-permute-start(bf16[72,768]{1,0:T(8,128)(2,1)S(1)} %get-tuple-element.60), channel_id=1, source_target_pairs={{28,0},{1,1},{30,2},{3,3},{0,4},{5,5},{2,6},{7,7},{4,8},{9,9},{6,1... | collective-permute-start | bytes 331784 | tf_op jit(solution)/shard_map/ppermute | solution.py:684
  27.6 6.6 %collective-permute-start.7 = (bf16[72,768]{1,0:T(8,128)(2,1)S(1)}, bf16[72,768]{1,0:T(8,128)(2,1)S(1)}, u32[]{:S(2)}, u32[]{:S(2)}) collective-permute-start(bf16[72,768]{1,0:T(8,128)(2,1)S(1)} %get-tuple-element.61), channel_id=1, source_target_pairs={{29,0},{0,1},{31,2},{2,3},{1,4},{4,5},{3,6},{6,7},{5,8},{8,9},{7,1... | collective-permute-start | bytes 331784 | tf_op jit(solution)/shard_map/ppermute | solution.py:684
  34.2 10.0 %collective-permute-start.8 = (bf16[72,768]{1,0:T(8,128)(2,1)S(1)}, bf16[72,768]{1,0:T(8,128)(2,1)S(1)}, u32[]{:S(2)}, u32[]{:S(2)}) collective-permute-start(bf16[72,768]{1,0:T(8,128)(2,1)S(1)} %relay.1), channel_id=1, source_target_pairs={{2,0},{3,1},{0,2},{1,3},{6,4},{7,5},{4,6},{5,7},{10,8},{11,9},{8,1... | collective-permute-start | bytes 331784 | tf_op jit(solution)/shard_map/ppermute | solution.py:684
  37.0 8.5 %collective-permute-start.9 = (bf16[36,768]{1,0:T(8,128)(2,1)S(1)}, bf16[36,768]{1,0:T(8,128)(2,1)S(1)}, u32[]{:S(2)}, u32[]{:S(2)}) collective-permute-start(bf16[36,768]{1,0:T(8,128)(2,1)S(1)} %get-tuple-element.68), channel_id=1, source_target_pairs={{2,0},{3,1},{0,2},{1,3},{6,4},{7,5},{4,6},{5,7},{10,8},{11,9},{8,1... | collective-permute-start | bytes 165896 | tf_op jit(solution)/shard_map/ppermute | solution.py:684
  38.7 9.4 %collective-permute-start.10 = (bf16[36,768]{1,0:T(8,128)(2,1)S(1)}, bf16[36,768]{1,0:T(8,128)(2,1)S(1)}, u32[]{:S(2)}, u32[]{:S(2)}) collective-permute-start(bf16[36,768]{1,0:T(8,128)(2,1)S(1)} %get-tuple-element.69), channel_id=1, source_target_pairs={{30,0},{31,1},{28,2},{29,3},{2,4},{3,5},{0,6},{1,7},{6,8},{7,9},{4... | collective-permute-start | bytes 165896 | tf_op jit(solution)/shard_map/ppermute | solution.py:684
  38.7 9.4 %collective-permute-start.11 = (bf16[36,768]{1,0:T(8,128)(2,1)S(1)}, bf16[36,768]{1,0:T(8,128)(2,1)S(1)}, u32[]{:S(2)}, u32[]{:S(2)}) collective-permute-start(bf16[36,768]{1,0:T(8,128)(2,1)S(1)} %get-tuple-element.70), channel_id=1, source_target_pairs={{28,0},{29,1},{30,2},{31,3},{0,4},{1,5},{2,6},{3,7},{4,8},{5,9},{6... | collective-permute-start | bytes 165896 | tf_op jit(solution)/shard_map/ppermute | solution.py:684

commit v9 on v8

--- a/solution.py
+++ b/solution.py
@@ -434,7 +434,7 @@
     return out
 
 
-def moments_kernel(residual, kept, first, third, fourth, fifth, gain, scaled, moments, sent, near, over, factors):
+def moments_kernel(residual, kept, first, third, fourth, fifth, gain, scaled, moments, sent, same_here, same_next, other_here, other_next, factors):
     width = residual.shape[-1]
     upper = lax.axis_index("lev") == 1
     own, a, b = kept[...].astype(f32), fourth[...].astype(f32), fifth[...].astype(f32)
@@ -469,9 +469,11 @@
     sent[...] = exact(jnp.where(pick, 1.0, 0.0).astype(f32), sums)
     scale = lax.rsqrt(sums[:, 0:1] * (1 / (4 * width)) + epsilon)
     out = jnp.where(split_row(down), data, center * scale * factors[...])
-    left, right = out[: 2 * QUAD], out[2 * QUAD :]
-    near[...] = jnp.where(upper, left, right).astype(bf16)
-    over[...] = jnp.where(upper, right, left).astype(bf16)
+    parts = [quadrant(out, quad) for quad in range(4)]
+    same_here[...] = jnp.where(upper, parts[0], parts[2]).astype(bf16)
+    same_next[...] = jnp.where(upper, parts[1], parts[3]).astype(bf16)
+    other_here[...] = jnp.where(upper, parts[2], parts[0]).astype(bf16)
+    other_next[...] = jnp.where(upper, parts[3], parts[1]).astype(bf16)
 
 
 def cell_moments(residual, pieces, gain):
@@ -479,7 +481,7 @@
     return pl.pallas_call(
         moments_kernel,
         out_shape=[shape((WIN, width), f32), shape((WIN, 128), f32), shape((4 * CELLS, 128), f32)]
-        + [shape((2 * QUAD, width), bf16)] * 2,
+        + [shape((QUAD, width), bf16)] * 4,
         scratch_shapes=[pltpu.VMEM((WIN, width), f32)],
         compiler_params=params(),
         cost_estimate=cost(10**8, 10**6),
@@ -586,19 +588,6 @@
     )(grad, joined, tokens, packed, gain)
 
 
-def relay_kernel(near, cross, out):
-    out[...] = jnp.concatenate((near[...].astype(f32)[QUAD:], cross[...].astype(f32)[QUAD:]), axis=0).astype(bf16)
-
-
-def relay(near, cross):
-    return pl.pallas_call(
-        relay_kernel,
-        out_shape=shape(near.shape, bf16),
-        compiler_params=params(),
-        name="relay",
-    )(near, cross)
-
-
 def token_kernel(own, lat, lon, both, tokens):
     quads = [piece[...].astype(f32) for piece in (own, lat, lon, both)]
     for line in range(WLAT):
@@ -619,12 +608,11 @@
     )(*pieces)
 
 
-def cell_kernel(near, cross, onward, gain, merged):
-    width = near.shape[-1]
+def cell_kernel(same_here, same_next, other_here, other_next, gain, merged):
+    width = same_here.shape[-1]
     upper = lax.axis_index("lev") == 1
-    arrived = onward[...].astype(f32)
-    same = (near[...].astype(f32)[:QUAD], arrived[:QUAD])
-    other = (cross[...].astype(f32)[:QUAD], arrived[QUAD:])
+    same = (same_here[...].astype(f32), same_next[...].astype(f32))
+    other = (other_here[...].astype(f32), other_next[...].astype(f32))
     levels = (
         [jnp.where(upper, b, a) for a, b in zip(same, other)],
         [jnp.where(upper, a, b) for a, b in zip(same, other)],
@@ -652,15 +640,15 @@
                 ).astype(bf16)
 
 
-def unpack_cells(near, cross, onward, gain):
-    width = near.shape[-1]
+def unpack_cells(pieces, gain):
+    width = pieces[0].shape[-1]
     return pl.pallas_call(
         cell_kernel,
         out_shape=shape((HALF_LAT, PAIRS, 2 * LEVELS, 4 * width), bf16),
         compiler_params=params(),
-        cost_estimate=cost(10**6, 10**5),
+        cost_estimate=cost(10**9, 10**6),
         name="unpack_cells",
-    )(near, cross, onward, gain)
+    )(*pieces, gain)
 
 
 def routes(sizes, target):
@@ -714,31 +702,27 @@
     first = send(first, sizes, FIRST)
     second = send(second, sizes, SECOND)
     third = send(third, sizes, THIRD)
+    fourth = send(fourth, sizes, FOURTH)
+    fifth = send(fifth, sizes, FIFTH)
     main, tail = window_bias(table, index, row_labels, column_valid)
-    main, fourth, fifth = lax.optimization_barrier((main, fourth, fifth))
-    fifth = send(fifth, sizes, FIFTH)
-    fourth = send(fourth, sizes, FOURTH)
     cell_gain = merge_gain.reshape(1, -1)
     weights, triple, keys_t, residual, data = forward(
         (own, first, second, third), packed_weight, output_weight, norm_gain, main, tail
     )
-    scaled, moments, sent, near, cross = cell_moments(
+    scaled, moments, sent, *merged = cell_moments(
         residual, (kept, first, third, fourth, fifth), cell_gain
     )
     before = send(sent, sizes, lambda i, a, k: (i, a + 1, k))
     after = before if sizes[1] == 2 else send(sent, sizes, lambda i, a, k: (i, a - 1, k))
-    near = send(near, sizes, HERE, True)
-    cross = send(cross, sizes, FOURTH, True)
+    merged = [send(x, sizes, target, True) for x, target in zip(merged, (HERE, FIRST, FOURTH, FIFTH))]
     grad = merge_back(residual, scaled, moments, before, after)
     joined = backward(grad, weights, triple, keys_t, output_weight)
-    joined, near, cross = lax.optimization_barrier((joined, near, cross))
-    onward, joined = lax.optimization_barrier((relay(near, cross), joined))
-    onward = send(onward, sizes, LAT, True)
     own, lat, lon, both = finish(grad, joined, data, packed_weight, norm_gain)
+    lat, lon, both, *merged = lax.optimization_barrier((lat, lon, both, *merged))
     lat = send(lat, sizes, LAT, True)
     both = send(both, sizes, BOTH, True)
     lon = send(lon, sizes, LON, True)
-    merged = unpack_cells(near, cross, onward, cell_gain)
+    merged = unpack_cells(merged, cell_gain)
     merged, lat, both, lon = lax.optimization_barrier((merged, lat, both, lon))
     grads = unpack_tokens(own, lat, lon, both)
     return merged.transpose(2, 0, 1, 3), grads.transpose(2, 0, 1, 3)

time: 49 us -> 46.8 us (0.955)
  waiting for transfers between devices: 11.3 us -> 7.03 us
  starting transfers between devices: 17.6 us -> 19.5 us
    ppermute x12 -> x13, waiting for transfers between devices: 11.3 us -> 7.03 us  [send(): return lax.ppermute(block, ('lon', 'lat', 'lev'), pairs)]
    ppermute x12 -> x13, starting transfers between devices: 17.6 us -> 19.5 us  [send(): return lax.ppermute(block, ('lon', 'lat', 'lev'), pairs)]
  transfers between devices with their start and end apart: 12 -> 13, of which waited for: 7 -> 4; matrix products, arithmetic and copies ran while one was open for 0% -> 0% of each run, Pallas kernels for 33% -> 34%
where the time goes in v9:
time: 46.8 us; the launch traced here: 46.6 us
  starting transfers between devices  19.5 us (42%)
  Pallas kernels  19.2 us (41%)
  waiting for transfers between devices  7.03 us (15%)
  between operations  0.78 us (2%)
    ppermute x13, starting transfers between devices, send(): return lax.ppermute(block, ('lon', 'lat', 'lev'), pairs)  19.5 us
    ppermute x13, waiting for transfers between devices, send(): return lax.ppermute(block, ('lon', 'lat', 'lev'), pairs)  7.03 us
    pallas_call x1, Pallas kernels, window_bias(): pl.pallas_call(bias_kernel, out_shape=[shape((heads * WIN, 128), f32)] *...  6.57 us
    pallas_call x1, Pallas kernels, forward(): pl.pallas_call(forward_kernel, out_shape=[shape((HEADS * WIN, WIN), bf16)...  3.4 us
    pallas_call x1, Pallas kernels, backward(): pl.pallas_call(backward_kernel, out_shape=shape((WIN, 3 * width), bf16),...  2.81 us
    pallas_call x1, Pallas kernels, finish(): pl.pallas_call(finish_kernel, out_shape=[shape((QUAD, width), bf16)] * 4,...  1.53 us
    pallas_call x1, Pallas kernels, pack_pieces(): pl.pallas_call(pack_kernel, out_shape=[piece, double, piece, double, piec...  1.32 us
    pallas_call x1, Pallas kernels, cell_moments(): pl.pallas_call(moments_kernel, out_shape=[shape((WIN, width), f32), shape...  1.2 us
  transfers between devices with their start and end apart: 13, of which 4 were waited for; matrix products, arithmetic and copies ran while one was open for 0% of the time, Pallas kernels for 34%

profile of v9, /device:TPU:0, one launch (start us, length us, event | category | flops | bytes accessed | tf_op | source)
XLA Modules:
  0.0 46.6 jit_solution(12030512816344185996)
XLA Ops:
  0.6 1.3 %pack.1 = (bf16[36,768]{1,0:T(8,128)(2,1)S(1)}, bf16[72,768]{1,0:T(8,128)(2,1)S(1)}, bf16[36,768]{1,0:T(8,128)(2,1)S(1)}, bf16[72,768]{1,0:T(8,128)(2,1)S(1)}, b...) custom-call(bf16[6,12,2,768]{3,2,1,0:T(2,128)(2,1)} %bitcast.7, ...), custom_call_target="tpu_custom_call" | custom-call | tf_op jit(solution)/shard_map/pack/pallas_call | solution.py:140
  2.0 4.1 %collective-permute-start.1 = (bf16[36,768]{1,0:T(8,128)(2,1)S(1)}, bf16[36,768]{1,0:T(8,128)(2,1)S(1)}, u32[]{:S(2)}, u32[]{:S(2)}) collective-permute-start(bf16[36,768]{1,0:T(8,128)(2,1)S(1)} %get-tuple-element.42), channel_id=1, source_target_pairs={{0,2},{1,31},{2,0},{3,29},{4,6},{5,3},{6,4},{7,1},{8,10},{9,7},{10... | collective-permute-start | bytes 165896 | tf_op jit(solution)/shard_map/ppermute | solution.py:672
  6.0 3.2 %collective-permute-start.3 = (bf16[36,768]{1,0:T(8,128)(2,1)S(1)}, bf16[36,768]{1,0:T(8,128)(2,1)S(1)}, u32[]{:S(2)}, u32[]{:S(2)}) collective-permute-start(bf16[36,768]{1,0:T(8,128)(2,1)S(1)} %get-tuple-element.50), channel_id=1, source_target_pairs={{0,29},{1,0},{2,31},{3,2},{4,1},{5,4},{6,3},{7,6},{8,5},{9,8},{10,... | collective-permute-start | bytes 165896 | tf_op jit(solution)/shard_map/ppermute | solution.py:672
  9.2 0.0 collective-permute-start.4
  9.2 1.9 %collective-permute-start = (bf16[72,768]{1,0:T(8,128)(2,1)S(1)}, bf16[72,768]{1,0:T(8,128)(2,1)S(1)}, u32[]{:S(2)}, u32[]{:S(2)}) collective-permute-start(bf16[72,768]{1,0:T(8,128)(2,1)S(1)} %get-tuple-element.41), channel_id=1, source_target_pairs={{0,30},{1,3},{2,28},{3,1},{4,2},{5,7},{6,0},{7,5},{8,6},{9,11},{10... | collective-permute-start | bytes 331784 | tf_op jit(solution)/shard_map/ppermute | solution.py:672
  11.1 0.0 collective-permute-start.2
  11.1 0.0 copy-start.1
  11.1 0.0 copy-start.2
  11.1 0.0 copy-start.3
  11.2 6.6 %bias.1 = (f32[3456,128]{1,0:T(8,128)S(1)}, f32[3456,128]{1,0:T(8,128)S(1)}) custom-call(f32[24,3312]{1,0:T(8,128)S(1)} %get-tuple-element.44.table, s32[144,144]{1,0:T(8,128)S(1)} %get-tuple-element.45.index, s32[6]{0:T(128)} %labels_at.1, s32[96]{0:T(128)} %valid_at.1), custom_call_target="tpu_custom_call" | custom-call | flops 10000000000 | bytes 20000000 | tf_op jit(solution)/shard_map/bias/pallas_call | solution.py:289
  17.7 0.0 collective-permute-done.1.second
  17.7 1.0 %collective-permute-done.first = bf16[72,768]{1,0:T(8,128)(2,1)S(1)} collective-permute-done((bf16[72,768]{1,0:T(8,128)(2,1)S(1)}, bf16[72,768]{1,0:T(8,128)(2,1)S(1)}, u32[]{:S(2)}, u32[]{:S(2)}) %collective-permute-start) | collective-permute-done | bytes 110624 | tf_op jit(solution)/shard_map/ppermute | solution.py:672
  18.8 0.0 collective-permute-done.2.third
  18.8 0.0 copy-done.1
  18.8 0.0 copy-done.2
  18.8 0.0 copy-done.3
  18.8 0.0 copy-start
  18.8 3.4 %forward.1 = (bf16[3456,144]{1,0:T(8,128)(2,1)S(1)}, bf16[144,2304]{1,0:T(8,128)(2,1)S(1)}, bf16[768,144]{1,0:T(8,128)(2,1)S(1)}, bf16[144,768]{1,0:T(8,128)(2,1)S(1)}, bf16[144,768]{1,0:T(8,128)(2,1)S(1)}) custom-call(bf16[36,768]{1,0:T(8,128)(2,1)S(1)} %get-tuple-element.40.own, bf16[72,768]{1,0:T(8,128)(2,1)S(1)} %collective-permute-done.first, ...), custom_call_target="tpu_custom_call" | custom-call | flops 10000000000 | bytes 20000000 | tf_op jit(solution)/shard_map/forward/pallas_call | solution.py:378
  22.2 0.0 collective-permute-done.3.fourth
  22.2 0.0 collective-permute-done.4.fifth
  22.2 0.0 copy-done
  22.2 1.2 %moments.1 = (f32[144,768]{1,0:T(8,128)S(1)}, f32[144,128]{1,0:T(8,128)S(1)}, f32[24,128]{1,0:T(8,128)S(1)}, bf16[36,768]{1,0:T(8,128)(2,1)S(1)}, bf16[36,768]{1...) custom-call(bf16[144,768]{1,0:T(8,128)(2,1)S(1)} %get-tuple-element.48.residual, ...), custom_call_target="tpu_custom_call" | custom-call | flops 100000000 | bytes 1000000 | tf_op jit(solution)/shard_map/moments/pallas_call | solution.py:481
  23.4 0.3 collective-permute-start.5
  23.7 2.1 %collective-permute-start.6 = (bf16[36,768]{1,0:T(8,128)(2,1)S(1)}, bf16[36,768]{1,0:T(8,128)(2,1)S(1)}, u32[]{:S(2)}, u32[]{:S(2)}) collective-permute-start(bf16[36,768]{1,0:T(8,128)(2,1)S(1)} %get-tuple-element.62), channel_id=1, source_target_pairs={{28,0},{1,1},{30,2},{3,3},{0,4},{5,5},{2,6},{7,7},{4,8},{9,9},{6,1... | collective-permute-start | bytes 165896 | tf_op jit(solution)/shard_map/ppermute | solution.py:672
  25.8 2.6 %collective-permute-start.7 = (bf16[36,768]{1,0:T(8,128)(2,1)S(1)}, bf16[36,768]{1,0:T(8,128)(2,1)S(1)}, u32[]{:S(2)}, u32[]{:S(2)}) collective-permute-start(bf16[36,768]{1,0:T(8,128)(2,1)S(1)} %get-tuple-element.63), channel_id=1, source_target_pairs={{30,0},{3,1},{28,2},{1,3},{2,4},{7,5},{0,6},{5,7},{6,8},{11,9},{4,... | collective-permute-start | bytes 165896 | tf_op jit(solution)/shard_map/ppermute | solution.py:672
  28.4 0.2 collective-permute-start.8
  28.6 2.1 %collective-permute-start.9 = (bf16[36,768]{1,0:T(8,128)(2,1)S(1)}, bf16[36,768]{1,0:T(8,128)(2,1)S(1)}, u32[]{:S(2)}, u32[]{:S(2)}) collective-permute-start(bf16[36,768]{1,0:T(8,128)(2,1)S(1)} %get-tuple-element.65), channel_id=1, source_target_pairs={{31,0},{2,1},{29,2},{0,3},{3,4},{6,5},{1,6},{4,7},{7,8},{10,9},{5,... | collective-permute-start | bytes 165896 | tf_op jit(solution)/shard_map/ppermute | solution.py:672
  30.7 0.0 collective-permute-done.5.before.after
  30.7 0.5 %merge.1.grad = bf16[144,768]{1,0:T(8,128)(2,1)S(1)} custom-call(bf16[144,768]{1,0:T(8,128)(2,1)S(1)} %get-tuple-element.48.residual, f32[144,768]{1,0:T(8,128)S(1)} %get-tuple-element.52.scaled, f32[144,128]{1,0:T(8,128)S(1)} %get-tuple-element.53.moments, f32[24,128]{1,0:T(8,128)S(1)} %collective-permute-done.5.before.after, ...), custom_call_target="tpu_custom_call" | custom-call | flops 100000000 | bytes 1000000 | tf_op jit(solution)/shard_map/merge/pallas_call | solution.py:519
  31.3 2.8 %backward.1.joined = bf16[144,2304]{1,0:T(8,128)(2,1)S(1)} custom-call(bf16[144,768]{1,0:T(8,128)(2,1)S(1)} %merge.1.grad, bf16[3456,144]{1,0:T(8,128)(2,1)S(1)} %get-tuple-element.55.weights, bf16[144,2304]{1,0:T(8,128)(2,1)S(1)} %get-tuple-element.56.triple, bf16[768,144]{1,0:T(8,128)(2,1)S(1)} %get-tuple-element.57.keys_t, bf16[768,768]{1,0:T(8,128)(2,1)S(1)} %copy-done.2), custom_call_target="tpu_custom_call" | custom-call | flops 10000000000 | bytes 20000000 | tf_op jit(solution)/shard_map/backward/pallas_call | solution.py:561
  34.1 1.5 %finish.1 = (bf16[36,768]{1,0:T(8,128)(2,1)S(1)}, bf16[36,768]{1,0:T(8,128)(2,1)S(1)}, bf16[36,768]{1,0:T(8,128)(2,1)S(1)}, bf16[36,768]{1,0:T(8,128)(2,1)S(1)}) custom-call(bf16[144,768]{1,0:T(8,128)(2,1)S(1)} %merge.1.grad, bf16[144,2304]{1,0:T(8,128)(2,1)S(1)} %backward.1.joined, bf16[144,768]{1,0:T(8,128)(2,1)S(1)} %get-tuple-element.58.tokens, ...), custom_call_target="tpu_custom_call" | custom-call | flops 10000000000 | bytes 2000000 | tf_op jit(solution)/shard_map/finish/pallas_call | solution.py:582
  35.6 0.0 collective-permute-done.6.same_here
  35.6 0.0 collective-permute-done.7.same_next
  35.6 0.0 collective-permute-done.8.other_here
  35.6 0.9 %collective-permute-done.9.other_next = bf16[36,768]{1,0:T(8,128)(2,1)S(1)} collective-permute-done((bf16[36,768]{1,0:T(8,128)(2,1)S(1)}, bf16[36,768]{1,0:T(8,128)(2,1)S(1)}, u32[]{:S(2)}, u32[]{:S(2)}) %collective-permute-start.9) | collective-permute-done | bytes 55328 | tf_op jit(solution)/shard_map/ppermute | solution.py:672
  36.5 0.8 %collective-permute-start.10 = (bf16[36,768]{1,0:T(8,128)(2,1)S(1)}, bf16[36,768]{1,0:T(8,128)(2,1)S(1)}, u32[]{:S(2)}, u32[]{:S(2)}) collective-permute-start(bf16[36,768]{1,0:T(8,128)(2,1)S(1)} %get-tuple-element.70), channel_id=1, source_target_pairs={{2,0},{3,1},{0,2},{1,3},{6,4},{7,5},{4,6},{5,7},{10,8},{11,9},{8,1... | collective-permute-start | bytes 165896 | tf_op jit(solution)/shard_map/ppermute | solution.py:672
  37.3 1.0 %collective-permute-start.11 = (bf16[36,768]{1,0:T(8,128)(2,1)S(1)}, bf16[36,768]{1,0:T(8,128)(2,1)S(1)}, u32[]{:S(2)}, u32[]{:S(2)}) collective-permute-start(bf16[36,768]{1,0:T(8,128)(2,1)S(1)} %get-tuple-element.71), channel_id=1, source_target_pairs={{30,0},{31,1},{28,2},{29,3},{2,4},{3,5},{0,6},{1,7},{6,8},{7,9},{4... | collective-permute-start | bytes 165896 | tf_op jit(solution)/shard_map/ppermute | solution.py:672
  38.3 1.3 %collective-permute-start.12 = (bf16[36,768]{1,0:T(8,128)(2,1)S(1)}, bf16[36,768]{1,0:T(8,128)(2,1)S(1)}, u32[]{:S(2)}, u32[]{:S(2)}) collective-permute-start(bf16[36,768]{1,0:T(8,128)(2,1)S(1)} %get-tuple-element.72), channel_id=1, source_target_pairs={{28,0},{29,1},{30,2},{31,3},{0,4},{1,5},{2,6},{3,7},{4,8},{5,9},{6... | collective-permute-start | bytes 165896 | tf_op jit(solution)/shard_map/ppermute | solution.py:672
  39.6 1.2 %unpack_cells.1 = bf16[3,3,4,3072]{3,2,1,0:T(4,128)(2,1)} custom-call(bf16[36,768]{1,0:T(8,128)(2,1)S(1)} %collective-permute-done.6.same_here, bf16[36,768]{1,0:T(8,128)(2,1)S(1)} %collective-permute-done.7.same_next, bf16[36,768]{1,0:T(8,128)(2,1)S(1)} %collective-permute-done.8.other_here, bf16[36,768]{1,0:T(8,128)(2,1)S(1)} %collective-permute-done.9.other_next, ...), custom_call_target="tpu_custom_call" | custom-call | flops 1000000000 | bytes 1000000 | tf_op jit(solution)/shard_map/unpack_cells/pallas_call | solution.py:645
  40.7 3.2 %collective-permute-done.10.lat = bf16[36,768]{1,0:T(8,128)(2,1)S(1)} collective-permute-done((bf16[36,768]{1,0:T(8,128)(2,1)S(1)}, bf16[36,768]{1,0:T(8,128)(2,1)S(1)}, u32[]{:S(2)}, u32[]{:S(2)}) %collective-permute-start.10) | collective-permute-done | bytes 55328 | tf_op jit(solution)/shard_map/ppermute | solution.py:672
  43.9 1.9 %collective-permute-done.11.both = bf16[36,768]{1,0:T(8,128)(2,1)S(1)} collective-permute-done((bf16[36,768]{1,0:T(8,128)(2,1)S(1)}, bf16[36,768]{1,0:T(8,128)(2,1)S(1)}, u32[]{:S(2)}, u32[]{:S(2)}) %collective-permute-start.11) | collective-permute-done | bytes 55328 | tf_op jit(solution)/shard_map/ppermute | solution.py:672
  45.9 0.0 collective-permute-done.12.lon
  45.9 0.7 %unpack_tokens.1 = bf16[6,12,2,768]{3,2,1,0:T(2,128)(2,1)} custom-call(bf16[36,768]{1,0:T(8,128)(2,1)S(1)} %get-tuple-element.74.own, bf16[36,768]{1,0:T(8,128)(2,1)S(1)} %collective-permute-done.10.lat, bf16[36,768]{1,0:T(8,128)(2,1)S(1)} %collective-permute-done.12.lon, bf16[36,768]{1,0:T(8,128)(2,1)S(1)} %collective-permute-done.11.both), custom_call_target="tpu_custom_call" | custom-call | tf_op jit(solution)/shard_map/unpack_tokens/pallas_call | solution.py:603
Async XLA Ops:
  2.0 15.8 %collective-permute-start.1 = (bf16[36,768]{1,0:T(8,128)(2,1)S(1)}, bf16[36,768]{1,0:T(8,128)(2,1)S(1)}, u32[]{:S(2)}, u32[]{:S(2)}) collective-permute-start(bf16[36,768]{1,0:T(8,128)(2,1)S(1)} %get-tuple-element.42), channel_id=1, source_target_pairs={{0,2},{1,31},{2,0},{3,29},{4,6},{5,3},{6,4},{7,1},{8,10},{9,7},{10... | collective-permute-start | bytes 165896 | tf_op jit(solution)/shard_map/ppermute | solution.py:672
  6.0 16.2 %collective-permute-start.3 = (bf16[36,768]{1,0:T(8,128)(2,1)S(1)}, bf16[36,768]{1,0:T(8,128)(2,1)S(1)}, u32[]{:S(2)}, u32[]{:S(2)}) collective-permute-start(bf16[36,768]{1,0:T(8,128)(2,1)S(1)} %get-tuple-element.50), channel_id=1, source_target_pairs={{0,29},{1,0},{2,31},{3,2},{4,1},{5,4},{6,3},{7,6},{8,5},{9,8},{10,... | collective-permute-start | bytes 165896 | tf_op jit(solution)/shard_map/ppermute | solution.py:672
  9.2 13.0 %collective-permute-start.4 = (bf16[36,768]{1,0:T(8,128)(2,1)S(1)}, bf16[36,768]{1,0:T(8,128)(2,1)S(1)}, u32[]{:S(2)}, u32[]{:S(2)}) collective-permute-start(bf16[36,768]{1,0:T(8,128)(2,1)S(1)} %get-tuple-element.51), channel_id=1, source_target_pairs={{0,31},{1,2},{2,29},{3,0},{4,3},{5,6},{6,1},{7,4},{8,7},{9,10},{10... | collective-permute-start | bytes 165896 | tf_op jit(solution)/shard_map/ppermute | solution.py:672
  9.2 9.5 %collective-permute-start = (bf16[72,768]{1,0:T(8,128)(2,1)S(1)}, bf16[72,768]{1,0:T(8,128)(2,1)S(1)}, u32[]{:S(2)}, u32[]{:S(2)}) collective-permute-start(bf16[72,768]{1,0:T(8,128)(2,1)S(1)} %get-tuple-element.41), channel_id=1, source_target_pairs={{0,30},{1,3},{2,28},{3,1},{4,2},{5,7},{6,0},{7,5},{8,6},{9,11},{10... | collective-permute-start | bytes 331784 | tf_op jit(solution)/shard_map/ppermute | solution.py:672
  11.1 7.6 %collective-permute-start.2 = (bf16[72,768]{1,0:T(8,128)(2,1)S(1)}, bf16[72,768]{1,0:T(8,128)(2,1)S(1)}, u32[]{:S(2)}, u32[]{:S(2)}) collective-permute-start(bf16[72,768]{1,0:T(8,128)(2,1)S(1)} %get-tuple-element.43), channel_id=1, source_target_pairs={{0,28},{1,29},{2,30},{3,31},{4,0},{5,1},{6,2},{7,3},{8,4},{9,5},{1... | collective-permute-start | bytes 331784 | tf_op jit(solution)/shard_map/ppermute | solution.py:672
  11.1 7.6 %copy-start.1 = (bf16[768,2304]{1,0:T(8,128)(2,1)S(1)}, bf16[768,2304]{1,0:T(8,128)(2,1)}, u32[]{:S(2)}) copy-start(bf16[768,2304]{1,0:T(8,128)(2,1)} %packed.3) | copy-start | bytes 10616836
  11.1 7.6 %copy-start.2 = (bf16[768,768]{1,0:T(8,128)(2,1)S(1)}, bf16[768,768]{1,0:T(8,128)(2,1)}, u32[]{:S(2)}) copy-start(bf16[768,768]{1,0:T(8,128)(2,1)} %output.3) | copy-start | bytes 3538948
  11.1 7.6 %copy-start.3 = (f32[768]{0:T(1024)S(1)}, f32[768]{0:T(1024)}, u32[]{:S(2)}) copy-start(f32[768]{0:T(1024)} %gain.3) | copy-start | bytes 9220
  18.8 3.4 %copy-start = (f32[3072]{0:T(1024)S(1)}, f32[3072]{0:T(1024)}, u32[]{:S(2)}) copy-start(f32[3072]{0:T(1024)} %param.14) | copy-start | bytes 36868
  23.4 7.3 %collective-permute-start.5 = (f32[24,128]{1,0:T(8,128)S(1)}, f32[24,128]{1,0:T(8,128)S(1)}, u32[]{:S(2)}, u32[]{:S(2)}) collective-permute-start(f32[24,128]{1,0:T(8,128)S(1)} %get-tuple-element.54), channel_id=1, source_target_pairs={{0,2},{1,3},{2,0},{3,1},{4,6},{5,7},{6,4},{7,5},{8,10},{9,11},{10,... | collective-permute-start | bytes 36872 | tf_op jit(solution)/shard_map/ppermute | solution.py:672
  23.7 11.9 %collective-permute-start.6 = (bf16[36,768]{1,0:T(8,128)(2,1)S(1)}, bf16[36,768]{1,0:T(8,128)(2,1)S(1)}, u32[]{:S(2)}, u32[]{:S(2)}) collective-permute-start(bf16[36,768]{1,0:T(8,128)(2,1)S(1)} %get-tuple-element.62), channel_id=1, source_target_pairs={{28,0},{1,1},{30,2},{3,3},{0,4},{5,5},{2,6},{7,7},{4,8},{9,9},{6,1... | collective-permute-start | bytes 165896 | tf_op jit(solution)/shard_map/ppermute | solution.py:672
  25.8 9.8 %collective-permute-start.7 = (bf16[36,768]{1,0:T(8,128)(2,1)S(1)}, bf16[36,768]{1,0:T(8,128)(2,1)S(1)}, u32[]{:S(2)}, u32[]{:S(2)}) collective-permute-start(bf16[36,768]{1,0:T(8,128)(2,1)S(1)} %get-tuple-element.63), channel_id=1, source_target_pairs={{30,0},{3,1},{28,2},{1,3},{2,4},{7,5},{0,6},{5,7},{6,8},{11,9},{4,... | collective-permute-start | bytes 165896 | tf_op jit(solution)/shard_map/ppermute | solution.py:672
  28.4 7.2 %collective-permute-start.8 = (bf16[36,768]{1,0:T(8,128)(2,1)S(1)}, bf16[36,768]{1,0:T(8,128)(2,1)S(1)}, u32[]{:S(2)}, u32[]{:S(2)}) collective-permute-start(bf16[36,768]{1,0:T(8,128)(2,1)S(1)} %get-tuple-element.64), channel_id=1, source_target_pairs={{29,0},{0,1},{31,2},{2,3},{1,4},{4,5},{3,6},{6,7},{5,8},{8,9},{7,1... | collective-permute-start | bytes 165896 | tf_op jit(solution)/shard_map/ppermute | solution.py:672
  28.6 7.9 %collective-permute-start.9 = (bf16[36,768]{1,0:T(8,128)(2,1)S(1)}, bf16[36,768]{1,0:T(8,128)(2,1)S(1)}, u32[]{:S(2)}, u32[]{:S(2)}) collective-permute-start(bf16[36,768]{1,0:T(8,128)(2,1)S(1)} %get-tuple-element.65), channel_id=1, source_target_pairs={{31,0},{2,1},{29,2},{0,3},{3,4},{6,5},{1,6},{4,7},{7,8},{10,9},{5,... | collective-permute-start | bytes 165896 | tf_op jit(solution)/shard_map/ppermute | solution.py:672
  36.5 7.4 %collective-permute-start.10 = (bf16[36,768]{1,0:T(8,128)(2,1)S(1)}, bf16[36,768]{1,0:T(8,128)(2,1)S(1)}, u32[]{:S(2)}, u32[]{:S(2)}) collective-permute-start(bf16[36,768]{1,0:T(8,128)(2,1)S(1)} %get-tuple-element.70), channel_id=1, source_target_pairs={{2,0},{3,1},{0,2},{1,3},{6,4},{7,5},{4,6},{5,7},{10,8},{11,9},{8,1... | collective-permute-start | bytes 165896 | tf_op jit(solution)/shard_map/ppermute | solution.py:672
  37.3 8.5 %collective-permute-start.11 = (bf16[36,768]{1,0:T(8,128)(2,1)S(1)}, bf16[36,768]{1,0:T(8,128)(2,1)S(1)}, u32[]{:S(2)}, u32[]{:S(2)}) collective-permute-start(bf16[36,768]{1,0:T(8,128)(2,1)S(1)} %get-tuple-element.71), channel_id=1, source_target_pairs={{30,0},{31,1},{28,2},{29,3},{2,4},{3,5},{0,6},{1,7},{6,8},{7,9},{4... | collective-permute-start | bytes 165896 | tf_op jit(solution)/shard_map/ppermute | solution.py:672
  38.3 7.6 %collective-permute-start.12 = (bf16[36,768]{1,0:T(8,128)(2,1)S(1)}, bf16[36,768]{1,0:T(8,128)(2,1)S(1)}, u32[]{:S(2)}, u32[]{:S(2)}) collective-permute-start(bf16[36,768]{1,0:T(8,128)(2,1)S(1)} %get-tuple-element.72), channel_id=1, source_target_pairs={{28,0},{29,1},{30,2},{31,3},{0,4},{1,5},{2,6},{3,7},{4,8},{5,9},{6... | collective-permute-start | bytes 165896 | tf_op jit(solution)/shard_map/ppermute | solution.py:672

commit v10 on v9

--- a/solution.py
+++ b/solution.py
@@ -154,9 +154,8 @@
     )(*in_hbm(tokens, grad, table, index))
 
 
-def bias_kernel(
-    table, index, labels_at, valid_at, main, tail,
-    labels, valid, split, fine, high, low, fine_high, fine_low, rest_rows, mask, mask_tail, done,
+def index_kernel(
+    index, labels_at, valid_at, high, low, fine_high, fine_low, mask, mask_tail, labels, valid, rest_rows, done
 ):
     copies = start_copies(done, (labels_at, labels), (valid_at, valid))
     row_k, column_k, level_k, _ = token_places((WIN, 1), 0)
@@ -165,6 +164,65 @@
     columns = lax.broadcasted_iota(jnp.int32, (WIN, WIN), 1)
     rows = lax.broadcasted_iota(jnp.int32, (WIN, WIN), 0)
     permute = jnp.where(natural == columns, 1.0, 0.0).astype(bf16)
+    def place(values, out):
+        moved = mxu(mxu(permute, values.astype(f32).astype(bf16), NT).astype(bf16), permute, NT)
+        out[0:WIN, :] = moved[:, :128]
+        rest_rows[...] = jnp.concatenate((moved[:, 128:], jnp.zeros((WIN, 128 - TAIL), f32)), axis=1)
+        total = None
+        for g in range(8):
+            piece = rest_rows[pl.ds(g, TAIL_GROUPS, stride=8), :]
+            if g:
+                piece = pltpu.roll(piece, TAIL * g, 1)
+            total = piece if total is None else total + piece
+        out[WIN : WIN + TAIL_GROUPS, :] = total
+
+    entry = index[...]
+    place(lax.shift_right_logical(entry, 8), high)
+    place(entry & 255, low)
+    upper, lower = high[...], low[...]
+    far = lower >= 128.0
+    fine_high[...] = (2.0 * upper + jnp.where(far, 1.0, 0.0)).astype(jnp.int32)
+    fine_low[...] = jnp.where(far, lower - 128.0, lower).astype(jnp.int32)
+    for copy in copies:
+        copy.wait()
+
+    label_q, label_k = jnp.zeros_like(row_q), jnp.zeros_like(row_k)
+    for r in range(WLAT):
+        label_q = jnp.where(row_q == r, labels[r], label_q)
+        label_k = jnp.where(row_k == r, labels[r], label_k)
+    valid_k = jnp.zeros_like(column_k)
+    start = lax.axis_index("lon") * WLON + HALF_LON
+    total = valid.shape[0]
+    for c in range(WLON):
+        at = start + c
+        at = jnp.where(at >= total, at - total, at)
+        valid_k = jnp.where(column_k == c, valid[at], valid_k)
+    seen = (label_k == label_q) & ((valid_k > 0) | (rows == columns))
+    added = jnp.where(seen, 0.0, BLOCKED).astype(f32)
+    mask[...] = added[:, :128]
+    mask_tail[...] = jnp.concatenate((added[:, 128:], jnp.zeros((WIN, 128 - TAIL), f32)), axis=1)
+
+
+def window_index(index, labels, valid):
+    rows = (WIN + TAIL_GROUPS, 128)
+    return pl.pallas_call(
+        index_kernel,
+        out_shape=[shape(rows, f32)] * 2 + [shape(rows, jnp.int32)] * 2 + [shape((WIN, 128), f32)] * 2,
+        in_specs=[pl.BlockSpec(memory_space=pltpu.MemorySpace.VMEM)]
+        + [pl.BlockSpec(memory_space=pltpu.MemorySpace.HBM)] * 2,
+        scratch_shapes=[
+            pltpu.SMEM(labels.shape, jnp.int32),
+            pltpu.SMEM(valid.shape, jnp.int32),
+            pltpu.VMEM((WIN, 128), f32),
+            pltpu.SemaphoreType.DMA((2,)),
+        ],
+        compiler_params=params(),
+        cost_estimate=cost(10**8, 10**6),
+        name="index",
+    )(index, *in_hbm(labels, valid))
+
+
+def bias_kernel(table, high, low, fine_high, fine_low, mask, mask_tail, main, tail, split, fine):
     heads, entries = table.shape
     chunks = (entries + 255) // 256
     small_chunks = (entries + 127) // 128
@@ -185,44 +243,6 @@
     source = split[...].astype(bf16)
     part_rows = chunks * heads
 
-    def place(values, out):
-        moved = mxu(mxu(permute, values.astype(f32).astype(bf16), NT).astype(bf16), permute, NT)
-        out[0:WIN, :] = moved[:, :128]
-        rest_rows[...] = jnp.concatenate((moved[:, 128:], jnp.zeros((WIN, 128 - TAIL), f32)), axis=1)
-        total = None
-        for g in range(8):
-            piece = rest_rows[pl.ds(g, TAIL_GROUPS, stride=8), :]
-            if g:
-                piece = pltpu.roll(piece, TAIL * g, 1)
-            total = piece if total is None else total + piece
-        out[WIN : WIN + TAIL_GROUPS, :] = total
-
-    entry = index[...]
-    place(lax.shift_right_logical(entry, 8), high)
-    place(entry & 255, low)
-    upper, lower = high[...], low[...]
-    far = lower >= 128.0
-    fine_high[...] = (2.0 * upper + jnp.where(far, 1.0, 0.0)).astype(jnp.int32)
-    fine_low[...] = jnp.where(far, lower - 128.0, lower).astype(jnp.int32)
-    for copy in copies:
-        copy.wait()
-
-    label_q, label_k = jnp.zeros_like(row_q), jnp.zeros_like(row_k)
-    for r in range(WLAT):
-        label_q = jnp.where(row_q == r, labels[r], label_q)
-        label_k = jnp.where(row_k == r, labels[r], label_k)
-    valid_k = jnp.zeros_like(column_k)
-    start = lax.axis_index("lon") * WLON + HALF_LON
-    total = valid.shape[0]
-    for c in range(WLON):
-        at = start + c
-        at = jnp.where(at >= total, at - total, at)
-        valid_k = jnp.where(column_k == c, valid[at], valid_k)
-    seen = (label_k == label_q) & ((valid_k > 0) | (rows == columns))
-    added = jnp.where(seen, 0.0, BLOCKED).astype(f32)
-    mask[...] = added[:, :128]
-    mask_tail[...] = jnp.concatenate((added[:, 128:], jnp.zeros((WIN, 128 - TAIL), f32)), axis=1)
-
     depth = lax.broadcasted_iota(jnp.int32, (256, 128), 0).astype(f32).astype(bf16)
     one, zero = jnp.ones((), bf16), jnp.zeros((), bf16)
 
@@ -282,33 +302,20 @@
                     tail[pl.ds(block * 8 * WIN + key, 8, stride=WIN), :] = moved + extra
 
 
-def window_bias(table, index, labels, valid):
+def window_bias(table, places):
     heads, entries = table.shape
     whole = (entries + 255) // 256
-    index_rows = WIN + TAIL_GROUPS
     return pl.pallas_call(
         bias_kernel,
         out_shape=[shape((heads * WIN, 128), f32)] * 2,
-        in_specs=[pl.BlockSpec(memory_space=pltpu.MemorySpace.VMEM)] * 2
-        + [pl.BlockSpec(memory_space=pltpu.MemorySpace.HBM)] * 2,
         scratch_shapes=[
-            pltpu.SMEM(labels.shape, jnp.int32),
-            pltpu.SMEM(valid.shape, jnp.int32),
             pltpu.VMEM((2 * whole * heads, 256), f32),
             pltpu.VMEM((heads, (entries + 127) // 128 * 128), f32),
-            pltpu.VMEM((index_rows, 128), f32),
-            pltpu.VMEM((index_rows, 128), f32),
-            pltpu.VMEM((index_rows, 128), jnp.int32),
-            pltpu.VMEM((index_rows, 128), jnp.int32),
-            pltpu.VMEM((WIN, 128), f32),
-            pltpu.VMEM((WIN, 128), f32),
-            pltpu.VMEM((WIN, 128), f32),
-            pltpu.SemaphoreType.DMA((2,)),
         ],
         compiler_params=params(),
         cost_estimate=cost(10**10, 2 * 10**7),
         name="bias",
-    )(table, index, *in_hbm(labels, valid))
+    )(table, *places)
 
 
 def row_mean(values):
@@ -702,9 +709,11 @@
     first = send(first, sizes, FIRST)
     second = send(second, sizes, SECOND)
     third = send(third, sizes, THIRD)
+    places = window_index(index, row_labels, column_valid)
+    fourth, fifth, *places = lax.optimization_barrier((fourth, fifth, *places))
     fourth = send(fourth, sizes, FOURTH)
     fifth = send(fifth, sizes, FIFTH)
-    main, tail = window_bias(table, index, row_labels, column_valid)
+    main, tail = window_bias(table, places)
     cell_gain = merge_gain.reshape(1, -1)
     weights, triple, keys_t, residual, data = forward(
         (own, first, second, third), packed_weight, output_weight, norm_gain, main, tail
@@ -714,15 +723,19 @@
     )
     before = send(sent, sizes, lambda i, a, k: (i, a + 1, k))
     after = before if sizes[1] == 2 else send(sent, sizes, lambda i, a, k: (i, a - 1, k))
-    merged = [send(x, sizes, target, True) for x, target in zip(merged, (HERE, FIRST, FOURTH, FIFTH))]
+    same_here, same_next, other_here, other_next = merged
+    other_next = send(other_next, sizes, FIFTH, True)
+    same_next = send(same_next, sizes, FIRST, True)
+    other_here = send(other_here, sizes, FOURTH, True)
+    same_here = send(same_here, sizes, HERE, True)
     grad = merge_back(residual, scaled, moments, before, after)
     joined = backward(grad, weights, triple, keys_t, output_weight)
     own, lat, lon, both = finish(grad, joined, data, packed_weight, norm_gain)
-    lat, lon, both, *merged = lax.optimization_barrier((lat, lon, both, *merged))
+    other_next, same_next, lat, both, lon = lax.optimization_barrier((other_next, same_next, lat, both, lon))
     lat = send(lat, sizes, LAT, True)
     both = send(both, sizes, BOTH, True)
     lon = send(lon, sizes, LON, True)
-    merged = unpack_cells(merged, cell_gain)
+    merged = unpack_cells((same_here, same_next, other_here, other_next), cell_gain)
     merged, lat, both, lon = lax.optimization_barrier((merged, lat, both, lon))
     grads = unpack_tokens(own, lat, lon, both)
     return merged.transpose(2, 0, 1, 3), grads.transpose(2, 0, 1, 3)

time: 46.8 us -> 46.4 us (level)
  waiting for transfers between devices: 7.03 us -> 4.55 us
  starting transfers between devices: 19.5 us -> 21 us
  Pallas kernels: 19.2 us -> 19.8 us
    ppermute x13, waiting for transfers between devices: 7.03 us -> 4.55 us  [send(): return lax.ppermute(block, ('lon', 'lat', 'lev'), pairs)]
    ppermute x13, starting transfers between devices: 19.5 us -> 21 us  [send(): return lax.ppermute(block, ('lon', 'lat', 'lev'), pairs)]
    pallas_call x0 -> x1, Pallas kernels: none -> 1.17 us  [window_index(): pl.pallas_call(index_kernel, out_shape=[shape(rows, f32)] * 2 + [shape(ro...]
    pallas_call x1, Pallas kernels: 6.57 us -> 5.98 us  [window_bias(): pl.pallas_call(bias_kernel, out_shape=[shape((heads * WIN, 128), f32)] *...]
  transfers between devices with their start and end apart: 13 -> 13, of which waited for: 4 -> 3; matrix products, arithmetic and copies ran while one was open for 0% -> 0% of each run, Pallas kernels for 34% -> 36%
where the time goes in v10:
time: 46.4 us; the launch traced here: 46.2 us
  starting transfers between devices  21 us (45%)
  Pallas kernels  19.8 us (43%)
  waiting for transfers between devices  4.55 us (10%)
  between operations  0.79 us (2%)
    ppermute x13, starting transfers between devices, send(): return lax.ppermute(block, ('lon', 'lat', 'lev'), pairs)  21 us
    pallas_call x1, Pallas kernels, window_bias(): pl.pallas_call(bias_kernel, out_shape=[shape((heads * WIN, 128), f32)] *...  5.98 us
    ppermute x13, waiting for transfers between devices, send(): return lax.ppermute(block, ('lon', 'lat', 'lev'), pairs)  4.55 us
    pallas_call x1, Pallas kernels, forward(): pl.pallas_call(forward_kernel, out_shape=[shape((HEADS * WIN, WIN), bf16)...  3.41 us
    pallas_call x1, Pallas kernels, backward(): pl.pallas_call(backward_kernel, out_shape=shape((WIN, 3 * width), bf16),...  2.81 us
    pallas_call x1, Pallas kernels, finish(): pl.pallas_call(finish_kernel, out_shape=[shape((QUAD, width), bf16)] * 4,...  1.52 us
    pallas_call x1, Pallas kernels, pack_pieces(): pl.pallas_call(pack_kernel, out_shape=[piece, double, piece, double, piec...  1.32 us
    pallas_call x1, Pallas kernels, cell_moments(): pl.pallas_call(moments_kernel, out_shape=[shape((WIN, width), f32), shape...  1.2 us
  transfers between devices with their start and end apart: 13, of which 3 were waited for; matrix products, arithmetic and copies ran while one was open for 0% of the time, Pallas kernels for 36%

profile of v10, /device:TPU:0, one launch (start us, length us, event | category | flops | bytes accessed | tf_op | source)
XLA Modules:
  0.0 46.2 jit_solution(12182916297088984037)
XLA Ops:
  0.6 1.3 %pack.1 = (bf16[36,768]{1,0:T(8,128)(2,1)S(1)}, bf16[72,768]{1,0:T(8,128)(2,1)S(1)}, bf16[36,768]{1,0:T(8,128)(2,1)S(1)}, bf16[72,768]{1,0:T(8,128)(2,1)S(1)}, b...) custom-call(bf16[6,12,2,768]{3,2,1,0:T(2,128)(2,1)} %bitcast.7, ...), custom_call_target="tpu_custom_call" | custom-call | tf_op jit(solution)/shard_map/pack/pallas_call | solution.py:140
  2.0 4.1 %collective-permute-start.1 = (bf16[36,768]{1,0:T(8,128)(2,1)S(1)}, bf16[36,768]{1,0:T(8,128)(2,1)S(1)}, u32[]{:S(2)}, u32[]{:S(2)}) collective-permute-start(bf16[36,768]{1,0:T(8,128)(2,1)S(1)} %get-tuple-element.54), channel_id=1, source_target_pairs={{0,2},{1,31},{2,0},{3,29},{4,6},{5,3},{6,4},{7,1},{8,10},{9,7},{10... | collective-permute-start | bytes 165896 | tf_op jit(solution)/shard_map/ppermute | solution.py:679
  6.0 1.4 %collective-permute-start = (bf16[72,768]{1,0:T(8,128)(2,1)S(1)}, bf16[72,768]{1,0:T(8,128)(2,1)S(1)}, u32[]{:S(2)}, u32[]{:S(2)}) collective-permute-start(bf16[72,768]{1,0:T(8,128)(2,1)S(1)} %get-tuple-element.53), channel_id=1, source_target_pairs={{0,30},{1,3},{2,28},{3,1},{4,2},{5,7},{6,0},{7,5},{8,6},{9,11},{10... | collective-permute-start | bytes 331784 | tf_op jit(solution)/shard_map/ppermute | solution.py:679
  7.4 1.1 %collective-permute-start.2 = (bf16[72,768]{1,0:T(8,128)(2,1)S(1)}, bf16[72,768]{1,0:T(8,128)(2,1)S(1)}, u32[]{:S(2)}, u32[]{:S(2)}) collective-permute-start(bf16[72,768]{1,0:T(8,128)(2,1)S(1)} %get-tuple-element.55), channel_id=1, source_target_pairs={{0,28},{1,29},{2,30},{3,31},{4,0},{5,1},{6,2},{7,3},{8,4},{9,5},{1... | collective-permute-start | bytes 331784 | tf_op jit(solution)/shard_map/ppermute | solution.py:679
  8.5 1.2 %index.1 = (f32[162,128]{1,0:T(8,128)S(1)}, f32[162,128]{1,0:T(8,128)S(1)}, s32[162,128]{1,0:T(8,128)S(1)}, s32[162,128]{1,0:T(8,128)S(1)}, f32[144,128]{1,0:T(8,128)S(1)}, /*index=5*/f32[144,128]{1,0:T(8,128)S(1)}) custom-call(s32[144,144]{1,0:T(8,128)S(1)} %get-tuple-element.59.index, s32[6]{0:T(128)} %labels_at.1, s32[96]{0:T(128)} %valid_at.1), custom_call_target="tpu_custom_call" | custom-call | flops 100000000 | bytes 1000000 | tf_op jit(solution)/shard_map/index/pallas_call | solution.py:208
  9.7 1.2 %collective-permute-start.3 = (bf16[36,768]{1,0:T(8,128)(2,1)S(1)}, bf16[36,768]{1,0:T(8,128)(2,1)S(1)}, u32[]{:S(2)}, u32[]{:S(2)}) collective-permute-start(bf16[36,768]{1,0:T(8,128)(2,1)S(1)} %get-tuple-element.76), channel_id=1, source_target_pairs={{0,29},{1,0},{2,31},{3,2},{4,1},{5,4},{6,3},{7,6},{8,5},{9,8},{10,... | collective-permute-start | bytes 165896 | tf_op jit(solution)/shard_map/ppermute | solution.py:679
  11.0 2.1 %collective-permute-start.4 = (bf16[36,768]{1,0:T(8,128)(2,1)S(1)}, bf16[36,768]{1,0:T(8,128)(2,1)S(1)}, u32[]{:S(2)}, u32[]{:S(2)}) collective-permute-start(bf16[36,768]{1,0:T(8,128)(2,1)S(1)} %get-tuple-element.77), channel_id=1, source_target_pairs={{0,31},{1,2},{2,29},{3,0},{4,3},{5,6},{6,1},{7,4},{8,7},{9,10},{10... | collective-permute-start | bytes 165896 | tf_op jit(solution)/shard_map/ppermute | solution.py:679
  13.0 0.0 copy-start.1
  13.0 0.0 copy-start.2
  13.0 0.0 copy-start.3
  13.0 6.0 %bias.1 = (f32[3456,128]{1,0:T(8,128)S(1)}, f32[3456,128]{1,0:T(8,128)S(1)}) custom-call(f32[24,3312]{1,0:T(8,128)S(1)} %get-tuple-element.56.table, f32[162,128]{1,0:T(8,128)S(1)} %get-tuple-element.66.high, f32[162,128]{1,0:T(8,128)S(1)} %get-tuple-element.67.low, s32[162,128]{1,0:T(8,128)S(1)} %get-tuple-element.68.fine_high, ...), custom_call_target="tpu_custom_call" | custom-call | flops 10000000000 | bytes 20000000 | tf_op jit(solution)/shard_map/bias/pallas_call | solution.py:308
  19.0 0.0 collective-permute-done.1.second
  19.0 0.0 collective-permute-done.first
  19.0 0.0 collective-permute-done.2.third
  19.0 0.0 copy-done.1
  19.0 0.0 copy-done.2
  19.0 0.0 copy-done.3
  19.1 0.0 copy-start
  19.1 3.4 %forward.1 = (bf16[3456,144]{1,0:T(8,128)(2,1)S(1)}, bf16[144,2304]{1,0:T(8,128)(2,1)S(1)}, bf16[768,144]{1,0:T(8,128)(2,1)S(1)}, bf16[144,768]{1,0:T(8,128)(2,1)S(1)}, bf16[144,768]{1,0:T(8,128)(2,1)S(1)}) custom-call(bf16[36,768]{1,0:T(8,128)(2,1)S(1)} %get-tuple-element.52.own, bf16[72,768]{1,0:T(8,128)(2,1)S(1)} %collective-permute-done.first, ...), custom_call_target="tpu_custom_call" | custom-call | flops 10000000000 | bytes 20000000 | tf_op jit(solution)/shard_map/forward/pallas_call | solution.py:385
  22.5 0.0 collective-permute-done.3.fourth
  22.5 0.0 collective-permute-done.4.fifth
  22.5 0.0 copy-done
  22.5 1.2 %moments.1 = (f32[144,768]{1,0:T(8,128)S(1)}, f32[144,128]{1,0:T(8,128)S(1)}, f32[24,128]{1,0:T(8,128)S(1)}, bf16[36,768]{1,0:T(8,128)(2,1)S(1)}, bf16[36,768]{1...) custom-call(bf16[144,768]{1,0:T(8,128)(2,1)S(1)} %get-tuple-element.74.residual, ...), custom_call_target="tpu_custom_call" | custom-call | flops 100000000 | bytes 1000000 | tf_op jit(solution)/shard_map/moments/pallas_call | solution.py:488
  23.7 0.2 collective-permute-start.8
  24.0 2.7 %collective-permute-start.5 = (bf16[36,768]{1,0:T(8,128)(2,1)S(1)}, bf16[36,768]{1,0:T(8,128)(2,1)S(1)}, u32[]{:S(2)}, u32[]{:S(2)}) collective-permute-start(bf16[36,768]{1,0:T(8,128)(2,1)S(1)} %get-tuple-element.78), channel_id=1, source_target_pairs={{28,0},{1,1},{30,2},{3,3},{0,4},{5,5},{2,6},{7,7},{4,8},{9,9},{6,1... | collective-permute-start | bytes 165896 | tf_op jit(solution)/shard_map/ppermute | solution.py:679
  26.6 1.0 %collective-permute-start.6 = (bf16[36,768]{1,0:T(8,128)(2,1)S(1)}, bf16[36,768]{1,0:T(8,128)(2,1)S(1)}, u32[]{:S(2)}, u32[]{:S(2)}) collective-permute-start(bf16[36,768]{1,0:T(8,128)(2,1)S(1)} %get-tuple-element.79), channel_id=1, source_target_pairs={{31,0},{2,1},{29,2},{0,3},{3,4},{6,5},{1,6},{4,7},{7,8},{10,9},{5,... | collective-permute-start | bytes 165896 | tf_op jit(solution)/shard_map/ppermute | solution.py:679
  27.6 2.0 %collective-permute-start.7 = (bf16[36,768]{1,0:T(8,128)(2,1)S(1)}, bf16[36,768]{1,0:T(8,128)(2,1)S(1)}, u32[]{:S(2)}, u32[]{:S(2)}) collective-permute-start(bf16[36,768]{1,0:T(8,128)(2,1)S(1)} %get-tuple-element.80), channel_id=1, source_target_pairs={{30,0},{3,1},{28,2},{1,3},{2,4},{7,5},{0,6},{5,7},{6,8},{11,9},{4,... | collective-permute-start | bytes 165896 | tf_op jit(solution)/shard_map/ppermute | solution.py:679
  29.6 1.9 %collective-permute-start.9 = (bf16[36,768]{1,0:T(8,128)(2,1)S(1)}, bf16[36,768]{1,0:T(8,128)(2,1)S(1)}, u32[]{:S(2)}, u32[]{:S(2)}) collective-permute-start(bf16[36,768]{1,0:T(8,128)(2,1)S(1)} %get-tuple-element.92), channel_id=1, source_target_pairs={{29,0},{0,1},{31,2},{2,3},{1,4},{4,5},{3,6},{6,7},{5,8},{8,9},{7,1... | collective-permute-start | bytes 165896 | tf_op jit(solution)/shard_map/ppermute | solution.py:679
  31.5 0.0 collective-permute-done.8.before.after
  31.5 0.5 %merge.1.grad = bf16[144,768]{1,0:T(8,128)(2,1)S(1)} custom-call(bf16[144,768]{1,0:T(8,128)(2,1)S(1)} %get-tuple-element.74.residual, f32[144,768]{1,0:T(8,128)S(1)} %get-tuple-element.81.scaled, f32[144,128]{1,0:T(8,128)S(1)} %get-tuple-element.82.moments, f32[24,128]{1,0:T(8,128)S(1)} %collective-permute-done.8.before.after, ...), custom_call_target="tpu_custom_call" | custom-call | flops 100000000 | bytes 1000000 | tf_op jit(solution)/shard_map/merge/pallas_call | solution.py:526
  32.1 2.8 %backward.1.joined = bf16[144,2304]{1,0:T(8,128)(2,1)S(1)} custom-call(bf16[144,768]{1,0:T(8,128)(2,1)S(1)} %merge.1.grad, bf16[3456,144]{1,0:T(8,128)(2,1)S(1)} %get-tuple-element.84.weights, bf16[144,2304]{1,0:T(8,128)(2,1)S(1)} %get-tuple-element.85.triple, bf16[768,144]{1,0:T(8,128)(2,1)S(1)} %get-tuple-element.86.keys_t, bf16[768,768]{1,0:T(8,128)(2,1)S(1)} %copy-done.2), custom_call_target="tpu_custom_call" | custom-call | flops 10000000000 | bytes 20000000 | tf_op jit(solution)/shard_map/backward/pallas_call | solution.py:568
  34.9 1.5 %finish.1 = (bf16[36,768]{1,0:T(8,128)(2,1)S(1)}, bf16[36,768]{1,0:T(8,128)(2,1)S(1)}, bf16[36,768]{1,0:T(8,128)(2,1)S(1)}, bf16[36,768]{1,0:T(8,128)(2,1)S(1)}) custom-call(bf16[144,768]{1,0:T(8,128)(2,1)S(1)} %merge.1.grad, bf16[144,2304]{1,0:T(8,128)(2,1)S(1)} %backward.1.joined, bf16[144,768]{1,0:T(8,128)(2,1)S(1)} %get-tuple-element.87.tokens, ...), custom_call_target="tpu_custom_call" | custom-call | flops 10000000000 | bytes 2000000 | tf_op jit(solution)/shard_map/finish/pallas_call | solution.py:589
  36.4 0.0 collective-permute-done.6.other_next
  36.4 0.2 collective-permute-done.7.same_next
  36.6 1.4 %collective-permute-start.10 = (bf16[36,768]{1,0:T(8,128)(2,1)S(1)}, bf16[36,768]{1,0:T(8,128)(2,1)S(1)}, u32[]{:S(2)}, u32[]{:S(2)}) collective-permute-start(bf16[36,768]{1,0:T(8,128)(2,1)S(1)} %get-tuple-element.94), channel_id=1, source_target_pairs={{2,0},{3,1},{0,2},{1,3},{6,4},{7,5},{4,6},{5,7},{10,8},{11,9},{8,1... | collective-permute-start | bytes 165896 | tf_op jit(solution)/shard_map/ppermute | solution.py:679
  38.0 0.4 collective-permute-start.11
  38.4 1.5 %collective-permute-start.12 = (bf16[36,768]{1,0:T(8,128)(2,1)S(1)}, bf16[36,768]{1,0:T(8,128)(2,1)S(1)}, u32[]{:S(2)}, u32[]{:S(2)}) collective-permute-start(bf16[36,768]{1,0:T(8,128)(2,1)S(1)} %get-tuple-element.96), channel_id=1, source_target_pairs={{28,0},{29,1},{30,2},{31,3},{0,4},{1,5},{2,6},{3,7},{4,8},{5,9},{6... | collective-permute-start | bytes 165896 | tf_op jit(solution)/shard_map/ppermute | solution.py:679
  40.0 0.0 collective-permute-done.5.same_here
  40.0 0.0 collective-permute-done.9.other_here
  40.0 1.2 %unpack_cells.1 = bf16[3,3,4,3072]{3,2,1,0:T(4,128)(2,1)} custom-call(bf16[36,768]{1,0:T(8,128)(2,1)S(1)} %collective-permute-done.5.same_here, bf16[36,768]{1,0:T(8,128)(2,1)S(1)} %collective-permute-done.7.same_next, bf16[36,768]{1,0:T(8,128)(2,1)S(1)} %collective-permute-done.9.other_here, bf16[36,768]{1,0:T(8,128)(2,1)S(1)} %collective-permute-done.6.other_next, ...), custom_call_target="tpu_custom_call" | custom-call | flops 1000000000 | bytes 1000000 | tf_op jit(solution)/shard_map/unpack_cells/pallas_call | solution.py:652
  41.1 2.8 %collective-permute-done.10.lat = bf16[36,768]{1,0:T(8,128)(2,1)S(1)} collective-permute-done((bf16[36,768]{1,0:T(8,128)(2,1)S(1)}, bf16[36,768]{1,0:T(8,128)(2,1)S(1)}, u32[]{:S(2)}, u32[]{:S(2)}) %collective-permute-start.10) | collective-permute-done | bytes 55328 | tf_op jit(solution)/shard_map/ppermute | solution.py:679
  43.9 1.6 %collective-permute-done.11.both = bf16[36,768]{1,0:T(8,128)(2,1)S(1)} collective-permute-done((bf16[36,768]{1,0:T(8,128)(2,1)S(1)}, bf16[36,768]{1,0:T(8,128)(2,1)S(1)}, u32[]{:S(2)}, u32[]{:S(2)}) %collective-permute-start.11) | collective-permute-done | bytes 55328 | tf_op jit(solution)/shard_map/ppermute | solution.py:679
  45.5 0.0 collective-permute-done.12.lon
  45.5 0.7 %unpack_tokens.1 = bf16[6,12,2,768]{3,2,1,0:T(2,128)(2,1)} custom-call(bf16[36,768]{1,0:T(8,128)(2,1)S(1)} %get-tuple-element.98.own, bf16[36,768]{1,0:T(8,128)(2,1)S(1)} %collective-permute-done.10.lat, bf16[36,768]{1,0:T(8,128)(2,1)S(1)} %collective-permute-done.12.lon, bf16[36,768]{1,0:T(8,128)(2,1)S(1)} %collective-permute-done.11.both), custom_call_target="tpu_custom_call" | custom-call | tf_op jit(solution)/shard_map/unpack_tokens/pallas_call | solution.py:610
Async XLA Ops:
  2.0 17.0 %collective-permute-start.1 = (bf16[36,768]{1,0:T(8,128)(2,1)S(1)}, bf16[36,768]{1,0:T(8,128)(2,1)S(1)}, u32[]{:S(2)}, u32[]{:S(2)}) collective-permute-start(bf16[36,768]{1,0:T(8,128)(2,1)S(1)} %get-tuple-element.54), channel_id=1, source_target_pairs={{0,2},{1,31},{2,0},{3,29},{4,6},{5,3},{6,4},{7,1},{8,10},{9,7},{10... | collective-permute-start | bytes 165896 | tf_op jit(solution)/shard_map/ppermute | solution.py:679
  6.0 13.0 %collective-permute-start = (bf16[72,768]{1,0:T(8,128)(2,1)S(1)}, bf16[72,768]{1,0:T(8,128)(2,1)S(1)}, u32[]{:S(2)}, u32[]{:S(2)}) collective-permute-start(bf16[72,768]{1,0:T(8,128)(2,1)S(1)} %get-tuple-element.53), channel_id=1, source_target_pairs={{0,30},{1,3},{2,28},{3,1},{4,2},{5,7},{6,0},{7,5},{8,6},{9,11},{10... | collective-permute-start | bytes 331784 | tf_op jit(solution)/shard_map/ppermute | solution.py:679
  7.4 11.6 %collective-permute-start.2 = (bf16[72,768]{1,0:T(8,128)(2,1)S(1)}, bf16[72,768]{1,0:T(8,128)(2,1)S(1)}, u32[]{:S(2)}, u32[]{:S(2)}) collective-permute-start(bf16[72,768]{1,0:T(8,128)(2,1)S(1)} %get-tuple-element.55), channel_id=1, source_target_pairs={{0,28},{1,29},{2,30},{3,31},{4,0},{5,1},{6,2},{7,3},{8,4},{9,5},{1... | collective-permute-start | bytes 331784 | tf_op jit(solution)/shard_map/ppermute | solution.py:679
  9.7 12.8 %collective-permute-start.3 = (bf16[36,768]{1,0:T(8,128)(2,1)S(1)}, bf16[36,768]{1,0:T(8,128)(2,1)S(1)}, u32[]{:S(2)}, u32[]{:S(2)}) collective-permute-start(bf16[36,768]{1,0:T(8,128)(2,1)S(1)} %get-tuple-element.76), channel_id=1, source_target_pairs={{0,29},{1,0},{2,31},{3,2},{4,1},{5,4},{6,3},{7,6},{8,5},{9,8},{10,... | collective-permute-start | bytes 165896 | tf_op jit(solution)/shard_map/ppermute | solution.py:679
  11.0 11.5 %collective-permute-start.4 = (bf16[36,768]{1,0:T(8,128)(2,1)S(1)}, bf16[36,768]{1,0:T(8,128)(2,1)S(1)}, u32[]{:S(2)}, u32[]{:S(2)}) collective-permute-start(bf16[36,768]{1,0:T(8,128)(2,1)S(1)} %get-tuple-element.77), channel_id=1, source_target_pairs={{0,31},{1,2},{2,29},{3,0},{4,3},{5,6},{6,1},{7,4},{8,7},{9,10},{10... | collective-permute-start | bytes 165896 | tf_op jit(solution)/shard_map/ppermute | solution.py:679
  13.0 6.0 %copy-start.1 = (bf16[768,2304]{1,0:T(8,128)(2,1)S(1)}, bf16[768,2304]{1,0:T(8,128)(2,1)}, u32[]{:S(2)}) copy-start(bf16[768,2304]{1,0:T(8,128)(2,1)} %packed.3) | copy-start | bytes 10616836
  13.0 6.0 %copy-start.2 = (bf16[768,768]{1,0:T(8,128)(2,1)S(1)}, bf16[768,768]{1,0:T(8,128)(2,1)}, u32[]{:S(2)}) copy-start(bf16[768,768]{1,0:T(8,128)(2,1)} %output.3) | copy-start | bytes 3538948
  13.0 6.0 %copy-start.3 = (f32[768]{0:T(1024)S(1)}, f32[768]{0:T(1024)}, u32[]{:S(2)}) copy-start(f32[768]{0:T(1024)} %gain.3) | copy-start | bytes 9220
  19.1 3.5 %copy-start = (f32[3072]{0:T(1024)S(1)}, f32[3072]{0:T(1024)}, u32[]{:S(2)}) copy-start(f32[3072]{0:T(1024)} %param.14) | copy-start | bytes 36868
  23.7 7.8 %collective-permute-start.8 = (f32[24,128]{1,0:T(8,128)S(1)}, f32[24,128]{1,0:T(8,128)S(1)}, u32[]{:S(2)}, u32[]{:S(2)}) collective-permute-start(f32[24,128]{1,0:T(8,128)S(1)} %get-tuple-element.83), channel_id=1, source_target_pairs={{0,2},{1,3},{2,0},{3,1},{4,6},{5,7},{6,4},{7,5},{8,10},{9,11},{10,... | collective-permute-start | bytes 36872 | tf_op jit(solution)/shard_map/ppermute | solution.py:679
  24.0 16.0 %collective-permute-start.5 = (bf16[36,768]{1,0:T(8,128)(2,1)S(1)}, bf16[36,768]{1,0:T(8,128)(2,1)S(1)}, u32[]{:S(2)}, u32[]{:S(2)}) collective-permute-start(bf16[36,768]{1,0:T(8,128)(2,1)S(1)} %get-tuple-element.78), channel_id=1, source_target_pairs={{28,0},{1,1},{30,2},{3,3},{0,4},{5,5},{2,6},{7,7},{4,8},{9,9},{6,1... | collective-permute-start | bytes 165896 | tf_op jit(solution)/shard_map/ppermute | solution.py:679
  26.6 9.8 %collective-permute-start.6 = (bf16[36,768]{1,0:T(8,128)(2,1)S(1)}, bf16[36,768]{1,0:T(8,128)(2,1)S(1)}, u32[]{:S(2)}, u32[]{:S(2)}) collective-permute-start(bf16[36,768]{1,0:T(8,128)(2,1)S(1)} %get-tuple-element.79), channel_id=1, source_target_pairs={{31,0},{2,1},{29,2},{0,3},{3,4},{6,5},{1,6},{4,7},{7,8},{10,9},{5,... | collective-permute-start | bytes 165896 | tf_op jit(solution)/shard_map/ppermute | solution.py:679
  27.6 9.0 %collective-permute-start.7 = (bf16[36,768]{1,0:T(8,128)(2,1)S(1)}, bf16[36,768]{1,0:T(8,128)(2,1)S(1)}, u32[]{:S(2)}, u32[]{:S(2)}) collective-permute-start(bf16[36,768]{1,0:T(8,128)(2,1)S(1)} %get-tuple-element.80), channel_id=1, source_target_pairs={{30,0},{3,1},{28,2},{1,3},{2,4},{7,5},{0,6},{5,7},{6,8},{11,9},{4,... | collective-permute-start | bytes 165896 | tf_op jit(solution)/shard_map/ppermute | solution.py:679
  29.6 10.3 %collective-permute-start.9 = (bf16[36,768]{1,0:T(8,128)(2,1)S(1)}, bf16[36,768]{1,0:T(8,128)(2,1)S(1)}, u32[]{:S(2)}, u32[]{:S(2)}) collective-permute-start(bf16[36,768]{1,0:T(8,128)(2,1)S(1)} %get-tuple-element.92), channel_id=1, source_target_pairs={{29,0},{0,1},{31,2},{2,3},{1,4},{4,5},{3,6},{6,7},{5,8},{8,9},{7,1... | collective-permute-start | bytes 165896 | tf_op jit(solution)/shard_map/ppermute | solution.py:679
  36.6 7.3 %collective-permute-start.10 = (bf16[36,768]{1,0:T(8,128)(2,1)S(1)}, bf16[36,768]{1,0:T(8,128)(2,1)S(1)}, u32[]{:S(2)}, u32[]{:S(2)}) collective-permute-start(bf16[36,768]{1,0:T(8,128)(2,1)S(1)} %get-tuple-element.94), channel_id=1, source_target_pairs={{2,0},{3,1},{0,2},{1,3},{6,4},{7,5},{4,6},{5,7},{10,8},{11,9},{8,1... | collective-permute-start | bytes 165896 | tf_op jit(solution)/shard_map/ppermute | solution.py:679
  38.0 7.5 %collective-permute-start.11 = (bf16[36,768]{1,0:T(8,128)(2,1)S(1)}, bf16[36,768]{1,0:T(8,128)(2,1)S(1)}, u32[]{:S(2)}, u32[]{:S(2)}) collective-permute-start(bf16[36,768]{1,0:T(8,128)(2,1)S(1)} %get-tuple-element.95), channel_id=1, source_target_pairs={{30,0},{31,1},{28,2},{29,3},{2,4},{3,5},{0,6},{1,7},{6,8},{7,9},{4... | collective-permute-start | bytes 165896 | tf_op jit(solution)/shard_map/ppermute | solution.py:679
  38.4 7.1 %collective-permute-start.12 = (bf16[36,768]{1,0:T(8,128)(2,1)S(1)}, bf16[36,768]{1,0:T(8,128)(2,1)S(1)}, u32[]{:S(2)}, u32[]{:S(2)}) collective-permute-start(bf16[36,768]{1,0:T(8,128)(2,1)S(1)} %get-tuple-element.96), channel_id=1, source_target_pairs={{28,0},{29,1},{30,2},{31,3},{0,4},{1,5},{2,6},{3,7},{4,8},{5,9},{6... | collective-permute-start | bytes 165896 | tf_op jit(solution)/shard_map/ppermute | solution.py:679

commit v11 on v10

--- a/solution.py
+++ b/solution.py
@@ -424,15 +424,6 @@
     return (places[0] == 0) | (places[0] == WLAT - 1)
 
 
-def sent_tokens(dims, axis):
-    i = lax.broadcasted_iota(jnp.int32, dims, axis)
-    last = (i >= 2 * CELLS).astype(jnp.int32)
-    i = i - last * 2 * CELLS
-    right = (i >= CELLS).astype(jnp.int32)
-    cell = i - right * CELLS
-    return (2 * right + last) * QUAD + last * (HALF_LAT - 1) * 2 * CELLS + cell
-
-
 def columns_of(parts):
     lane = lax.broadcasted_iota(jnp.int32, (1, 128), 1)
     out = jnp.zeros((WIN, 128), f32)
@@ -472,8 +463,8 @@
     lane = lax.broadcasted_iota(jnp.int32, (1, 128), 1)
     sums = jnp.where(lane == 3, middle, sums)
     moments[...] = sums
-    pick = sent_tokens((4 * CELLS, 1), 0) == lax.broadcasted_iota(jnp.int32, (4 * CELLS, WIN), 1)
-    sent[...] = exact(jnp.where(pick, 1.0, 0.0).astype(f32), sums)
+    starts = [token_row(quad, row, 0, 0) for quad, row in ((0, 0), (2, 0), (1, HALF_LAT - 1), (3, HALF_LAT - 1))]
+    sent[...] = jnp.concatenate([sums[at : at + CELLS] for at in starts], axis=0)
     scale = lax.rsqrt(sums[:, 0:1] * (1 / (4 * width)) + epsilon)
     out = jnp.where(split_row(down), data, center * scale * factors[...])
     parts = [quadrant(out, quad) for quad in range(4)]
@@ -500,11 +491,12 @@
     width = residual.shape[-1]
     down = token_places((WIN, 1), 0)
     shared = split_row(down)
-    row = down[0]
-    sender = split_tokens(sent_tokens((1, 4 * CELLS), 1))
-    match = (cell_number(down) == cell_number(sender)) & shared
     there = jnp.concatenate((before[2 * CELLS :], after[: 2 * CELLS]), axis=0)
-    theirs = exact(jnp.where(match, 1.0, 0.0).astype(f32), there)
+    none = jnp.zeros((QUAD - 2 * CELLS, there.shape[1]), f32)
+    parts = [there[i * CELLS : (i + 1) * CELLS] for i in range(4)]
+    theirs = jnp.concatenate(
+        (parts[0], parts[0], none, none, parts[2], parts[2], parts[1], parts[1], none, none, parts[3], parts[3]), axis=0
+    )
     mine = moments[...]
     full = 4.0 * width
     middle = jnp.where(shared, 0.5 * (mine[:, 3:4] + theirs[:, 3:4]), mine[:, 3:4])

time: 46.4 us -> 46.3 us (level)
  no operation moved by 1% of the time
where the time goes in v11:
time: 46.3 us; the launch traced here: 46.1 us
  starting transfers between devices  21.1 us (46%)
  Pallas kernels  19.7 us (43%)
  waiting for transfers between devices  4.57 us (10%)
  between operations  0.8 us (2%)
    ppermute x13, starting transfers between devices, send(): return lax.ppermute(block, ('lon', 'lat', 'lev'), pairs)  21.1 us
    pallas_call x1, Pallas kernels, window_bias(): pl.pallas_call(bias_kernel, out_shape=[shape((heads * WIN, 128), f32)] *...  5.98 us
    ppermute x13, waiting for transfers between devices, send(): return lax.ppermute(block, ('lon', 'lat', 'lev'), pairs)  4.57 us
    pallas_call x1, Pallas kernels, forward(): pl.pallas_call(forward_kernel, out_shape=[shape((HEADS * WIN, WIN), bf16)...  3.41 us
    pallas_call x1, Pallas kernels, backward(): pl.pallas_call(backward_kernel, out_shape=shape((WIN, 3 * width), bf16),...  2.81 us
    pallas_call x1, Pallas kernels, finish(): pl.pallas_call(finish_kernel, out_shape=[shape((QUAD, width), bf16)] * 4,...  1.52 us
    pallas_call x1, Pallas kernels, pack_pieces(): pl.pallas_call(pack_kernel, out_shape=[piece, double, piece, double, piec...  1.32 us
    pallas_call x1, Pallas kernels, unpack_cells(): pl.pallas_call(cell_kernel, out_shape=shape((HALF_LAT, PAIRS, 2 * LEVELS,...  1.18 us
  transfers between devices with their start and end apart: 13, of which 3 were waited for; matrix products, arithmetic and copies ran while one was open for 0% of the time, Pallas kernels for 36%

profile of v11, /device:TPU:0, one launch (start us, length us, event | category | flops | bytes accessed | tf_op | source)
XLA Modules:
  0.0 46.1 jit_solution(16530864596774892647)
XLA Ops:
  0.6 1.3 %pack.1 = (bf16[36,768]{1,0:T(8,128)(2,1)S(1)}, bf16[72,768]{1,0:T(8,128)(2,1)S(1)}, bf16[36,768]{1,0:T(8,128)(2,1)S(1)}, bf16[72,768]{1,0:T(8,128)(2,1)S(1)}, b...) custom-call(bf16[6,12,2,768]{3,2,1,0:T(2,128)(2,1)} %bitcast.7, ...), custom_call_target="tpu_custom_call" | custom-call | tf_op jit(solution)/shard_map/pack/pallas_call | solution.py:140
  2.0 4.1 %collective-permute-start.1 = (bf16[36,768]{1,0:T(8,128)(2,1)S(1)}, bf16[36,768]{1,0:T(8,128)(2,1)S(1)}, u32[]{:S(2)}, u32[]{:S(2)}) collective-permute-start(bf16[36,768]{1,0:T(8,128)(2,1)S(1)} %get-tuple-element.54), channel_id=1, source_target_pairs={{0,2},{1,31},{2,0},{3,29},{4,6},{5,3},{6,4},{7,1},{8,10},{9,7},{10... | collective-permute-start | bytes 165896 | tf_op jit(solution)/shard_map/ppermute | solution.py:671
  6.0 1.4 %collective-permute-start = (bf16[72,768]{1,0:T(8,128)(2,1)S(1)}, bf16[72,768]{1,0:T(8,128)(2,1)S(1)}, u32[]{:S(2)}, u32[]{:S(2)}) collective-permute-start(bf16[72,768]{1,0:T(8,128)(2,1)S(1)} %get-tuple-element.53), channel_id=1, source_target_pairs={{0,30},{1,3},{2,28},{3,1},{4,2},{5,7},{6,0},{7,5},{8,6},{9,11},{10... | collective-permute-start | bytes 331784 | tf_op jit(solution)/shard_map/ppermute | solution.py:671
  7.4 1.1 %collective-permute-start.2 = (bf16[72,768]{1,0:T(8,128)(2,1)S(1)}, bf16[72,768]{1,0:T(8,128)(2,1)S(1)}, u32[]{:S(2)}, u32[]{:S(2)}) collective-permute-start(bf16[72,768]{1,0:T(8,128)(2,1)S(1)} %get-tuple-element.55), channel_id=1, source_target_pairs={{0,28},{1,29},{2,30},{3,31},{4,0},{5,1},{6,2},{7,3},{8,4},{9,5},{1... | collective-permute-start | bytes 331784 | tf_op jit(solution)/shard_map/ppermute | solution.py:671
  8.5 1.2 %index.1 = (f32[162,128]{1,0:T(8,128)S(1)}, f32[162,128]{1,0:T(8,128)S(1)}, s32[162,128]{1,0:T(8,128)S(1)}, s32[162,128]{1,0:T(8,128)S(1)}, f32[144,128]{1,0:T(8,128)S(1)}, /*index=5*/f32[144,128]{1,0:T(8,128)S(1)}) custom-call(s32[144,144]{1,0:T(8,128)S(1)} %get-tuple-element.59.index, s32[6]{0:T(128)} %labels_at.1, s32[96]{0:T(128)} %valid_at.1), custom_call_target="tpu_custom_call" | custom-call | flops 100000000 | bytes 1000000 | tf_op jit(solution)/shard_map/index/pallas_call | solution.py:208
  9.7 1.2 %collective-permute-start.3 = (bf16[36,768]{1,0:T(8,128)(2,1)S(1)}, bf16[36,768]{1,0:T(8,128)(2,1)S(1)}, u32[]{:S(2)}, u32[]{:S(2)}) collective-permute-start(bf16[36,768]{1,0:T(8,128)(2,1)S(1)} %get-tuple-element.76), channel_id=1, source_target_pairs={{0,29},{1,0},{2,31},{3,2},{4,1},{5,4},{6,3},{7,6},{8,5},{9,8},{10,... | collective-permute-start | bytes 165896 | tf_op jit(solution)/shard_map/ppermute | solution.py:671
  11.0 2.1 %collective-permute-start.4 = (bf16[36,768]{1,0:T(8,128)(2,1)S(1)}, bf16[36,768]{1,0:T(8,128)(2,1)S(1)}, u32[]{:S(2)}, u32[]{:S(2)}) collective-permute-start(bf16[36,768]{1,0:T(8,128)(2,1)S(1)} %get-tuple-element.77), channel_id=1, source_target_pairs={{0,31},{1,2},{2,29},{3,0},{4,3},{5,6},{6,1},{7,4},{8,7},{9,10},{10... | collective-permute-start | bytes 165896 | tf_op jit(solution)/shard_map/ppermute | solution.py:671
  13.0 0.0 copy-start.1
  13.0 0.0 copy-start.2
  13.0 0.0 copy-start.3
  13.0 6.0 %bias.1 = (f32[3456,128]{1,0:T(8,128)S(1)}, f32[3456,128]{1,0:T(8,128)S(1)}) custom-call(f32[24,3312]{1,0:T(8,128)S(1)} %get-tuple-element.56.table, f32[162,128]{1,0:T(8,128)S(1)} %get-tuple-element.66.high, f32[162,128]{1,0:T(8,128)S(1)} %get-tuple-element.67.low, s32[162,128]{1,0:T(8,128)S(1)} %get-tuple-element.68.fine_high, ...), custom_call_target="tpu_custom_call" | custom-call | flops 10000000000 | bytes 20000000 | tf_op jit(solution)/shard_map/bias/pallas_call | solution.py:308
  19.0 0.0 collective-permute-done.1.second
  19.0 0.0 collective-permute-done.first
  19.0 0.0 collective-permute-done.2.third
  19.0 0.0 copy-done.1
  19.0 0.0 copy-done.2
  19.0 0.0 copy-done.3
  19.1 0.0 copy-start
  19.1 3.4 %forward.1 = (bf16[3456,144]{1,0:T(8,128)(2,1)S(1)}, bf16[144,2304]{1,0:T(8,128)(2,1)S(1)}, bf16[768,144]{1,0:T(8,128)(2,1)S(1)}, bf16[144,768]{1,0:T(8,128)(2,1)S(1)}, bf16[144,768]{1,0:T(8,128)(2,1)S(1)}) custom-call(bf16[36,768]{1,0:T(8,128)(2,1)S(1)} %get-tuple-element.52.own, bf16[72,768]{1,0:T(8,128)(2,1)S(1)} %collective-permute-done.first, ...), custom_call_target="tpu_custom_call" | custom-call | flops 10000000000 | bytes 20000000 | tf_op jit(solution)/shard_map/forward/pallas_call | solution.py:385
  22.5 0.0 collective-permute-done.3.fourth
  22.5 0.0 collective-permute-done.4.fifth
  22.5 0.0 copy-done
  22.5 1.2 %moments.1 = (f32[144,768]{1,0:T(8,128)S(1)}, f32[144,128]{1,0:T(8,128)S(1)}, f32[24,128]{1,0:T(8,128)S(1)}, bf16[36,768]{1,0:T(8,128)(2,1)S(1)}, bf16[36,768]{1...) custom-call(bf16[144,768]{1,0:T(8,128)(2,1)S(1)} %get-tuple-element.74.residual, ...), custom_call_target="tpu_custom_call" | custom-call | flops 100000000 | bytes 1000000 | tf_op jit(solution)/shard_map/moments/pallas_call | solution.py:479
  23.7 0.3 collective-permute-start.8
  24.0 2.7 %collective-permute-start.5 = (bf16[36,768]{1,0:T(8,128)(2,1)S(1)}, bf16[36,768]{1,0:T(8,128)(2,1)S(1)}, u32[]{:S(2)}, u32[]{:S(2)}) collective-permute-start(bf16[36,768]{1,0:T(8,128)(2,1)S(1)} %get-tuple-element.78), channel_id=1, source_target_pairs={{28,0},{1,1},{30,2},{3,3},{0,4},{5,5},{2,6},{7,7},{4,8},{9,9},{6,1... | collective-permute-start | bytes 165896 | tf_op jit(solution)/shard_map/ppermute | solution.py:671
  26.6 1.0 %collective-permute-start.6 = (bf16[36,768]{1,0:T(8,128)(2,1)S(1)}, bf16[36,768]{1,0:T(8,128)(2,1)S(1)}, u32[]{:S(2)}, u32[]{:S(2)}) collective-permute-start(bf16[36,768]{1,0:T(8,128)(2,1)S(1)} %get-tuple-element.79), channel_id=1, source_target_pairs={{31,0},{2,1},{29,2},{0,3},{3,4},{6,5},{1,6},{4,7},{7,8},{10,9},{5,... | collective-permute-start | bytes 165896 | tf_op jit(solution)/shard_map/ppermute | solution.py:671
  27.6 2.0 %collective-permute-start.7 = (bf16[36,768]{1,0:T(8,128)(2,1)S(1)}, bf16[36,768]{1,0:T(8,128)(2,1)S(1)}, u32[]{:S(2)}, u32[]{:S(2)}) collective-permute-start(bf16[36,768]{1,0:T(8,128)(2,1)S(1)} %get-tuple-element.80), channel_id=1, source_target_pairs={{30,0},{3,1},{28,2},{1,3},{2,4},{7,5},{0,6},{5,7},{6,8},{11,9},{4,... | collective-permute-start | bytes 165896 | tf_op jit(solution)/shard_map/ppermute | solution.py:671
  29.6 1.9 %collective-permute-start.9 = (bf16[36,768]{1,0:T(8,128)(2,1)S(1)}, bf16[36,768]{1,0:T(8,128)(2,1)S(1)}, u32[]{:S(2)}, u32[]{:S(2)}) collective-permute-start(bf16[36,768]{1,0:T(8,128)(2,1)S(1)} %get-tuple-element.92), channel_id=1, source_target_pairs={{29,0},{0,1},{31,2},{2,3},{1,4},{4,5},{3,6},{6,7},{5,8},{8,9},{7,1... | collective-permute-start | bytes 165896 | tf_op jit(solution)/shard_map/ppermute | solution.py:671
  31.5 0.0 collective-permute-done.8.before.after
  31.5 0.4 merge.1.grad
  31.9 2.8 %backward.1.joined = bf16[144,2304]{1,0:T(8,128)(2,1)S(1)} custom-call(bf16[144,768]{1,0:T(8,128)(2,1)S(1)} %merge.1.grad, bf16[3456,144]{1,0:T(8,128)(2,1)S(1)} %get-tuple-element.84.weights, bf16[144,2304]{1,0:T(8,128)(2,1)S(1)} %get-tuple-element.85.triple, bf16[768,144]{1,0:T(8,128)(2,1)S(1)} %get-tuple-element.86.keys_t, bf16[768,768]{1,0:T(8,128)(2,1)S(1)} %copy-done.2), custom_call_target="tpu_custom_call" | custom-call | flops 10000000000 | bytes 20000000 | tf_op jit(solution)/shard_map/backward/pallas_call | solution.py:560
  34.7 1.5 %finish.1 = (bf16[36,768]{1,0:T(8,128)(2,1)S(1)}, bf16[36,768]{1,0:T(8,128)(2,1)S(1)}, bf16[36,768]{1,0:T(8,128)(2,1)S(1)}, bf16[36,768]{1,0:T(8,128)(2,1)S(1)}) custom-call(bf16[144,768]{1,0:T(8,128)(2,1)S(1)} %merge.1.grad, bf16[144,2304]{1,0:T(8,128)(2,1)S(1)} %backward.1.joined, bf16[144,768]{1,0:T(8,128)(2,1)S(1)} %get-tuple-element.87.tokens, ...), custom_call_target="tpu_custom_call" | custom-call | flops 10000000000 | bytes 2000000 | tf_op jit(solution)/shard_map/finish/pallas_call | solution.py:581
  36.3 0.0 collective-permute-done.6.other_next
  36.3 0.3 collective-permute-done.7.same_next
  36.6 1.3 %collective-permute-start.10 = (bf16[36,768]{1,0:T(8,128)(2,1)S(1)}, bf16[36,768]{1,0:T(8,128)(2,1)S(1)}, u32[]{:S(2)}, u32[]{:S(2)}) collective-permute-start(bf16[36,768]{1,0:T(8,128)(2,1)S(1)} %get-tuple-element.94), channel_id=1, source_target_pairs={{2,0},{3,1},{0,2},{1,3},{6,4},{7,5},{4,6},{5,7},{10,8},{11,9},{8,1... | collective-permute-start | bytes 165896 | tf_op jit(solution)/shard_map/ppermute | solution.py:671
  37.9 0.6 %collective-permute-start.11 = (bf16[36,768]{1,0:T(8,128)(2,1)S(1)}, bf16[36,768]{1,0:T(8,128)(2,1)S(1)}, u32[]{:S(2)}, u32[]{:S(2)}) collective-permute-start(bf16[36,768]{1,0:T(8,128)(2,1)S(1)} %get-tuple-element.95), channel_id=1, source_target_pairs={{30,0},{31,1},{28,2},{29,3},{2,4},{3,5},{0,6},{1,7},{6,8},{7,9},{4... | collective-permute-start | bytes 165896 | tf_op jit(solution)/shard_map/ppermute | solution.py:671
  38.4 1.5 %collective-permute-start.12 = (bf16[36,768]{1,0:T(8,128)(2,1)S(1)}, bf16[36,768]{1,0:T(8,128)(2,1)S(1)}, u32[]{:S(2)}, u32[]{:S(2)}) collective-permute-start(bf16[36,768]{1,0:T(8,128)(2,1)S(1)} %get-tuple-element.96), channel_id=1, source_target_pairs={{28,0},{29,1},{30,2},{31,3},{0,4},{1,5},{2,6},{3,7},{4,8},{5,9},{6... | collective-permute-start | bytes 165896 | tf_op jit(solution)/shard_map/ppermute | solution.py:671
  40.0 0.0 collective-permute-done.5.same_here
  40.0 0.0 collective-permute-done.9.other_here
  40.0 1.2 %unpack_cells.1 = bf16[3,3,4,3072]{3,2,1,0:T(4,128)(2,1)} custom-call(bf16[36,768]{1,0:T(8,128)(2,1)S(1)} %collective-permute-done.5.same_here, bf16[36,768]{1,0:T(8,128)(2,1)S(1)} %collective-permute-done.7.same_next, bf16[36,768]{1,0:T(8,128)(2,1)S(1)} %collective-permute-done.9.other_here, bf16[36,768]{1,0:T(8,128)(2,1)S(1)} %collective-permute-done.6.other_next, ...), custom_call_target="tpu_custom_call" | custom-call | flops 1000000000 | bytes 1000000 | tf_op jit(solution)/shard_map/unpack_cells/pallas_call | solution.py:644
  41.2 2.6 %collective-permute-done.10.lat = bf16[36,768]{1,0:T(8,128)(2,1)S(1)} collective-permute-done((bf16[36,768]{1,0:T(8,128)(2,1)S(1)}, bf16[36,768]{1,0:T(8,128)(2,1)S(1)}, u32[]{:S(2)}, u32[]{:S(2)}) %collective-permute-start.10) | collective-permute-done | bytes 55328 | tf_op jit(solution)/shard_map/ppermute | solution.py:671
  43.8 1.6 %collective-permute-done.11.both = bf16[36,768]{1,0:T(8,128)(2,1)S(1)} collective-permute-done((bf16[36,768]{1,0:T(8,128)(2,1)S(1)}, bf16[36,768]{1,0:T(8,128)(2,1)S(1)}, u32[]{:S(2)}, u32[]{:S(2)}) %collective-permute-start.11) | collective-permute-done | bytes 55328 | tf_op jit(solution)/shard_map/ppermute | solution.py:671
  45.4 0.0 collective-permute-done.12.lon
  45.4 0.7 %unpack_tokens.1 = bf16[6,12,2,768]{3,2,1,0:T(2,128)(2,1)} custom-call(bf16[36,768]{1,0:T(8,128)(2,1)S(1)} %get-tuple-element.98.own, bf16[36,768]{1,0:T(8,128)(2,1)S(1)} %collective-permute-done.10.lat, bf16[36,768]{1,0:T(8,128)(2,1)S(1)} %collective-permute-done.12.lon, bf16[36,768]{1,0:T(8,128)(2,1)S(1)} %collective-permute-done.11.both), custom_call_target="tpu_custom_call" | custom-call | tf_op jit(solution)/shard_map/unpack_tokens/pallas_call | solution.py:602
Async XLA Ops:
  2.0 17.0 %collective-permute-start.1 = (bf16[36,768]{1,0:T(8,128)(2,1)S(1)}, bf16[36,768]{1,0:T(8,128)(2,1)S(1)}, u32[]{:S(2)}, u32[]{:S(2)}) collective-permute-start(bf16[36,768]{1,0:T(8,128)(2,1)S(1)} %get-tuple-element.54), channel_id=1, source_target_pairs={{0,2},{1,31},{2,0},{3,29},{4,6},{5,3},{6,4},{7,1},{8,10},{9,7},{10... | collective-permute-start | bytes 165896 | tf_op jit(solution)/shard_map/ppermute | solution.py:671
  6.0 13.0 %collective-permute-start = (bf16[72,768]{1,0:T(8,128)(2,1)S(1)}, bf16[72,768]{1,0:T(8,128)(2,1)S(1)}, u32[]{:S(2)}, u32[]{:S(2)}) collective-permute-start(bf16[72,768]{1,0:T(8,128)(2,1)S(1)} %get-tuple-element.53), channel_id=1, source_target_pairs={{0,30},{1,3},{2,28},{3,1},{4,2},{5,7},{6,0},{7,5},{8,6},{9,11},{10... | collective-permute-start | bytes 331784 | tf_op jit(solution)/shard_map/ppermute | solution.py:671
  7.4 11.6 %collective-permute-start.2 = (bf16[72,768]{1,0:T(8,128)(2,1)S(1)}, bf16[72,768]{1,0:T(8,128)(2,1)S(1)}, u32[]{:S(2)}, u32[]{:S(2)}) collective-permute-start(bf16[72,768]{1,0:T(8,128)(2,1)S(1)} %get-tuple-element.55), channel_id=1, source_target_pairs={{0,28},{1,29},{2,30},{3,31},{4,0},{5,1},{6,2},{7,3},{8,4},{9,5},{1... | collective-permute-start | bytes 331784 | tf_op jit(solution)/shard_map/ppermute | solution.py:671
  9.7 12.8 %collective-permute-start.3 = (bf16[36,768]{1,0:T(8,128)(2,1)S(1)}, bf16[36,768]{1,0:T(8,128)(2,1)S(1)}, u32[]{:S(2)}, u32[]{:S(2)}) collective-permute-start(bf16[36,768]{1,0:T(8,128)(2,1)S(1)} %get-tuple-element.76), channel_id=1, source_target_pairs={{0,29},{1,0},{2,31},{3,2},{4,1},{5,4},{6,3},{7,6},{8,5},{9,8},{10,... | collective-permute-start | bytes 165896 | tf_op jit(solution)/shard_map/ppermute | solution.py:671
  11.0 11.5 %collective-permute-start.4 = (bf16[36,768]{1,0:T(8,128)(2,1)S(1)}, bf16[36,768]{1,0:T(8,128)(2,1)S(1)}, u32[]{:S(2)}, u32[]{:S(2)}) collective-permute-start(bf16[36,768]{1,0:T(8,128)(2,1)S(1)} %get-tuple-element.77), channel_id=1, source_target_pairs={{0,31},{1,2},{2,29},{3,0},{4,3},{5,6},{6,1},{7,4},{8,7},{9,10},{10... | collective-permute-start | bytes 165896 | tf_op jit(solution)/shard_map/ppermute | solution.py:671
  13.0 6.0 %copy-start.1 = (bf16[768,2304]{1,0:T(8,128)(2,1)S(1)}, bf16[768,2304]{1,0:T(8,128)(2,1)}, u32[]{:S(2)}) copy-start(bf16[768,2304]{1,0:T(8,128)(2,1)} %packed.3) | copy-start | bytes 10616836
  13.0 6.0 %copy-start.2 = (bf16[768,768]{1,0:T(8,128)(2,1)S(1)}, bf16[768,768]{1,0:T(8,128)(2,1)}, u32[]{:S(2)}) copy-start(bf16[768,768]{1,0:T(8,128)(2,1)} %output.3) | copy-start | bytes 3538948
  13.0 6.0 %copy-start.3 = (f32[768]{0:T(1024)S(1)}, f32[768]{0:T(1024)}, u32[]{:S(2)}) copy-start(f32[768]{0:T(1024)} %gain.3) | copy-start | bytes 9220
  19.1 3.5 %copy-start = (f32[3072]{0:T(1024)S(1)}, f32[3072]{0:T(1024)}, u32[]{:S(2)}) copy-start(f32[3072]{0:T(1024)} %param.14) | copy-start | bytes 36868
  23.7 7.8 %collective-permute-start.8 = (f32[24,128]{1,0:T(8,128)S(1)}, f32[24,128]{1,0:T(8,128)S(1)}, u32[]{:S(2)}, u32[]{:S(2)}) collective-permute-start(f32[24,128]{1,0:T(8,128)S(1)} %get-tuple-element.83), channel_id=1, source_target_pairs={{0,2},{1,3},{2,0},{3,1},{4,6},{5,7},{6,4},{7,5},{8,10},{9,11},{10,... | collective-permute-start | bytes 36872 | tf_op jit(solution)/shard_map/ppermute | solution.py:671
  24.0 16.0 %collective-permute-start.5 = (bf16[36,768]{1,0:T(8,128)(2,1)S(1)}, bf16[36,768]{1,0:T(8,128)(2,1)S(1)}, u32[]{:S(2)}, u32[]{:S(2)}) collective-permute-start(bf16[36,768]{1,0:T(8,128)(2,1)S(1)} %get-tuple-element.78), channel_id=1, source_target_pairs={{28,0},{1,1},{30,2},{3,3},{0,4},{5,5},{2,6},{7,7},{4,8},{9,9},{6,1... | collective-permute-start | bytes 165896 | tf_op jit(solution)/shard_map/ppermute | solution.py:671
  26.6 9.6 %collective-permute-start.6 = (bf16[36,768]{1,0:T(8,128)(2,1)S(1)}, bf16[36,768]{1,0:T(8,128)(2,1)S(1)}, u32[]{:S(2)}, u32[]{:S(2)}) collective-permute-start(bf16[36,768]{1,0:T(8,128)(2,1)S(1)} %get-tuple-element.79), channel_id=1, source_target_pairs={{31,0},{2,1},{29,2},{0,3},{3,4},{6,5},{1,6},{4,7},{7,8},{10,9},{5,... | collective-permute-start | bytes 165896 | tf_op jit(solution)/shard_map/ppermute | solution.py:671
  27.6 9.0 %collective-permute-start.7 = (bf16[36,768]{1,0:T(8,128)(2,1)S(1)}, bf16[36,768]{1,0:T(8,128)(2,1)S(1)}, u32[]{:S(2)}, u32[]{:S(2)}) collective-permute-start(bf16[36,768]{1,0:T(8,128)(2,1)S(1)} %get-tuple-element.80), channel_id=1, source_target_pairs={{30,0},{3,1},{28,2},{1,3},{2,4},{7,5},{0,6},{5,7},{6,8},{11,9},{4,... | collective-permute-start | bytes 165896 | tf_op jit(solution)/shard_map/ppermute | solution.py:671
  29.6 10.3 %collective-permute-start.9 = (bf16[36,768]{1,0:T(8,128)(2,1)S(1)}, bf16[36,768]{1,0:T(8,128)(2,1)S(1)}, u32[]{:S(2)}, u32[]{:S(2)}) collective-permute-start(bf16[36,768]{1,0:T(8,128)(2,1)S(1)} %get-tuple-element.92), channel_id=1, source_target_pairs={{29,0},{0,1},{31,2},{2,3},{1,4},{4,5},{3,6},{6,7},{5,8},{8,9},{7,1... | collective-permute-start | bytes 165896 | tf_op jit(solution)/shard_map/ppermute | solution.py:671
  36.6 7.2 %collective-permute-start.10 = (bf16[36,768]{1,0:T(8,128)(2,1)S(1)}, bf16[36,768]{1,0:T(8,128)(2,1)S(1)}, u32[]{:S(2)}, u32[]{:S(2)}) collective-permute-start(bf16[36,768]{1,0:T(8,128)(2,1)S(1)} %get-tuple-element.94), channel_id=1, source_target_pairs={{2,0},{3,1},{0,2},{1,3},{6,4},{7,5},{4,6},{5,7},{10,8},{11,9},{8,1... | collective-permute-start | bytes 165896 | tf_op jit(solution)/shard_map/ppermute | solution.py:671
  37.9 7.5 %collective-permute-start.11 = (bf16[36,768]{1,0:T(8,128)(2,1)S(1)}, bf16[36,768]{1,0:T(8,128)(2,1)S(1)}, u32[]{:S(2)}, u32[]{:S(2)}) collective-permute-start(bf16[36,768]{1,0:T(8,128)(2,1)S(1)} %get-tuple-element.95), channel_id=1, source_target_pairs={{30,0},{31,1},{28,2},{29,3},{2,4},{3,5},{0,6},{1,7},{6,8},{7,9},{4... | collective-permute-start | bytes 165896 | tf_op jit(solution)/shard_map/ppermute | solution.py:671
  38.4 6.9 %collective-permute-start.12 = (bf16[36,768]{1,0:T(8,128)(2,1)S(1)}, bf16[36,768]{1,0:T(8,128)(2,1)S(1)}, u32[]{:S(2)}, u32[]{:S(2)}) collective-permute-start(bf16[36,768]{1,0:T(8,128)(2,1)S(1)} %get-tuple-element.96), channel_id=1, source_target_pairs={{28,0},{29,1},{30,2},{31,3},{0,4},{1,5},{2,6},{3,7},{4,8},{5,9},{6... | collective-permute-start | bytes 165896 | tf_op jit(solution)/shard_map/ppermute | solution.py:671
